TPU v7x, 256 devices: a whole 4x4x8 slice. The times are simulated.
256 devices in a mesh: shot: 2 (over x_lo), space: 128 (over z, x_hi, y, core).
Axes of the slice: x: 4 (x_hi: 2, x_lo: 2; x = x_hi * 2 + x_lo), y: 4, z: 8, core: 2. Of those that a mesh axis runs over, the one named last changes fastest.
Arguments:
- pressure_now: float32 [4, 128, 4, 128, 128], P('shot', 'space'), may hold values from -6 to 6
- pressure_old: float32 [4, 128, 4, 128, 128], P('shot', 'space'), may hold values from -6 to 6
- auxiliary_now: float32 [4, 128, 4, 128, 128], P('shot', 'space'), may hold values from -6 to 6
- auxiliary_old: float32 [4, 128, 4, 128, 128], P('shot', 'space'), may hold values from -6 to 6
- velocity: float32 [128, 4, 128, 128], P('space', 'shot'), may hold values from 1.5 to 4
- epsilon_field: float32 [128, 4, 128, 128], P('space', 'shot'), may hold values from 0.1 to 0.3
- delta_field: float32 [128, 4, 128, 128], P('space', 'shot'), may hold values from 0 to 0.1
- active_blocks: int32 [4, 128], P('shot', 'space'), may hold values 0 or 1
- source_cells: int32 [4], P('shot'), may hold values from 0 to 8388607
- receiver_cells: int32 [4, 256], P('shot'), may hold values from 0 to 8388607
- wavelet: float32 [4, 4], P('shot'), may hold values from -4 to 4
Outputs:
- pressure_final: float32 [4, 128, 4, 128, 128], P('shot', 'space')
- auxiliary_final: float32 [4, 128, 4, 128, 128], P('shot', 'space')
- traces: float32 [4, 4, 256], P('shot')
Inputs may be any that keep to these rules, and one draw needn't show every extreme that they name: `source_cells`: cell numbers of the aperture. `receiver_cells`: cell numbers of the aperture.
All inputs are finite; a program needn't handle non-finite values. No bound on the sum of `active_blocks` on one device may be relied on, other than what follows from the above.
Results may differ from a plain program's by a relative error of at most 0.00002.
Values sent between devices are 32-bit elements; how exact they have to be, the bound alone decides.
No kernel may reach another device: no remote copies, remote signals or barrier semaphores. Data moves between devices by JAX's collectives and lax.ppermute only.
A program may use at most 64 MiB of HBM per device.

v0:
```python
import jax
import jax.numpy as jnp
from jax import lax
from jax.sharding import PartitionSpec as P

STEPS = 4


stencil_taps = (-205.0 / 72.0, 8.0 / 5.0, -1.0 / 5.0, 8.0 / 315.0, -1.0 / 560.0)
step_ratio = 0.08


def passed_along(value, axis, by):
    count = lax.axis_size(axis)
    pairs = [(i, i + by) for i in range(count) if 0 <= i + by < count]
    return lax.ppermute(value, axis, pairs)


def second_diff(padded, along, length):

    def window(offset):
        return lax.slice_in_dim(padded, 4 + offset, 4 + offset + length, axis=along)

    summed = stencil_taps[0] * window(0)
    for offset in range(1, 5):
        summed = summed + stencil_taps[offset] * (window(offset) + window(-offset))
    return summed


def padded_fields(pressure, auxiliary):
    lower_x = passed_along(pressure, "space", 1)
    upper_x = passed_along(pressure, "space", -1)
    padded_x = jnp.concatenate([lower_x, pressure, upper_x], axis=1)
    padded_y = jnp.pad(pressure, ((0, 0), (0, 0), (4, 4), (0, 0)))
    padded_z = jnp.pad(auxiliary, ((0, 0), (0, 0), (0, 0), (4, 4)))
    return (padded_x, padded_y, padded_z)


def advance(state, padded, medium, source_local, source_gain, live_mask):
    pressure, pressure_prev, auxiliary, auxiliary_prev = state
    padded_x, padded_y, padded_z = padded
    courant, stretch, coupling = medium
    horizontal = second_diff(padded_x, 1, pressure.shape[1]) + second_diff(
        padded_y, 2, pressure.shape[2]
    )
    vertical = second_diff(padded_z, 3, auxiliary.shape[3])
    new_p = 2.0 * pressure - pressure_prev + courant * (stretch * horizontal + coupling * vertical)
    new_q = 2.0 * auxiliary - auxiliary_prev + courant * (coupling * horizontal + vertical)
    count = pressure.shape[0]
    shape_now = pressure.shape
    rows = jnp.arange(count, dtype=jnp.int32)
    new_p = new_p.reshape(count, -1).at[rows, source_local].add(source_gain).reshape(shape_now)
    new_q = new_q.reshape(count, -1).at[rows, source_local].add(source_gain).reshape(shape_now)
    gains = live_mask[:, None, None, None]
    return (new_p * gains, new_q * gains)


def per_device(
    pressure_now,
    pressure_old,
    auxiliary_now,
    auxiliary_old,
    velocity,
    epsilon_field,
    delta_field,
    active_blocks,
    source_cells,
    receiver_cells,
    wavelet,
):
    shots = pressure_now.shape[0]
    rows_x, rows_y, rows_z = (pressure_now.shape[2], pressure_now.shape[3], pressure_now.shape[4])
    cells = rows_x * rows_y * rows_z
    position = lax.axis_index("space")
    speed, aniso_eps, aniso_delta = (
        lax.all_gather(velocity, "shot", axis=1, tiled=True),
        lax.all_gather(epsilon_field, "shot", axis=1, tiled=True),
        lax.all_gather(delta_field, "shot", axis=1, tiled=True),
    )
    courant = (speed[0] * step_ratio) ** 2
    stretch = 1.0 + 2.0 * aniso_eps[0]
    coupling = jnp.sqrt(1.0 + 2.0 * aniso_delta[0])
    medium = (courant, stretch, coupling)
    source_block = source_cells // cells
    source_here = (source_block == position).astype(jnp.float32)
    live_all = jnp.maximum(
        active_blocks[:, 0], (source_block == position).astype(jnp.int32)
    ).astype(jnp.float32)
    source_local = source_cells % cells
    receiver_here = (receiver_cells // cells == position).astype(jnp.float32)
    receiver_local = receiver_cells % cells
    fields = [
        member.reshape(shots, rows_x, rows_y, rows_z) * live_all[:, None, None, None]
        for member in (pressure_now, pressure_old, auxiliary_now, auxiliary_old)
    ]
    groups = [(0, shots)]
    states = [tuple((member for member in fields)) for start, stop in groups]
    recorded = [[] for start, stop in groups]
    for time_step in range(STEPS):
        start, stop = groups[0]
        state = states[0]
        padded = padded_fields(state[0], state[2])
        gains_now = wavelet[start:stop, time_step] * source_here
        new_p, new_q = advance(state, padded, medium, source_local, gains_now, live_all)
        sampled = jnp.take_along_axis(new_p.reshape(stop - start, cells), receiver_local, axis=1)
        recorded[0].append(sampled * receiver_here)
        states[0] = (new_p, state[0], new_q, state[2])
    local_traces = jnp.concatenate([jnp.stack(samples, axis=1) for samples in recorded], axis=0)
    traces = lax.psum(local_traces, "space")
    pressure_final = jnp.concatenate([state[0] for state in states], axis=0).reshape(
        shots, 1, rows_x, rows_y, rows_z
    )
    auxiliary_final = jnp.concatenate([state[2] for state in states], axis=0).reshape(
        shots, 1, rows_x, rows_y, rows_z
    )
    return (pressure_final, auxiliary_final, traces)


def solution(mesh):
    return jax.shard_map(
        per_device,
        mesh=mesh,
        in_specs=(
            P("shot", "space", None, None, None),
            P("shot", "space", None, None, None),
            P("shot", "space", None, None, None),
            P("shot", "space", None, None, None),
            P("space", "shot", None, None),
            P("space", "shot", None, None),
            P("space", "shot", None, None),
            P("shot", "space"),
            P("shot"),
            P("shot", None),
            P("shot", None),
        ),
        out_specs=(
            P("shot", "space", None, None, None),
            P("shot", "space", None, None, None),
            P("shot", None, None),
        ),
        check_vma=False,
    )
```

profile of v0, /device:TPU:128, one launch (start us, length us, event | category | flops | bytes accessed | tf_op | source)
XLA Modules:
  0.0 473.6 jit_solution(8549668667365122625)
XLA Ops:
  2.9 1.4 bitcast_multiply_fusion.3
  4.3 6.4 %collective-permute-start = (f32[2,4,128,128]{3,2,1,0:T(8,128)S(1)}, f32[2,4,128,128]{3,2,1,0:T(8,128)S(1)}, u32[]{:S(2)}, u32[]{:S(2)}) collective-permute-start(f32[2,4,128,128]{3,2,1,0:T(8,128)S(1)} %get-tuple-element.52), channel_id=1, source_target_pairs={{1,0},{2,1},{3,2},{4,3},{5,4},{6,5},{7,6},{8,7},{9,8},{10,9},{11,1... | collective-permute-start | bytes 1572872 | tf_op jit(solution)/shard_map/ppermute | solution.py:16
  10.7 1.9 collective-permute-start.1
  12.6 8.9 %all_gather.9 = f32[1,4,128,128]{3,2,0,1:T(8,128)S(1)} all-gather(f32[1,2,128,128]{3,2,0,1:T(8,128)S(1)} %bitcast.155), channel_id=1, replica_groups=mesh['shot'=2,'space'=128] {'shot'}, dimensions={1}, use_global_device_ids=true | all-gather | bytes 393216 | tf_op jit(solution)/shard_map/all_gather | solution.py:76
  22.5 5.8 %all_gather.11 = f32[1,4,128,128]{3,2,0,1:T(8,128)S(1)} all-gather(f32[1,2,128,128]{3,2,0,1:T(8,128)S(1)} %bitcast.156), channel_id=1, replica_groups=mesh['shot'=2,'space'=128] {'shot'}, dimensions={1}, use_global_device_ids=true | all-gather | bytes 393216 | tf_op jit(solution)/shard_map/all_gather | solution.py:78
  28.2 5.6 %all_gather.10 = f32[1,4,128,128]{3,2,0,1:T(8,128)S(1)} all-gather(f32[1,2,128,128]{3,2,0,1:T(8,128)S(1)} %bitcast.157), channel_id=1, replica_groups=mesh['shot'=2,'space'=128] {'shot'}, dimensions={1}, use_global_device_ids=true | all-gather | bytes 393216 | tf_op jit(solution)/shard_map/all_gather | solution.py:77
  34.9 1.5 fusion.111
  40.8 8.4 %collective-permute-start.2 = (f32[2,4,128,128]{3,2,1,0:T(8,128)S(1)}, f32[2,4,128,128]{3,2,1,0:T(8,128)S(1)}, u32[]{:S(2)}, u32[]{:S(2)}) collective-permute-start(f32[2,4,128,128]{3,2,1,0:T(8,128)S(1)} %get-tuple-element.50), channel_id=1, source_target_pairs={{1,0},{2,1},{3,2},{4,3},{5,4},{6,5},{7,6},{8,7},{9,8},{10,9},{11,1... | collective-permute-start | bytes 1572872 | tf_op jit(solution)/shard_map/ppermute | solution.py:16
  49.2 1.9 collective-permute-start.3
  51.2 4.7 %collective-permute-done.2 = f32[2,4,128,128]{3,2,1,0:T(8,128)S(1)} collective-permute-done((f32[2,4,128,128]{3,2,1,0:T(8,128)S(1)}, f32[2,4,128,128]{3,2,1,0:T(8,128)S(1)}, u32[]{:S(2)}, u32[]{:S(2)}) %collective-permute-start.2) | collective-permute-done | bytes 524320 | tf_op jit(solution)/shard_map/ppermute | solution.py:16
  55.9 9.5 %collective-permute-done.3 = f32[2,4,128,128]{3,2,1,0:T(8,128)S(1)} collective-permute-done((f32[2,4,128,128]{3,2,1,0:T(8,128)S(1)}, f32[2,4,128,128]{3,2,1,0:T(8,128)S(1)}, u32[]{:S(2)}, u32[]{:S(2)}) %collective-permute-start.3) | collective-permute-done | bytes 524320 | tf_op jit(solution)/shard_map/ppermute | solution.py:16
  65.4 2.1 multiply_add_fusion.5
  72.2 1.9 collective-permute-start.4
  74.2 2.4 collective-permute-start.5
  76.6 4.3 collective-permute-done.4
  80.8 9.5 %collective-permute-done.5 = f32[2,4,128,128]{3,2,1,0:T(8,128)S(1)} collective-permute-done((f32[2,4,128,128]{3,2,1,0:T(8,128)S(1)}, f32[2,4,128,128]{3,2,1,0:T(8,128)S(1)}, u32[]{:S(2)}, u32[]{:S(2)}) %collective-permute-start.5) | collective-permute-done | bytes 524320 | tf_op jit(solution)/shard_map/ppermute | solution.py:16
  90.4 2.1 multiply_add_fusion.3
  96.8 1.9 collective-permute-start.6
  98.7 2.6 collective-permute-start.7
  101.3 4.0 collective-permute-done.6
  105.4 9.5 %collective-permute-done.7 = f32[2,4,128,128]{3,2,1,0:T(8,128)S(1)} collective-permute-done((f32[2,4,128,128]{3,2,1,0:T(8,128)S(1)}, f32[2,4,128,128]{3,2,1,0:T(8,128)S(1)}, u32[]{:S(2)}, u32[]{:S(2)}) %collective-permute-start.7) | collective-permute-done | bytes 524320 | tf_op jit(solution)/shard_map/ppermute | solution.py:16
  114.9 2.1 multiply_add_fusion
  117.2 1.2 copy.54
  118.4 1.9 scatter_fusion.6
  120.3 2.0 broadcast_multiply_fusion.2
  122.2 4.8 %gather_fusion = f32[512]{0:T(512)S(1)} fusion(f32[2,65536]{1,0:T(2,128)S(1)} %get-tuple-element.39, s32[512]{0:T(512)S(1)} %bitcast.121), kind=kCustom, calls=%fused_computation.clone | custom fusion | bytes 8192 | tf_op jit(solution)/shard_map/jit(take_along_axis)/gather | solution.py:105
  127.1 4.8 %gather_fusion.1 = f32[512]{0:T(512)S(1)} fusion(f32[2,65536]{1,0:T(2,128)S(1)} %get-tuple-element.36, s32[512]{0:T(512)S(1)} %bitcast.122), kind=kCustom, calls=%fused_computation.1.clone | custom fusion | bytes 8192 | tf_op jit(solution)/shard_map/jit(take_along_axis)/gather | solution.py:105
  132.0 4.8 %gather_fusion.2 = f32[512]{0:T(512)S(1)} fusion(f32[2,65536]{1,0:T(2,128)S(1)} %get-tuple-element.37, s32[512]{0:T(512)S(1)} %bitcast.123), kind=kCustom, calls=%fused_computation.2.clone | custom fusion | bytes 8192 | tf_op jit(solution)/shard_map/jit(take_along_axis)/gather | solution.py:105
  136.8 4.8 %gather_fusion.3 = f32[512]{0:T(512)S(1)} fusion(f32[2,65536]{1,0:T(2,128)S(1)} %get-tuple-element.38, s32[512]{0:T(512)S(1)} %bitcast.124), kind=kCustom, calls=%fused_computation.3.clone | custom fusion | bytes 8192 | tf_op jit(solution)/shard_map/jit(take_along_axis)/gather | solution.py:105
  141.8 327.8 %psum.7 = f32[2,4,256]{2,0,1:T(2,128)S(1)} all-reduce(f32[2,4,256]{2,0,1:T(2,128)S(1)} %pad_maximum_fusion.8), channel_id=1, replica_groups=mesh['shot'=2,'space'=128] {'space'}, use_global_device_ids=true, to_apply=%region_8.10 | all-reduce | flops 2048 | bytes 16384 | tf_op jit(solution)/shard_map/psum | solution.py:109
  470.2 1.1 copy.41
  472.5 1.1 bitcast_multiply_fusion
  (82 shorter events, 19.5 us)
Async XLA Ops:
  0.6 0.7 copy-start.13
  1.5 0.7 copy-start.15
  2.2 0.7 copy-start.16
  2.9 9.7 %copy-start.10 = (f32[1,2,128,128]{3,2,1,0:T(8,128)S(1)}, f32[1,2,128,128]{3,2,1,0:T(8,128)}, u32[]{:S(2)}) copy-start(f32[1,2,128,128]{3,2,1,0:T(8,128)} %param.17) | copy-start | bytes 393220
  4.3 29.7 %collective-permute-start = (f32[2,4,128,128]{3,2,1,0:T(8,128)S(1)}, f32[2,4,128,128]{3,2,1,0:T(8,128)S(1)}, u32[]{:S(2)}, u32[]{:S(2)}) collective-permute-start(f32[2,4,128,128]{3,2,1,0:T(8,128)S(1)} %get-tuple-element.52), channel_id=1, source_target_pairs={{1,0},{2,1},{3,2},{4,3},{5,4},{6,5},{7,6},{8,7},{9,8},{10,9},{11,1... | collective-permute-start | bytes 1572872 | tf_op jit(solution)/shard_map/ppermute | solution.py:16
  10.7 23.3 %collective-permute-start.1 = (f32[2,4,128,128]{3,2,1,0:T(8,128)S(1)}, f32[2,4,128,128]{3,2,1,0:T(8,128)S(1)}, u32[]{:S(2)}, u32[]{:S(2)}) collective-permute-start(f32[2,4,128,128]{3,2,1,0:T(8,128)S(1)} %get-tuple-element.52), channel_id=1, source_target_pairs={{0,1},{1,2},{2,3},{3,4},{4,5},{5,6},{6,7},{7,8},{8,9},{9,10},{10,1... | collective-permute-start | bytes 1572872 | tf_op jit(solution)/shard_map/ppermute | solution.py:16
  21.5 0.9 copy-start.11
  22.5 5.8 %copy-start.12 = (f32[1,2,128,128]{3,2,1,0:T(8,128)S(1)}, f32[1,2,128,128]{3,2,1,0:T(8,128)}, u32[]{:S(2)}) copy-start(f32[1,2,128,128]{3,2,1,0:T(8,128)} %param.18) | copy-start | bytes 393220
  33.9 1.0 copy-start.8
  34.9 1.5 copy-start.9
  39.5 1.0 copy-start.6
  40.8 15.1 %collective-permute-start.2 = (f32[2,4,128,128]{3,2,1,0:T(8,128)S(1)}, f32[2,4,128,128]{3,2,1,0:T(8,128)S(1)}, u32[]{:S(2)}, u32[]{:S(2)}) collective-permute-start(f32[2,4,128,128]{3,2,1,0:T(8,128)S(1)} %get-tuple-element.50), channel_id=1, source_target_pairs={{1,0},{2,1},{3,2},{4,3},{5,4},{6,5},{7,6},{8,7},{9,8},{10,9},{11,1... | collective-permute-start | bytes 1572872 | tf_op jit(solution)/shard_map/ppermute | solution.py:16
  49.2 16.2 %collective-permute-start.3 = (f32[2,4,128,128]{3,2,1,0:T(8,128)S(1)}, f32[2,4,128,128]{3,2,1,0:T(8,128)S(1)}, u32[]{:S(2)}, u32[]{:S(2)}) collective-permute-start(f32[2,4,128,128]{3,2,1,0:T(8,128)S(1)} %get-tuple-element.50), channel_id=1, source_target_pairs={{0,1},{1,2},{2,3},{3,4},{4,5},{5,6},{6,7},{7,8},{8,9},{9,10},{10,1... | collective-permute-start | bytes 1572872 | tf_op jit(solution)/shard_map/ppermute | solution.py:16
  68.8 1.2 copy-start.5
  71.0 1.0 copy-start.7
  72.2 20.2 %copy-start.1 = (f32[2,4,128,128]{3,2,1,0:T(8,128)}, f32[2,4,128,128]{3,2,1,0:T(8,128)S(1)}, u32[]{:S(2)}) copy-start(f32[2,4,128,128]{3,2,1,0:T(8,128)S(1)} %get-tuple-element.47) | copy-start | bytes 1572868
  72.2 8.6 %collective-permute-start.4 = (f32[2,4,128,128]{3,2,1,0:T(8,128)S(1)}, f32[2,4,128,128]{3,2,1,0:T(8,128)S(1)}, u32[]{:S(2)}, u32[]{:S(2)}) collective-permute-start(f32[2,4,128,128]{3,2,1,0:T(8,128)S(1)} %get-tuple-element.47), channel_id=1, source_target_pairs={{1,0},{2,1},{3,2},{4,3},{5,4},{6,5},{7,6},{8,7},{9,8},{10,9},{11,1... | collective-permute-start | bytes 1572872 | tf_op jit(solution)/shard_map/ppermute | solution.py:16
  74.2 16.2 %collective-permute-start.5 = (f32[2,4,128,128]{3,2,1,0:T(8,128)S(1)}, f32[2,4,128,128]{3,2,1,0:T(8,128)S(1)}, u32[]{:S(2)}, u32[]{:S(2)}) collective-permute-start(f32[2,4,128,128]{3,2,1,0:T(8,128)S(1)} %get-tuple-element.47), channel_id=1, source_target_pairs={{0,1},{1,2},{2,3},{3,4},{4,5},{5,6},{6,7},{7,8},{8,9},{9,10},{10,1... | collective-permute-start | bytes 1572872 | tf_op jit(solution)/shard_map/ppermute | solution.py:16
  93.7 1.0 copy-start.4
  95.8 0.8 copy-start
  96.6 4.7 copy-start.14
  96.8 8.6 %collective-permute-start.6 = (f32[2,4,128,128]{3,2,1,0:T(8,128)S(1)}, f32[2,4,128,128]{3,2,1,0:T(8,128)S(1)}, u32[]{:S(2)}, u32[]{:S(2)}) collective-permute-start(f32[2,4,128,128]{3,2,1,0:T(8,128)S(1)} %get-tuple-element.42), channel_id=1, source_target_pairs={{1,0},{2,1},{3,2},{4,3},{5,4},{6,5},{7,6},{8,7},{9,8},{10,9},{11,1... | collective-permute-start | bytes 1572872 | tf_op jit(solution)/shard_map/ppermute | solution.py:16
  98.7 16.2 %collective-permute-start.7 = (f32[2,4,128,128]{3,2,1,0:T(8,128)S(1)}, f32[2,4,128,128]{3,2,1,0:T(8,128)S(1)}, u32[]{:S(2)}, u32[]{:S(2)}) collective-permute-start(f32[2,4,128,128]{3,2,1,0:T(8,128)S(1)} %get-tuple-element.42), channel_id=1, source_target_pairs={{0,1},{1,2},{2,3},{3,4},{4,5},{5,6},{6,7},{7,8},{8,9},{9,10},{10,1... | collective-permute-start | bytes 1572872 | tf_op jit(solution)/shard_map/ppermute | solution.py:16
  114.9 2.1 copy-start.2
  470.2 1.2 copy-start.3
where the time goes:
time: 474 us
  blocking collectives  348 us (73%)
  waiting for transfers between devices  41.7 us (9%)
  local copies, waits for them, and re-layouts  35.2 us (7%)
  starting transfers between devices  27.5 us (6%)
  other arithmetic  20 us (4%)
    psum x1, blocking collectives, per_device(): traces = lax.psum(local_traces, 'space')  328 us
    ppermute x8, waiting for transfers between devices, passed_along(): return lax.ppermute(value, axis, pairs)  41.7 us
    ppermute x8, starting transfers between devices, passed_along(): return lax.ppermute(value, axis, pairs)  27.5 us
    gather x8, local copies, waits for them, and re-layouts, per_device(): jnp.take_along_axis(new_p.reshape(stop - start, cells), receiver_local, a...  19.4 us
    unnamed x52, local copies, waits for them, and re-layouts  15.6 us
  transfers between devices with their start and end apart: 8, of which 6 were waited for; matrix products, arithmetic and copies ran while one was open for 0% of the time, Pallas kernels for 0%

commit v1 on v0

v1 whole, which is shorter than its diff:
```python
import functools

import jax
import jax.numpy as jnp
from jax import lax
from jax.experimental import pallas as pl
from jax.experimental.pallas import tpu as pltpu
from jax.sharding import PartitionSpec as P

STEPS = 4
CX, CY, CZ = 4, 128, 128
ROWS = CX * CY
CELLS = ROWS * CZ

taps = (-205.0 / 72.0, 8.0 / 5.0, -1.0 / 5.0, 8.0 / 315.0, -1.0 / 560.0)
step_ratio = 0.08

VMEM = pl.BlockSpec(memory_space=pltpu.VMEM)
SMEM = pl.BlockSpec(memory_space=pltpu.SMEM)
EXACT = lax.Precision.HIGHEST


def shape(*dims, dtype=jnp.float32):
    return jax.ShapeDtypeStruct(dims, dtype)


def call(kernel, ins, outs, flops, name):
    moved = 4 * sum(int(jnp.size(a)) for a in ins) + 4 * sum(o.size for o in outs)
    specs = [SMEM if a.size <= 64 else VMEM for a in ins]
    return pl.pallas_call(
        kernel,
        out_shape=tuple(outs),
        in_specs=specs,
        out_specs=tuple(VMEM for _ in outs),
        compiler_params=pltpu.CompilerParams(vmem_limit_bytes=24 << 20),
        cost_estimate=pl.CostEstimate(flops=flops, bytes_accessed=moved, transcendentals=0),
        name=name,
    )(*ins)


def live_of(at_ref, active_ref, source_ref, s):
    here = source_ref[s] // CELLS == at_ref[0]
    return jnp.where(here | (active_ref[s, 0] == 1), 1.0, 0.0)


def row(x):
    return pl.ds(x * CY, CY)


def begin_kernel(at_ref, active_ref, source_ref, p_ref, v_ref, e_ref, d_ref, p0_ref, own_ref, odd_ref):
    for s in range(2):
        p0_ref[s] = p_ref[s] * live_of(at_ref, active_ref, source_ref, s)
    courant = (v_ref[...] * step_ratio) * (v_ref[...] * step_ratio)
    coupling = jnp.sqrt(1.0 + 2.0 * d_ref[...])
    own_ref[0] = courant
    own_ref[1] = courant * (1.0 + 2.0 * e_ref[...])
    own_ref[2] = courant * coupling
    odd_ref[...] = jnp.full(odd_ref.shape, at_ref[0] & 1, jnp.int32)


def band():
    apart = jnp.abs(lax.broadcasted_iota(jnp.int32, (CZ, CZ), 0) - lax.broadcasted_iota(jnp.int32, (CZ, CZ), 1))
    out = jnp.zeros((CZ, CZ), jnp.float32)
    for k in range(5):
        out = jnp.where(apart == k, taps[k], out)
    return out


def local_part(s, at_ref, source_ref, wavelet_ref, step, p, po, q, qo, c_ref, cs_ref, ck_ref, pre_p, pre_q, mat):
    for x in range(CX):
        here = row(x)
        hor = jnp.dot(mat, p[s, here, :], precision=EXACT, preferred_element_type=jnp.float32)
        for other in range(CX):
            hor = hor + taps[abs(other - x)] * p[s, row(other), :]
        ver = jnp.dot(q[s, here, :], mat, precision=EXACT, preferred_element_type=jnp.float32)
        pre_p[s, here, :] = 2.0 * p[s, here, :] - po[s, here, :] + (cs_ref[s, here, :] * hor + ck_ref[s, here, :] * ver)
        pre_q[s, here, :] = 2.0 * q[s, here, :] - qo[s, here, :] + (ck_ref[s, here, :] * hor + c_ref[s, here, :] * ver)
    cell = source_ref[s] % CELLS
    gain = jnp.where(source_ref[s] // CELLS == at_ref[0], wavelet_ref[s, step], 0.0)
    lane = lax.broadcasted_iota(jnp.int32, (1, CZ), 1)
    add = jnp.where(lane == cell % CZ, gain, 0.0)
    line = pl.ds(cell // CZ, 1)
    pre_p[s, line, :] = pre_p[s, line, :] + add
    pre_q[s, line, :] = pre_q[s, line, :] + add


def first_kernel(at_ref, side_ref, active_ref, source_ref, wavelet_ref, p0, p_old, q_now, q_old, own, other,
                 pre_p, pre_q, po, q, c_ref, cs_ref, ck_ref):
    half = ROWS // 2
    mat = band()
    for s in range(2):
        live = live_of(at_ref, active_ref, source_ref, s)
        po[s] = p_old[s] * live
        q[s] = q_now[s] * live
        for k, ref in enumerate((c_ref, cs_ref, ck_ref)):
            mine = pl.ds(pl.multiple_of(side_ref[0] * half, half), half)
            theirs = pl.ds(pl.multiple_of((1 - side_ref[0]) * half, half), half)
            ref[s, mine, :] = own[k] * live
            ref[s, theirs, :] = other[k] * live
    for s in range(2):
        live = live_of(at_ref, active_ref, source_ref, s)
        pre_q[s] = q_old[s] * live
        local_part(s, at_ref, source_ref, wavelet_ref, 0, p0, po, q, pre_q, c_ref, cs_ref, ck_ref, pre_p, pre_q, mat)


def local_kernel(step, at_ref, source_ref, wavelet_ref, p, po, q, qo, c_ref, cs_ref, ck_ref, pre_p, pre_q):
    mat = band()
    for s in range(2):
        local_part(s, at_ref, source_ref, wavelet_ref, step, p, po, q, qo, c_ref, cs_ref, ck_ref, pre_p, pre_q, mat)


def halo_kernel(odd_ref, even_pair, odd_pair, pre_p, pre_q, cs_ref, ck_ref, p, q):
    odd = odd_ref[...] == 1
    for s in range(2):
        for tile in range(CY // 8):
            def at(x):
                return pl.ds(x * CY + tile * 8, 8)
            a = [even_pair[s, at(x), :] for x in range(CX)]
            b = [odd_pair[s, at(x), :] for x in range(CX)]
            lower = [jnp.where(odd, a[x], b[x]) for x in range(CX)]
            upper = [jnp.where(odd, b[x], a[x]) for x in range(CX)]
            for x in range(CX):
                hor = taps[4] * (lower[x] + upper[x])
                for k in range(1, 4):
                    if x + k < CX:
                        hor = hor + taps[4 - k] * lower[x + k]
                    if x - k >= 0:
                        hor = hor + taps[4 - k] * upper[x - k]
                p[s, at(x), :] = pre_p[s, at(x), :] + cs_ref[s, at(x), :] * hor
                q[s, at(x), :] = pre_q[s, at(x), :] + ck_ref[s, at(x), :] * hor


def samples(field, s, pick_z, pick_y):
    out = []
    for x in range(CX):
        spread = jnp.dot(field[s, row(x), :], pick_z, precision=EXACT, preferred_element_type=jnp.float32)
        out.append(jnp.sum(jnp.where(pick_y, spread, 0.0), axis=0, keepdims=True))
    return out


def picks(cells_ref, s):
    cells = cells_ref[pl.ds(s, 1), :]
    n = cells.shape[1]
    inside = cells % CELLS
    pick_z = jnp.where(lax.broadcasted_iota(jnp.int32, (CZ, n), 0) == inside % CZ, 1.0, 0.0)
    pick_y = lax.broadcasted_iota(jnp.int32, (CY, n), 0) == (inside // CZ) % CY
    return cells // CELLS, inside // (CY * CZ), pick_z, pick_y


def own_sample(values, block, x_at, me):
    out = jnp.zeros(block.shape, jnp.float32)
    for x in range(CX):
        out = jnp.where((x_at == x) & (block == me), values[x], out)
    return out


def sample_kernel(at_ref, cells_ref, *refs):
    fields, out_ref = refs[:-1], refs[-1]
    out_ref[...] = jnp.zeros(out_ref.shape, jnp.float32)
    for s in range(2):
        block, x_at, pick_z, pick_y = picks(cells_ref, s)
        for n, field in enumerate(fields):
            out_ref[s, pl.ds(n, 1), :] = own_sample(samples(field, s, pick_z, pick_y), block, x_at, at_ref[0])


def last_sample_kernel(at_ref, cells_ref, early_ref, p3, pre_p, out_ref):
    me = at_ref[0]
    out_ref[...] = early_ref[...]
    for s in range(2):
        block, x_at, pick_z, pick_y = picks(cells_ref, s)
        values = samples(p3, s, pick_z, pick_y)
        out_ref[s, pl.ds(3, 1), :] = own_sample(values, block, x_at, me)
        out_ref[s, pl.ds(4, 1), :] = own_sample(samples(pre_p, s, pick_z, pick_y), block, x_at, me)
        hor = jnp.zeros(block.shape, jnp.float32)
        for x in range(CX):
            apart = jnp.where(block == me + 1, x_at + 4 - x, jnp.where(block == me - 1, 4 + x - x_at, 9))
            for k in range(1, 5):
                hor = hor + jnp.where(apart == k, taps[k] * values[x], 0.0)
        out_ref[s, pl.ds(5, 1), :] = hor


def even_pairs(n):
    return [(i, i ^ 1) for i in range(n)]


def odd_pairs(n):
    up = [(i, i + 1) for i in range(1, n - 1, 2)]
    return up + [(b, a) for a, b in up]


def stages(n):
    if n != 128:
        bit, out = 1, []
        while bit < n:
            out.append([(i, i ^ bit) for i in range(n)])
            bit *= 2
        return out

    def device(z, xh, y, core):
        return ((z * 2 + xh) * 4 + y) * 2 + core

    def pairs(move):
        return [
            (device(z, xh, y, core), device(*move(z, xh, y, core)))
            for z in range(8) for xh in range(2) for y in range(4) for core in range(2)
        ]

    far = {0: 3, 3: 0, 4: 7, 7: 4, 1: 6, 6: 1, 2: 5, 5: 2}
    return [
        pairs(lambda z, xh, y, core: (z, xh, y, 1 - core)),
        pairs(lambda z, xh, y, core: (z, xh, y ^ 1, core)),
        pairs(lambda z, xh, y, core: (z, xh, 3 - y, core)),
        pairs(lambda z, xh, y, core: (z, 1 - xh, y, core)),
        pairs(lambda z, xh, y, core: (z ^ 1, xh, y, core)),
        pairs(lambda z, xh, y, core: ((z + 1 if z % 2 else z - 1) % 8, xh, y, core)),
        pairs(lambda z, xh, y, core: (far[z], xh, y, core)),
    ]


def per_device(pressure_now, pressure_old, auxiliary_now, auxiliary_old, velocity, epsilon_field, delta_field,
               active_blocks, source_cells, receiver_cells, wavelet):
    blocks = lax.axis_size("space")
    at = lax.axis_index("space").astype(jnp.int32).reshape(1)
    side = lax.axis_index("shot").astype(jnp.int32).reshape(1)
    fields = (2, ROWS, CZ)
    p_now, p_old, q_now, q_old = (a.reshape(fields) for a in (pressure_now, pressure_old, auxiliary_now, auxiliary_old))
    half = (ROWS // 2, CZ)
    speed, eps, delta = (a.reshape(half) for a in (velocity, epsilon_field, delta_field))
    field = shape(*fields)

    p, own, odd = call(
        begin_kernel, (at, active_blocks, source_cells, p_now, speed, eps, delta),
        (field, shape(3, *half), shape(8, CZ, dtype=jnp.int32)), 10**6, "begin")

    def exchange(values):
        return (lax.ppermute(values, "space", even_pairs(blocks)), lax.ppermute(values, "space", odd_pairs(blocks)))

    halos = exchange(p)
    other = lax.ppermute(own, "shot", [(0, 1), (1, 0)])
    pre_p, pre_q, po, q, c, cs, ck = call(
        first_kernel, (at, side, active_blocks, source_cells, wavelet, p, p_old, q_now, q_old, own, other),
        (field,) * 7, 10**8, "first")
    kept = []
    for step in range(STEPS):
        if step:
            pre_p, pre_q = call(
                functools.partial(local_kernel, step), (at, source_cells, wavelet, p, po, q, qo, c, cs, ck),
                (field, field), 10**8, f"local{step}")
        if step == 3:
            early, = call(
                sample_kernel, (at, receiver_cells, cs, kept[0], kept[1]),
                (shape(2, 8, receiver_cells.shape[1]),), 10**8, "sample_early")
            total, = call(
                last_sample_kernel, (at, receiver_cells, early, p, pre_p),
                (shape(2, 8, receiver_cells.shape[1]),), 10**8, "sample_late")
            for pairs in stages(blocks):
                total = total + lax.ppermute(total, "space", pairs)
        po, qo = p, q
        p, q = call(
            halo_kernel, (odd, *halos, pre_p, pre_q, cs, ck), (field, field), 10**6, f"halo{step}")
        kept.append(p)
        if step < STEPS - 1:
            halos = exchange(p)
    last = total[:, 4] + total[:, 0] * total[:, 5]
    traces = jnp.stack([total[:, 1], total[:, 2], total[:, 3], last], axis=1)
    return (p.reshape(pressure_now.shape), q.reshape(pressure_now.shape), traces)


def solution(mesh):
    grid = P("shot", "space", None, None, None)
    model = P("space", "shot", None, None)
    return jax.shard_map(
        per_device,
        mesh=mesh,
        in_specs=(grid, grid, grid, grid, model, model, model, P("shot", "space"), P("shot"), P("shot", None), P("shot", None)),
        out_specs=(grid, grid, P("shot", None, None)),
        check_vma=False,
    )
```

time: 474 us -> 111 us (0.23)
  blocking collectives: 348 us -> 0 us
  local copies, waits for them, and re-layouts: 35.2 us -> 7.98 us
  other arithmetic: 20 us -> 0.64 us
  Pallas kernels: 0 us -> 15.5 us
  waiting for transfers between devices: 41.7 us -> 57.1 us
    psum x1 -> x0, blocking collectives: 328 us -> none  [per_device(): traces = lax.psum(local_traces, 'space')]
    all_gather x3 -> x0, blocking collectives: 20.3 us -> none  [the longest x1 8.93 us: per_device(): lax.all_gather(velocity, 'shot', axis=1, tiled=True)]
    gather x8 -> x0, local copies, waits for them, and re-layouts: 19.4 us -> none  [per_device(): jnp.take_along_axis(new_p.reshape(stop - start, cells), receiver_local, a...]
    pallas_call x0 -> x11, Pallas kernels: none -> 15.5 us  [call(): pl.pallas_call(kernel, out_shape=tuple(outs), in_specs=specs, out_specs=t...]
    ppermute x8 -> x16, waiting for transfers between devices: 41.7 us -> 57.1 us  [the longest x7 29.1 us: per_device(): total = total + lax.ppermute(total, 'space', pairs)]
    add x8, other arithmetic: 8.45 us -> 0.04 us  [the longest x7 0.03 us: per_device(): total = total + lax.ppermute(total, 'space', pairs)]
    unnamed x52 -> x23, local copies, waits for them, and re-layouts: 15.6 us -> 7.97 us
    scatter-add x8 -> x0, other arithmetic: 6.36 us -> none  [the longest x4 3.8 us: advance(): new_p.reshape(count, -1).at[rows, source_local].add(source_gain)]
  transfers between devices with their start and end apart: 8 -> 16, of which waited for: 6 -> 10; matrix products, arithmetic and copies ran while one was open for 0% -> 1% of each run, Pallas kernels for 0% -> 12%
where the time goes in v1:
time: 111 us
  waiting for transfers between devices  57.1 us (51%)
  starting transfers between devices  28.5 us (26%)
  Pallas kernels  15.5 us (14%)
  local copies, waits for them, and re-layouts  7.98 us (7%)
    ppermute x7, waiting for transfers between devices, per_device(): total = total + lax.ppermute(total, 'space', pairs)  29.1 us
    ppermute x4, starting transfers between devices, exchange(): lax.ppermute(values, 'space', odd_pairs(blocks))  27.1 us
    pallas_call x11, Pallas kernels, call(): pl.pallas_call(kernel, out_shape=tuple(outs), in_specs=specs, out_specs=t...  15.5 us
    ppermute x4, waiting for transfers between devices, exchange(): lax.ppermute(values, 'space', odd_pairs(blocks))  15.3 us
    ppermute x1, waiting for transfers between devices, per_device(): other = lax.ppermute(own, 'shot', [(0, 1), (1, 0)])  12.6 us
    unnamed x23, local copies, waits for them, and re-layouts  7.97 us
  transfers between devices with their start and end apart: 16, of which 10 were waited for; matrix products, arithmetic and copies ran while one was open for 1% of the time, Pallas kernels for 12%

profile of v1, /device:TPU:128, one launch (start us, length us, event | category | flops | bytes accessed | tf_op | source)
XLA Modules:
  0.0 110.5 jit_solution(6339635291289599179)
XLA Ops:
  0.6 0.8 copy.14.active_ref
  1.4 1.0 copy-done.3
  2.5 0.9 copy-done.4
  3.4 0.9 copy-done.5
  4.3 0.9 copy-done.6
  5.2 0.7 copy-done.8
  5.9 0.7 begin.1
  6.6 7.0 %collective-permute-start.1 = (f32[2,512,128]{2,1,0:T(8,128)S(1)}, f32[2,512,128]{2,1,0:T(8,128)S(1)}, u32[]{:S(2)}, u32[]{:S(2)}) collective-permute-start(f32[2,512,128]{2,1,0:T(8,128)S(1)} %get-tuple-element.27.p0.po), channel_id=1, source_target_pairs={{1,2},{3,4},{5,6},{7,8},{9,10},{11,12},{13,14},{15,16},{17,18},{19... | collective-permute-start | bytes 1572872 | tf_op jit(solution)/shard_map/ppermute | solution.py:236
  13.6 0.7 collective-permute-start.2
  14.3 12.6 %collective-permute-done.2.other = f32[3,256,128]{2,1,0:T(8,128)S(1)} collective-permute-done((f32[3,256,128]{2,1,0:T(8,128)S(1)}, f32[3,256,128]{2,1,0:T(8,128)S(1)}, u32[]{:S(2)}, u32[]{:S(2)}) %collective-permute-start.2) | collective-permute-done | bytes 393248 | tf_op jit(solution)/shard_map/ppermute | solution.py:239
  27.0 0.7 copy-done.7
  27.6 1.0 copy-done.1
  28.7 1.0 copy-done.2
  29.7 2.7 %first.1 = (f32[2,512,128]{2,1,0:T(8,128)S(1)}, f32[2,512,128]{2,1,0:T(8,128)S(1)}, f32[2,512,128]{2,1,0:T(8,128)}, f32[2,512,128]{2,1,0:T(8,128)S(1)}, f32[2,51...) custom-call(s32[1]{0:T(128)} %bitcast.at_ref, s32[1]{0:T(128)} %bitcast.5.side_ref, ...), custom_call_target="tpu_custom_call" | custom-call | flops 100000000 | bytes 6553656 | tf_op jit(solution)/shard_map/first/pallas_call | solution.py:30
  32.9 6.6 %collective-permute-start.4 = (f32[2,512,128]{2,1,0:T(8,128)S(1)}, f32[2,512,128]{2,1,0:T(8,128)S(1)}, u32[]{:S(2)}, u32[]{:S(2)}) collective-permute-start(f32[2,512,128]{2,1,0:T(8,128)S(1)} %get-tuple-element.33.p.po.refs_1_), channel_id=1, source_target_pairs={{1,2},{3,4},{5,6},{7,8},{9,10},{11,12},{13,14},{15,16},{17,18},{19... | collective-permute-start | bytes 1572872 | tf_op jit(solution)/shard_map/ppermute | solution.py:236
  39.5 1.9 %local1.1 = (f32[2,512,128]{2,1,0:T(8,128)S(1)}, f32[2,512,128]{2,1,0:T(8,128)S(1)}) custom-call(s32[1]{0:T(128)} %bitcast.at_ref, s32[2]{0:T(128)S(1)} %copy-done.9, f32[2,4]{1,0:T(2,128)S(1)} %copy-done.7, f32[2,512,128]{2,1,0:T(8,128)S(1)} %get-tuple-element.33.p.po.refs_1_, f32[2,512,128]{2,1,0:T(8,128)S(1)} %get-tuple-element.27.p0.po, ...), custom_call_target="tpu_custom_call" | custom-call | flops 100000000 | bytes 4718636 | tf_op jit(solution)/shard_map/local1/pallas_call | solution.py:30
  41.4 7.7 %collective-permute-done.4.odd_pair = f32[2,512,128]{2,1,0:T(8,128)S(1)} collective-permute-done((f32[2,512,128]{2,1,0:T(8,128)S(1)}, f32[2,512,128]{2,1,0:T(8,128)S(1)}, u32[]{:S(2)}, u32[]{:S(2)}) %collective-permute-start.4) | collective-permute-done | bytes 524320 | tf_op jit(solution)/shard_map/ppermute | solution.py:236
  49.4 6.6 %collective-permute-start.6 = (f32[2,512,128]{2,1,0:T(8,128)S(1)}, f32[2,512,128]{2,1,0:T(8,128)S(1)}, u32[]{:S(2)}, u32[]{:S(2)}) collective-permute-start(f32[2,512,128]{2,1,0:T(8,128)S(1)} %get-tuple-element.39.p.po.refs_2_), channel_id=1, source_target_pairs={{1,2},{3,4},{5,6},{7,8},{9,10},{11,12},{13,14},{15,16},{17,18},{19... | collective-permute-start | bytes 1572872 | tf_op jit(solution)/shard_map/ppermute | solution.py:236
  56.1 1.9 %local2.1 = (f32[2,512,128]{2,1,0:T(8,128)S(1)}, f32[2,512,128]{2,1,0:T(8,128)S(1)}) custom-call(s32[1]{0:T(128)} %bitcast.at_ref, s32[2]{0:T(128)S(1)} %copy-done.9, f32[2,4]{1,0:T(2,128)S(1)} %copy-done.7, f32[2,512,128]{2,1,0:T(8,128)S(1)} %get-tuple-element.39.p.po.refs_2_, f32[2,512,128]{2,1,0:T(8,128)S(1)} %get-tuple-element.33.p.po.refs_1_, ...), custom_call_target="tpu_custom_call" | custom-call | flops 100000000 | bytes 4718636 | tf_op jit(solution)/shard_map/local2/pallas_call | solution.py:30
  58.0 7.7 %collective-permute-done.6.odd_pair = f32[2,512,128]{2,1,0:T(8,128)S(1)} collective-permute-done((f32[2,512,128]{2,1,0:T(8,128)S(1)}, f32[2,512,128]{2,1,0:T(8,128)S(1)}, u32[]{:S(2)}, u32[]{:S(2)}) %collective-permute-start.6) | collective-permute-done | bytes 524320 | tf_op jit(solution)/shard_map/ppermute | solution.py:236
  66.0 6.8 %collective-permute-start.8 = (f32[2,512,128]{2,1,0:T(8,128)S(1)}, f32[2,512,128]{2,1,0:T(8,128)S(1)}, u32[]{:S(2)}, u32[]{:S(2)}) collective-permute-start(f32[2,512,128]{2,1,0:T(8,128)S(1)} %get-tuple-element.43.p.p3), channel_id=1, source_target_pairs={{1,2},{3,4},{5,6},{7,8},{9,10},{11,12},{13,14},{15,16},{17,18},{19... | collective-permute-start | bytes 1572872 | tf_op jit(solution)/shard_map/ppermute | solution.py:236
  72.8 2.6 %sample_early.1.early_ref = f32[2,8,256]{2,1,0:T(8,128)S(1)} custom-call(s32[1]{0:T(128)} %bitcast.at_ref, s32[2,256]{1,0:T(2,128)S(1)} %copy-done.10, f32[2,512,128]{2,1,0:T(8,128)S(1)} %get-tuple-element.31.cs_ref.refs_0_, f32[2,512,128]{2,1,0:T(8,128)S(1)} %get-tuple-element.33.p.po.refs_1_, f32[2,512,128]{2,1,0:T(8,128)S(1)} %get-tuple-element.39.p.po.refs_2_), custom_call_target="tpu_custom_call" | custom-call | flops 100000000 | bytes 1591300 | tf_op jit(solution)/shard_map/sample_early/pallas_call | solution.py:30
  75.5 1.9 %local3.1 = (f32[2,512,128]{2,1,0:T(8,128)S(1)}, f32[2,512,128]{2,1,0:T(8,128)S(1)}) custom-call(s32[1]{0:T(128)} %bitcast.at_ref, s32[2]{0:T(128)S(1)} %copy-done.9, f32[2,4]{1,0:T(2,128)S(1)} %copy-done.7, f32[2,512,128]{2,1,0:T(8,128)S(1)} %get-tuple-element.43.p.p3, f32[2,512,128]{2,1,0:T(8,128)S(1)} %get-tuple-element.39.p.po.refs_2_, ...), custom_call_target="tpu_custom_call" | custom-call | flops 100000000 | bytes 4718636 | tf_op jit(solution)/shard_map/local3/pallas_call | solution.py:30
  77.4 1.8 %sample_late.1 = f32[2,8,256]{2,1,0:T(8,128)S(1)} custom-call(s32[1]{0:T(128)} %bitcast.at_ref, s32[2,256]{1,0:T(2,128)S(1)} %copy-done.10, f32[2,8,256]{2,1,0:T(8,128)S(1)} %sample_early.1.early_ref, f32[2,512,128]{2,1,0:T(8,128)S(1)} %get-tuple-element.43.p.p3, f32[2,512,128]{2,1,0:T(8,128)S(1)} %get-tuple-element.45.pre_p), custom_call_target="tpu_custom_call" | custom-call | flops 100000000 | bytes 1083396 | tf_op jit(solution)/shard_map/sample_late/pallas_call | solution.py:30
  79.3 1.2 %collective-permute-done.9 = f32[2,8,256]{2,1,0:T(8,128)S(1)} collective-permute-done((f32[2,8,256]{2,1,0:T(8,128)S(1)}, f32[2,8,256]{2,1,0:T(8,128)S(1)}, u32[]{:S(2)}, u32[]{:S(2)}) %collective-permute-start.9) | collective-permute-done | bytes 16416 | tf_op jit(solution)/shard_map/ppermute | solution.py:257
  80.5 3.7 %collective-permute-done.10 = f32[2,8,256]{2,1,0:T(8,128)S(1)} collective-permute-done((f32[2,8,256]{2,1,0:T(8,128)S(1)}, f32[2,8,256]{2,1,0:T(8,128)S(1)}, u32[]{:S(2)}, u32[]{:S(2)}) %collective-permute-start.10) | collective-permute-done | bytes 16416 | tf_op jit(solution)/shard_map/ppermute | solution.py:257
  84.2 4.9 %collective-permute-done.11 = f32[2,8,256]{2,1,0:T(8,128)S(1)} collective-permute-done((f32[2,8,256]{2,1,0:T(8,128)S(1)}, f32[2,8,256]{2,1,0:T(8,128)S(1)}, u32[]{:S(2)}, u32[]{:S(2)}) %collective-permute-start.11) | collective-permute-done | bytes 16416 | tf_op jit(solution)/shard_map/ppermute | solution.py:257
  89.2 5.2 %collective-permute-done.12 = f32[2,8,256]{2,1,0:T(8,128)S(1)} collective-permute-done((f32[2,8,256]{2,1,0:T(8,128)S(1)}, f32[2,8,256]{2,1,0:T(8,128)S(1)}, u32[]{:S(2)}, u32[]{:S(2)}) %collective-permute-start.12) | collective-permute-done | bytes 16416 | tf_op jit(solution)/shard_map/ppermute | solution.py:257
  94.5 3.7 %collective-permute-done.13 = f32[2,8,256]{2,1,0:T(8,128)S(1)} collective-permute-done((f32[2,8,256]{2,1,0:T(8,128)S(1)}, f32[2,8,256]{2,1,0:T(8,128)S(1)}, u32[]{:S(2)}, u32[]{:S(2)}) %collective-permute-start.13) | collective-permute-done | bytes 16416 | tf_op jit(solution)/shard_map/ppermute | solution.py:257
  98.2 4.9 %collective-permute-done.14 = f32[2,8,256]{2,1,0:T(8,128)S(1)} collective-permute-done((f32[2,8,256]{2,1,0:T(8,128)S(1)}, f32[2,8,256]{2,1,0:T(8,128)S(1)}, u32[]{:S(2)}, u32[]{:S(2)}) %collective-permute-start.14) | collective-permute-done | bytes 16416 | tf_op jit(solution)/shard_map/ppermute | solution.py:257
  103.3 5.4 %collective-permute-done.15 = f32[2,8,256]{2,1,0:T(8,128)S(1)} collective-permute-done((f32[2,8,256]{2,1,0:T(8,128)S(1)}, f32[2,8,256]{2,1,0:T(8,128)S(1)}, u32[]{:S(2)}, u32[]{:S(2)}) %collective-permute-start.15) | collective-permute-done | bytes 16416 | tf_op jit(solution)/shard_map/ppermute | solution.py:257
  109.3 1.2 %halo3.1 = (f32[2,512,128]{2,1,0:T(8,128)}, f32[2,512,128]{2,1,0:T(8,128)}) custom-call(s32[8,128]{1,0:T(8,128)S(1)} %get-tuple-element.26.odd_ref, f32[2,512,128]{2,1,0:T(8,128)S(1)} %collective-permute-done.7.even_pair, f32[2,512,128]{2,1,0:T(8,128)S(1)} %collective-permute-done.8.odd_pair, f32[2,512,128]{2,1,0:T(8,128)S(1)} %get-tuple-element.45.pre_p, ...), custom_call_target="tpu_custom_call" | custom-call | flops 1000000 | bytes 4198400 | tf_op jit(solution)/shard_map/halo3/pallas_call | solution.py:30
  (44 shorter events, 2.2 us)
Async XLA Ops:
  0.6 26.3 %copy-start = (f32[2,1,4,128,128]{4,3,2,1,0:T(8,128)S(1)}, f32[2,1,4,128,128]{4,3,2,1,0:T(8,128)}, u32[]{:S(2)}) copy-start(f32[2,1,4,128,128]{4,3,2,1,0:T(8,128)} %param.12) | copy-start | bytes 1572868
  1.4 1.0 copy-start.3
  2.5 0.9 copy-start.4
  3.4 0.9 copy-start.5
  4.3 0.9 copy-start.6
  5.2 0.7 copy-start.8
  6.5 25.9 %collective-permute-start = (f32[2,512,128]{2,1,0:T(8,128)S(1)}, f32[2,512,128]{2,1,0:T(8,128)S(1)}, u32[]{:S(2)}, u32[]{:S(2)}) collective-permute-start(f32[2,512,128]{2,1,0:T(8,128)S(1)} %get-tuple-element.27.p0.po), channel_id=1, source_target_pairs={{0,1},{1,0},{2,3},{3,2},{4,5},{5,4},{6,7},{7,6},{8,9},{9,8},{10,11... | collective-permute-start | bytes 1572872 | tf_op jit(solution)/shard_map/ppermute | solution.py:236
  6.6 25.8 %collective-permute-start.1 = (f32[2,512,128]{2,1,0:T(8,128)S(1)}, f32[2,512,128]{2,1,0:T(8,128)S(1)}, u32[]{:S(2)}, u32[]{:S(2)}) collective-permute-start(f32[2,512,128]{2,1,0:T(8,128)S(1)} %get-tuple-element.27.p0.po), channel_id=1, source_target_pairs={{1,2},{3,4},{5,6},{7,8},{9,10},{11,12},{13,14},{15,16},{17,18},{19... | collective-permute-start | bytes 1572872 | tf_op jit(solution)/shard_map/ppermute | solution.py:236
  13.6 13.3 %collective-permute-start.2 = (f32[3,256,128]{2,1,0:T(8,128)S(1)}, f32[3,256,128]{2,1,0:T(8,128)S(1)}, u32[]{:S(2)}, u32[]{:S(2)}) collective-permute-start(f32[3,256,128]{2,1,0:T(8,128)S(1)} %get-tuple-element.28.own), channel_id=1, source_target_pairs={{0,128},{128,0},{1,129},{129,1},{2,130},{130,2},{3,131},{131,3},{4... | collective-permute-start | bytes 1179656 | tf_op jit(solution)/shard_map/ppermute | solution.py:239
  27.0 0.7 copy-start.7
  27.0 0.7 copy-start.9
  27.6 1.0 copy-start.1
  28.7 1.0 copy-start.2
  32.8 8.6 %collective-permute-start.3 = (f32[2,512,128]{2,1,0:T(8,128)S(1)}, f32[2,512,128]{2,1,0:T(8,128)S(1)}, u32[]{:S(2)}, u32[]{:S(2)}) collective-permute-start(f32[2,512,128]{2,1,0:T(8,128)S(1)} %get-tuple-element.33.p.po.refs_1_), channel_id=1, source_target_pairs={{0,1},{1,0},{2,3},{3,2},{4,5},{5,4},{6,7},{7,6},{8,9},{9,8},{10,11... | collective-permute-start | bytes 1572872 | tf_op jit(solution)/shard_map/ppermute | solution.py:236
  32.9 16.2 %collective-permute-start.4 = (f32[2,512,128]{2,1,0:T(8,128)S(1)}, f32[2,512,128]{2,1,0:T(8,128)S(1)}, u32[]{:S(2)}, u32[]{:S(2)}) collective-permute-start(f32[2,512,128]{2,1,0:T(8,128)S(1)} %get-tuple-element.33.p.po.refs_1_), channel_id=1, source_target_pairs={{1,2},{3,4},{5,6},{7,8},{9,10},{11,12},{13,14},{15,16},{17,18},{19... | collective-permute-start | bytes 1572872 | tf_op jit(solution)/shard_map/ppermute | solution.py:236
  49.3 8.6 %collective-permute-start.5 = (f32[2,512,128]{2,1,0:T(8,128)S(1)}, f32[2,512,128]{2,1,0:T(8,128)S(1)}, u32[]{:S(2)}, u32[]{:S(2)}) collective-permute-start(f32[2,512,128]{2,1,0:T(8,128)S(1)} %get-tuple-element.39.p.po.refs_2_), channel_id=1, source_target_pairs={{0,1},{1,0},{2,3},{3,2},{4,5},{5,4},{6,7},{7,6},{8,9},{9,8},{10,11... | collective-permute-start | bytes 1572872 | tf_op jit(solution)/shard_map/ppermute | solution.py:236
  49.4 16.2 %collective-permute-start.6 = (f32[2,512,128]{2,1,0:T(8,128)S(1)}, f32[2,512,128]{2,1,0:T(8,128)S(1)}, u32[]{:S(2)}, u32[]{:S(2)}) collective-permute-start(f32[2,512,128]{2,1,0:T(8,128)S(1)} %get-tuple-element.39.p.po.refs_2_), channel_id=1, source_target_pairs={{1,2},{3,4},{5,6},{7,8},{9,10},{11,12},{13,14},{15,16},{17,18},{19... | collective-permute-start | bytes 1572872 | tf_op jit(solution)/shard_map/ppermute | solution.py:236
  65.7 7.2 %copy-start.10 = (s32[2,256]{1,0:T(2,128)S(1)}, s32[2,256]{1,0:T(2,128)}, u32[]{:S(2)}) copy-start(s32[2,256]{1,0:T(2,128)} %cells_ref.3) | copy-start | bytes 6148
  65.9 43.4 %collective-permute-start.7 = (f32[2,512,128]{2,1,0:T(8,128)S(1)}, f32[2,512,128]{2,1,0:T(8,128)S(1)}, u32[]{:S(2)}, u32[]{:S(2)}) collective-permute-start(f32[2,512,128]{2,1,0:T(8,128)S(1)} %get-tuple-element.43.p.p3), channel_id=1, source_target_pairs={{0,1},{1,0},{2,3},{3,2},{4,5},{5,4},{6,7},{7,6},{8,9},{9,8},{10,11... | collective-permute-start | bytes 1572872 | tf_op jit(solution)/shard_map/ppermute | solution.py:236
  66.0 43.3 %collective-permute-start.8 = (f32[2,512,128]{2,1,0:T(8,128)S(1)}, f32[2,512,128]{2,1,0:T(8,128)S(1)}, u32[]{:S(2)}, u32[]{:S(2)}) collective-permute-start(f32[2,512,128]{2,1,0:T(8,128)S(1)} %get-tuple-element.43.p.p3), channel_id=1, source_target_pairs={{1,2},{3,4},{5,6},{7,8},{9,10},{11,12},{13,14},{15,16},{17,18},{19... | collective-permute-start | bytes 1572872 | tf_op jit(solution)/shard_map/ppermute | solution.py:236
  79.2 1.3 %collective-permute-start.9 = (f32[2,8,256]{2,1,0:T(8,128)S(1)}, f32[2,8,256]{2,1,0:T(8,128)S(1)}, u32[]{:S(2)}, u32[]{:S(2)}) collective-permute-start(f32[2,8,256]{2,1,0:T(8,128)S(1)} %sample_late.1), channel_id=1, source_target_pairs={{0,1},{1,0},{2,3},{3,2},{4,5},{5,4},{6,7},{7,6},{8,9},{9,8},{10,11... | collective-permute-start | bytes 49160 | tf_op jit(solution)/shard_map/ppermute | solution.py:257
  80.5 3.7 %collective-permute-start.10 = (f32[2,8,256]{2,1,0:T(8,128)S(1)}, f32[2,8,256]{2,1,0:T(8,128)S(1)}, u32[]{:S(2)}, u32[]{:S(2)}) collective-permute-start(f32[2,8,256]{2,1,0:T(8,128)S(1)} %add.25), channel_id=1, source_target_pairs={{0,2},{1,3},{2,0},{3,1},{4,6},{5,7},{6,4},{7,5},{8,10},{9,11},{10,... | collective-permute-start | bytes 49160 | tf_op jit(solution)/shard_map/ppermute | solution.py:257
  84.2 4.9 %collective-permute-start.11 = (f32[2,8,256]{2,1,0:T(8,128)S(1)}, f32[2,8,256]{2,1,0:T(8,128)S(1)}, u32[]{:S(2)}, u32[]{:S(2)}) collective-permute-start(f32[2,8,256]{2,1,0:T(8,128)S(1)} %add.26), channel_id=1, source_target_pairs={{0,6},{1,7},{2,4},{3,5},{4,2},{5,3},{6,0},{7,1},{8,14},{9,15},{10,... | collective-permute-start | bytes 49160 | tf_op jit(solution)/shard_map/ppermute | solution.py:257
  89.2 5.2 %collective-permute-start.12 = (f32[2,8,256]{2,1,0:T(8,128)S(1)}, f32[2,8,256]{2,1,0:T(8,128)S(1)}, u32[]{:S(2)}, u32[]{:S(2)}) collective-permute-start(f32[2,8,256]{2,1,0:T(8,128)S(1)} %add.27), channel_id=1, source_target_pairs={{0,8},{1,9},{2,10},{3,11},{4,12},{5,13},{6,14},{7,15},{8,0},{9,1},... | collective-permute-start | bytes 49160 | tf_op jit(solution)/shard_map/ppermute | solution.py:257
  94.4 3.7 %collective-permute-start.13 = (f32[2,8,256]{2,1,0:T(8,128)S(1)}, f32[2,8,256]{2,1,0:T(8,128)S(1)}, u32[]{:S(2)}, u32[]{:S(2)}) collective-permute-start(f32[2,8,256]{2,1,0:T(8,128)S(1)} %add.28), channel_id=1, source_target_pairs={{0,16},{1,17},{2,18},{3,19},{4,20},{5,21},{6,22},{7,23},{8,24},{9,... | collective-permute-start | bytes 49160 | tf_op jit(solution)/shard_map/ppermute | solution.py:257
  98.2 4.9 %collective-permute-start.14 = (f32[2,8,256]{2,1,0:T(8,128)S(1)}, f32[2,8,256]{2,1,0:T(8,128)S(1)}, u32[]{:S(2)}, u32[]{:S(2)}) collective-permute-start(f32[2,8,256]{2,1,0:T(8,128)S(1)} %add.29), channel_id=1, source_target_pairs={{0,112},{1,113},{2,114},{3,115},{4,116},{5,117},{6,118},{7,119},{8... | collective-permute-start | bytes 49160 | tf_op jit(solution)/shard_map/ppermute | solution.py:257
  103.1 5.5 %collective-permute-start.15 = (f32[2,8,256]{2,1,0:T(8,128)S(1)}, f32[2,8,256]{2,1,0:T(8,128)S(1)}, u32[]{:S(2)}, u32[]{:S(2)}) collective-permute-start(f32[2,8,256]{2,1,0:T(8,128)S(1)} %add.30), channel_id=1, source_target_pairs={{0,48},{1,49},{2,50},{3,51},{4,52},{5,53},{6,54},{7,55},{8,56},{9,... | collective-permute-start | bytes 49160 | tf_op jit(solution)/shard_map/ppermute | solution.py:257

commit v2 on v1

v2 whole, which is shorter than its diff:
```python
import functools

import jax
import jax.numpy as jnp
from jax import lax
from jax.experimental import pallas as pl
from jax.experimental.pallas import tpu as pltpu
from jax.sharding import PartitionSpec as P

STEPS = 4
CX, CY, CZ = 4, 128, 128
ROWS = CX * CY
CELLS = ROWS * CZ

taps = (-205.0 / 72.0, 8.0 / 5.0, -1.0 / 5.0, 8.0 / 315.0, -1.0 / 560.0)
step_ratio = 0.08

VMEM = pl.BlockSpec(memory_space=pltpu.VMEM)
SMEM = pl.BlockSpec(memory_space=pltpu.SMEM)
FAR = pl.BlockSpec(memory_space=pltpu.HBM)
EXACT = lax.Precision.HIGHEST


def shape(*dims, dtype=jnp.float32):
    return jax.ShapeDtypeStruct(dims, dtype)


def call(kernel, ins, outs, flops, name, far=(), scratch=()):
    moved = 4 * sum(int(jnp.size(a)) for a in ins) + 4 * sum(o.size for o in outs)
    ins = [pltpu.with_memory_space_constraint(a, pltpu.HBM) if n in far else a for n, a in enumerate(ins)]
    specs = [FAR if n in far else SMEM if a.size <= 64 else VMEM for n, a in enumerate(ins)]
    return pl.pallas_call(
        kernel,
        out_shape=tuple(outs),
        in_specs=specs,
        out_specs=tuple(VMEM for _ in outs),
        scratch_shapes=scratch,
        compiler_params=pltpu.CompilerParams(vmem_limit_bytes=24 << 20),
        cost_estimate=pl.CostEstimate(flops=flops, bytes_accessed=moved, transcendentals=0),
        name=name,
    )(*ins)


def live_of(at_ref, active_ref, source_ref, s):
    here = source_ref[s] // CELLS == at_ref[0]
    return jnp.where(here | (active_ref[s] == 1), 1.0, 0.0)


def row(x):
    return pl.ds(x * CY, CY)


def model_kernel(v_far, e_far, d_far, own_ref, sems):
    copies = [pltpu.make_async_copy(src, own_ref.at[n], sems.at[n]) for n, src in enumerate((v_far, e_far, d_far))]
    for copy in copies:
        copy.start()
    for copy in copies:
        copy.wait()
    courant = (own_ref[0] * step_ratio) * (own_ref[0] * step_ratio)
    coupling = jnp.sqrt(1.0 + 2.0 * own_ref[2])
    own_ref[0] = courant
    own_ref[1] = courant * (1.0 + 2.0 * own_ref[1])
    own_ref[2] = courant * coupling


def begin_kernel(at_far, active_far, source_far, p_far, own_ref, p0_ref, odd_ref, live_ref, at_ref, active_ref, source_ref, sems):
    copies = [
        pltpu.make_async_copy(src, dst, sems.at[n])
        for n, (src, dst) in enumerate((
            (at_far, at_ref), (active_far, active_ref), (source_far, source_ref), (p_far, p0_ref)))
    ]
    for copy in copies:
        copy.start()
    for copy in copies:
        copy.wait()
    for s in range(2):
        live = live_of(at_ref, active_ref, source_ref, s)
        p0_ref[s] = p0_ref[s] * live
        live_ref[pl.ds(8 * s, 8), :] = jnp.full((8, CZ), live, jnp.float32)
    odd_ref[...] = jnp.full(odd_ref.shape, at_ref[0] & 1, jnp.int32)


def band():
    apart = jnp.abs(lax.broadcasted_iota(jnp.int32, (CZ, CZ), 0) - lax.broadcasted_iota(jnp.int32, (CZ, CZ), 1))
    out = jnp.zeros((CZ, CZ), jnp.float32)
    for k in range(5):
        out = jnp.where(apart == k, taps[k], out)
    return out


def second_diffs(s, x, p, q, mat):
    hor = jnp.dot(mat, p[s, row(x), :], precision=EXACT, preferred_element_type=jnp.float32)
    for other in range(CX):
        hor = hor + taps[abs(other - x)] * p[s, row(other), :]
    ver = jnp.dot(q[s, row(x), :], mat, precision=EXACT, preferred_element_type=jnp.float32)
    return hor, ver


def add_source(s, step, at_ref, source_ref, wavelet_ref, *refs):
    cell = source_ref[s] % CELLS
    gain = jnp.where(source_ref[s] // CELLS == at_ref[0], wavelet_ref[s, step], 0.0)
    lane = lax.broadcasted_iota(jnp.int32, (1, CZ), 1)
    add = jnp.where(lane == cell % CZ, gain, 0.0)
    line = pl.ds(cell // CZ, 1)
    for ref in refs:
        ref[s, line, :] = ref[s, line, :] + add


def ready_kernel(at_ref, active_ref, source_ref, wavelet_ref, p0, po_far, q_far, qo_far,
                 base_p, base_q, q, hor_ref, ver_ref, sems):
    copies = [
        pltpu.make_async_copy(src, dst, sems.at[n])
        for n, (src, dst) in enumerate(((q_far, q), (po_far, base_p), (qo_far, base_q)))
    ]
    for copy in copies:
        copy.start()
    mat = band()
    for copy in copies:
        copy.wait()
    for s in range(2):
        live = live_of(at_ref, active_ref, source_ref, s)
        q[s] = q[s] * live
        base_p[s] = 2.0 * p0[s] - base_p[s] * live
        base_q[s] = 2.0 * q[s] - base_q[s] * live
        for x in range(CX):
            hor_ref[s, row(x), :], ver_ref[s, row(x), :] = second_diffs(s, x, p0, q, mat)
        add_source(s, 0, at_ref, source_ref, wavelet_ref, base_p, base_q)


def halo_diff(x, lower, upper):
    hor = taps[4] * (lower[x] + upper[x])
    for k in range(1, 4):
        if x + k < CX:
            hor = hor + taps[4 - k] * lower[x + k]
        if x - k >= 0:
            hor = hor + taps[4 - k] * upper[x - k]
    return hor


def tile_at(x, tile):
    return pl.ds(x * CY + tile * 8, 8)


def halo_rows(s, tile, odd, even_pair, odd_pair):
    a = [even_pair[s, tile_at(x, tile), :] for x in range(CX)]
    b = [odd_pair[s, tile_at(x, tile), :] for x in range(CX)]
    return [jnp.where(odd, a[x], b[x]) for x in range(CX)], [jnp.where(odd, b[x], a[x]) for x in range(CX)]


def first_kernel(side_ref, live_ref, odd_ref, even_pair, odd_pair, own, other, base_p, base_q, hor_ref, ver_ref,
                 p, q, c_ref, cs_ref, ck_ref):
    odd = odd_ref[...] == 1

    def work(first, second):
        for tile in range(CY // 8):
            model = []
            for x in range(CX):
                half = (first, second)[x // 2]
                at = tile_at(x % 2, tile)
                model.append((half[0, at, :], half[1, at, :], half[2, at, :]))
            for s in range(2):
                live = live_ref[pl.ds(8 * s, 8), :]
                lower, upper = halo_rows(s, tile, odd, even_pair, odd_pair)
                for x in range(CX):
                    at = tile_at(x, tile)
                    c, cs, ck = (m * live for m in model[x])
                    c_ref[s, at, :], cs_ref[s, at, :], ck_ref[s, at, :] = c, cs, ck
                    hor = hor_ref[s, at, :] + halo_diff(x, lower, upper)
                    ver = ver_ref[s, at, :]
                    p[s, at, :] = base_p[s, at, :] + (cs * hor + ck * ver)
                    q[s, at, :] = base_q[s, at, :] + (ck * hor + c * ver)

    @pl.when(side_ref[0] == 0)
    def _():
        work(own, other)

    @pl.when(side_ref[0] == 1)
    def _():
        work(other, own)


def local_part(step, at_ref, source_ref, wavelet_ref, p, po, q, qo, c_ref, cs_ref, ck_ref, pre_p, pre_q):
    mat = band()
    for s in range(2):
        for x in range(CX):
            here = row(x)
            hor, ver = second_diffs(s, x, p, q, mat)
            pre_p[s, here, :] = 2.0 * p[s, here, :] - po[s, here, :] + (cs_ref[s, here, :] * hor + ck_ref[s, here, :] * ver)
            pre_q[s, here, :] = 2.0 * q[s, here, :] - qo[s, here, :] + (ck_ref[s, here, :] * hor + c_ref[s, here, :] * ver)
        add_source(s, step, at_ref, source_ref, wavelet_ref, pre_p, pre_q)


def halo_kernel(odd_ref, even_pair, odd_pair, pre_p, pre_q, cs_ref, ck_ref, p, q):
    odd = odd_ref[...] == 1
    for s in range(2):
        for tile in range(CY // 8):
            lower, upper = halo_rows(s, tile, odd, even_pair, odd_pair)
            for x in range(CX):
                at = tile_at(x, tile)
                hor = halo_diff(x, lower, upper)
                p[s, at, :] = pre_p[s, at, :] + cs_ref[s, at, :] * hor
                q[s, at, :] = pre_q[s, at, :] + ck_ref[s, at, :] * hor


def samples(field, s, pick_z, pick_y):
    out = []
    for x in range(CX):
        rest, spread = field[s, row(x), :], None
        for _ in range(3):
            part = rest.astype(jnp.bfloat16)
            rest = rest - part.astype(jnp.float32)
            picked = jnp.dot(part, pick_z, preferred_element_type=jnp.float32)
            spread = picked if spread is None else spread + picked
        out.append(jnp.sum(jnp.where(pick_y, spread, 0.0), axis=0, keepdims=True))
    return out


def picks(cells_ref, s):
    cells = cells_ref[pl.ds(s, 1), :]
    n = cells.shape[1]
    inside = cells % CELLS
    pick_z = jnp.where(lax.broadcasted_iota(jnp.int32, (CZ, n), 0) == inside % CZ, 1.0, 0.0).astype(jnp.bfloat16)
    pick_y = lax.broadcasted_iota(jnp.int32, (CY, n), 0) == (inside // CZ) % CY
    return cells // CELLS, inside // (CY * CZ), pick_z, pick_y


def own_sample(values, block, x_at, me):
    out = jnp.zeros(block.shape, jnp.float32)
    for x in range(CX):
        out = jnp.where((x_at == x) & (block == me), values[x], out)
    return out


def local_kernel(step, at_ref, source_ref, wavelet_ref, p, po, q, qo, c_ref, cs_ref, ck_ref, pre_p, pre_q):
    local_part(step, at_ref, source_ref, wavelet_ref, p, po, q, qo, c_ref, cs_ref, ck_ref, pre_p, pre_q)


def early_kernel(step, at_ref, source_ref, wavelet_ref, p, po, q, qo, c_ref, cs_ref, ck_ref, cells_ref, pre_p, pre_q, out_ref):
    local_part(step, at_ref, source_ref, wavelet_ref, p, po, q, qo, c_ref, cs_ref, ck_ref, pre_p, pre_q)
    out_ref[...] = jnp.zeros(out_ref.shape, jnp.float32)
    for s in range(2):
        block, x_at, pick_z, pick_y = picks(cells_ref, s)
        for n, field in enumerate((cs_ref, po, p)):
            out_ref[s, pl.ds(n, 1), :] = own_sample(samples(field, s, pick_z, pick_y), block, x_at, at_ref[0])


def late_kernel(step, at_ref, source_ref, wavelet_ref, p, po, q, qo, c_ref, cs_ref, ck_ref, cells_ref, early_ref,
                pre_p, pre_q, out_ref):
    local_part(step, at_ref, source_ref, wavelet_ref, p, po, q, qo, c_ref, cs_ref, ck_ref, pre_p, pre_q)
    me = at_ref[0]
    out_ref[...] = early_ref[...]
    for s in range(2):
        block, x_at, pick_z, pick_y = picks(cells_ref, s)
        values = samples(p, s, pick_z, pick_y)
        out_ref[s, pl.ds(3, 1), :] = own_sample(values, block, x_at, me)
        out_ref[s, pl.ds(4, 1), :] = own_sample(samples(pre_p, s, pick_z, pick_y), block, x_at, me)
        hor = jnp.zeros(block.shape, jnp.float32)
        for x in range(CX):
            apart = jnp.where(block == me + 1, x_at + 4 - x, jnp.where(block == me - 1, 4 + x - x_at, 9))
            for k in range(1, 5):
                hor = hor + jnp.where(apart == k, taps[k] * values[x], 0.0)
        out_ref[s, pl.ds(5, 1), :] = hor


def even_pairs(n):
    return [(i, i ^ 1) for i in range(n)]


def odd_pairs(n):
    up = [(i, i + 1) for i in range(1, n - 1, 2)]
    return up + [(b, a) for a, b in up]


def stages(n):
    if n != 128:
        bit, out = 1, []
        while bit < n:
            out.append([(i, i ^ bit) for i in range(n)])
            bit *= 2
        return out

    def device(z, xh, y, core):
        return ((z * 2 + xh) * 4 + y) * 2 + core

    def pairs(move):
        return [
            (device(z, xh, y, core), device(*move(z, xh, y, core)))
            for z in range(8) for xh in range(2) for y in range(4) for core in range(2)
        ]

    far = {0: 3, 3: 0, 4: 7, 7: 4, 1: 6, 6: 1, 2: 5, 5: 2}
    return [
        pairs(lambda z, xh, y, core: (z, xh, y, 1 - core)),
        pairs(lambda z, xh, y, core: (z, xh, y ^ 1, core)),
        pairs(lambda z, xh, y, core: (z, xh, 3 - y, core)),
        pairs(lambda z, xh, y, core: (z, 1 - xh, y, core)),
        pairs(lambda z, xh, y, core: (z ^ 1, xh, y, core)),
        pairs(lambda z, xh, y, core: ((z + 1 if z % 2 else z - 1) % 8, xh, y, core)),
        pairs(lambda z, xh, y, core: (far[z], xh, y, core)),
    ]


def per_device(pressure_now, pressure_old, auxiliary_now, auxiliary_old, velocity, epsilon_field, delta_field,
               active_blocks, source_cells, receiver_cells, wavelet):
    blocks = lax.axis_size("space")
    at = lax.axis_index("space").astype(jnp.int32).reshape(1)
    side = lax.axis_index("shot").astype(jnp.int32).reshape(1)
    fields = (2, ROWS, CZ)
    p_now, p_old, q_now, q_old = (a.reshape(fields) for a in (pressure_now, pressure_old, auxiliary_now, auxiliary_old))
    half = (ROWS // 2, CZ)
    speed, eps, delta = (a.reshape(half) for a in (velocity, epsilon_field, delta_field))
    field = shape(*fields)
    active = active_blocks.reshape(2)
    ints = [pltpu.SMEM((1,), jnp.int32), pltpu.SMEM((2,), jnp.int32), pltpu.SMEM((2,), jnp.int32)]

    own, = call(
        model_kernel, (speed, eps, delta), (shape(3, *half),), 10**6, "model", far=range(3),
        scratch=[pltpu.SemaphoreType.DMA((3,))])
    p, odd, live = call(
        begin_kernel, (at, active, source_cells, p_now, own), (field, shape(8, CZ, dtype=jnp.int32), shape(16, CZ)), 10**6, "begin",
        far=range(4), scratch=ints + [pltpu.SemaphoreType.DMA((4,))])

    def exchange(values):
        return (lax.ppermute(values, "space", even_pairs(blocks)), lax.ppermute(values, "space", odd_pairs(blocks)))

    other = lax.ppermute(own, "shot", [(0, 1), (1, 0)])
    halos = exchange(p)
    base_p, base_q, q, hor, ver = call(
        ready_kernel, (at, active, source_cells, wavelet, p, p_old, q_now, q_old), (field,) * 5, 10**8, "ready",
        far=(5, 6, 7), scratch=[pltpu.SemaphoreType.DMA((3,))])
    po, qo = p, q
    p, q, c, cs, ck = call(
        first_kernel, (side, live, odd, *halos, own, other, base_p, base_q, hor, ver), (field,) * 5, 10**7, "first")
    halos = exchange(p)
    traced = shape(2, 8, receiver_cells.shape[1])
    for step in range(1, STEPS):
        now = (at, source_cells, wavelet, p, po, q, qo, c, cs, ck)
        if step == 1:
            pre_p, pre_q = call(functools.partial(local_kernel, step), now, (field, field), 10**8, "local")
        if step == 2:
            pre_p, pre_q, early = call(
                functools.partial(early_kernel, step), (*now, receiver_cells), (field, field, traced), 10**8, "local_early")
        if step == 3:
            pre_p, pre_q, total = call(
                functools.partial(late_kernel, step), (*now, receiver_cells, early), (field, field, traced), 10**8, "local_late")
            todo = stages(blocks)
            for pairs in todo[:-2]:
                total = total + lax.ppermute(total, "space", pairs)
        po, qo = p, q
        p, q = call(
            halo_kernel, (odd, *halos, pre_p, pre_q, cs, ck), (field, field), 10**6, f"halo{step}")
        if step < STEPS - 1:
            halos = exchange(p)
    total, p, q = lax.optimization_barrier((total, p, q))
    for pairs in todo[-2:]:
        total = total + lax.ppermute(total, "space", pairs)
    last = total[:, 4] + total[:, 0] * total[:, 5]
    traces = jnp.stack([total[:, 1], total[:, 2], total[:, 3], last], axis=1)
    return (p.reshape(pressure_now.shape), q.reshape(pressure_now.shape), traces)


def solution(mesh):
    grid = P("shot", "space", None, None, None)
    model = P("space", "shot", None, None)
    return jax.shard_map(
        per_device,
        mesh=mesh,
        in_specs=(grid, grid, grid, grid, model, model, model, P("shot", "space"), P("shot"), P("shot", None), P("shot", None)),
        out_specs=(grid, grid, P("shot", None, None)),
        check_vma=False,
    )
```

time: 111 us -> 100 us (0.901)
  the two profiles are of different devices: /device:TPU:128 before, /device:TPU:28 now
where the time goes in v2:
time: 100 us
  starting transfers between devices  54 us (54%)
  waiting for transfers between devices  28.5 us (28%)
  Pallas kernels  15.3 us (15%)
    ppermute x4, starting transfers between devices, exchange(): lax.ppermute(values, 'space', even_pairs(blocks))  33.1 us
    ppermute x7, waiting for transfers between devices, per_device(): total = total + lax.ppermute(total, 'space', pairs)  23.1 us
    pallas_call x10, Pallas kernels, call(): pl.pallas_call(kernel, out_shape=tuple(outs), in_specs=specs, out_specs=t...  15.3 us
    ppermute x7, starting transfers between devices, per_device(): total = total + lax.ppermute(total, 'space', pairs)  10.9 us
    ppermute x4, starting transfers between devices, exchange(): lax.ppermute(values, 'space', odd_pairs(blocks))  7.85 us
    ppermute x1, waiting for transfers between devices, per_device(): other = lax.ppermute(own, 'shot', [(0, 1), (1, 0)])  5.43 us
    ppermute x1, starting transfers between devices, per_device(): other = lax.ppermute(own, 'shot', [(0, 1), (1, 0)])  2.1 us
  transfers between devices with their start and end apart: 16, of which 8 were waited for; matrix products, arithmetic and copies ran while one was open for 0% of the time, Pallas kernels for 11%

profile of v2, /device:TPU:28, one launch (start us, length us, event | category | flops | bytes accessed | tf_op | source)
XLA Modules:
  0.0 100.0 jit_solution(16278793635758954745)
XLA Ops:
  0.6 1.1 %model.1.own_ref.own = f32[3,256,128]{2,1,0:T(8,128)S(1)} custom-call(f32[256,128]{1,0:T(8,128)} %bitcast.22, f32[256,128]{1,0:T(8,128)} %bitcast.23, f32[256,128]{1,0:T(8,128)} %bitcast.24), custom_call_target="tpu_custom_call" | custom-call | flops 1000000 | bytes 786432 | tf_op jit(solution)/shard_map/model/pallas_call | solution.py:32
  1.8 1.1 %begin.1 = (f32[2,512,128]{2,1,0:T(8,128)S(1)}, s32[8,128]{1,0:T(8,128)S(1)}, f32[16,128]{1,0:T(8,128)S(1)}) custom-call(s32[1]{0:T(128)} %bitcast.at_far.at_ref, s32[2]{0:T(128)} %bitcast.16, s32[2]{0:T(128)} %source_ref.7, f32[2,512,128]{2,1,0:T(8,128)} %bitcast.18, f32[3,256,128]{2,1,0:T(8,128)S(1)} %model.1.own_ref.own), custom_call_target="tpu_custom_call" | custom-call | flops 1000000 | bytes 1454100 | tf_op jit(solution)/shard_map/begin/pallas_call | solution.py:32
  2.9 2.1 %collective-permute-start.1 = (f32[2,512,128]{2,1,0:T(8,128)S(1)}, f32[2,512,128]{2,1,0:T(8,128)S(1)}, u32[]{:S(2)}, u32[]{:S(2)}) collective-permute-start(f32[2,512,128]{2,1,0:T(8,128)S(1)} %get-tuple-element.35.p0.po), channel_id=1, source_target_pairs={{1,2},{3,4},{5,6},{7,8},{9,10},{11,12},{13,14},{15,16},{17,18},{19... | collective-permute-start | bytes 1572872 | tf_op jit(solution)/shard_map/ppermute | solution.py:324
  5.0 1.5 %collective-permute-start = (f32[2,512,128]{2,1,0:T(8,128)S(1)}, f32[2,512,128]{2,1,0:T(8,128)S(1)}, u32[]{:S(2)}, u32[]{:S(2)}) collective-permute-start(f32[2,512,128]{2,1,0:T(8,128)S(1)} %get-tuple-element.35.p0.po), channel_id=1, source_target_pairs={{0,1},{1,0},{2,3},{3,2},{4,5},{5,4},{6,7},{7,6},{8,9},{9,8},{10,11... | collective-permute-start | bytes 1572872 | tf_op jit(solution)/shard_map/ppermute | solution.py:324
  6.6 2.1 %collective-permute-start.2 = (f32[3,256,128]{2,1,0:T(8,128)S(1)}, f32[3,256,128]{2,1,0:T(8,128)S(1)}, u32[]{:S(2)}, u32[]{:S(2)}) collective-permute-start(f32[3,256,128]{2,1,0:T(8,128)S(1)} %model.1.own_ref.own), channel_id=1, source_target_pairs={{0,128},{128,0},{1,129},{129,1},{2,130},{130,2},{3,131},{131,3},{4... | collective-permute-start | bytes 1179656 | tf_op jit(solution)/shard_map/ppermute | solution.py:326
  8.7 0.7 copy-done
  9.3 3.3 %ready.1 = (f32[2,512,128]{2,1,0:T(8,128)S(1)}, f32[2,512,128]{2,1,0:T(8,128)S(1)}, f32[2,512,128]{2,1,0:T(8,128)S(1)}, f32[2,512,128]{2,1,0:T(8,128)S(1)}, f32[2,512,128]{2,1,0:T(8,128)S(1)}) custom-call(s32[1]{0:T(128)} %bitcast.at_far.at_ref, s32[2]{0:T(128)S(1)} %bitcast.17, s32[2]{0:T(128)S(1)} %copy-done.1, f32[2,4]{1,0:T(2,128)S(1)} %copy-done, ...), custom_call_target="tpu_custom_call" | custom-call | flops 100000000 | bytes 4718644 | tf_op jit(solution)/shard_map/ready/pallas_call | solution.py:32
  12.6 5.4 %collective-permute-done.2.other = f32[3,256,128]{2,1,0:T(8,128)S(1)} collective-permute-done((f32[3,256,128]{2,1,0:T(8,128)S(1)}, f32[3,256,128]{2,1,0:T(8,128)S(1)}, u32[]{:S(2)}, u32[]{:S(2)}) %collective-permute-start.2) | collective-permute-done | bytes 393248 | tf_op jit(solution)/shard_map/ppermute | solution.py:326
  18.0 0.6 first.1
  18.6 1.9 %collective-permute-start.4 = (f32[2,512,128]{2,1,0:T(8,128)S(1)}, f32[2,512,128]{2,1,0:T(8,128)S(1)}, u32[]{:S(2)}, u32[]{:S(2)}) collective-permute-start(f32[2,512,128]{2,1,0:T(8,128)S(1)} %get-tuple-element.40.p.po), channel_id=1, source_target_pairs={{1,2},{3,4},{5,6},{7,8},{9,10},{11,12},{13,14},{15,16},{17,18},{19... | collective-permute-start | bytes 1572872 | tf_op jit(solution)/shard_map/ppermute | solution.py:324
  20.6 10.2 %collective-permute-start.3 = (f32[2,512,128]{2,1,0:T(8,128)S(1)}, f32[2,512,128]{2,1,0:T(8,128)S(1)}, u32[]{:S(2)}, u32[]{:S(2)}) collective-permute-start(f32[2,512,128]{2,1,0:T(8,128)S(1)} %get-tuple-element.40.p.po), channel_id=1, source_target_pairs={{0,1},{1,0},{2,3},{3,2},{4,5},{5,4},{6,7},{7,6},{8,9},{9,8},{10,11... | collective-permute-start | bytes 1572872 | tf_op jit(solution)/shard_map/ppermute | solution.py:324
  30.8 1.7 %local.1 = (f32[2,512,128]{2,1,0:T(8,128)S(1)}, f32[2,512,128]{2,1,0:T(8,128)S(1)}) custom-call(s32[1]{0:T(128)} %bitcast.at_far.at_ref, s32[2]{0:T(128)S(1)} %copy-done.1, f32[2,4]{1,0:T(2,128)S(1)} %copy-done, f32[2,512,128]{2,1,0:T(8,128)S(1)} %get-tuple-element.40.p.po, f32[2,512,128]{2,1,0:T(8,128)S(1)} %get-tuple-element.35.p0.po, ...), custom_call_target="tpu_custom_call" | custom-call | flops 100000000 | bytes 4718636 | tf_op jit(solution)/shard_map/local/pallas_call | solution.py:32
  32.8 1.9 %collective-permute-start.6 = (f32[2,512,128]{2,1,0:T(8,128)S(1)}, f32[2,512,128]{2,1,0:T(8,128)S(1)}, u32[]{:S(2)}, u32[]{:S(2)}) collective-permute-start(f32[2,512,128]{2,1,0:T(8,128)S(1)} %get-tuple-element.48.p.po), channel_id=1, source_target_pairs={{1,2},{3,4},{5,6},{7,8},{9,10},{11,12},{13,14},{15,16},{17,18},{19... | collective-permute-start | bytes 1572872 | tf_op jit(solution)/shard_map/ppermute | solution.py:324
  34.8 11.3 %collective-permute-start.5 = (f32[2,512,128]{2,1,0:T(8,128)S(1)}, f32[2,512,128]{2,1,0:T(8,128)S(1)}, u32[]{:S(2)}, u32[]{:S(2)}) collective-permute-start(f32[2,512,128]{2,1,0:T(8,128)S(1)} %get-tuple-element.48.p.po), channel_id=1, source_target_pairs={{0,1},{1,0},{2,3},{3,2},{4,5},{5,4},{6,7},{7,6},{8,9},{9,8},{10,11... | collective-permute-start | bytes 1572872 | tf_op jit(solution)/shard_map/ppermute | solution.py:324
  46.1 3.1 %local_early.1 = (f32[2,512,128]{2,1,0:T(8,128)S(1)}, f32[2,512,128]{2,1,0:T(8,128)S(1)}, f32[2,8,256]{2,1,0:T(8,128)S(1)}) custom-call(s32[1]{0:T(128)} %bitcast.at_far.at_ref, s32[2]{0:T(128)S(1)} %copy-done.1, f32[2,4]{1,0:T(2,128)S(1)} %copy-done, f32[2,512,128]{2,1,0:T(8,128)S(1)} %get-tuple-element.48.p.po, f32[2,512,128]{2,1,0:T(8,128)S(1)} %get-tuple-element.40.p.po, ...), custom_call_target="tpu_custom_call" | custom-call | flops 100000000 | bytes 4737068 | tf_op jit(solution)/shard_map/local_early/pallas_call | solution.py:32
  49.2 0.3 halo2.1
  49.5 1.9 %collective-permute-start.13 = (f32[2,512,128]{2,1,0:T(8,128)S(1)}, f32[2,512,128]{2,1,0:T(8,128)S(1)}, u32[]{:S(2)}, u32[]{:S(2)}) collective-permute-start(f32[2,512,128]{2,1,0:T(8,128)S(1)} %get-tuple-element.52.p), channel_id=1, source_target_pairs={{1,2},{3,4},{5,6},{7,8},{9,10},{11,12},{13,14},{15,16},{17,18},{19... | collective-permute-start | bytes 1572872 | tf_op jit(solution)/shard_map/ppermute | solution.py:324
  51.4 10.0 %collective-permute-start.12 = (f32[2,512,128]{2,1,0:T(8,128)S(1)}, f32[2,512,128]{2,1,0:T(8,128)S(1)}, u32[]{:S(2)}, u32[]{:S(2)}) collective-permute-start(f32[2,512,128]{2,1,0:T(8,128)S(1)} %get-tuple-element.52.p), channel_id=1, source_target_pairs={{0,1},{1,0},{2,3},{3,2},{4,5},{5,4},{6,7},{7,6},{8,9},{9,8},{10,11... | collective-permute-start | bytes 1572872 | tf_op jit(solution)/shard_map/ppermute | solution.py:324
  61.4 2.6 %local_late.1 = (f32[2,512,128]{2,1,0:T(8,128)S(1)}, f32[2,512,128]{2,1,0:T(8,128)S(1)}, f32[2,8,256]{2,1,0:T(8,128)S(1)}) custom-call(s32[1]{0:T(128)} %bitcast.at_far.at_ref, s32[2]{0:T(128)S(1)} %copy-done.1, f32[2,4]{1,0:T(2,128)S(1)} %copy-done, f32[2,512,128]{2,1,0:T(8,128)S(1)} %get-tuple-element.52.p, f32[2,512,128]{2,1,0:T(8,128)S(1)} %get-tuple-element.48.p.po, ...), custom_call_target="tpu_custom_call" | custom-call | flops 100000000 | bytes 4753452 | tf_op jit(solution)/shard_map/local_late/pallas_call | solution.py:32
  64.0 0.3 collective-permute-start.7
  64.3 1.2 %collective-permute-done.7 = f32[2,8,256]{2,1,0:T(8,128)S(1)} collective-permute-done((f32[2,8,256]{2,1,0:T(8,128)S(1)}, f32[2,8,256]{2,1,0:T(8,128)S(1)}, u32[]{:S(2)}, u32[]{:S(2)}) %collective-permute-start.7) | collective-permute-done | bytes 16416 | tf_op jit(solution)/shard_map/ppermute | solution.py:348
  65.5 3.7 %collective-permute-done.8 = f32[2,8,256]{2,1,0:T(8,128)S(1)} collective-permute-done((f32[2,8,256]{2,1,0:T(8,128)S(1)}, f32[2,8,256]{2,1,0:T(8,128)S(1)}, u32[]{:S(2)}, u32[]{:S(2)}) %collective-permute-start.8) | collective-permute-done | bytes 16416 | tf_op jit(solution)/shard_map/ppermute | solution.py:348
  69.2 4.9 %collective-permute-done.9 = f32[2,8,256]{2,1,0:T(8,128)S(1)} collective-permute-done((f32[2,8,256]{2,1,0:T(8,128)S(1)}, f32[2,8,256]{2,1,0:T(8,128)S(1)}, u32[]{:S(2)}, u32[]{:S(2)}) %collective-permute-start.9) | collective-permute-done | bytes 16416 | tf_op jit(solution)/shard_map/ppermute | solution.py:348
  74.2 5.2 %collective-permute-done.10 = f32[2,8,256]{2,1,0:T(8,128)S(1)} collective-permute-done((f32[2,8,256]{2,1,0:T(8,128)S(1)}, f32[2,8,256]{2,1,0:T(8,128)S(1)}, u32[]{:S(2)}, u32[]{:S(2)}) %collective-permute-start.10) | collective-permute-done | bytes 16416 | tf_op jit(solution)/shard_map/ppermute | solution.py:348
  79.4 1.9 %collective-permute-start.11 = (f32[2,8,256]{2,1,0:T(8,128)S(1)}, f32[2,8,256]{2,1,0:T(8,128)S(1)}, u32[]{:S(2)}, u32[]{:S(2)}) collective-permute-start(f32[2,8,256]{2,1,0:T(8,128)S(1)} %add.28), channel_id=1, source_target_pairs={{0,16},{1,17},{2,18},{3,19},{4,20},{5,21},{6,22},{7,23},{8,24},{9,... | collective-permute-start | bytes 49160 | tf_op jit(solution)/shard_map/ppermute | solution.py:348
  81.3 1.8 %collective-permute-done.11 = f32[2,8,256]{2,1,0:T(8,128)S(1)} collective-permute-done((f32[2,8,256]{2,1,0:T(8,128)S(1)}, f32[2,8,256]{2,1,0:T(8,128)S(1)}, u32[]{:S(2)}, u32[]{:S(2)}) %collective-permute-start.11) | collective-permute-done | bytes 16416 | tf_op jit(solution)/shard_map/ppermute | solution.py:348
  83.2 1.2 %halo3.1 = (f32[2,512,128]{2,1,0:T(8,128)}, f32[2,512,128]{2,1,0:T(8,128)}) custom-call(s32[8,128]{1,0:T(8,128)S(1)} %get-tuple-element.33.odd_ref, f32[2,512,128]{2,1,0:T(8,128)S(1)} %collective-permute-done.12.even_pair, f32[2,512,128]{2,1,0:T(8,128)S(1)} %collective-permute-done.13.odd_pair, f32[2,512,128]{2,1,0:T(8,128)S(1)} %get-tuple-element.56.pre_p, ...), custom_call_target="tpu_custom_call" | custom-call | flops 1000000 | bytes 4198400 | tf_op jit(solution)/shard_map/halo3/pallas_call | solution.py:32
  84.4 0.5 collective-permute-start.14
  84.9 4.5 %collective-permute-done.14 = f32[2,8,256]{2,1,0:T(8,128)S(1)} collective-permute-done((f32[2,8,256]{2,1,0:T(8,128)S(1)}, f32[2,8,256]{2,1,0:T(8,128)S(1)}, u32[]{:S(2)}, u32[]{:S(2)}) %collective-permute-start.14) | collective-permute-done | bytes 16416 | tf_op jit(solution)/shard_map/ppermute | solution.py:356
  89.3 8.3 %collective-permute-start.15 = (f32[2,8,256]{2,1,0:T(8,128)S(1)}, f32[2,8,256]{2,1,0:T(8,128)S(1)}, u32[]{:S(2)}, u32[]{:S(2)}) collective-permute-start(f32[2,8,256]{2,1,0:T(8,128)S(1)} %add.30), channel_id=1, source_target_pairs={{0,48},{1,49},{2,50},{3,51},{4,52},{5,53},{6,54},{7,55},{8,56},{9,... | collective-permute-start | bytes 49160 | tf_op jit(solution)/shard_map/ppermute | solution.py:356
  97.6 1.7 %collective-permute-done.15 = f32[2,8,256]{2,1,0:T(8,128)S(1)} collective-permute-done((f32[2,8,256]{2,1,0:T(8,128)S(1)}, f32[2,8,256]{2,1,0:T(8,128)S(1)}, u32[]{:S(2)}, u32[]{:S(2)}) %collective-permute-start.15) | collective-permute-done | bytes 16416 | tf_op jit(solution)/shard_map/ppermute | solution.py:356
  99.3 0.6 pad_maximum_fusion
  (28 shorter events, 0.4 us)
Async XLA Ops:
  1.8 6.9 %copy-start.3 = (s32[2,1]{0,1:T(1,128)S(1)}, s32[2,1]{0,1:T(1,128)}, u32[]{:S(2)}) copy-start(s32[2,1]{0,1:T(1,128)} %param.18) | copy-start | bytes 28
  2.9 15.1 %collective-permute-start.1 = (f32[2,512,128]{2,1,0:T(8,128)S(1)}, f32[2,512,128]{2,1,0:T(8,128)S(1)}, u32[]{:S(2)}, u32[]{:S(2)}) collective-permute-start(f32[2,512,128]{2,1,0:T(8,128)S(1)} %get-tuple-element.35.p0.po), channel_id=1, source_target_pairs={{1,2},{3,4},{5,6},{7,8},{9,10},{11,12},{13,14},{15,16},{17,18},{19... | collective-permute-start | bytes 1572872 | tf_op jit(solution)/shard_map/ppermute | solution.py:324
  5.0 13.0 %collective-permute-start = (f32[2,512,128]{2,1,0:T(8,128)S(1)}, f32[2,512,128]{2,1,0:T(8,128)S(1)}, u32[]{:S(2)}, u32[]{:S(2)}) collective-permute-start(f32[2,512,128]{2,1,0:T(8,128)S(1)} %get-tuple-element.35.p0.po), channel_id=1, source_target_pairs={{0,1},{1,0},{2,3},{3,2},{4,5},{5,4},{6,7},{7,6},{8,9},{9,8},{10,11... | collective-permute-start | bytes 1572872 | tf_op jit(solution)/shard_map/ppermute | solution.py:324
  6.6 11.5 %collective-permute-start.2 = (f32[3,256,128]{2,1,0:T(8,128)S(1)}, f32[3,256,128]{2,1,0:T(8,128)S(1)}, u32[]{:S(2)}, u32[]{:S(2)}) collective-permute-start(f32[3,256,128]{2,1,0:T(8,128)S(1)} %model.1.own_ref.own), channel_id=1, source_target_pairs={{0,128},{128,0},{1,129},{129,1},{2,130},{130,2},{3,131},{131,3},{4... | collective-permute-start | bytes 1179656 | tf_op jit(solution)/shard_map/ppermute | solution.py:326
  8.7 0.7 copy-start
  8.7 0.7 copy-start.1
  18.6 13.9 %collective-permute-start.4 = (f32[2,512,128]{2,1,0:T(8,128)S(1)}, f32[2,512,128]{2,1,0:T(8,128)S(1)}, u32[]{:S(2)}, u32[]{:S(2)}) collective-permute-start(f32[2,512,128]{2,1,0:T(8,128)S(1)} %get-tuple-element.40.p.po), channel_id=1, source_target_pairs={{1,2},{3,4},{5,6},{7,8},{9,10},{11,12},{13,14},{15,16},{17,18},{19... | collective-permute-start | bytes 1572872 | tf_op jit(solution)/shard_map/ppermute | solution.py:324
  20.6 12.0 %collective-permute-start.3 = (f32[2,512,128]{2,1,0:T(8,128)S(1)}, f32[2,512,128]{2,1,0:T(8,128)S(1)}, u32[]{:S(2)}, u32[]{:S(2)}) collective-permute-start(f32[2,512,128]{2,1,0:T(8,128)S(1)} %get-tuple-element.40.p.po), channel_id=1, source_target_pairs={{0,1},{1,0},{2,3},{3,2},{4,5},{5,4},{6,7},{7,6},{8,9},{9,8},{10,11... | collective-permute-start | bytes 1572872 | tf_op jit(solution)/shard_map/ppermute | solution.py:324
  32.8 13.3 %copy-start.2 = (s32[2,256]{1,0:T(2,128)S(1)}, s32[2,256]{1,0:T(2,128)}, u32[]{:S(2)}) copy-start(s32[2,256]{1,0:T(2,128)} %cells_ref.3) | copy-start | bytes 6148
  32.8 16.3 %collective-permute-start.6 = (f32[2,512,128]{2,1,0:T(8,128)S(1)}, f32[2,512,128]{2,1,0:T(8,128)S(1)}, u32[]{:S(2)}, u32[]{:S(2)}) collective-permute-start(f32[2,512,128]{2,1,0:T(8,128)S(1)} %get-tuple-element.48.p.po), channel_id=1, source_target_pairs={{1,2},{3,4},{5,6},{7,8},{9,10},{11,12},{13,14},{15,16},{17,18},{19... | collective-permute-start | bytes 1572872 | tf_op jit(solution)/shard_map/ppermute | solution.py:324
  34.8 14.4 %collective-permute-start.5 = (f32[2,512,128]{2,1,0:T(8,128)S(1)}, f32[2,512,128]{2,1,0:T(8,128)S(1)}, u32[]{:S(2)}, u32[]{:S(2)}) collective-permute-start(f32[2,512,128]{2,1,0:T(8,128)S(1)} %get-tuple-element.48.p.po), channel_id=1, source_target_pairs={{0,1},{1,0},{2,3},{3,2},{4,5},{5,4},{6,7},{7,6},{8,9},{9,8},{10,11... | collective-permute-start | bytes 1572872 | tf_op jit(solution)/shard_map/ppermute | solution.py:324
  49.5 33.7 %collective-permute-start.13 = (f32[2,512,128]{2,1,0:T(8,128)S(1)}, f32[2,512,128]{2,1,0:T(8,128)S(1)}, u32[]{:S(2)}, u32[]{:S(2)}) collective-permute-start(f32[2,512,128]{2,1,0:T(8,128)S(1)} %get-tuple-element.52.p), channel_id=1, source_target_pairs={{1,2},{3,4},{5,6},{7,8},{9,10},{11,12},{13,14},{15,16},{17,18},{19... | collective-permute-start | bytes 1572872 | tf_op jit(solution)/shard_map/ppermute | solution.py:324
  51.4 31.8 %collective-permute-start.12 = (f32[2,512,128]{2,1,0:T(8,128)S(1)}, f32[2,512,128]{2,1,0:T(8,128)S(1)}, u32[]{:S(2)}, u32[]{:S(2)}) collective-permute-start(f32[2,512,128]{2,1,0:T(8,128)S(1)} %get-tuple-element.52.p), channel_id=1, source_target_pairs={{0,1},{1,0},{2,3},{3,2},{4,5},{5,4},{6,7},{7,6},{8,9},{9,8},{10,11... | collective-permute-start | bytes 1572872 | tf_op jit(solution)/shard_map/ppermute | solution.py:324
  64.0 1.5 %collective-permute-start.7 = (f32[2,8,256]{2,1,0:T(8,128)S(1)}, f32[2,8,256]{2,1,0:T(8,128)S(1)}, u32[]{:S(2)}, u32[]{:S(2)}) collective-permute-start(f32[2,8,256]{2,1,0:T(8,128)S(1)} %get-tuple-element.55), channel_id=1, source_target_pairs={{0,1},{1,0},{2,3},{3,2},{4,5},{5,4},{6,7},{7,6},{8,9},{9,8},{10,11... | collective-permute-start | bytes 49160 | tf_op jit(solution)/shard_map/ppermute | solution.py:348
  65.5 3.7 %collective-permute-start.8 = (f32[2,8,256]{2,1,0:T(8,128)S(1)}, f32[2,8,256]{2,1,0:T(8,128)S(1)}, u32[]{:S(2)}, u32[]{:S(2)}) collective-permute-start(f32[2,8,256]{2,1,0:T(8,128)S(1)} %add.25), channel_id=1, source_target_pairs={{0,2},{1,3},{2,0},{3,1},{4,6},{5,7},{6,4},{7,5},{8,10},{9,11},{10,... | collective-permute-start | bytes 49160 | tf_op jit(solution)/shard_map/ppermute | solution.py:348
  69.2 4.9 %collective-permute-start.9 = (f32[2,8,256]{2,1,0:T(8,128)S(1)}, f32[2,8,256]{2,1,0:T(8,128)S(1)}, u32[]{:S(2)}, u32[]{:S(2)}) collective-permute-start(f32[2,8,256]{2,1,0:T(8,128)S(1)} %add.26), channel_id=1, source_target_pairs={{0,6},{1,7},{2,4},{3,5},{4,2},{5,3},{6,0},{7,1},{8,14},{9,15},{10,... | collective-permute-start | bytes 49160 | tf_op jit(solution)/shard_map/ppermute | solution.py:348
  74.2 5.2 %collective-permute-start.10 = (f32[2,8,256]{2,1,0:T(8,128)S(1)}, f32[2,8,256]{2,1,0:T(8,128)S(1)}, u32[]{:S(2)}, u32[]{:S(2)}) collective-permute-start(f32[2,8,256]{2,1,0:T(8,128)S(1)} %add.27), channel_id=1, source_target_pairs={{0,8},{1,9},{2,10},{3,11},{4,12},{5,13},{6,14},{7,15},{8,0},{9,1},... | collective-permute-start | bytes 49160 | tf_op jit(solution)/shard_map/ppermute | solution.py:348
  79.4 3.7 %collective-permute-start.11 = (f32[2,8,256]{2,1,0:T(8,128)S(1)}, f32[2,8,256]{2,1,0:T(8,128)S(1)}, u32[]{:S(2)}, u32[]{:S(2)}) collective-permute-start(f32[2,8,256]{2,1,0:T(8,128)S(1)} %add.28), channel_id=1, source_target_pairs={{0,16},{1,17},{2,18},{3,19},{4,20},{5,21},{6,22},{7,23},{8,24},{9,... | collective-permute-start | bytes 49160 | tf_op jit(solution)/shard_map/ppermute | solution.py:348
  84.4 4.9 %collective-permute-start.14 = (f32[2,8,256]{2,1,0:T(8,128)S(1)}, f32[2,8,256]{2,1,0:T(8,128)S(1)}, u32[]{:S(2)}, u32[]{:S(2)}) collective-permute-start(f32[2,8,256]{2,1,0:T(8,128)S(1)} %add.29), channel_id=1, source_target_pairs={{0,112},{1,113},{2,114},{3,115},{4,116},{5,117},{6,118},{7,119},{8... | collective-permute-start | bytes 49160 | tf_op jit(solution)/shard_map/ppermute | solution.py:356
  89.3 10.0 %collective-permute-start.15 = (f32[2,8,256]{2,1,0:T(8,128)S(1)}, f32[2,8,256]{2,1,0:T(8,128)S(1)}, u32[]{:S(2)}, u32[]{:S(2)}) collective-permute-start(f32[2,8,256]{2,1,0:T(8,128)S(1)} %add.30), channel_id=1, source_target_pairs={{0,48},{1,49},{2,50},{3,51},{4,52},{5,53},{6,54},{7,55},{8,56},{9,... | collective-permute-start | bytes 49160 | tf_op jit(solution)/shard_map/ppermute | solution.py:356

commit v3 on v2

--- a/solution.py
+++ b/solution.py
@@ -147,10 +147,7 @@
     return [jnp.where(odd, a[x], b[x]) for x in range(CX)], [jnp.where(odd, b[x], a[x]) for x in range(CX)]
 
 
-def first_kernel(side_ref, live_ref, odd_ref, even_pair, odd_pair, own, other, base_p, base_q, hor_ref, ver_ref,
-                 p, q, c_ref, cs_ref, ck_ref):
-    odd = odd_ref[...] == 1
-
+def first_kernel(side_ref, live_ref, own, other, base_p, base_q, hor_ref, ver_ref, pre_p, pre_q, c_ref, cs_ref, ck_ref):
     def work(first, second):
         for tile in range(CY // 8):
             model = []
@@ -160,15 +157,13 @@
                 model.append((half[0, at, :], half[1, at, :], half[2, at, :]))
             for s in range(2):
                 live = live_ref[pl.ds(8 * s, 8), :]
-                lower, upper = halo_rows(s, tile, odd, even_pair, odd_pair)
                 for x in range(CX):
                     at = tile_at(x, tile)
                     c, cs, ck = (m * live for m in model[x])
                     c_ref[s, at, :], cs_ref[s, at, :], ck_ref[s, at, :] = c, cs, ck
-                    hor = hor_ref[s, at, :] + halo_diff(x, lower, upper)
-                    ver = ver_ref[s, at, :]
-                    p[s, at, :] = base_p[s, at, :] + (cs * hor + ck * ver)
-                    q[s, at, :] = base_q[s, at, :] + (ck * hor + c * ver)
+                    hor, ver = hor_ref[s, at, :], ver_ref[s, at, :]
+                    pre_p[s, at, :] = base_p[s, at, :] + (cs * hor + ck * ver)
+                    pre_q[s, at, :] = base_q[s, at, :] + (ck * hor + c * ver)
 
     @pl.when(side_ref[0] == 0)
     def _():
@@ -275,7 +270,7 @@
     if n != 128:
         bit, out = 1, []
         while bit < n:
-            out.append([(i, i ^ bit) for i in range(n)])
+            out.append([[(i, i ^ bit) for i in range(n)]])
             bit *= 2
         return out
 
@@ -290,14 +285,22 @@
 
     far = {0: 3, 3: 0, 4: 7, 7: 4, 1: 6, 6: 1, 2: 5, 5: 2}
     return [
-        pairs(lambda z, xh, y, core: (z, xh, y, 1 - core)),
-        pairs(lambda z, xh, y, core: (z, xh, y ^ 1, core)),
-        pairs(lambda z, xh, y, core: (z, xh, 3 - y, core)),
-        pairs(lambda z, xh, y, core: (z, 1 - xh, y, core)),
-        pairs(lambda z, xh, y, core: (z ^ 1, xh, y, core)),
-        pairs(lambda z, xh, y, core: ((z + 1 if z % 2 else z - 1) % 8, xh, y, core)),
-        pairs(lambda z, xh, y, core: (far[z], xh, y, core)),
+        [pairs(lambda z, xh, y, core, k=k: (z, xh, y ^ k, core)) for k in (1, 3, 2)],
+        [
+            pairs(lambda z, xh, y, core: (z, xh, y, 1 - core)),
+            pairs(lambda z, xh, y, core: (z, 1 - xh, y, core)),
+            pairs(lambda z, xh, y, core: (z, 1 - xh, y, 1 - core)),
+        ],
+        [pairs(lambda z, xh, y, core: (z ^ 1, xh, y, core))],
+        [pairs(lambda z, xh, y, core: ((z + 1 if z % 2 else z - 1) % 8, xh, y, core))],
+        [pairs(lambda z, xh, y, core: (far[z], xh, y, core))],
     ]
+
+
+def summed(total, stage):
+    for part in [lax.ppermute(total, "space", pairs) for pairs in stage]:
+        total = total + part
+    return total
 
 
 def per_device(pressure_now, pressure_old, auxiliary_now, auxiliary_old, velocity, epsilon_field, delta_field,
@@ -329,8 +332,9 @@
         ready_kernel, (at, active, source_cells, wavelet, p, p_old, q_now, q_old), (field,) * 5, 10**8, "ready",
         far=(5, 6, 7), scratch=[pltpu.SemaphoreType.DMA((3,))])
     po, qo = p, q
-    p, q, c, cs, ck = call(
-        first_kernel, (side, live, odd, *halos, own, other, base_p, base_q, hor, ver), (field,) * 5, 10**7, "first")
+    pre_p, pre_q, c, cs, ck = call(
+        first_kernel, (side, live, own, other, base_p, base_q, hor, ver), (field,) * 5, 2 * 10**10, "first")
+    p, q = call(halo_kernel, (odd, *halos, pre_p, pre_q, cs, ck), (field, field), 10**6, "halo")
     halos = exchange(p)
     traced = shape(2, 8, receiver_cells.shape[1])
     for step in range(1, STEPS):
@@ -344,16 +348,16 @@
             pre_p, pre_q, total = call(
                 functools.partial(late_kernel, step), (*now, receiver_cells, early), (field, field, traced), 10**8, "local_late")
             todo = stages(blocks)
-            for pairs in todo[:-2]:
-                total = total + lax.ppermute(total, "space", pairs)
+            for stage in todo[:-2]:
+                total = summed(total, stage)
         po, qo = p, q
         p, q = call(
             halo_kernel, (odd, *halos, pre_p, pre_q, cs, ck), (field, field), 10**6, f"halo{step}")
         if step < STEPS - 1:
             halos = exchange(p)
     total, p, q = lax.optimization_barrier((total, p, q))
-    for pairs in todo[-2:]:
-        total = total + lax.ppermute(total, "space", pairs)
+    for stage in todo[-2:]:
+        total = summed(total, stage)
     last = total[:, 4] + total[:, 0] * total[:, 5]
     traces = jnp.stack([total[:, 1], total[:, 2], total[:, 3], last], axis=1)
     return (p.reshape(pressure_now.shape), q.reshape(pressure_now.shape), traces)

time: 100 us -> 96.4 us (0.964)
  the two profiles are of different devices: /device:TPU:28 before, /device:TPU:24 now
where the time goes in v3:
time: 96.4 us; the launch traced here: 96.1 us
  starting transfers between devices  46.9 us (49%)
  waiting for transfers between devices  31.3 us (32%)
  Pallas kernels  15.7 us (16%)
    ppermute x9, starting transfers between devices, summed(): lax.ppermute(total, 'space', pairs)  24.3 us
    ppermute x9, waiting for transfers between devices, summed(): lax.ppermute(total, 'space', pairs)  15.8 us
    pallas_call x11, Pallas kernels, call(): pl.pallas_call(kernel, out_shape=tuple(outs), in_specs=specs, out_specs=t...  15.7 us
    ppermute x4, waiting for transfers between devices, exchange(): lax.ppermute(values, 'space', odd_pairs(blocks))  13 us
    ppermute x4, starting transfers between devices, exchange(): lax.ppermute(values, 'space', even_pairs(blocks))  12.5 us
    ppermute x4, starting transfers between devices, exchange(): lax.ppermute(values, 'space', odd_pairs(blocks))  8.47 us
    ppermute x1, waiting for transfers between devices, per_device(): other = lax.ppermute(own, 'shot', [(0, 1), (1, 0)])  2.53 us
  transfers between devices with their start and end apart: 18, of which 10 were waited for; matrix products, arithmetic and copies ran while one was open for 0% of the time, Pallas kernels for 13%

profile of v3, /device:TPU:24, one launch (start us, length us, event | category | flops | bytes accessed | tf_op | source)
XLA Modules:
  0.0 96.1 jit_solution(4091815923649513847)
XLA Ops:
  0.6 1.1 %model.1.own_ref.own = f32[3,256,128]{2,1,0:T(8,128)S(1)} custom-call(f32[256,128]{1,0:T(8,128)} %bitcast.22, f32[256,128]{1,0:T(8,128)} %bitcast.23, f32[256,128]{1,0:T(8,128)} %bitcast.24), custom_call_target="tpu_custom_call" | custom-call | flops 1000000 | bytes 786432 | tf_op jit(solution)/shard_map/model/pallas_call | solution.py:32
  1.8 1.6 %collective-permute-start.2 = (f32[3,256,128]{2,1,0:T(8,128)S(1)}, f32[3,256,128]{2,1,0:T(8,128)S(1)}, u32[]{:S(2)}, u32[]{:S(2)}) collective-permute-start(f32[3,256,128]{2,1,0:T(8,128)S(1)} %model.1.own_ref.own), channel_id=1, source_target_pairs={{0,128},{128,0},{1,129},{129,1},{2,130},{130,2},{3,131},{131,3},{4... | collective-permute-start | bytes 1179656 | tf_op jit(solution)/shard_map/ppermute | solution.py:329
  3.3 1.1 %begin.1 = (f32[2,512,128]{2,1,0:T(8,128)S(1)}, s32[8,128]{1,0:T(8,128)S(1)}, f32[16,128]{1,0:T(8,128)S(1)}) custom-call(s32[1]{0:T(128)} %bitcast.at_far.at_ref, s32[2]{0:T(128)} %bitcast.16, s32[2]{0:T(128)} %source_ref.7, f32[2,512,128]{2,1,0:T(8,128)} %bitcast.18, f32[3,256,128]{2,1,0:T(8,128)S(1)} %model.1.own_ref.own), custom_call_target="tpu_custom_call" | custom-call | flops 1000000 | bytes 1454100 | tf_op jit(solution)/shard_map/begin/pallas_call | solution.py:32
  4.6 2.7 %collective-permute-start.1 = (f32[2,512,128]{2,1,0:T(8,128)S(1)}, f32[2,512,128]{2,1,0:T(8,128)S(1)}, u32[]{:S(2)}, u32[]{:S(2)}) collective-permute-start(f32[2,512,128]{2,1,0:T(8,128)S(1)} %get-tuple-element.36.p0.po), channel_id=1, source_target_pairs={{1,2},{3,4},{5,6},{7,8},{9,10},{11,12},{13,14},{15,16},{17,18},{19... | collective-permute-start | bytes 1572872 | tf_op jit(solution)/shard_map/ppermute | solution.py:327
  7.4 0.6 copy-done
  8.0 3.3 %ready.1 = (f32[2,512,128]{2,1,0:T(8,128)S(1)}, f32[2,512,128]{2,1,0:T(8,128)S(1)}, f32[2,512,128]{2,1,0:T(8,128)S(1)}, f32[2,512,128]{2,1,0:T(8,128)S(1)}, f32[2,512,128]{2,1,0:T(8,128)S(1)}) custom-call(s32[1]{0:T(128)} %bitcast.at_far.at_ref, s32[2]{0:T(128)S(1)} %bitcast.17, s32[2]{0:T(128)S(1)} %copy-done.1, f32[2,4]{1,0:T(2,128)S(1)} %copy-done, ...), custom_call_target="tpu_custom_call" | custom-call | flops 100000000 | bytes 4718644 | tf_op jit(solution)/shard_map/ready/pallas_call | solution.py:32
  11.3 2.5 %collective-permute-done.2.other = f32[3,256,128]{2,1,0:T(8,128)S(1)} collective-permute-done((f32[3,256,128]{2,1,0:T(8,128)S(1)}, f32[3,256,128]{2,1,0:T(8,128)S(1)}, u32[]{:S(2)}, u32[]{:S(2)}) %collective-permute-start.2) | collective-permute-done | bytes 393248 | tf_op jit(solution)/shard_map/ppermute | solution.py:329
  14.2 0.9 collective-permute-done.1.odd_pair
  15.3 5.0 %collective-permute-start.3 = (f32[2,512,128]{2,1,0:T(8,128)S(1)}, f32[2,512,128]{2,1,0:T(8,128)S(1)}, u32[]{:S(2)}, u32[]{:S(2)}) collective-permute-start(f32[2,512,128]{2,1,0:T(8,128)S(1)} %get-tuple-element.46.p.po), channel_id=1, source_target_pairs={{0,1},{1,0},{2,3},{3,2},{4,5},{5,4},{6,7},{7,6},{8,9},{9,8},{10,11... | collective-permute-start | bytes 1572872 | tf_op jit(solution)/shard_map/ppermute | solution.py:327
  20.3 1.9 %collective-permute-start.4 = (f32[2,512,128]{2,1,0:T(8,128)S(1)}, f32[2,512,128]{2,1,0:T(8,128)S(1)}, u32[]{:S(2)}, u32[]{:S(2)}) collective-permute-start(f32[2,512,128]{2,1,0:T(8,128)S(1)} %get-tuple-element.46.p.po), channel_id=1, source_target_pairs={{1,2},{3,4},{5,6},{7,8},{9,10},{11,12},{13,14},{15,16},{17,18},{19... | collective-permute-start | bytes 1572872 | tf_op jit(solution)/shard_map/ppermute | solution.py:327
  22.3 1.9 %local.1 = (f32[2,512,128]{2,1,0:T(8,128)S(1)}, f32[2,512,128]{2,1,0:T(8,128)S(1)}) custom-call(s32[1]{0:T(128)} %bitcast.at_far.at_ref, s32[2]{0:T(128)S(1)} %copy-done.1, f32[2,4]{1,0:T(2,128)S(1)} %copy-done, f32[2,512,128]{2,1,0:T(8,128)S(1)} %get-tuple-element.46.p.po, f32[2,512,128]{2,1,0:T(8,128)S(1)} %get-tuple-element.36.p0.po, ...), custom_call_target="tpu_custom_call" | custom-call | flops 100000000 | bytes 4718636 | tf_op jit(solution)/shard_map/local/pallas_call | solution.py:32
  24.1 6.7 %collective-permute-done.4.odd_pair = f32[2,512,128]{2,1,0:T(8,128)S(1)} collective-permute-done((f32[2,512,128]{2,1,0:T(8,128)S(1)}, f32[2,512,128]{2,1,0:T(8,128)S(1)}, u32[]{:S(2)}, u32[]{:S(2)}) %collective-permute-start.4) | collective-permute-done | bytes 524320 | tf_op jit(solution)/shard_map/ppermute | solution.py:327
  31.1 3.7 %collective-permute-start.5 = (f32[2,512,128]{2,1,0:T(8,128)S(1)}, f32[2,512,128]{2,1,0:T(8,128)S(1)}, u32[]{:S(2)}, u32[]{:S(2)}) collective-permute-start(f32[2,512,128]{2,1,0:T(8,128)S(1)} %get-tuple-element.52.p.po), channel_id=1, source_target_pairs={{0,1},{1,0},{2,3},{3,2},{4,5},{5,4},{6,7},{7,6},{8,9},{9,8},{10,11... | collective-permute-start | bytes 1572872 | tf_op jit(solution)/shard_map/ppermute | solution.py:327
  34.8 1.9 %collective-permute-start.6 = (f32[2,512,128]{2,1,0:T(8,128)S(1)}, f32[2,512,128]{2,1,0:T(8,128)S(1)}, u32[]{:S(2)}, u32[]{:S(2)}) collective-permute-start(f32[2,512,128]{2,1,0:T(8,128)S(1)} %get-tuple-element.52.p.po), channel_id=1, source_target_pairs={{1,2},{3,4},{5,6},{7,8},{9,10},{11,12},{13,14},{15,16},{17,18},{19... | collective-permute-start | bytes 1572872 | tf_op jit(solution)/shard_map/ppermute | solution.py:327
  36.8 3.2 %local_early.1 = (f32[2,512,128]{2,1,0:T(8,128)S(1)}, f32[2,512,128]{2,1,0:T(8,128)S(1)}, f32[2,8,256]{2,1,0:T(8,128)S(1)}) custom-call(s32[1]{0:T(128)} %bitcast.at_far.at_ref, s32[2]{0:T(128)S(1)} %copy-done.1, f32[2,4]{1,0:T(2,128)S(1)} %copy-done, f32[2,512,128]{2,1,0:T(8,128)S(1)} %get-tuple-element.52.p.po, f32[2,512,128]{2,1,0:T(8,128)S(1)} %get-tuple-element.46.p.po, ...), custom_call_target="tpu_custom_call" | custom-call | flops 100000000 | bytes 4737068 | tf_op jit(solution)/shard_map/local_early/pallas_call | solution.py:32
  39.9 5.4 %collective-permute-done.6.odd_pair = f32[2,512,128]{2,1,0:T(8,128)S(1)} collective-permute-done((f32[2,512,128]{2,1,0:T(8,128)S(1)}, f32[2,512,128]{2,1,0:T(8,128)S(1)}, u32[]{:S(2)}, u32[]{:S(2)}) %collective-permute-start.6) | collective-permute-done | bytes 524320 | tf_op jit(solution)/shard_map/ppermute | solution.py:327
  45.6 3.7 %collective-permute-start.14 = (f32[2,512,128]{2,1,0:T(8,128)S(1)}, f32[2,512,128]{2,1,0:T(8,128)S(1)}, u32[]{:S(2)}, u32[]{:S(2)}) collective-permute-start(f32[2,512,128]{2,1,0:T(8,128)S(1)} %get-tuple-element.56.p), channel_id=1, source_target_pairs={{0,1},{1,0},{2,3},{3,2},{4,5},{5,4},{6,7},{7,6},{8,9},{9,8},{10,11... | collective-permute-start | bytes 1572872 | tf_op jit(solution)/shard_map/ppermute | solution.py:327
  49.3 1.9 %collective-permute-start.15 = (f32[2,512,128]{2,1,0:T(8,128)S(1)}, f32[2,512,128]{2,1,0:T(8,128)S(1)}, u32[]{:S(2)}, u32[]{:S(2)}) collective-permute-start(f32[2,512,128]{2,1,0:T(8,128)S(1)} %get-tuple-element.56.p), channel_id=1, source_target_pairs={{1,2},{3,4},{5,6},{7,8},{9,10},{11,12},{13,14},{15,16},{17,18},{19... | collective-permute-start | bytes 1572872 | tf_op jit(solution)/shard_map/ppermute | solution.py:327
  51.3 2.8 %local_late.1 = (f32[2,512,128]{2,1,0:T(8,128)S(1)}, f32[2,512,128]{2,1,0:T(8,128)S(1)}, f32[2,8,256]{2,1,0:T(8,128)S(1)}) custom-call(s32[1]{0:T(128)} %bitcast.at_far.at_ref, s32[2]{0:T(128)S(1)} %copy-done.1, f32[2,4]{1,0:T(2,128)S(1)} %copy-done, f32[2,512,128]{2,1,0:T(8,128)S(1)} %get-tuple-element.56.p, f32[2,512,128]{2,1,0:T(8,128)S(1)} %get-tuple-element.52.p.po, ...), custom_call_target="tpu_custom_call" | custom-call | flops 100000000 | bytes 4753452 | tf_op jit(solution)/shard_map/local_late/pallas_call | solution.py:32
  54.4 4.0 %collective-permute-start.9 = (f32[2,8,256]{2,1,0:T(8,128)S(1)}, f32[2,8,256]{2,1,0:T(8,128)S(1)}, u32[]{:S(2)}, u32[]{:S(2)}) collective-permute-start(f32[2,8,256]{2,1,0:T(8,128)S(1)} %get-tuple-element.59), channel_id=1, source_target_pairs={{0,4},{1,5},{2,6},{3,7},{4,0},{5,1},{6,2},{7,3},{8,12},{9,13},{10,... | collective-permute-start | bytes 49160 | tf_op jit(solution)/shard_map/ppermute | solution.py:301
  58.4 5.9 %collective-permute-done.8 = f32[2,8,256]{2,1,0:T(8,128)S(1)} collective-permute-done((f32[2,8,256]{2,1,0:T(8,128)S(1)}, f32[2,8,256]{2,1,0:T(8,128)S(1)}, u32[]{:S(2)}, u32[]{:S(2)}) %collective-permute-start.8) | collective-permute-done | bytes 16416 | tf_op jit(solution)/shard_map/ppermute | solution.py:301
  64.5 5.6 %collective-permute-start.11 = (f32[2,8,256]{2,1,0:T(8,128)S(1)}, f32[2,8,256]{2,1,0:T(8,128)S(1)}, u32[]{:S(2)}, u32[]{:S(2)}) collective-permute-start(f32[2,8,256]{2,1,0:T(8,128)S(1)} %add_add_fusion.1), channel_id=1, source_target_pairs={{0,8},{1,9},{2,10},{3,11},{4,12},{5,13},{6,14},{7,15},{8,0},{9,1},... | collective-permute-start | bytes 49160 | tf_op jit(solution)/shard_map/ppermute | solution.py:301
  70.1 1.7 %collective-permute-done.11 = f32[2,8,256]{2,1,0:T(8,128)S(1)} collective-permute-done((f32[2,8,256]{2,1,0:T(8,128)S(1)}, f32[2,8,256]{2,1,0:T(8,128)S(1)}, u32[]{:S(2)}, u32[]{:S(2)}) %collective-permute-start.11) | collective-permute-done | bytes 16416 | tf_op jit(solution)/shard_map/ppermute | solution.py:301
  71.7 3.0 %collective-permute-done.12 = f32[2,8,256]{2,1,0:T(8,128)S(1)} collective-permute-done((f32[2,8,256]{2,1,0:T(8,128)S(1)}, f32[2,8,256]{2,1,0:T(8,128)S(1)}, u32[]{:S(2)}, u32[]{:S(2)}) %collective-permute-start.12) | collective-permute-done | bytes 16416 | tf_op jit(solution)/shard_map/ppermute | solution.py:301
  74.7 1.9 %collective-permute-start.13 = (f32[2,8,256]{2,1,0:T(8,128)S(1)}, f32[2,8,256]{2,1,0:T(8,128)S(1)}, u32[]{:S(2)}, u32[]{:S(2)}) collective-permute-start(f32[2,8,256]{2,1,0:T(8,128)S(1)} %add_add_fusion), channel_id=1, source_target_pairs={{0,16},{1,17},{2,18},{3,19},{4,20},{5,21},{6,22},{7,23},{8,24},{9,... | collective-permute-start | bytes 49160 | tf_op jit(solution)/shard_map/ppermute | solution.py:301
  76.6 1.8 %collective-permute-done.13 = f32[2,8,256]{2,1,0:T(8,128)S(1)} collective-permute-done((f32[2,8,256]{2,1,0:T(8,128)S(1)}, f32[2,8,256]{2,1,0:T(8,128)S(1)}, u32[]{:S(2)}, u32[]{:S(2)}) %collective-permute-start.13) | collective-permute-done | bytes 16416 | tf_op jit(solution)/shard_map/ppermute | solution.py:301
  78.5 1.3 %halo3.1 = (f32[2,512,128]{2,1,0:T(8,128)}, f32[2,512,128]{2,1,0:T(8,128)}) custom-call(s32[8,128]{1,0:T(8,128)S(1)} %get-tuple-element.35.odd_ref, f32[2,512,128]{2,1,0:T(8,128)S(1)} %collective-permute-done.14.even_pair, f32[2,512,128]{2,1,0:T(8,128)S(1)} %collective-permute-done.15.odd_pair, f32[2,512,128]{2,1,0:T(8,128)S(1)} %get-tuple-element.60.pre_p, ...), custom_call_target="tpu_custom_call" | custom-call | flops 1000000 | bytes 4198400 | tf_op jit(solution)/shard_map/halo3/pallas_call | solution.py:32
  79.8 4.8 %collective-permute-start.16 = (f32[2,8,256]{2,1,0:T(8,128)S(1)}, f32[2,8,256]{2,1,0:T(8,128)S(1)}, u32[]{:S(2)}, u32[]{:S(2)}) collective-permute-start(f32[2,8,256]{2,1,0:T(8,128)S(1)} %add.37), channel_id=1, source_target_pairs={{0,112},{1,113},{2,114},{3,115},{4,116},{5,117},{6,118},{7,119},{8... | collective-permute-start | bytes 49160 | tf_op jit(solution)/shard_map/ppermute | solution.py:301
  84.6 1.7 %collective-permute-done.16 = f32[2,8,256]{2,1,0:T(8,128)S(1)} collective-permute-done((f32[2,8,256]{2,1,0:T(8,128)S(1)}, f32[2,8,256]{2,1,0:T(8,128)S(1)}, u32[]{:S(2)}, u32[]{:S(2)}) %collective-permute-start.16) | collective-permute-done | bytes 16416 | tf_op jit(solution)/shard_map/ppermute | solution.py:301
  86.3 7.4 %collective-permute-start.17 = (f32[2,8,256]{2,1,0:T(8,128)S(1)}, f32[2,8,256]{2,1,0:T(8,128)S(1)}, u32[]{:S(2)}, u32[]{:S(2)}) collective-permute-start(f32[2,8,256]{2,1,0:T(8,128)S(1)} %add.38), channel_id=1, source_target_pairs={{0,48},{1,49},{2,50},{3,51},{4,52},{5,53},{6,54},{7,55},{8,56},{9,... | collective-permute-start | bytes 49160 | tf_op jit(solution)/shard_map/ppermute | solution.py:301
  93.8 1.7 %collective-permute-done.17 = f32[2,8,256]{2,1,0:T(8,128)S(1)} collective-permute-done((f32[2,8,256]{2,1,0:T(8,128)S(1)}, f32[2,8,256]{2,1,0:T(8,128)S(1)}, u32[]{:S(2)}, u32[]{:S(2)}) %collective-permute-start.17) | collective-permute-done | bytes 16416 | tf_op jit(solution)/shard_map/ppermute | solution.py:301
  95.5 0.6 pad_maximum_fusion
  (31 shorter events, 1.9 us)
Async XLA Ops:
  1.8 12.1 %collective-permute-start.2 = (f32[3,256,128]{2,1,0:T(8,128)S(1)}, f32[3,256,128]{2,1,0:T(8,128)S(1)}, u32[]{:S(2)}, u32[]{:S(2)}) collective-permute-start(f32[3,256,128]{2,1,0:T(8,128)S(1)} %model.1.own_ref.own), channel_id=1, source_target_pairs={{0,128},{128,0},{1,129},{129,1},{2,130},{130,2},{3,131},{131,3},{4... | collective-permute-start | bytes 1179656 | tf_op jit(solution)/shard_map/ppermute | solution.py:329
  3.3 4.0 %copy-start.3 = (s32[2,1]{0,1:T(1,128)S(1)}, s32[2,1]{0,1:T(1,128)}, u32[]{:S(2)}) copy-start(s32[2,1]{0,1:T(1,128)} %param.18) | copy-start | bytes 28
  4.5 9.7 %collective-permute-start = (f32[2,512,128]{2,1,0:T(8,128)S(1)}, f32[2,512,128]{2,1,0:T(8,128)S(1)}, u32[]{:S(2)}, u32[]{:S(2)}) collective-permute-start(f32[2,512,128]{2,1,0:T(8,128)S(1)} %get-tuple-element.36.p0.po), channel_id=1, source_target_pairs={{0,1},{1,0},{2,3},{3,2},{4,5},{5,4},{6,7},{7,6},{8,9},{9,8},{10,11... | collective-permute-start | bytes 1572872 | tf_op jit(solution)/shard_map/ppermute | solution.py:327
  4.6 10.5 %collective-permute-start.1 = (f32[2,512,128]{2,1,0:T(8,128)S(1)}, f32[2,512,128]{2,1,0:T(8,128)S(1)}, u32[]{:S(2)}, u32[]{:S(2)}) collective-permute-start(f32[2,512,128]{2,1,0:T(8,128)S(1)} %get-tuple-element.36.p0.po), channel_id=1, source_target_pairs={{1,2},{3,4},{5,6},{7,8},{9,10},{11,12},{13,14},{15,16},{17,18},{19... | collective-permute-start | bytes 1572872 | tf_op jit(solution)/shard_map/ppermute | solution.py:327
  7.3 0.7 copy-start
  7.4 0.7 copy-start.1
  15.3 8.8 %collective-permute-start.3 = (f32[2,512,128]{2,1,0:T(8,128)S(1)}, f32[2,512,128]{2,1,0:T(8,128)S(1)}, u32[]{:S(2)}, u32[]{:S(2)}) collective-permute-start(f32[2,512,128]{2,1,0:T(8,128)S(1)} %get-tuple-element.46.p.po), channel_id=1, source_target_pairs={{0,1},{1,0},{2,3},{3,2},{4,5},{5,4},{6,7},{7,6},{8,9},{9,8},{10,11... | collective-permute-start | bytes 1572872 | tf_op jit(solution)/shard_map/ppermute | solution.py:327
  20.3 10.5 %collective-permute-start.4 = (f32[2,512,128]{2,1,0:T(8,128)S(1)}, f32[2,512,128]{2,1,0:T(8,128)S(1)}, u32[]{:S(2)}, u32[]{:S(2)}) collective-permute-start(f32[2,512,128]{2,1,0:T(8,128)S(1)} %get-tuple-element.46.p.po), channel_id=1, source_target_pairs={{1,2},{3,4},{5,6},{7,8},{9,10},{11,12},{13,14},{15,16},{17,18},{19... | collective-permute-start | bytes 1572872 | tf_op jit(solution)/shard_map/ppermute | solution.py:327
  31.1 5.7 %copy-start.2 = (s32[2,256]{1,0:T(2,128)S(1)}, s32[2,256]{1,0:T(2,128)}, u32[]{:S(2)}) copy-start(s32[2,256]{1,0:T(2,128)} %cells_ref.3) | copy-start | bytes 6148
  31.1 8.8 %collective-permute-start.5 = (f32[2,512,128]{2,1,0:T(8,128)S(1)}, f32[2,512,128]{2,1,0:T(8,128)S(1)}, u32[]{:S(2)}, u32[]{:S(2)}) collective-permute-start(f32[2,512,128]{2,1,0:T(8,128)S(1)} %get-tuple-element.52.p.po), channel_id=1, source_target_pairs={{0,1},{1,0},{2,3},{3,2},{4,5},{5,4},{6,7},{7,6},{8,9},{9,8},{10,11... | collective-permute-start | bytes 1572872 | tf_op jit(solution)/shard_map/ppermute | solution.py:327
  34.8 10.5 %collective-permute-start.6 = (f32[2,512,128]{2,1,0:T(8,128)S(1)}, f32[2,512,128]{2,1,0:T(8,128)S(1)}, u32[]{:S(2)}, u32[]{:S(2)}) collective-permute-start(f32[2,512,128]{2,1,0:T(8,128)S(1)} %get-tuple-element.52.p.po), channel_id=1, source_target_pairs={{1,2},{3,4},{5,6},{7,8},{9,10},{11,12},{13,14},{15,16},{17,18},{19... | collective-permute-start | bytes 1572872 | tf_op jit(solution)/shard_map/ppermute | solution.py:327
  45.6 32.8 %collective-permute-start.14 = (f32[2,512,128]{2,1,0:T(8,128)S(1)}, f32[2,512,128]{2,1,0:T(8,128)S(1)}, u32[]{:S(2)}, u32[]{:S(2)}) collective-permute-start(f32[2,512,128]{2,1,0:T(8,128)S(1)} %get-tuple-element.56.p), channel_id=1, source_target_pairs={{0,1},{1,0},{2,3},{3,2},{4,5},{5,4},{6,7},{7,6},{8,9},{9,8},{10,11... | collective-permute-start | bytes 1572872 | tf_op jit(solution)/shard_map/ppermute | solution.py:327
  49.3 29.1 %collective-permute-start.15 = (f32[2,512,128]{2,1,0:T(8,128)S(1)}, f32[2,512,128]{2,1,0:T(8,128)S(1)}, u32[]{:S(2)}, u32[]{:S(2)}) collective-permute-start(f32[2,512,128]{2,1,0:T(8,128)S(1)} %get-tuple-element.56.p), channel_id=1, source_target_pairs={{1,2},{3,4},{5,6},{7,8},{9,10},{11,12},{13,14},{15,16},{17,18},{19... | collective-permute-start | bytes 1572872 | tf_op jit(solution)/shard_map/ppermute | solution.py:327
  54.0 4.4 %collective-permute-start.7 = (f32[2,8,256]{2,1,0:T(8,128)S(1)}, f32[2,8,256]{2,1,0:T(8,128)S(1)}, u32[]{:S(2)}, u32[]{:S(2)}) collective-permute-start(f32[2,8,256]{2,1,0:T(8,128)S(1)} %get-tuple-element.59), channel_id=1, source_target_pairs={{0,2},{1,3},{2,0},{3,1},{4,6},{5,7},{6,4},{7,5},{8,10},{9,11},{10,... | collective-permute-start | bytes 49160 | tf_op jit(solution)/shard_map/ppermute | solution.py:301
  54.3 9.9 %collective-permute-start.8 = (f32[2,8,256]{2,1,0:T(8,128)S(1)}, f32[2,8,256]{2,1,0:T(8,128)S(1)}, u32[]{:S(2)}, u32[]{:S(2)}) collective-permute-start(f32[2,8,256]{2,1,0:T(8,128)S(1)} %get-tuple-element.59), channel_id=1, source_target_pairs={{0,6},{1,7},{2,4},{3,5},{4,2},{5,3},{6,0},{7,1},{8,14},{9,15},{10,... | collective-permute-start | bytes 49160 | tf_op jit(solution)/shard_map/ppermute | solution.py:301
  54.4 9.8 %collective-permute-start.9 = (f32[2,8,256]{2,1,0:T(8,128)S(1)}, f32[2,8,256]{2,1,0:T(8,128)S(1)}, u32[]{:S(2)}, u32[]{:S(2)}) collective-permute-start(f32[2,8,256]{2,1,0:T(8,128)S(1)} %get-tuple-element.59), channel_id=1, source_target_pairs={{0,4},{1,5},{2,6},{3,7},{4,0},{5,1},{6,2},{7,3},{8,12},{9,13},{10,... | collective-permute-start | bytes 49160 | tf_op jit(solution)/shard_map/ppermute | solution.py:301
  64.3 5.8 %collective-permute-start.10 = (f32[2,8,256]{2,1,0:T(8,128)S(1)}, f32[2,8,256]{2,1,0:T(8,128)S(1)}, u32[]{:S(2)}, u32[]{:S(2)}) collective-permute-start(f32[2,8,256]{2,1,0:T(8,128)S(1)} %add_add_fusion.1), channel_id=1, source_target_pairs={{0,1},{1,0},{2,3},{3,2},{4,5},{5,4},{6,7},{7,6},{8,9},{9,8},{10,11... | collective-permute-start | bytes 49160 | tf_op jit(solution)/shard_map/ppermute | solution.py:301
  64.5 7.2 %collective-permute-start.11 = (f32[2,8,256]{2,1,0:T(8,128)S(1)}, f32[2,8,256]{2,1,0:T(8,128)S(1)}, u32[]{:S(2)}, u32[]{:S(2)}) collective-permute-start(f32[2,8,256]{2,1,0:T(8,128)S(1)} %add_add_fusion.1), channel_id=1, source_target_pairs={{0,8},{1,9},{2,10},{3,11},{4,12},{5,13},{6,14},{7,15},{8,0},{9,1},... | collective-permute-start | bytes 49160 | tf_op jit(solution)/shard_map/ppermute | solution.py:301
  70.0 4.7 %collective-permute-start.12 = (f32[2,8,256]{2,1,0:T(8,128)S(1)}, f32[2,8,256]{2,1,0:T(8,128)S(1)}, u32[]{:S(2)}, u32[]{:S(2)}) collective-permute-start(f32[2,8,256]{2,1,0:T(8,128)S(1)} %add_add_fusion.1), channel_id=1, source_target_pairs={{0,9},{1,8},{2,11},{3,10},{4,13},{5,12},{6,15},{7,14},{8,1},{9,0},... | collective-permute-start | bytes 49160 | tf_op jit(solution)/shard_map/ppermute | solution.py:301
  74.7 3.7 %collective-permute-start.13 = (f32[2,8,256]{2,1,0:T(8,128)S(1)}, f32[2,8,256]{2,1,0:T(8,128)S(1)}, u32[]{:S(2)}, u32[]{:S(2)}) collective-permute-start(f32[2,8,256]{2,1,0:T(8,128)S(1)} %add_add_fusion), channel_id=1, source_target_pairs={{0,16},{1,17},{2,18},{3,19},{4,20},{5,21},{6,22},{7,23},{8,24},{9,... | collective-permute-start | bytes 49160 | tf_op jit(solution)/shard_map/ppermute | solution.py:301
  79.8 6.6 %collective-permute-start.16 = (f32[2,8,256]{2,1,0:T(8,128)S(1)}, f32[2,8,256]{2,1,0:T(8,128)S(1)}, u32[]{:S(2)}, u32[]{:S(2)}) collective-permute-start(f32[2,8,256]{2,1,0:T(8,128)S(1)} %add.37), channel_id=1, source_target_pairs={{0,112},{1,113},{2,114},{3,115},{4,116},{5,117},{6,118},{7,119},{8... | collective-permute-start | bytes 49160 | tf_op jit(solution)/shard_map/ppermute | solution.py:301
  86.3 9.1 %collective-permute-start.17 = (f32[2,8,256]{2,1,0:T(8,128)S(1)}, f32[2,8,256]{2,1,0:T(8,128)S(1)}, u32[]{:S(2)}, u32[]{:S(2)}) collective-permute-start(f32[2,8,256]{2,1,0:T(8,128)S(1)} %add.38), channel_id=1, source_target_pairs={{0,48},{1,49},{2,50},{3,51},{4,52},{5,53},{6,54},{7,55},{8,56},{9,... | collective-permute-start | bytes 49160 | tf_op jit(solution)/shard_map/ppermute | solution.py:301

commit v4 on v3

--- a/solution.py
+++ b/solution.py
@@ -35,7 +35,7 @@
         in_specs=specs,
         out_specs=tuple(VMEM for _ in outs),
         scratch_shapes=scratch,
-        compiler_params=pltpu.CompilerParams(vmem_limit_bytes=24 << 20),
+        compiler_params=pltpu.CompilerParams(vmem_limit_bytes=16 << 20),
         cost_estimate=pl.CostEstimate(flops=flops, bytes_accessed=moved, transcendentals=0),
         name=name,
     )(*ins)
@@ -235,26 +235,52 @@
     out_ref[...] = jnp.zeros(out_ref.shape, jnp.float32)
     for s in range(2):
         block, x_at, pick_z, pick_y = picks(cells_ref, s)
-        for n, field in enumerate((cs_ref, po, p)):
+        for n, field in ((0, cs_ref), (1, po), (2, p), (7, ck_ref)):
             out_ref[s, pl.ds(n, 1), :] = own_sample(samples(field, s, pick_z, pick_y), block, x_at, at_ref[0])
 
 
-def late_kernel(step, at_ref, source_ref, wavelet_ref, p, po, q, qo, c_ref, cs_ref, ck_ref, cells_ref, early_ref,
-                pre_p, pre_q, out_ref):
-    local_part(step, at_ref, source_ref, wavelet_ref, p, po, q, qo, c_ref, cs_ref, ck_ref, pre_p, pre_q)
+def weights(apart):
+    out = jnp.zeros(apart.shape, jnp.float32)
+    for k in range(5):
+        out = jnp.where(apart == k, taps[k], out)
+    return out
+
+
+def late_kernel(at_ref, source_ref, wavelet_ref, cells_ref, early_ref, p, q, out_ref):
     me = at_ref[0]
     out_ref[...] = early_ref[...]
     for s in range(2):
         block, x_at, pick_z, pick_y = picks(cells_ref, s)
-        values = samples(p, s, pick_z, pick_y)
-        out_ref[s, pl.ds(3, 1), :] = own_sample(values, block, x_at, me)
-        out_ref[s, pl.ds(4, 1), :] = own_sample(samples(pre_p, s, pick_z, pick_y), block, x_at, me)
-        hor = jnp.zeros(block.shape, jnp.float32)
+        cells = cells_ref[pl.ds(s, 1), :]
+        n = cells.shape[1]
+        band_z = weights(jnp.abs(lax.broadcasted_iota(jnp.int32, (CZ, n), 0) - cells % CZ))
+        band_y = weights(jnp.abs(lax.broadcasted_iota(jnp.int32, (CY, n), 0) - (cells // CZ) % CY))
+        here = jnp.zeros(block.shape, jnp.float32)
+        hor, ver, across = here, here, here
         for x in range(CX):
+            rest, spread = p[s, row(x), :], None
+            for _ in range(3):
+                part = rest.astype(jnp.bfloat16)
+                rest = rest - part.astype(jnp.float32)
+                picked = jnp.dot(part, pick_z, preferred_element_type=jnp.float32)
+                spread = picked if spread is None else spread + picked
+            value = jnp.sum(jnp.where(pick_y, spread, 0.0), axis=0, keepdims=True)
+            along_y = jnp.sum(band_y * spread, axis=0, keepdims=True)
+            along_z = jnp.dot(q[s, row(x), :], band_z, precision=EXACT, preferred_element_type=jnp.float32)
+            along_z = jnp.sum(jnp.where(pick_y, along_z, 0.0), axis=0, keepdims=True)
+            here = jnp.where(x_at == x, value, here)
+            hor = hor + weights(jnp.abs(x_at - x)) * value + jnp.where(x_at == x, along_y, 0.0)
+            ver = jnp.where(x_at == x, along_z, ver)
             apart = jnp.where(block == me + 1, x_at + 4 - x, jnp.where(block == me - 1, 4 + x - x_at, 9))
             for k in range(1, 5):
-                hor = hor + jnp.where(apart == k, taps[k] * values[x], 0.0)
-        out_ref[s, pl.ds(5, 1), :] = hor
+                across = across + jnp.where(apart == k, taps[k] * value, 0.0)
+        mine = jnp.where(block == me, 1.0, 0.0)
+        here = mine * here
+        gain = mine * jnp.where(cells == source_ref[s], wavelet_ref[s, STEPS - 1], 0.0)
+        early = [early_ref[s, pl.ds(k, 1), :] for k in (0, 2, 7)]
+        out_ref[s, pl.ds(3, 1), :] = here
+        out_ref[s, pl.ds(4, 1), :] = 2.0 * here - early[1] + (early[0] * hor + early[2] * ver) + gain
+        out_ref[s, pl.ds(5, 1), :] = across
 
 
 def even_pairs(n):
@@ -283,7 +309,6 @@
             for z in range(8) for xh in range(2) for y in range(4) for core in range(2)
         ]
 
-    far = {0: 3, 3: 0, 4: 7, 7: 4, 1: 6, 6: 1, 2: 5, 5: 2}
     return [
         [pairs(lambda z, xh, y, core, k=k: (z, xh, y ^ k, core)) for k in (1, 3, 2)],
         [
@@ -291,9 +316,14 @@
             pairs(lambda z, xh, y, core: (z, 1 - xh, y, core)),
             pairs(lambda z, xh, y, core: (z, 1 - xh, y, 1 - core)),
         ],
-        [pairs(lambda z, xh, y, core: (z ^ 1, xh, y, core))],
-        [pairs(lambda z, xh, y, core: ((z + 1 if z % 2 else z - 1) % 8, xh, y, core))],
-        [pairs(lambda z, xh, y, core: (far[z], xh, y, core))],
+        [
+            pairs(lambda z, xh, y, core: (z ^ 1, xh, y, core)),
+            pairs(lambda z, xh, y, core: ((z + 1 if z % 2 else z - 1) % 8, xh, y, core)),
+        ],
+        [
+            pairs(lambda z, xh, y, core: ((z - 3 if z % 2 else z + 3) % 8, xh, y, core)),
+            pairs(lambda z, xh, y, core: ((z + 3 if z % 2 else z - 3) % 8, xh, y, core)),
+        ],
     ]
 
 
@@ -301,6 +331,24 @@
     for part in [lax.ppermute(total, "space", pairs) for pairs in stage]:
         total = total + part
     return total
+
+
+def reduced(total, n, finish):
+    todo = stages(n)
+    if n != 128:
+        for stage in todo:
+            total = summed(total, stage)
+        return finish(total)
+    total = summed(summed(total, todo[0]), todo[1])
+    odd = (lax.axis_index("space") // 16) % 2 == 1
+    first, second = (lax.ppermute(total, "space", pairs) for pairs in todo[2])
+    two = total + jnp.where(odd, first, second)
+    three = total + (first + second)
+    even_part, odd_part = jnp.where(odd, two, three), jnp.where(odd, three, two)
+    (even_part, odd_part, three), p, q = finish((even_part, odd_part, three))
+    plus = lax.ppermute(even_part, "space", todo[3][0])
+    minus = lax.ppermute(odd_part, "space", todo[3][1])
+    return three + (plus + minus), p, q
 
 
 def per_device(pressure_now, pressure_old, auxiliary_now, auxiliary_old, velocity, epsilon_field, delta_field,
@@ -345,19 +393,22 @@
             pre_p, pre_q, early = call(
                 functools.partial(early_kernel, step), (*now, receiver_cells), (field, field, traced), 10**8, "local_early")
         if step == 3:
-            pre_p, pre_q, total = call(
-                functools.partial(late_kernel, step), (*now, receiver_cells, early), (field, field, traced), 10**8, "local_late")
-            todo = stages(blocks)
-            for stage in todo[:-2]:
-                total = summed(total, stage)
+            break
         po, qo = p, q
         p, q = call(
             halo_kernel, (odd, *halos, pre_p, pre_q, cs, ck), (field, field), 10**6, f"halo{step}")
-        if step < STEPS - 1:
+        if step < 2:
             halos = exchange(p)
-    total, p, q = lax.optimization_barrier((total, p, q))
-    for stage in todo[-2:]:
-        total = summed(total, stage)
+    total, = call(late_kernel, (at, source_cells, wavelet, receiver_cells, early, p, q), (traced,), 10**8, "late")
+    sent, total = lax.optimization_barrier((p, total))
+    halos = exchange(sent)
+
+    def finish(total):
+        pre_p, pre_q = call(functools.partial(local_kernel, 3), now, (field, field), 10**8, "local3")
+        last = call(halo_kernel, (odd, *halos, pre_p, pre_q, cs, ck), (field, field), 10**6, "halo3")
+        return lax.optimization_barrier((total, *last))
+
+    total, p, q = reduced(total, blocks, finish)
     last = total[:, 4] + total[:, 0] * total[:, 5]
     traces = jnp.stack([total[:, 1], total[:, 2], total[:, 3], last], axis=1)
     return (p.reshape(pressure_now.shape), q.reshape(pressure_now.shape), traces)

time: 96.4 us -> 97.5 us (1.011)
  the two profiles are of different devices: /device:TPU:24 before, /device:TPU:4 now
where the time goes in v4:
time: 97.5 us; the launch traced here: 97.1 us
  starting transfers between devices  42.5 us (44%)
  waiting for transfers between devices  32.1 us (33%)
  Pallas kernels  19.2 us (20%)
  local copies, waits for them, and re-layouts  1.72 us (2%)
    ppermute x4, waiting for transfers between devices, exchange(): lax.ppermute(values, 'space', odd_pairs(blocks))  23.6 us
    pallas_call x12, Pallas kernels, call(): pl.pallas_call(kernel, out_shape=tuple(outs), in_specs=specs, out_specs=t...  19.2 us
    ppermute x4, starting transfers between devices, exchange(): lax.ppermute(values, 'space', odd_pairs(blocks))  15.1 us
    ppermute x6, starting transfers between devices, summed(): lax.ppermute(total, 'space', pairs)  9.08 us
    ppermute x1, starting transfers between devices, reduced(): plus = lax.ppermute(even_part, 'space', todo[3][0])  8.25 us
    ppermute x2, starting transfers between devices, reduced(): first, second = (lax.ppermute(total, 'space', pairs) for pairs in todo[2])  7.81 us
    ppermute x1, waiting for transfers between devices, reduced(): minus = lax.ppermute(odd_part, 'space', todo[3][1])  5.03 us
  transfers between devices with their start and end apart: 19, of which 8 were waited for; matrix products, arithmetic and copies ran while one was open for 0% of the time, Pallas kernels for 12%

profile of v4, /device:TPU:4, one launch (start us, length us, event | category | flops | bytes accessed | tf_op | source)
XLA Modules:
  0.0 97.1 jit_solution(11438164671153554375)
XLA Ops:
  0.6 1.1 %model.1.own_ref.own = f32[3,256,128]{2,1,0:T(8,128)S(1)} custom-call(f32[256,128]{1,0:T(8,128)} %bitcast.22, f32[256,128]{1,0:T(8,128)} %bitcast.23, f32[256,128]{1,0:T(8,128)} %bitcast.24), custom_call_target="tpu_custom_call" | custom-call | flops 1000000 | bytes 786432 | tf_op jit(solution)/shard_map/model/pallas_call | solution.py:32
  1.8 1.3 %collective-permute-start.2 = (f32[3,256,128]{2,1,0:T(8,128)S(1)}, f32[3,256,128]{2,1,0:T(8,128)S(1)}, u32[]{:S(2)}, u32[]{:S(2)}) collective-permute-start(f32[3,256,128]{2,1,0:T(8,128)S(1)} %model.1.own_ref.own), channel_id=1, source_target_pairs={{0,128},{128,0},{1,129},{129,1},{2,130},{130,2},{3,131},{131,3},{4... | collective-permute-start | bytes 1179656 | tf_op jit(solution)/shard_map/ppermute | solution.py:377
  3.1 1.1 %begin.1 = (f32[2,512,128]{2,1,0:T(8,128)S(1)}, s32[8,128]{1,0:T(8,128)S(1)}, f32[16,128]{1,0:T(8,128)S(1)}) custom-call(s32[1]{0:T(128)} %bitcast.at_far.at_ref, s32[2]{0:T(128)} %bitcast.16, s32[2]{0:T(128)} %source_ref.9, f32[2,512,128]{2,1,0:T(8,128)} %bitcast.18, f32[3,256,128]{2,1,0:T(8,128)S(1)} %model.1.own_ref.own), custom_call_target="tpu_custom_call" | custom-call | flops 1000000 | bytes 1454100 | tf_op jit(solution)/shard_map/begin/pallas_call | solution.py:32
  4.3 5.2 %collective-permute-start.1 = (f32[2,512,128]{2,1,0:T(8,128)S(1)}, f32[2,512,128]{2,1,0:T(8,128)}, u32[]{:S(2)}, u32[]{:S(2)}) collective-permute-start(f32[2,512,128]{2,1,0:T(8,128)S(1)} %get-tuple-element.39.p0.po), channel_id=1, source_target_pairs={{1,2},{3,4},{5,6},{7,8},{9,10},{11,12},{13,14},{15,16},{17,18},{19... | collective-permute-start | bytes 1572872 | tf_op jit(solution)/shard_map/ppermute | solution.py:375
  9.6 0.6 copy-done.2
  10.2 3.3 %ready.1 = (f32[2,512,128]{2,1,0:T(8,128)S(1)}, f32[2,512,128]{2,1,0:T(8,128)S(1)}, f32[2,512,128]{2,1,0:T(8,128)S(1)}, f32[2,512,128]{2,1,0:T(8,128)S(1)}, f32[2,512,128]{2,1,0:T(8,128)S(1)}) custom-call(s32[1]{0:T(128)} %bitcast.at_far.at_ref, s32[2]{0:T(128)S(1)} %bitcast.17, s32[2]{0:T(128)S(1)} %copy-done.3, f32[2,4]{1,0:T(2,128)S(1)} %copy-done.2, ...), custom_call_target="tpu_custom_call" | custom-call | flops 100000000 | bytes 4718644 | tf_op jit(solution)/shard_map/ready/pallas_call | solution.py:32
  13.8 7.0 %collective-permute-done.1.odd_pair = f32[2,512,128]{2,1,0:T(8,128)} collective-permute-done((f32[2,512,128]{2,1,0:T(8,128)S(1)}, f32[2,512,128]{2,1,0:T(8,128)}, u32[]{:S(2)}, u32[]{:S(2)}) %collective-permute-start.1) | collective-permute-done | bytes 524320 | tf_op jit(solution)/shard_map/ppermute | solution.py:375
  20.9 1.3 %halo.1 = (f32[2,512,128]{2,1,0:T(8,128)S(1)}, f32[2,512,128]{2,1,0:T(8,128)S(1)}) custom-call(s32[8,128]{1,0:T(8,128)S(1)} %get-tuple-element.38.odd_ref, f32[2,512,128]{2,1,0:T(8,128)S(1)} %collective-permute-done.even_pair, f32[2,512,128]{2,1,0:T(8,128)} %collective-permute-done.1.odd_pair, f32[2,512,128]{2,1,0:T(8,128)S(1)} %get-tuple-element.45.pre_p, ...), custom_call_target="tpu_custom_call" | custom-call | flops 1000000 | bytes 4198400 | tf_op jit(solution)/shard_map/halo/pallas_call | solution.py:32
  22.3 3.7 %collective-permute-start.4 = (f32[2,512,128]{2,1,0:T(8,128)S(1)}, f32[2,512,128]{2,1,0:T(8,128)S(1)}, u32[]{:S(2)}, u32[]{:S(2)}) collective-permute-start(f32[2,512,128]{2,1,0:T(8,128)S(1)} %get-tuple-element.49.p.po), channel_id=1, source_target_pairs={{1,2},{3,4},{5,6},{7,8},{9,10},{11,12},{13,14},{15,16},{17,18},{19... | collective-permute-start | bytes 1572872 | tf_op jit(solution)/shard_map/ppermute | solution.py:375
  26.0 1.7 %local.1 = (f32[2,512,128]{2,1,0:T(8,128)S(1)}, f32[2,512,128]{2,1,0:T(8,128)S(1)}) custom-call(s32[1]{0:T(128)} %bitcast.at_far.at_ref, s32[2]{0:T(128)S(1)} %copy-done.3, f32[2,4]{1,0:T(2,128)S(1)} %copy-done.2, f32[2,512,128]{2,1,0:T(8,128)S(1)} %get-tuple-element.49.p.po, f32[2,512,128]{2,1,0:T(8,128)S(1)} %get-tuple-element.39.p0.po, ...), custom_call_target="tpu_custom_call" | custom-call | flops 100000000 | bytes 4718636 | tf_op jit(solution)/shard_map/local/pallas_call | solution.py:32
  27.8 8.6 %collective-permute-done.4.odd_pair = f32[2,512,128]{2,1,0:T(8,128)S(1)} collective-permute-done((f32[2,512,128]{2,1,0:T(8,128)S(1)}, f32[2,512,128]{2,1,0:T(8,128)S(1)}, u32[]{:S(2)}, u32[]{:S(2)}) %collective-permute-start.4) | collective-permute-done | bytes 524320 | tf_op jit(solution)/shard_map/ppermute | solution.py:375
  36.8 3.7 %collective-permute-start.6 = (f32[2,512,128]{2,1,0:T(8,128)S(1)}, f32[2,512,128]{2,1,0:T(8,128)S(1)}, u32[]{:S(2)}, u32[]{:S(2)}) collective-permute-start(f32[2,512,128]{2,1,0:T(8,128)S(1)} %get-tuple-element.55.p.po), channel_id=1, source_target_pairs={{1,2},{3,4},{5,6},{7,8},{9,10},{11,12},{13,14},{15,16},{17,18},{19... | collective-permute-start | bytes 1572872 | tf_op jit(solution)/shard_map/ppermute | solution.py:375
  40.5 3.5 %local_early.1 = (f32[2,512,128]{2,1,0:T(8,128)S(1)}, f32[2,512,128]{2,1,0:T(8,128)S(1)}, f32[2,8,256]{2,1,0:T(8,128)S(1)}) custom-call(s32[1]{0:T(128)} %bitcast.at_far.at_ref, s32[2]{0:T(128)S(1)} %copy-done.3, f32[2,4]{1,0:T(2,128)S(1)} %copy-done.2, f32[2,512,128]{2,1,0:T(8,128)S(1)} %get-tuple-element.55.p.po, ...), custom_call_target="tpu_custom_call" | custom-call | flops 100000000 | bytes 4737068 | tf_op jit(solution)/shard_map/local_early/pallas_call | solution.py:32
  44.0 6.9 %collective-permute-done.6.odd_pair = f32[2,512,128]{2,1,0:T(8,128)S(1)} collective-permute-done((f32[2,512,128]{2,1,0:T(8,128)S(1)}, f32[2,512,128]{2,1,0:T(8,128)S(1)}, u32[]{:S(2)}, u32[]{:S(2)}) %collective-permute-start.6) | collective-permute-done | bytes 524320 | tf_op jit(solution)/shard_map/ppermute | solution.py:375
  51.2 2.1 %late.1 = f32[2,8,256]{2,1,0:T(8,128)S(1)} custom-call(s32[1]{0:T(128)} %bitcast.at_far.at_ref, s32[2]{0:T(128)S(1)} %copy-done.3, f32[2,4]{1,0:T(2,128)S(1)} %copy-done.2, s32[2,256]{1,0:T(2,128)S(1)} %copy-done.4, f32[2,8,256]{2,1,0:T(8,128)S(1)} %get-tuple-element.60.early_ref, f32[2,512,128]{2,1,0:T(8,128)S(1)} %get-tuple-element.63.p, ...), custom_call_target="tpu_custom_call" | custom-call | flops 100000000 | bytes 1083436 | tf_op jit(solution)/shard_map/late/pallas_call | solution.py:32
  53.5 4.0 %collective-permute-start.9 = (f32[2,8,256]{2,1,0:T(8,128)S(1)}, f32[2,8,256]{2,1,0:T(8,128)S(1)}, u32[]{:S(2)}, u32[]{:S(2)}) collective-permute-start(f32[2,8,256]{2,1,0:T(8,128)S(1)} %late.1), channel_id=1, source_target_pairs={{0,4},{1,5},{2,6},{3,7},{4,0},{5,1},{6,2},{7,3},{8,12},{9,13},{10,... | collective-permute-start | bytes 49160 | tf_op jit(solution)/shard_map/ppermute | solution.py:331
  57.5 1.1 %collective-permute-done.8 = f32[2,8,256]{2,1,0:T(8,128)S(1)} collective-permute-done((f32[2,8,256]{2,1,0:T(8,128)S(1)}, f32[2,8,256]{2,1,0:T(8,128)S(1)}, u32[]{:S(2)}, u32[]{:S(2)}) %collective-permute-start.8) | collective-permute-done | bytes 16416 | tf_op jit(solution)/shard_map/ppermute | solution.py:331
  58.6 0.6 collective-permute-done.9
  59.2 2.0 %collective-permute-start.10 = (f32[2,8,256]{2,1,0:T(8,128)S(1)}, f32[2,8,256]{2,1,0:T(8,128)S(1)}, u32[]{:S(2)}, u32[]{:S(2)}) collective-permute-start(f32[2,8,256]{2,1,0:T(8,128)S(1)} %add_add_fusion.3), channel_id=1, source_target_pairs={{0,1},{1,0},{2,3},{3,2},{4,5},{5,4},{6,7},{7,6},{8,9},{9,8},{10,11... | collective-permute-start | bytes 49160 | tf_op jit(solution)/shard_map/ppermute | solution.py:331
  61.2 2.9 %collective-permute-start.12 = (f32[2,8,256]{2,1,0:T(8,128)S(1)}, f32[2,8,256]{2,1,0:T(8,128)S(1)}, u32[]{:S(2)}, u32[]{:S(2)}) collective-permute-start(f32[2,8,256]{2,1,0:T(8,128)S(1)} %add_add_fusion.3), channel_id=1, source_target_pairs={{0,9},{1,8},{2,11},{3,10},{4,13},{5,12},{6,15},{7,14},{8,1},{9,0},... | collective-permute-start | bytes 49160 | tf_op jit(solution)/shard_map/ppermute | solution.py:331
  64.2 0.7 collective-permute-start.15
  64.8 2.4 %collective-permute-start.16 = (f32[2,512,128]{2,1,0:T(8,128)S(1)}, f32[2,512,128]{2,1,0:T(8,128)}, u32[]{:S(2)}, u32[]{:S(2)}) collective-permute-start(f32[2,512,128]{2,1,0:T(8,128)S(1)} %get-tuple-element.63.p), channel_id=1, source_target_pairs={{1,2},{3,4},{5,6},{7,8},{9,10},{11,12},{13,14},{15,16},{17,18},{19... | collective-permute-start | bytes 1572872 | tf_op jit(solution)/shard_map/ppermute | solution.py:375
  67.3 2.9 %collective-permute-start.13 = (f32[2,8,256]{2,1,0:T(8,128)S(1)}, f32[2,8,256]{2,1,0:T(8,128)S(1)}, u32[]{:S(2)}, u32[]{:S(2)}) collective-permute-start(f32[2,8,256]{2,1,0:T(8,128)S(1)} %add_add_fusion.2), channel_id=1, source_target_pairs={{0,16},{1,17},{2,18},{3,19},{4,20},{5,21},{6,22},{7,23},{8,24},{9,... | collective-permute-start | bytes 49160 | tf_op jit(solution)/shard_map/ppermute | solution.py:344
  70.2 4.9 %collective-permute-start.14 = (f32[2,8,256]{2,1,0:T(8,128)S(1)}, f32[2,8,256]{2,1,0:T(8,128)S(1)}, u32[]{:S(2)}, u32[]{:S(2)}) collective-permute-start(f32[2,8,256]{2,1,0:T(8,128)S(1)} %add_add_fusion.2), channel_id=1, source_target_pairs={{0,112},{1,113},{2,114},{3,115},{4,116},{5,117},{6,118},{7,119},{8... | collective-permute-start | bytes 49160 | tf_op jit(solution)/shard_map/ppermute | solution.py:344
  75.1 1.0 %copy-done.1 = f32[2,512,128]{2,1,0:T(8,128)S(1)} copy-done((f32[2,512,128]{2,1,0:T(8,128)S(1)}, f32[2,512,128]{2,1,0:T(8,128)}, u32[]{:S(2)}) %copy-start.1) | copy-done | bytes 524312
  76.2 1.8 %local3.1 = (f32[2,512,128]{2,1,0:T(8,128)S(1)}, f32[2,512,128]{2,1,0:T(8,128)S(1)}) custom-call(s32[1]{0:T(128)} %bitcast.at_far.at_ref, s32[2]{0:T(128)S(1)} %copy-done.3, f32[2,4]{1,0:T(2,128)S(1)} %copy-done.2, f32[2,512,128]{2,1,0:T(8,128)S(1)} %get-tuple-element.63.p, f32[2,512,128]{2,1,0:T(8,128)S(1)} %get-tuple-element.55.p.po, ...), custom_call_target="tpu_custom_call" | custom-call | flops 100000000 | bytes 4718636 | tf_op jit(solution)/shard_map/local3/pallas_call | solution.py:32
  78.0 1.1 %collective-permute-done.16.odd_pair = f32[2,512,128]{2,1,0:T(8,128)} collective-permute-done((f32[2,512,128]{2,1,0:T(8,128)S(1)}, f32[2,512,128]{2,1,0:T(8,128)}, u32[]{:S(2)}, u32[]{:S(2)}) %collective-permute-start.16) | collective-permute-done | bytes 524320 | tf_op jit(solution)/shard_map/ppermute | solution.py:375
  79.1 2.4 %halo3.1 = (f32[2,512,128]{2,1,0:T(8,128)}, f32[2,512,128]{2,1,0:T(8,128)}) custom-call(s32[8,128]{1,0:T(8,128)S(1)} %get-tuple-element.38.odd_ref, f32[2,512,128]{2,1,0:T(8,128)} %collective-permute-done.15.even_pair, f32[2,512,128]{2,1,0:T(8,128)} %collective-permute-done.16.odd_pair, f32[2,512,128]{2,1,0:T(8,128)S(1)} %get-tuple-element.64.pre_p, ...), custom_call_target="tpu_custom_call" | custom-call | flops 1000000 | bytes 4198400 | tf_op jit(solution)/shard_map/halo3/pallas_call | solution.py:32
  81.5 8.3 %collective-permute-start.17 = (f32[2,8,256]{2,1,0:T(8,128)S(1)}, f32[2,8,256]{2,1,0:T(8,128)S(1)}, u32[]{:S(2)}, u32[]{:S(2)}) collective-permute-start(f32[2,8,256]{2,1,0:T(8,128)S(1)} %broadcast_select_fusion.1), channel_id=1, source_target_pairs={{0,48},{1,49},{2,50},{3,51},{4,52},{5,53},{6,54},{7,55},{8,56},{9,... | collective-permute-start | bytes 49160 | tf_op jit(solution)/shard_map/ppermute | solution.py:349
  89.7 1.7 %collective-permute-done.17 = f32[2,8,256]{2,1,0:T(8,128)S(1)} collective-permute-done((f32[2,8,256]{2,1,0:T(8,128)S(1)}, f32[2,8,256]{2,1,0:T(8,128)S(1)}, u32[]{:S(2)}, u32[]{:S(2)}) %collective-permute-start.17) | collective-permute-done | bytes 16416 | tf_op jit(solution)/shard_map/ppermute | solution.py:349
  91.4 5.0 %collective-permute-done.18 = f32[2,8,256]{2,1,0:T(8,128)S(1)} collective-permute-done((f32[2,8,256]{2,1,0:T(8,128)S(1)}, f32[2,8,256]{2,1,0:T(8,128)S(1)}, u32[]{:S(2)}, u32[]{:S(2)}) %collective-permute-start.18) | collective-permute-done | bytes 16416 | tf_op jit(solution)/shard_map/ppermute | solution.py:350
  96.5 0.6 pad_maximum_fusion
  (38 shorter events, 1.4 us)
Async XLA Ops:
  1.8 11.7 %collective-permute-start.2 = (f32[3,256,128]{2,1,0:T(8,128)S(1)}, f32[3,256,128]{2,1,0:T(8,128)S(1)}, u32[]{:S(2)}, u32[]{:S(2)}) collective-permute-start(f32[3,256,128]{2,1,0:T(8,128)S(1)} %model.1.own_ref.own), channel_id=1, source_target_pairs={{0,128},{128,0},{1,129},{129,1},{2,130},{130,2},{3,131},{131,3},{4... | collective-permute-start | bytes 1179656 | tf_op jit(solution)/shard_map/ppermute | solution.py:377
  3.1 6.5 %copy-start.5 = (s32[2,1]{0,1:T(1,128)S(1)}, s32[2,1]{0,1:T(1,128)}, u32[]{:S(2)}) copy-start(s32[2,1]{0,1:T(1,128)} %param.18) | copy-start | bytes 28
  4.2 9.6 %collective-permute-start = (f32[2,512,128]{2,1,0:T(8,128)S(1)}, f32[2,512,128]{2,1,0:T(8,128)S(1)}, u32[]{:S(2)}, u32[]{:S(2)}) collective-permute-start(f32[2,512,128]{2,1,0:T(8,128)S(1)} %get-tuple-element.39.p0.po), channel_id=1, source_target_pairs={{0,1},{1,0},{2,3},{3,2},{4,5},{5,4},{6,7},{7,6},{8,9},{9,8},{10,11... | collective-permute-start | bytes 1572872 | tf_op jit(solution)/shard_map/ppermute | solution.py:375
  4.3 16.6 %collective-permute-start.1 = (f32[2,512,128]{2,1,0:T(8,128)S(1)}, f32[2,512,128]{2,1,0:T(8,128)}, u32[]{:S(2)}, u32[]{:S(2)}) collective-permute-start(f32[2,512,128]{2,1,0:T(8,128)S(1)} %get-tuple-element.39.p0.po), channel_id=1, source_target_pairs={{1,2},{3,4},{5,6},{7,8},{9,10},{11,12},{13,14},{15,16},{17,18},{19... | collective-permute-start | bytes 1572872 | tf_op jit(solution)/shard_map/ppermute | solution.py:375
  9.6 0.7 copy-start.2
  9.6 0.7 copy-start.3
  22.2 5.6 %collective-permute-start.3 = (f32[2,512,128]{2,1,0:T(8,128)S(1)}, f32[2,512,128]{2,1,0:T(8,128)S(1)}, u32[]{:S(2)}, u32[]{:S(2)}) collective-permute-start(f32[2,512,128]{2,1,0:T(8,128)S(1)} %get-tuple-element.49.p.po), channel_id=1, source_target_pairs={{0,1},{1,0},{2,3},{3,2},{4,5},{5,4},{6,7},{7,6},{8,9},{9,8},{10,11... | collective-permute-start | bytes 1572872 | tf_op jit(solution)/shard_map/ppermute | solution.py:375
  22.3 14.1 %collective-permute-start.4 = (f32[2,512,128]{2,1,0:T(8,128)S(1)}, f32[2,512,128]{2,1,0:T(8,128)S(1)}, u32[]{:S(2)}, u32[]{:S(2)}) collective-permute-start(f32[2,512,128]{2,1,0:T(8,128)S(1)} %get-tuple-element.49.p.po), channel_id=1, source_target_pairs={{1,2},{3,4},{5,6},{7,8},{9,10},{11,12},{13,14},{15,16},{17,18},{19... | collective-permute-start | bytes 1572872 | tf_op jit(solution)/shard_map/ppermute | solution.py:375
  36.7 7.3 %copy-start = (f32[2,512,128]{2,1,0:T(8,128)}, f32[2,512,128]{2,1,0:T(8,128)S(1)}, u32[]{:S(2)}) copy-start(f32[2,512,128]{2,1,0:T(8,128)S(1)} %get-tuple-element.56.q.qo) | copy-start | bytes 1572868
  36.7 3.8 %copy-start.4 = (s32[2,256]{1,0:T(2,128)S(1)}, s32[2,256]{1,0:T(2,128)}, u32[]{:S(2)}) copy-start(s32[2,256]{1,0:T(2,128)} %cells_ref.3) | copy-start | bytes 6148
  36.7 7.3 %collective-permute-start.5 = (f32[2,512,128]{2,1,0:T(8,128)S(1)}, f32[2,512,128]{2,1,0:T(8,128)S(1)}, u32[]{:S(2)}, u32[]{:S(2)}) collective-permute-start(f32[2,512,128]{2,1,0:T(8,128)S(1)} %get-tuple-element.55.p.po), channel_id=1, source_target_pairs={{0,1},{1,0},{2,3},{3,2},{4,5},{5,4},{6,7},{7,6},{8,9},{9,8},{10,11... | collective-permute-start | bytes 1572872 | tf_op jit(solution)/shard_map/ppermute | solution.py:375
  36.8 14.1 %collective-permute-start.6 = (f32[2,512,128]{2,1,0:T(8,128)S(1)}, f32[2,512,128]{2,1,0:T(8,128)S(1)}, u32[]{:S(2)}, u32[]{:S(2)}) collective-permute-start(f32[2,512,128]{2,1,0:T(8,128)S(1)} %get-tuple-element.55.p.po), channel_id=1, source_target_pairs={{1,2},{3,4},{5,6},{7,8},{9,10},{11,12},{13,14},{15,16},{17,18},{19... | collective-permute-start | bytes 1572872 | tf_op jit(solution)/shard_map/ppermute | solution.py:375
  53.3 4.2 %collective-permute-start.7 = (f32[2,8,256]{2,1,0:T(8,128)S(1)}, f32[2,8,256]{2,1,0:T(8,128)S(1)}, u32[]{:S(2)}, u32[]{:S(2)}) collective-permute-start(f32[2,8,256]{2,1,0:T(8,128)S(1)} %late.1), channel_id=1, source_target_pairs={{0,2},{1,3},{2,0},{3,1},{4,6},{5,7},{6,4},{7,5},{8,10},{9,11},{10,... | collective-permute-start | bytes 49160 | tf_op jit(solution)/shard_map/ppermute | solution.py:331
  53.4 5.1 %collective-permute-start.8 = (f32[2,8,256]{2,1,0:T(8,128)S(1)}, f32[2,8,256]{2,1,0:T(8,128)S(1)}, u32[]{:S(2)}, u32[]{:S(2)}) collective-permute-start(f32[2,8,256]{2,1,0:T(8,128)S(1)} %late.1), channel_id=1, source_target_pairs={{0,6},{1,7},{2,4},{3,5},{4,2},{5,3},{6,0},{7,1},{8,14},{9,15},{10,... | collective-permute-start | bytes 49160 | tf_op jit(solution)/shard_map/ppermute | solution.py:331
  53.5 5.7 %collective-permute-start.9 = (f32[2,8,256]{2,1,0:T(8,128)S(1)}, f32[2,8,256]{2,1,0:T(8,128)S(1)}, u32[]{:S(2)}, u32[]{:S(2)}) collective-permute-start(f32[2,8,256]{2,1,0:T(8,128)S(1)} %late.1), channel_id=1, source_target_pairs={{0,4},{1,5},{2,6},{3,7},{4,0},{5,1},{6,2},{7,3},{8,12},{9,13},{10,... | collective-permute-start | bytes 49160 | tf_op jit(solution)/shard_map/ppermute | solution.py:331
  59.2 8.0 %collective-permute-start.10 = (f32[2,8,256]{2,1,0:T(8,128)S(1)}, f32[2,8,256]{2,1,0:T(8,128)S(1)}, u32[]{:S(2)}, u32[]{:S(2)}) collective-permute-start(f32[2,8,256]{2,1,0:T(8,128)S(1)} %add_add_fusion.3), channel_id=1, source_target_pairs={{0,1},{1,0},{2,3},{3,2},{4,5},{5,4},{6,7},{7,6},{8,9},{9,8},{10,11... | collective-permute-start | bytes 49160 | tf_op jit(solution)/shard_map/ppermute | solution.py:331
  61.2 6.1 %collective-permute-start.11 = (f32[2,8,256]{2,1,0:T(8,128)S(1)}, f32[2,8,256]{2,1,0:T(8,128)S(1)}, u32[]{:S(2)}, u32[]{:S(2)}) collective-permute-start(f32[2,8,256]{2,1,0:T(8,128)S(1)} %add_add_fusion.3), channel_id=1, source_target_pairs={{0,8},{1,9},{2,10},{3,11},{4,12},{5,13},{6,14},{7,15},{8,0},{9,1},... | collective-permute-start | bytes 49160 | tf_op jit(solution)/shard_map/ppermute | solution.py:331
  61.2 6.1 %collective-permute-start.12 = (f32[2,8,256]{2,1,0:T(8,128)S(1)}, f32[2,8,256]{2,1,0:T(8,128)S(1)}, u32[]{:S(2)}, u32[]{:S(2)}) collective-permute-start(f32[2,8,256]{2,1,0:T(8,128)S(1)} %add_add_fusion.3), channel_id=1, source_target_pairs={{0,9},{1,8},{2,11},{3,10},{4,13},{5,12},{6,15},{7,14},{8,1},{9,0},... | collective-permute-start | bytes 49160 | tf_op jit(solution)/shard_map/ppermute | solution.py:331
  64.2 13.8 %collective-permute-start.15 = (f32[2,512,128]{2,1,0:T(8,128)S(1)}, f32[2,512,128]{2,1,0:T(8,128)}, u32[]{:S(2)}, u32[]{:S(2)}) collective-permute-start(f32[2,512,128]{2,1,0:T(8,128)S(1)} %get-tuple-element.63.p), channel_id=1, source_target_pairs={{0,1},{1,0},{2,3},{3,2},{4,5},{5,4},{6,7},{7,6},{8,9},{9,8},{10,11... | collective-permute-start | bytes 1572872 | tf_op jit(solution)/shard_map/ppermute | solution.py:375
  64.8 14.2 %collective-permute-start.16 = (f32[2,512,128]{2,1,0:T(8,128)S(1)}, f32[2,512,128]{2,1,0:T(8,128)}, u32[]{:S(2)}, u32[]{:S(2)}) collective-permute-start(f32[2,512,128]{2,1,0:T(8,128)S(1)} %get-tuple-element.63.p), channel_id=1, source_target_pairs={{1,2},{3,4},{5,6},{7,8},{9,10},{11,12},{13,14},{15,16},{17,18},{19... | collective-permute-start | bytes 1572872 | tf_op jit(solution)/shard_map/ppermute | solution.py:375
  67.3 10.6 %collective-permute-start.13 = (f32[2,8,256]{2,1,0:T(8,128)S(1)}, f32[2,8,256]{2,1,0:T(8,128)S(1)}, u32[]{:S(2)}, u32[]{:S(2)}) collective-permute-start(f32[2,8,256]{2,1,0:T(8,128)S(1)} %add_add_fusion.2), channel_id=1, source_target_pairs={{0,16},{1,17},{2,18},{3,19},{4,20},{5,21},{6,22},{7,23},{8,24},{9,... | collective-permute-start | bytes 49160 | tf_op jit(solution)/shard_map/ppermute | solution.py:344
  70.2 7.8 %collective-permute-start.14 = (f32[2,8,256]{2,1,0:T(8,128)S(1)}, f32[2,8,256]{2,1,0:T(8,128)S(1)}, u32[]{:S(2)}, u32[]{:S(2)}) collective-permute-start(f32[2,8,256]{2,1,0:T(8,128)S(1)} %add_add_fusion.2), channel_id=1, source_target_pairs={{0,112},{1,113},{2,114},{3,115},{4,116},{5,117},{6,118},{7,119},{8... | collective-permute-start | bytes 49160 | tf_op jit(solution)/shard_map/ppermute | solution.py:344
  75.1 1.0 %copy-start.1 = (f32[2,512,128]{2,1,0:T(8,128)S(1)}, f32[2,512,128]{2,1,0:T(8,128)}, u32[]{:S(2)}) copy-start(f32[2,512,128]{2,1,0:T(8,128)} %copy-done) | copy-start | bytes 1572868
  81.5 10.0 %collective-permute-start.17 = (f32[2,8,256]{2,1,0:T(8,128)S(1)}, f32[2,8,256]{2,1,0:T(8,128)S(1)}, u32[]{:S(2)}, u32[]{:S(2)}) collective-permute-start(f32[2,8,256]{2,1,0:T(8,128)S(1)} %broadcast_select_fusion.1), channel_id=1, source_target_pairs={{0,48},{1,49},{2,50},{3,51},{4,52},{5,53},{6,54},{7,55},{8,56},{9,... | collective-permute-start | bytes 49160 | tf_op jit(solution)/shard_map/ppermute | solution.py:349
  89.7 6.7 %collective-permute-start.18 = (f32[2,8,256]{2,1,0:T(8,128)S(1)}, f32[2,8,256]{2,1,0:T(8,128)S(1)}, u32[]{:S(2)}, u32[]{:S(2)}) collective-permute-start(f32[2,8,256]{2,1,0:T(8,128)S(1)} %get-tuple-element.72), channel_id=1, source_target_pairs={{0,80},{1,81},{2,82},{3,83},{4,84},{5,85},{6,86},{7,87},{8,88},{9,... | collective-permute-start | bytes 49160 | tf_op jit(solution)/shard_map/ppermute | solution.py:350

commit v5 on v4

--- a/solution.py
+++ b/solution.py
@@ -333,22 +333,22 @@
     return total
 
 
-def reduced(total, n, finish):
+def reduced(total, n, gate, last_gate):
     todo = stages(n)
     if n != 128:
-        for stage in todo:
+        total = gate(summed(total, todo[0]))
+        for stage in todo[1:]:
             total = summed(total, stage)
-        return finish(total)
-    total = summed(summed(total, todo[0]), todo[1])
+        return last_gate(total)
     odd = (lax.axis_index("space") // 16) % 2 == 1
     first, second = (lax.ppermute(total, "space", pairs) for pairs in todo[2])
     two = total + jnp.where(odd, first, second)
     three = total + (first + second)
-    even_part, odd_part = jnp.where(odd, two, three), jnp.where(odd, three, two)
-    (even_part, odd_part, three), p, q = finish((even_part, odd_part, three))
+    even_part, odd_part, three = gate((jnp.where(odd, two, three), jnp.where(odd, three, two), three))
     plus = lax.ppermute(even_part, "space", todo[3][0])
     minus = lax.ppermute(odd_part, "space", todo[3][1])
-    return three + (plus + minus), p, q
+    total = three + (plus + minus)
+    return summed(last_gate(summed(total, todo[0])), todo[1])
 
 
 def per_device(pressure_now, pressure_old, auxiliary_now, auxiliary_old, velocity, epsilon_field, delta_field,
@@ -403,12 +403,20 @@
     sent, total = lax.optimization_barrier((p, total))
     halos = exchange(sent)
 
-    def finish(total):
-        pre_p, pre_q = call(functools.partial(local_kernel, 3), now, (field, field), 10**8, "local3")
-        last = call(halo_kernel, (odd, *halos, pre_p, pre_q, cs, ck), (field, field), 10**6, "halo3")
-        return lax.optimization_barrier((total, *last))
-
-    total, p, q = reduced(total, blocks, finish)
+    local = call(functools.partial(local_kernel, 3), now, (field, field), 10**8, "local3")
+
+    def gate(total):
+        nonlocal local
+        total, local = lax.optimization_barrier((total, local))
+        return total
+
+    def last_gate(total):
+        nonlocal halos
+        total, halos = lax.optimization_barrier((total, halos))
+        return total
+
+    total = reduced(total, blocks, gate, last_gate)
+    p, q = call(halo_kernel, (odd, *halos, *local, cs, ck), (field, field), 2 * 10**10, "halo3")
     last = total[:, 4] + total[:, 0] * total[:, 5]
     traces = jnp.stack([total[:, 1], total[:, 2], total[:, 3], last], axis=1)
     return (p.reshape(pressure_now.shape), q.reshape(pressure_now.shape), traces)

time: 97.5 us -> 93.9 us (0.963)
  the two profiles are of different devices: /device:TPU:4 before, /device:TPU:1 now
where the time goes in v5:
time: 93.9 us; the launch traced here: 93.5 us
  starting transfers between devices  54.9 us (58%)
  Pallas kernels  18 us (19%)
  waiting for transfers between devices  15.6 us (17%)
  local copies, waits for them, and re-layouts  3.45 us (4%)
    pallas_call x12, Pallas kernels, call(): pl.pallas_call(kernel, out_shape=tuple(outs), in_specs=specs, out_specs=t...  18 us
    ppermute x2, starting transfers between devices, reduced(): first, second = (lax.ppermute(total, 'space', pairs) for pairs in todo[2])  15.9 us
    ppermute x6, starting transfers between devices, summed(): lax.ppermute(total, 'space', pairs)  12.5 us
    ppermute x4, starting transfers between devices, exchange(): lax.ppermute(values, 'space', odd_pairs(blocks))  11.5 us
    ppermute x4, waiting for transfers between devices, exchange(): lax.ppermute(values, 'space', odd_pairs(blocks))  10.8 us
    ppermute x4, starting transfers between devices, exchange(): lax.ppermute(values, 'space', even_pairs(blocks))  6.3 us
    ppermute x1, starting transfers between devices, reduced(): minus = lax.ppermute(odd_part, 'space', todo[3][1])  4.02 us
    unnamed x16, local copies, waits for them, and re-layouts  3.45 us
  transfers between devices with their start and end apart: 19, of which 7 were waited for; matrix products, arithmetic and copies ran while one was open for 0% of the time, Pallas kernels for 14%

profile of v5, /device:TPU:1, one launch (start us, length us, event | category | flops | bytes accessed | tf_op | source)
XLA Modules:
  0.0 93.5 jit_solution(12031609758260962458)
XLA Ops:
  0.6 1.1 %model.1.own_ref.own = f32[3,256,128]{2,1,0:T(8,128)S(1)} custom-call(f32[256,128]{1,0:T(8,128)} %bitcast.22, f32[256,128]{1,0:T(8,128)} %bitcast.23, f32[256,128]{1,0:T(8,128)} %bitcast.24), custom_call_target="tpu_custom_call" | custom-call | flops 1000000 | bytes 786432 | tf_op jit(solution)/shard_map/model/pallas_call | solution.py:32
  1.8 2.1 %collective-permute-start.2 = (f32[3,256,128]{2,1,0:T(8,128)S(1)}, f32[3,256,128]{2,1,0:T(8,128)S(1)}, u32[]{:S(2)}, u32[]{:S(2)}) collective-permute-start(f32[3,256,128]{2,1,0:T(8,128)S(1)} %model.1.own_ref.own), channel_id=1, source_target_pairs={{0,128},{128,0},{1,129},{129,1},{2,130},{130,2},{3,131},{131,3},{4... | collective-permute-start | bytes 1179656 | tf_op jit(solution)/shard_map/ppermute | solution.py:377
  3.9 1.1 %begin.1 = (f32[2,512,128]{2,1,0:T(8,128)S(1)}, s32[8,128]{1,0:T(8,128)S(1)}, f32[16,128]{1,0:T(8,128)S(1)}) custom-call(s32[1]{0:T(128)} %bitcast.at_far.at_ref, s32[2]{0:T(128)} %bitcast.16, s32[2]{0:T(128)} %source_ref.9, f32[2,512,128]{2,1,0:T(8,128)} %bitcast.18, f32[3,256,128]{2,1,0:T(8,128)S(1)} %model.1.own_ref.own), custom_call_target="tpu_custom_call" | custom-call | flops 1000000 | bytes 1454100 | tf_op jit(solution)/shard_map/begin/pallas_call | solution.py:32
  5.0 1.3 %collective-permute-start = (f32[2,512,128]{2,1,0:T(8,128)S(1)}, f32[2,512,128]{2,1,0:T(8,128)S(1)}, u32[]{:S(2)}, u32[]{:S(2)}) collective-permute-start(f32[2,512,128]{2,1,0:T(8,128)S(1)} %get-tuple-element.42.p0.po), channel_id=1, source_target_pairs={{0,1},{1,0},{2,3},{3,2},{4,5},{5,4},{6,7},{7,6},{8,9},{9,8},{10,11... | collective-permute-start | bytes 1572872 | tf_op jit(solution)/shard_map/ppermute | solution.py:375
  6.3 2.8 %collective-permute-start.1 = (f32[2,512,128]{2,1,0:T(8,128)S(1)}, f32[2,512,128]{2,1,0:T(8,128)}, u32[]{:S(2)}, u32[]{:S(2)}) collective-permute-start(f32[2,512,128]{2,1,0:T(8,128)S(1)} %get-tuple-element.42.p0.po), channel_id=1, source_target_pairs={{1,2},{3,4},{5,6},{7,8},{9,10},{11,12},{13,14},{15,16},{17,18},{19... | collective-permute-start | bytes 1572872 | tf_op jit(solution)/shard_map/ppermute | solution.py:375
  9.9 3.3 %ready.1 = (f32[2,512,128]{2,1,0:T(8,128)S(1)}, f32[2,512,128]{2,1,0:T(8,128)S(1)}, f32[2,512,128]{2,1,0:T(8,128)S(1)}, f32[2,512,128]{2,1,0:T(8,128)S(1)}, f32[2,512,128]{2,1,0:T(8,128)S(1)}) custom-call(s32[1]{0:T(128)} %bitcast.at_far.at_ref, s32[2]{0:T(128)S(1)} %bitcast.17, s32[2]{0:T(128)S(1)} %copy-done.3, f32[2,4]{1,0:T(2,128)S(1)} %copy-done.2, ...), custom_call_target="tpu_custom_call" | custom-call | flops 100000000 | bytes 4718644 | tf_op jit(solution)/shard_map/ready/pallas_call | solution.py:32
  13.2 0.7 copy-done.6
  13.9 1.0 %copy-done.7 = f32[3,256,128]{2,1,0:T(8,128)S(1)} copy-done((f32[3,256,128]{2,1,0:T(8,128)S(1)}, f32[3,256,128]{2,1,0:T(8,128)}, u32[]{:S(2)}) %copy-start.7) | copy-done | bytes 393240
  15.2 1.8 %collective-permute-done.1.odd_pair = f32[2,512,128]{2,1,0:T(8,128)} collective-permute-done((f32[2,512,128]{2,1,0:T(8,128)S(1)}, f32[2,512,128]{2,1,0:T(8,128)}, u32[]{:S(2)}, u32[]{:S(2)}) %collective-permute-start.1) | collective-permute-done | bytes 524320 | tf_op jit(solution)/shard_map/ppermute | solution.py:375
  16.9 1.3 %halo.1 = (f32[2,512,128]{2,1,0:T(8,128)S(1)}, f32[2,512,128]{2,1,0:T(8,128)S(1)}) custom-call(s32[8,128]{1,0:T(8,128)S(1)} %get-tuple-element.41.odd_ref, f32[2,512,128]{2,1,0:T(8,128)S(1)} %collective-permute-done.even_pair, f32[2,512,128]{2,1,0:T(8,128)} %collective-permute-done.1.odd_pair, f32[2,512,128]{2,1,0:T(8,128)S(1)} %get-tuple-element.48.pre_p, ...), custom_call_target="tpu_custom_call" | custom-call | flops 1000000 | bytes 4198400 | tf_op jit(solution)/shard_map/halo/pallas_call | solution.py:32
  18.4 3.3 %collective-permute-start.4 = (f32[2,512,128]{2,1,0:T(8,128)S(1)}, f32[2,512,128]{2,1,0:T(8,128)S(1)}, u32[]{:S(2)}, u32[]{:S(2)}) collective-permute-start(f32[2,512,128]{2,1,0:T(8,128)S(1)} %get-tuple-element.52.p.po), channel_id=1, source_target_pairs={{1,2},{3,4},{5,6},{7,8},{9,10},{11,12},{13,14},{15,16},{17,18},{19... | collective-permute-start | bytes 1572872 | tf_op jit(solution)/shard_map/ppermute | solution.py:375
  21.7 1.7 %local.1 = (f32[2,512,128]{2,1,0:T(8,128)S(1)}, f32[2,512,128]{2,1,0:T(8,128)S(1)}) custom-call(s32[1]{0:T(128)} %bitcast.at_far.at_ref, s32[2]{0:T(128)S(1)} %copy-done.3, f32[2,4]{1,0:T(2,128)S(1)} %copy-done.2, f32[2,512,128]{2,1,0:T(8,128)S(1)} %get-tuple-element.52.p.po, f32[2,512,128]{2,1,0:T(8,128)S(1)} %get-tuple-element.42.p0.po, ...), custom_call_target="tpu_custom_call" | custom-call | flops 100000000 | bytes 4718636 | tf_op jit(solution)/shard_map/local/pallas_call | solution.py:32
  23.4 5.4 %collective-permute-done.4.odd_pair = f32[2,512,128]{2,1,0:T(8,128)S(1)} collective-permute-done((f32[2,512,128]{2,1,0:T(8,128)S(1)}, f32[2,512,128]{2,1,0:T(8,128)S(1)}, u32[]{:S(2)}, u32[]{:S(2)}) %collective-permute-start.4) | collective-permute-done | bytes 524320 | tf_op jit(solution)/shard_map/ppermute | solution.py:375
  29.3 3.4 %collective-permute-start.6 = (f32[2,512,128]{2,1,0:T(8,128)S(1)}, f32[2,512,128]{2,1,0:T(8,128)S(1)}, u32[]{:S(2)}, u32[]{:S(2)}) collective-permute-start(f32[2,512,128]{2,1,0:T(8,128)S(1)} %get-tuple-element.58.p.po), channel_id=1, source_target_pairs={{1,2},{3,4},{5,6},{7,8},{9,10},{11,12},{13,14},{15,16},{17,18},{19... | collective-permute-start | bytes 1572872 | tf_op jit(solution)/shard_map/ppermute | solution.py:375
  32.7 3.5 %local_early.1 = (f32[2,512,128]{2,1,0:T(8,128)S(1)}, f32[2,512,128]{2,1,0:T(8,128)S(1)}, f32[2,8,256]{2,1,0:T(8,128)S(1)}) custom-call(s32[1]{0:T(128)} %bitcast.at_far.at_ref, s32[2]{0:T(128)S(1)} %copy-done.3, f32[2,4]{1,0:T(2,128)S(1)} %copy-done.2, f32[2,512,128]{2,1,0:T(8,128)S(1)} %get-tuple-element.58.p.po, ...), custom_call_target="tpu_custom_call" | custom-call | flops 100000000 | bytes 4737068 | tf_op jit(solution)/shard_map/local_early/pallas_call | solution.py:32
  36.2 3.6 %collective-permute-done.6.odd_pair = f32[2,512,128]{2,1,0:T(8,128)S(1)} collective-permute-done((f32[2,512,128]{2,1,0:T(8,128)S(1)}, f32[2,512,128]{2,1,0:T(8,128)S(1)}, u32[]{:S(2)}, u32[]{:S(2)}) %collective-permute-start.6) | collective-permute-done | bytes 524320 | tf_op jit(solution)/shard_map/ppermute | solution.py:375
  40.0 2.1 %late.1 = f32[2,8,256]{2,1,0:T(8,128)S(1)} custom-call(s32[1]{0:T(128)} %bitcast.at_far.at_ref, s32[2]{0:T(128)S(1)} %copy-done.3, f32[2,4]{1,0:T(2,128)S(1)} %copy-done.2, s32[2,256]{1,0:T(2,128)S(1)} %copy-done.4, f32[2,8,256]{2,1,0:T(8,128)S(1)} %get-tuple-element.63.early_ref, f32[2,512,128]{2,1,0:T(8,128)S(1)} %get-tuple-element.71.p, ...), custom_call_target="tpu_custom_call" | custom-call | flops 100000000 | bytes 1083436 | tf_op jit(solution)/shard_map/late/pallas_call | solution.py:32
  42.2 10.9 %collective-permute-start.7 = (f32[2,8,256]{2,1,0:T(8,128)S(1)}, f32[2,8,256]{2,1,0:T(8,128)S(1)}, u32[]{:S(2)}, u32[]{:S(2)}) collective-permute-start(f32[2,8,256]{2,1,0:T(8,128)S(1)} %late.1), channel_id=1, source_target_pairs={{0,16},{1,17},{2,18},{3,19},{4,20},{5,21},{6,22},{7,23},{8,24},{9,... | collective-permute-start | bytes 49160 | tf_op jit(solution)/shard_map/ppermute | solution.py:344
  53.1 5.0 %collective-permute-start.8 = (f32[2,8,256]{2,1,0:T(8,128)S(1)}, f32[2,8,256]{2,1,0:T(8,128)S(1)}, u32[]{:S(2)}, u32[]{:S(2)}) collective-permute-start(f32[2,8,256]{2,1,0:T(8,128)S(1)} %late.1), channel_id=1, source_target_pairs={{0,112},{1,113},{2,114},{3,115},{4,116},{5,117},{6,118},{7,119},{8... | collective-permute-start | bytes 49160 | tf_op jit(solution)/shard_map/ppermute | solution.py:344
  58.1 4.8 %collective-permute-start.14 = (f32[2,512,128]{2,1,0:T(8,128)S(1)}, f32[2,512,128]{2,1,0:T(8,128)S(1)}, u32[]{:S(2)}, u32[]{:S(2)}) collective-permute-start(f32[2,512,128]{2,1,0:T(8,128)S(1)} %get-tuple-element.71.p), channel_id=1, source_target_pairs={{0,1},{1,0},{2,3},{3,2},{4,5},{5,4},{6,7},{7,6},{8,9},{9,8},{10,11... | collective-permute-start | bytes 1572872 | tf_op jit(solution)/shard_map/ppermute | solution.py:375
  62.9 1.9 %collective-permute-start.15 = (f32[2,512,128]{2,1,0:T(8,128)S(1)}, f32[2,512,128]{2,1,0:T(8,128)S(1)}, u32[]{:S(2)}, u32[]{:S(2)}) collective-permute-start(f32[2,512,128]{2,1,0:T(8,128)S(1)} %get-tuple-element.71.p), channel_id=1, source_target_pairs={{1,2},{3,4},{5,6},{7,8},{9,10},{11,12},{13,14},{15,16},{17,18},{19... | collective-permute-start | bytes 1572872 | tf_op jit(solution)/shard_map/ppermute | solution.py:375
  64.8 1.0 %copy-done.1 = f32[2,512,128]{2,1,0:T(8,128)S(1)} copy-done((f32[2,512,128]{2,1,0:T(8,128)S(1)}, f32[2,512,128]{2,1,0:T(8,128)}, u32[]{:S(2)}) %copy-start.1) | copy-done | bytes 524312
  65.8 1.8 %local3.1 = (f32[2,512,128]{2,1,0:T(8,128)S(1)}, f32[2,512,128]{2,1,0:T(8,128)S(1)}) custom-call(s32[1]{0:T(128)} %bitcast.at_far.at_ref, s32[2]{0:T(128)S(1)} %copy-done.3, f32[2,4]{1,0:T(2,128)S(1)} %copy-done.2, f32[2,512,128]{2,1,0:T(8,128)S(1)} %get-tuple-element.71.p, f32[2,512,128]{2,1,0:T(8,128)S(1)} %get-tuple-element.58.p.po, ...), custom_call_target="tpu_custom_call" | custom-call | flops 100000000 | bytes 4718636 | tf_op jit(solution)/shard_map/local3/pallas_call | solution.py:32
  67.6 4.0 %collective-permute-start.10 = (f32[2,8,256]{2,1,0:T(8,128)S(1)}, f32[2,8,256]{2,1,0:T(8,128)S(1)}, u32[]{:S(2)}, u32[]{:S(2)}) collective-permute-start(f32[2,8,256]{2,1,0:T(8,128)S(1)} %get-tuple-element.70), channel_id=1, source_target_pairs={{0,80},{1,81},{2,82},{3,83},{4,84},{5,85},{6,86},{7,87},{8,88},{9,... | collective-permute-start | bytes 49160 | tf_op jit(solution)/shard_map/ppermute | solution.py:349
  71.7 2.6 %collective-permute-start.9 = (f32[2,8,256]{2,1,0:T(8,128)S(1)}, f32[2,8,256]{2,1,0:T(8,128)S(1)}, u32[]{:S(2)}, u32[]{:S(2)}) collective-permute-start(f32[2,8,256]{2,1,0:T(8,128)S(1)} %broadcast_select_fusion.1), channel_id=1, source_target_pairs={{0,48},{1,49},{2,50},{3,51},{4,52},{5,53},{6,54},{7,55},{8,56},{9,... | collective-permute-start | bytes 49160 | tf_op jit(solution)/shard_map/ppermute | solution.py:348
  74.3 2.0 %collective-permute-done.9 = f32[2,8,256]{2,1,0:T(8,128)S(1)} collective-permute-done((f32[2,8,256]{2,1,0:T(8,128)S(1)}, f32[2,8,256]{2,1,0:T(8,128)S(1)}, u32[]{:S(2)}, u32[]{:S(2)}) %collective-permute-start.9) | collective-permute-done | bytes 16416 | tf_op jit(solution)/shard_map/ppermute | solution.py:348
  76.3 1.5 %collective-permute-start.12 = (f32[2,8,256]{2,1,0:T(8,128)S(1)}, f32[2,8,256]{2,1,0:T(8,128)S(1)}, u32[]{:S(2)}, u32[]{:S(2)}) collective-permute-start(f32[2,8,256]{2,1,0:T(8,128)S(1)} %add_add_fusion.2), channel_id=1, source_target_pairs={{0,6},{1,7},{2,4},{3,5},{4,2},{5,3},{6,0},{7,1},{8,14},{9,15},{10,... | collective-permute-start | bytes 49160 | tf_op jit(solution)/shard_map/ppermute | solution.py:331
  77.8 1.8 %collective-permute-start.13 = (f32[2,8,256]{2,1,0:T(8,128)S(1)}, f32[2,8,256]{2,1,0:T(8,128)S(1)}, u32[]{:S(2)}, u32[]{:S(2)}) collective-permute-start(f32[2,8,256]{2,1,0:T(8,128)S(1)} %add_add_fusion.2), channel_id=1, source_target_pairs={{0,4},{1,5},{2,6},{3,7},{4,0},{5,1},{6,2},{7,3},{8,12},{9,13},{10,... | collective-permute-start | bytes 49160 | tf_op jit(solution)/shard_map/ppermute | solution.py:331
  80.2 1.7 %collective-permute-done.13 = f32[2,8,256]{2,1,0:T(8,128)S(1)} collective-permute-done((f32[2,8,256]{2,1,0:T(8,128)S(1)}, f32[2,8,256]{2,1,0:T(8,128)S(1)}, u32[]{:S(2)}, u32[]{:S(2)}) %collective-permute-start.13) | collective-permute-done | bytes 16416 | tf_op jit(solution)/shard_map/ppermute | solution.py:331
  81.9 6.0 %collective-permute-start.16 = (f32[2,8,256]{2,1,0:T(8,128)S(1)}, f32[2,8,256]{2,1,0:T(8,128)S(1)}, u32[]{:S(2)}, u32[]{:S(2)}) collective-permute-start(f32[2,8,256]{2,1,0:T(8,128)S(1)} %add_add_fusion.1), channel_id=1, source_target_pairs={{0,1},{1,0},{2,3},{3,2},{4,5},{5,4},{6,7},{7,6},{8,9},{9,8},{10,11... | collective-permute-start | bytes 49160 | tf_op jit(solution)/shard_map/ppermute | solution.py:331
  87.9 3.2 %collective-permute-start.18 = (f32[2,8,256]{2,1,0:T(8,128)S(1)}, f32[2,8,256]{2,1,0:T(8,128)S(1)}, u32[]{:S(2)}, u32[]{:S(2)}) collective-permute-start(f32[2,8,256]{2,1,0:T(8,128)S(1)} %add_add_fusion.1), channel_id=1, source_target_pairs={{0,9},{1,8},{2,11},{3,10},{4,13},{5,12},{6,15},{7,14},{8,1},{9,0},... | collective-permute-start | bytes 49160 | tf_op jit(solution)/shard_map/ppermute | solution.py:331
  91.1 1.2 %halo3.1 = (f32[2,512,128]{2,1,0:T(8,128)}, f32[2,512,128]{2,1,0:T(8,128)}) custom-call(s32[8,128]{1,0:T(8,128)S(1)} %get-tuple-element.41.odd_ref, f32[2,512,128]{2,1,0:T(8,128)S(1)} %collective-permute-done.14.even_pair, f32[2,512,128]{2,1,0:T(8,128)S(1)} %collective-permute-done.15.odd_pair, f32[2,512,128]{2,1,0:T(8,128)S(1)} %get-tuple-element.74.pre_p, ...), custom_call_target="tpu_custom_call" | custom-call | flops 20000000000 | bytes 4198400 | tf_op jit(solution)/shard_map/halo3/pallas_call | solution.py:32
  (42 shorter events, 3.5 us)
Async XLA Ops:
  1.8 11.4 %collective-permute-start.2 = (f32[3,256,128]{2,1,0:T(8,128)S(1)}, f32[3,256,128]{2,1,0:T(8,128)S(1)}, u32[]{:S(2)}, u32[]{:S(2)}) collective-permute-start(f32[3,256,128]{2,1,0:T(8,128)S(1)} %model.1.own_ref.own), channel_id=1, source_target_pairs={{0,128},{128,0},{1,129},{129,1},{2,130},{130,2},{3,131},{131,3},{4... | collective-permute-start | bytes 1179656 | tf_op jit(solution)/shard_map/ppermute | solution.py:377
  3.9 5.3 %copy-start.5 = (s32[2,1]{0,1:T(1,128)S(1)}, s32[2,1]{0,1:T(1,128)}, u32[]{:S(2)}) copy-start(s32[2,1]{0,1:T(1,128)} %param.18) | copy-start | bytes 28
  5.0 10.1 %collective-permute-start = (f32[2,512,128]{2,1,0:T(8,128)S(1)}, f32[2,512,128]{2,1,0:T(8,128)S(1)}, u32[]{:S(2)}, u32[]{:S(2)}) collective-permute-start(f32[2,512,128]{2,1,0:T(8,128)S(1)} %get-tuple-element.42.p0.po), channel_id=1, source_target_pairs={{0,1},{1,0},{2,3},{3,2},{4,5},{5,4},{6,7},{7,6},{8,9},{9,8},{10,11... | collective-permute-start | bytes 1572872 | tf_op jit(solution)/shard_map/ppermute | solution.py:375
  6.3 10.6 %collective-permute-start.1 = (f32[2,512,128]{2,1,0:T(8,128)S(1)}, f32[2,512,128]{2,1,0:T(8,128)}, u32[]{:S(2)}, u32[]{:S(2)}) collective-permute-start(f32[2,512,128]{2,1,0:T(8,128)S(1)} %get-tuple-element.42.p0.po), channel_id=1, source_target_pairs={{1,2},{3,4},{5,6},{7,8},{9,10},{11,12},{13,14},{15,16},{17,18},{19... | collective-permute-start | bytes 1572872 | tf_op jit(solution)/shard_map/ppermute | solution.py:375
  9.2 0.7 copy-start.2
  9.2 0.7 copy-start.3
  13.2 0.7 copy-start.6
  13.9 1.0 %copy-start.7 = (f32[3,256,128]{2,1,0:T(8,128)S(1)}, f32[3,256,128]{2,1,0:T(8,128)}, u32[]{:S(2)}) copy-start(f32[3,256,128]{2,1,0:T(8,128)} %copy-done.6) | copy-start | bytes 1179652
  18.3 5.2 %collective-permute-start.3 = (f32[2,512,128]{2,1,0:T(8,128)S(1)}, f32[2,512,128]{2,1,0:T(8,128)S(1)}, u32[]{:S(2)}, u32[]{:S(2)}) collective-permute-start(f32[2,512,128]{2,1,0:T(8,128)S(1)} %get-tuple-element.52.p.po), channel_id=1, source_target_pairs={{0,1},{1,0},{2,3},{3,2},{4,5},{5,4},{6,7},{7,6},{8,9},{9,8},{10,11... | collective-permute-start | bytes 1572872 | tf_op jit(solution)/shard_map/ppermute | solution.py:375
  18.4 10.5 %collective-permute-start.4 = (f32[2,512,128]{2,1,0:T(8,128)S(1)}, f32[2,512,128]{2,1,0:T(8,128)S(1)}, u32[]{:S(2)}, u32[]{:S(2)}) collective-permute-start(f32[2,512,128]{2,1,0:T(8,128)S(1)} %get-tuple-element.52.p.po), channel_id=1, source_target_pairs={{1,2},{3,4},{5,6},{7,8},{9,10},{11,12},{13,14},{15,16},{17,18},{19... | collective-permute-start | bytes 1572872 | tf_op jit(solution)/shard_map/ppermute | solution.py:375
  29.1 7.0 %copy-start = (f32[2,512,128]{2,1,0:T(8,128)}, f32[2,512,128]{2,1,0:T(8,128)S(1)}, u32[]{:S(2)}) copy-start(f32[2,512,128]{2,1,0:T(8,128)S(1)} %get-tuple-element.59.q.qo) | copy-start | bytes 1572868
  29.1 3.5 %copy-start.4 = (s32[2,256]{1,0:T(2,128)S(1)}, s32[2,256]{1,0:T(2,128)}, u32[]{:S(2)}) copy-start(s32[2,256]{1,0:T(2,128)} %cells_ref.3) | copy-start | bytes 6148
  29.2 7.0 %collective-permute-start.5 = (f32[2,512,128]{2,1,0:T(8,128)S(1)}, f32[2,512,128]{2,1,0:T(8,128)S(1)}, u32[]{:S(2)}, u32[]{:S(2)}) collective-permute-start(f32[2,512,128]{2,1,0:T(8,128)S(1)} %get-tuple-element.58.p.po), channel_id=1, source_target_pairs={{0,1},{1,0},{2,3},{3,2},{4,5},{5,4},{6,7},{7,6},{8,9},{9,8},{10,11... | collective-permute-start | bytes 1572872 | tf_op jit(solution)/shard_map/ppermute | solution.py:375
  29.3 10.5 %collective-permute-start.6 = (f32[2,512,128]{2,1,0:T(8,128)S(1)}, f32[2,512,128]{2,1,0:T(8,128)S(1)}, u32[]{:S(2)}, u32[]{:S(2)}) collective-permute-start(f32[2,512,128]{2,1,0:T(8,128)S(1)} %get-tuple-element.58.p.po), channel_id=1, source_target_pairs={{1,2},{3,4},{5,6},{7,8},{9,10},{11,12},{13,14},{15,16},{17,18},{19... | collective-permute-start | bytes 1572872 | tf_op jit(solution)/shard_map/ppermute | solution.py:375
  42.2 25.4 %collective-permute-start.7 = (f32[2,8,256]{2,1,0:T(8,128)S(1)}, f32[2,8,256]{2,1,0:T(8,128)S(1)}, u32[]{:S(2)}, u32[]{:S(2)}) collective-permute-start(f32[2,8,256]{2,1,0:T(8,128)S(1)} %late.1), channel_id=1, source_target_pairs={{0,16},{1,17},{2,18},{3,19},{4,20},{5,21},{6,22},{7,23},{8,24},{9,... | collective-permute-start | bytes 49160 | tf_op jit(solution)/shard_map/ppermute | solution.py:344
  53.1 14.5 %collective-permute-start.8 = (f32[2,8,256]{2,1,0:T(8,128)S(1)}, f32[2,8,256]{2,1,0:T(8,128)S(1)}, u32[]{:S(2)}, u32[]{:S(2)}) collective-permute-start(f32[2,8,256]{2,1,0:T(8,128)S(1)} %late.1), channel_id=1, source_target_pairs={{0,112},{1,113},{2,114},{3,115},{4,116},{5,117},{6,118},{7,119},{8... | collective-permute-start | bytes 49160 | tf_op jit(solution)/shard_map/ppermute | solution.py:344
  58.1 23.8 %collective-permute-start.14 = (f32[2,512,128]{2,1,0:T(8,128)S(1)}, f32[2,512,128]{2,1,0:T(8,128)S(1)}, u32[]{:S(2)}, u32[]{:S(2)}) collective-permute-start(f32[2,512,128]{2,1,0:T(8,128)S(1)} %get-tuple-element.71.p), channel_id=1, source_target_pairs={{0,1},{1,0},{2,3},{3,2},{4,5},{5,4},{6,7},{7,6},{8,9},{9,8},{10,11... | collective-permute-start | bytes 1572872 | tf_op jit(solution)/shard_map/ppermute | solution.py:375
  62.9 19.0 %collective-permute-start.15 = (f32[2,512,128]{2,1,0:T(8,128)S(1)}, f32[2,512,128]{2,1,0:T(8,128)S(1)}, u32[]{:S(2)}, u32[]{:S(2)}) collective-permute-start(f32[2,512,128]{2,1,0:T(8,128)S(1)} %get-tuple-element.71.p), channel_id=1, source_target_pairs={{1,2},{3,4},{5,6},{7,8},{9,10},{11,12},{13,14},{15,16},{17,18},{19... | collective-permute-start | bytes 1572872 | tf_op jit(solution)/shard_map/ppermute | solution.py:375
  64.8 1.0 %copy-start.1 = (f32[2,512,128]{2,1,0:T(8,128)S(1)}, f32[2,512,128]{2,1,0:T(8,128)}, u32[]{:S(2)}) copy-start(f32[2,512,128]{2,1,0:T(8,128)} %copy-done) | copy-start | bytes 1572868
  67.6 6.7 %collective-permute-start.10 = (f32[2,8,256]{2,1,0:T(8,128)S(1)}, f32[2,8,256]{2,1,0:T(8,128)S(1)}, u32[]{:S(2)}, u32[]{:S(2)}) collective-permute-start(f32[2,8,256]{2,1,0:T(8,128)S(1)} %get-tuple-element.70), channel_id=1, source_target_pairs={{0,80},{1,81},{2,82},{3,83},{4,84},{5,85},{6,86},{7,87},{8,88},{9,... | collective-permute-start | bytes 49160 | tf_op jit(solution)/shard_map/ppermute | solution.py:349
  71.7 4.6 %collective-permute-start.9 = (f32[2,8,256]{2,1,0:T(8,128)S(1)}, f32[2,8,256]{2,1,0:T(8,128)S(1)}, u32[]{:S(2)}, u32[]{:S(2)}) collective-permute-start(f32[2,8,256]{2,1,0:T(8,128)S(1)} %broadcast_select_fusion.1), channel_id=1, source_target_pairs={{0,48},{1,49},{2,50},{3,51},{4,52},{5,53},{6,54},{7,55},{8,56},{9,... | collective-permute-start | bytes 49160 | tf_op jit(solution)/shard_map/ppermute | solution.py:348
  76.3 3.3 %collective-permute-start.11 = (f32[2,8,256]{2,1,0:T(8,128)S(1)}, f32[2,8,256]{2,1,0:T(8,128)S(1)}, u32[]{:S(2)}, u32[]{:S(2)}) collective-permute-start(f32[2,8,256]{2,1,0:T(8,128)S(1)} %add_add_fusion.2), channel_id=1, source_target_pairs={{0,2},{1,3},{2,0},{3,1},{4,6},{5,7},{6,4},{7,5},{8,10},{9,11},{10,... | collective-permute-start | bytes 49160 | tf_op jit(solution)/shard_map/ppermute | solution.py:331
  76.3 3.9 %collective-permute-start.12 = (f32[2,8,256]{2,1,0:T(8,128)S(1)}, f32[2,8,256]{2,1,0:T(8,128)S(1)}, u32[]{:S(2)}, u32[]{:S(2)}) collective-permute-start(f32[2,8,256]{2,1,0:T(8,128)S(1)} %add_add_fusion.2), channel_id=1, source_target_pairs={{0,6},{1,7},{2,4},{3,5},{4,2},{5,3},{6,0},{7,1},{8,14},{9,15},{10,... | collective-permute-start | bytes 49160 | tf_op jit(solution)/shard_map/ppermute | solution.py:331
  77.8 4.1 %collective-permute-start.13 = (f32[2,8,256]{2,1,0:T(8,128)S(1)}, f32[2,8,256]{2,1,0:T(8,128)S(1)}, u32[]{:S(2)}, u32[]{:S(2)}) collective-permute-start(f32[2,8,256]{2,1,0:T(8,128)S(1)} %add_add_fusion.2), channel_id=1, source_target_pairs={{0,4},{1,5},{2,6},{3,7},{4,0},{5,1},{6,2},{7,3},{8,12},{9,13},{10,... | collective-permute-start | bytes 49160 | tf_op jit(solution)/shard_map/ppermute | solution.py:331
  81.9 10.5 %collective-permute-start.16 = (f32[2,8,256]{2,1,0:T(8,128)S(1)}, f32[2,8,256]{2,1,0:T(8,128)S(1)}, u32[]{:S(2)}, u32[]{:S(2)}) collective-permute-start(f32[2,8,256]{2,1,0:T(8,128)S(1)} %add_add_fusion.1), channel_id=1, source_target_pairs={{0,1},{1,0},{2,3},{3,2},{4,5},{5,4},{6,7},{7,6},{8,9},{9,8},{10,11... | collective-permute-start | bytes 49160 | tf_op jit(solution)/shard_map/ppermute | solution.py:331
  87.9 4.5 %collective-permute-start.17 = (f32[2,8,256]{2,1,0:T(8,128)S(1)}, f32[2,8,256]{2,1,0:T(8,128)S(1)}, u32[]{:S(2)}, u32[]{:S(2)}) collective-permute-start(f32[2,8,256]{2,1,0:T(8,128)S(1)} %add_add_fusion.1), channel_id=1, source_target_pairs={{0,8},{1,9},{2,10},{3,11},{4,12},{5,13},{6,14},{7,15},{8,0},{9,1},... | collective-permute-start | bytes 49160 | tf_op jit(solution)/shard_map/ppermute | solution.py:331
  87.9 4.9 %collective-permute-start.18 = (f32[2,8,256]{2,1,0:T(8,128)S(1)}, f32[2,8,256]{2,1,0:T(8,128)S(1)}, u32[]{:S(2)}, u32[]{:S(2)}) collective-permute-start(f32[2,8,256]{2,1,0:T(8,128)S(1)} %add_add_fusion.1), channel_id=1, source_target_pairs={{0,9},{1,8},{2,11},{3,10},{4,13},{5,12},{6,15},{7,14},{8,1},{9,0},... | collective-permute-start | bytes 49160 | tf_op jit(solution)/shard_map/ppermute | solution.py:331

commit v6 on v5

--- a/solution.py
+++ b/solution.py
@@ -50,34 +50,29 @@
     return pl.ds(x * CY, CY)
 
 
-def model_kernel(v_far, e_far, d_far, own_ref, sems):
-    copies = [pltpu.make_async_copy(src, own_ref.at[n], sems.at[n]) for n, src in enumerate((v_far, e_far, d_far))]
+def begin_kernel(at_far, side_far, active_far, source_far, v_far, e_far, d_far, p_far,
+                 own_ref, p0_ref, odd_ref, live_ref, z_odd_ref, at_ref, active_ref, source_ref, sems):
+    pairs = (
+        (v_far, own_ref.at[0]), (e_far, own_ref.at[1]), (d_far, own_ref.at[2]),
+        (at_far, at_ref), (active_far, active_ref), (source_far, source_ref), (p_far, p0_ref))
+    copies = [pltpu.make_async_copy(src, dst, sems.at[n]) for n, (src, dst) in enumerate(pairs)]
     for copy in copies:
         copy.start()
-    for copy in copies:
+    for copy in copies[:3]:
         copy.wait()
     courant = (own_ref[0] * step_ratio) * (own_ref[0] * step_ratio)
     coupling = jnp.sqrt(1.0 + 2.0 * own_ref[2])
     own_ref[0] = courant
     own_ref[1] = courant * (1.0 + 2.0 * own_ref[1])
     own_ref[2] = courant * coupling
-
-
-def begin_kernel(at_far, active_far, source_far, p_far, own_ref, p0_ref, odd_ref, live_ref, at_ref, active_ref, source_ref, sems):
-    copies = [
-        pltpu.make_async_copy(src, dst, sems.at[n])
-        for n, (src, dst) in enumerate((
-            (at_far, at_ref), (active_far, active_ref), (source_far, source_ref), (p_far, p0_ref)))
-    ]
-    for copy in copies:
-        copy.start()
-    for copy in copies:
+    for copy in copies[3:]:
         copy.wait()
     for s in range(2):
         live = live_of(at_ref, active_ref, source_ref, s)
         p0_ref[s] = p0_ref[s] * live
         live_ref[pl.ds(8 * s, 8), :] = jnp.full((8, CZ), live, jnp.float32)
     odd_ref[...] = jnp.full(odd_ref.shape, at_ref[0] & 1, jnp.int32)
+    z_odd_ref[...] = jnp.full(z_odd_ref.shape, (at_ref[0] // 16) & 1, jnp.int32)
 
 
 def band():
@@ -333,21 +328,21 @@
     return total
 
 
-def reduced(total, n, gate, last_gate):
+def reduced(total, n, z_odd, gate, last_gate):
     todo = stages(n)
     if n != 128:
         total = gate(summed(total, todo[0]))
         for stage in todo[1:]:
             total = summed(total, stage)
         return last_gate(total)
-    odd = (lax.axis_index("space") // 16) % 2 == 1
+    odd = z_odd == 1
     first, second = (lax.ppermute(total, "space", pairs) for pairs in todo[2])
     two = total + jnp.where(odd, first, second)
     three = total + (first + second)
-    even_part, odd_part, three = gate((jnp.where(odd, two, three), jnp.where(odd, three, two), three))
+    even_part, odd_part = jnp.where(odd, two, three), jnp.where(odd, three, two)
     plus = lax.ppermute(even_part, "space", todo[3][0])
     minus = lax.ppermute(odd_part, "space", todo[3][1])
-    total = three + (plus + minus)
+    total = gate(three + (plus + minus))
     return summed(last_gate(summed(total, todo[0])), todo[1])
 
 
@@ -364,12 +359,11 @@
     active = active_blocks.reshape(2)
     ints = [pltpu.SMEM((1,), jnp.int32), pltpu.SMEM((2,), jnp.int32), pltpu.SMEM((2,), jnp.int32)]
 
-    own, = call(
-        model_kernel, (speed, eps, delta), (shape(3, *half),), 10**6, "model", far=range(3),
-        scratch=[pltpu.SemaphoreType.DMA((3,))])
-    p, odd, live = call(
-        begin_kernel, (at, active, source_cells, p_now, own), (field, shape(8, CZ, dtype=jnp.int32), shape(16, CZ)), 10**6, "begin",
-        far=range(4), scratch=ints + [pltpu.SemaphoreType.DMA((4,))])
+    own, p, odd, live, z_odd = call(
+        begin_kernel, (at, side, active, source_cells, speed, eps, delta, p_now),
+        (shape(3, *half), field, shape(8, CZ, dtype=jnp.int32), shape(16, CZ),
+         shape(2, 8, receiver_cells.shape[1], dtype=jnp.int32)),
+        10**6, "begin", far=range(8), scratch=ints + [pltpu.SemaphoreType.DMA((7,))])
 
     def exchange(values):
         return (lax.ppermute(values, "space", even_pairs(blocks)), lax.ppermute(values, "space", odd_pairs(blocks)))
@@ -415,7 +409,7 @@
         total, halos = lax.optimization_barrier((total, halos))
         return total
 
-    total = reduced(total, blocks, gate, last_gate)
+    total = reduced(total, blocks, z_odd, gate, last_gate)
     p, q = call(halo_kernel, (odd, *halos, *local, cs, ck), (field, field), 2 * 10**10, "halo3")
     last = total[:, 4] + total[:, 0] * total[:, 5]
     traces = jnp.stack([total[:, 1], total[:, 2], total[:, 3], last], axis=1)

time: 93.9 us -> 90.9 us (0.968)
  waiting for transfers between devices: 15.6 us -> 21 us
  starting transfers between devices: 54.9 us -> 51 us
  local copies, waits for them, and re-layouts: 3.45 us -> 0.68 us
  Pallas kernels: 18 us -> 16.5 us
    ppermute x1, starting transfers between devices: 4.02 us -> 0.01 us  [reduced(): minus = lax.ppermute(odd_part, 'space', todo[3][1])]
    ppermute x1, waiting for transfers between devices: 0.01 us -> 3.75 us  [reduced(): minus = lax.ppermute(odd_part, 'space', todo[3][1])]
    unnamed x16 -> x8, local copies, waits for them, and re-layouts: 3.45 us -> 0.67 us
    ppermute x6, waiting for transfers between devices: 2.81 us -> 4.89 us  [summed(): lax.ppermute(total, 'space', pairs)]
    ppermute x1, waiting for transfers between devices: 1.99 us -> 0.01 us  [reduced(): plus = lax.ppermute(even_part, 'space', todo[3][0])]
    ppermute x1, starting transfers between devices: 2.64 us -> 4.39 us  [reduced(): plus = lax.ppermute(even_part, 'space', todo[3][0])]
    ppermute x4, waiting for transfers between devices: 10.8 us -> 12.3 us  [exchange(): lax.ppermute(values, 'space', odd_pairs(blocks))]
    pallas_call x12 -> x11, Pallas kernels: 18 us -> 16.5 us  [call(): pl.pallas_call(kernel, out_shape=tuple(outs), in_specs=specs, out_specs=t...]
  transfers between devices with their start and end apart: 19 -> 19, of which waited for: 7 -> 7; matrix products, arithmetic and copies ran while one was open for 0% -> 0% of each run, Pallas kernels for 14% -> 13%
where the time goes in v6:
time: 90.9 us; the launch traced here: 90.7 us
  starting transfers between devices  51 us (56%)
  waiting for transfers between devices  21 us (23%)
  Pallas kernels  16.5 us (18%)
    pallas_call x11, Pallas kernels, call(): pl.pallas_call(kernel, out_shape=tuple(outs), in_specs=specs, out_specs=t...  16.5 us
    ppermute x2, starting transfers between devices, reduced(): first, second = (lax.ppermute(total, 'space', pairs) for pairs in todo[2])  15.5 us
    ppermute x4, waiting for transfers between devices, exchange(): lax.ppermute(values, 'space', odd_pairs(blocks))  12.3 us
    ppermute x6, starting transfers between devices, summed(): lax.ppermute(total, 'space', pairs)  11.5 us
    ppermute x4, starting transfers between devices, exchange(): lax.ppermute(values, 'space', odd_pairs(blocks))  11.2 us
    ppermute x4, starting transfers between devices, exchange(): lax.ppermute(values, 'space', even_pairs(blocks))  6.29 us
    ppermute x6, waiting for transfers between devices, summed(): lax.ppermute(total, 'space', pairs)  4.89 us
    ppermute x1, starting transfers between devices, reduced(): plus = lax.ppermute(even_part, 'space', todo[3][0])  4.39 us
  transfers between devices with their start and end apart: 19, of which 7 were waited for; matrix products, arithmetic and copies ran while one was open for 0% of the time, Pallas kernels for 13%

profile of v6, /device:TPU:1, one launch (start us, length us, event | category | flops | bytes accessed | tf_op | source)
XLA Modules:
  0.0 90.7 jit_solution(10646967975884385489)
XLA Ops:
  0.6 1.4 %begin.1 = (f32[3,256,128]{2,1,0:T(8,128)S(1)}, f32[2,512,128]{2,1,0:T(8,128)S(1)}, s32[8,128]{1,0:T(8,128)S(1)}, f32[16,128]{1,0:T(8,128)S(1)}, s32[2,8,256]{2,1,0:T(8,128)S(1)}) custom-call(s32[1]{0:T(128)} %bitcast.at_far.at_ref, s32[1]{0:T(128)} %bitcast.1.side_far.side_ref, s32[2]{0:T(128)} %bitcast.16, s32[2]{0:T(128)} %source_ref.9, ...), custom_call_target="tpu_custom_call" | custom-call | flops 1000000 | bytes 1863704 | tf_op jit(solution)/shard_map/begin/pallas_call | solution.py:32
  2.0 2.1 %collective-permute-start.2 = (f32[3,256,128]{2,1,0:T(8,128)S(1)}, f32[3,256,128]{2,1,0:T(8,128)S(1)}, u32[]{:S(2)}, u32[]{:S(2)}) collective-permute-start(f32[3,256,128]{2,1,0:T(8,128)S(1)} %get-tuple-element.44.own), channel_id=1, source_target_pairs={{0,128},{128,0},{1,129},{129,1},{2,130},{130,2},{3,131},{131,3},{4... | collective-permute-start | bytes 1179656 | tf_op jit(solution)/shard_map/ppermute | solution.py:371
  4.1 1.3 %collective-permute-start = (f32[2,512,128]{2,1,0:T(8,128)S(1)}, f32[2,512,128]{2,1,0:T(8,128)S(1)}, u32[]{:S(2)}, u32[]{:S(2)}) collective-permute-start(f32[2,512,128]{2,1,0:T(8,128)S(1)} %get-tuple-element.42.p0.po), channel_id=1, source_target_pairs={{0,1},{1,0},{2,3},{3,2},{4,5},{5,4},{6,7},{7,6},{8,9},{9,8},{10,11... | collective-permute-start | bytes 1572872 | tf_op jit(solution)/shard_map/ppermute | solution.py:369
  5.4 2.7 %collective-permute-start.1 = (f32[2,512,128]{2,1,0:T(8,128)S(1)}, f32[2,512,128]{2,1,0:T(8,128)S(1)}, u32[]{:S(2)}, u32[]{:S(2)}) collective-permute-start(f32[2,512,128]{2,1,0:T(8,128)S(1)} %get-tuple-element.42.p0.po), channel_id=1, source_target_pairs={{1,2},{3,4},{5,6},{7,8},{9,10},{11,12},{13,14},{15,16},{17,18},{19... | collective-permute-start | bytes 1572872 | tf_op jit(solution)/shard_map/ppermute | solution.py:369
  8.2 0.6 copy-done
  8.9 3.3 %ready.1 = (f32[2,512,128]{2,1,0:T(8,128)S(1)}, f32[2,512,128]{2,1,0:T(8,128)S(1)}, f32[2,512,128]{2,1,0:T(8,128)S(1)}, f32[2,512,128]{2,1,0:T(8,128)S(1)}, f32[2,512,128]{2,1,0:T(8,128)S(1)}) custom-call(s32[1]{0:T(128)} %bitcast.at_far.at_ref, s32[2]{0:T(128)S(1)} %bitcast.17, s32[2]{0:T(128)S(1)} %copy-done.1, f32[2,4]{1,0:T(2,128)S(1)} %copy-done, ...), custom_call_target="tpu_custom_call" | custom-call | flops 100000000 | bytes 4718644 | tf_op jit(solution)/shard_map/ready/pallas_call | solution.py:32
  12.2 0.4 first.1
  12.6 3.3 %collective-permute-done.1.odd_pair = f32[2,512,128]{2,1,0:T(8,128)S(1)} collective-permute-done((f32[2,512,128]{2,1,0:T(8,128)S(1)}, f32[2,512,128]{2,1,0:T(8,128)S(1)}, u32[]{:S(2)}, u32[]{:S(2)}) %collective-permute-start.1) | collective-permute-done | bytes 524320 | tf_op jit(solution)/shard_map/ppermute | solution.py:369
  16.3 3.2 %collective-permute-start.4 = (f32[2,512,128]{2,1,0:T(8,128)S(1)}, f32[2,512,128]{2,1,0:T(8,128)S(1)}, u32[]{:S(2)}, u32[]{:S(2)}) collective-permute-start(f32[2,512,128]{2,1,0:T(8,128)S(1)} %get-tuple-element.53.p.po), channel_id=1, source_target_pairs={{1,2},{3,4},{5,6},{7,8},{9,10},{11,12},{13,14},{15,16},{17,18},{19... | collective-permute-start | bytes 1572872 | tf_op jit(solution)/shard_map/ppermute | solution.py:369
  19.6 1.9 %local.1 = (f32[2,512,128]{2,1,0:T(8,128)S(1)}, f32[2,512,128]{2,1,0:T(8,128)S(1)}) custom-call(s32[1]{0:T(128)} %bitcast.at_far.at_ref, s32[2]{0:T(128)S(1)} %copy-done.1, f32[2,4]{1,0:T(2,128)S(1)} %copy-done, f32[2,512,128]{2,1,0:T(8,128)S(1)} %get-tuple-element.53.p.po, f32[2,512,128]{2,1,0:T(8,128)S(1)} %get-tuple-element.42.p0.po, ...), custom_call_target="tpu_custom_call" | custom-call | flops 100000000 | bytes 4718636 | tf_op jit(solution)/shard_map/local/pallas_call | solution.py:32
  21.4 5.4 %collective-permute-done.4.odd_pair = f32[2,512,128]{2,1,0:T(8,128)S(1)} collective-permute-done((f32[2,512,128]{2,1,0:T(8,128)S(1)}, f32[2,512,128]{2,1,0:T(8,128)S(1)}, u32[]{:S(2)}, u32[]{:S(2)}) %collective-permute-start.4) | collective-permute-done | bytes 524320 | tf_op jit(solution)/shard_map/ppermute | solution.py:369
  27.2 3.3 %collective-permute-start.6 = (f32[2,512,128]{2,1,0:T(8,128)S(1)}, f32[2,512,128]{2,1,0:T(8,128)S(1)}, u32[]{:S(2)}, u32[]{:S(2)}) collective-permute-start(f32[2,512,128]{2,1,0:T(8,128)S(1)} %get-tuple-element.59.p.po), channel_id=1, source_target_pairs={{1,2},{3,4},{5,6},{7,8},{9,10},{11,12},{13,14},{15,16},{17,18},{19... | collective-permute-start | bytes 1572872 | tf_op jit(solution)/shard_map/ppermute | solution.py:369
  30.5 3.6 %local_early.1 = (f32[2,512,128]{2,1,0:T(8,128)S(1)}, f32[2,512,128]{2,1,0:T(8,128)S(1)}, f32[2,8,256]{2,1,0:T(8,128)S(1)}) custom-call(s32[1]{0:T(128)} %bitcast.at_far.at_ref, s32[2]{0:T(128)S(1)} %copy-done.1, f32[2,4]{1,0:T(2,128)S(1)} %copy-done, f32[2,512,128]{2,1,0:T(8,128)S(1)} %get-tuple-element.59.p.po, f32[2,512,128]{2,1,0:T(8,128)S(1)} %get-tuple-element.53.p.po, ...), custom_call_target="tpu_custom_call" | custom-call | flops 100000000 | bytes 4737068 | tf_op jit(solution)/shard_map/local_early/pallas_call | solution.py:32
  34.1 3.6 %collective-permute-done.6.odd_pair = f32[2,512,128]{2,1,0:T(8,128)S(1)} collective-permute-done((f32[2,512,128]{2,1,0:T(8,128)S(1)}, f32[2,512,128]{2,1,0:T(8,128)S(1)}, u32[]{:S(2)}, u32[]{:S(2)}) %collective-permute-start.6) | collective-permute-done | bytes 524320 | tf_op jit(solution)/shard_map/ppermute | solution.py:369
  38.0 2.2 %late.1 = f32[2,8,256]{2,1,0:T(8,128)S(1)} custom-call(s32[1]{0:T(128)} %bitcast.at_far.at_ref, s32[2]{0:T(128)S(1)} %copy-done.1, f32[2,4]{1,0:T(2,128)S(1)} %copy-done, s32[2,256]{1,0:T(2,128)S(1)} %copy-done.2, f32[2,8,256]{2,1,0:T(8,128)S(1)} %get-tuple-element.64.early_ref, f32[2,512,128]{2,1,0:T(8,128)S(1)} %get-tuple-element.71.p, ...), custom_call_target="tpu_custom_call" | custom-call | flops 100000000 | bytes 1083436 | tf_op jit(solution)/shard_map/late/pallas_call | solution.py:32
  40.1 10.8 %collective-permute-start.7 = (f32[2,8,256]{2,1,0:T(8,128)S(1)}, f32[2,8,256]{2,1,0:T(8,128)S(1)}, u32[]{:S(2)}, u32[]{:S(2)}) collective-permute-start(f32[2,8,256]{2,1,0:T(8,128)S(1)} %late.1), channel_id=1, source_target_pairs={{0,16},{1,17},{2,18},{3,19},{4,20},{5,21},{6,22},{7,23},{8,24},{9,... | collective-permute-start | bytes 49160 | tf_op jit(solution)/shard_map/ppermute | solution.py:339
  50.9 4.7 %collective-permute-start.8 = (f32[2,8,256]{2,1,0:T(8,128)S(1)}, f32[2,8,256]{2,1,0:T(8,128)S(1)}, u32[]{:S(2)}, u32[]{:S(2)}) collective-permute-start(f32[2,8,256]{2,1,0:T(8,128)S(1)} %late.1), channel_id=1, source_target_pairs={{0,112},{1,113},{2,114},{3,115},{4,116},{5,117},{6,118},{7,119},{8... | collective-permute-start | bytes 49160 | tf_op jit(solution)/shard_map/ppermute | solution.py:339
  55.6 4.8 %collective-permute-start.14 = (f32[2,512,128]{2,1,0:T(8,128)S(1)}, f32[2,512,128]{2,1,0:T(8,128)S(1)}, u32[]{:S(2)}, u32[]{:S(2)}) collective-permute-start(f32[2,512,128]{2,1,0:T(8,128)S(1)} %get-tuple-element.71.p), channel_id=1, source_target_pairs={{0,1},{1,0},{2,3},{3,2},{4,5},{5,4},{6,7},{7,6},{8,9},{9,8},{10,11... | collective-permute-start | bytes 1572872 | tf_op jit(solution)/shard_map/ppermute | solution.py:369
  60.4 1.9 %collective-permute-start.15 = (f32[2,512,128]{2,1,0:T(8,128)S(1)}, f32[2,512,128]{2,1,0:T(8,128)S(1)}, u32[]{:S(2)}, u32[]{:S(2)}) collective-permute-start(f32[2,512,128]{2,1,0:T(8,128)S(1)} %get-tuple-element.71.p), channel_id=1, source_target_pairs={{1,2},{3,4},{5,6},{7,8},{9,10},{11,12},{13,14},{15,16},{17,18},{19... | collective-permute-start | bytes 1572872 | tf_op jit(solution)/shard_map/ppermute | solution.py:369
  62.4 4.4 %collective-permute-start.9 = (f32[2,8,256]{2,1,0:T(8,128)S(1)}, f32[2,8,256]{2,1,0:T(8,128)S(1)}, u32[]{:S(2)}, u32[]{:S(2)}) collective-permute-start(f32[2,8,256]{2,1,0:T(8,128)S(1)} %fusion.2), channel_id=1, source_target_pairs={{0,48},{1,49},{2,50},{3,51},{4,52},{5,53},{6,54},{7,55},{8,56},{9,... | collective-permute-start | bytes 49160 | tf_op jit(solution)/shard_map/ppermute | solution.py:343
  66.8 1.8 %local3.1 = (f32[2,512,128]{2,1,0:T(8,128)S(1)}, f32[2,512,128]{2,1,0:T(8,128)S(1)}) custom-call(s32[1]{0:T(128)} %bitcast.at_far.at_ref, s32[2]{0:T(128)S(1)} %copy-done.1, f32[2,4]{1,0:T(2,128)S(1)} %copy-done, f32[2,512,128]{2,1,0:T(8,128)S(1)} %get-tuple-element.71.p, f32[2,512,128]{2,1,0:T(8,128)S(1)} %get-tuple-element.59.p.po, ...), custom_call_target="tpu_custom_call" | custom-call | flops 100000000 | bytes 4718636 | tf_op jit(solution)/shard_map/local3/pallas_call | solution.py:32
  68.7 3.7 %collective-permute-done.10 = f32[2,8,256]{2,1,0:T(8,128)S(1)} collective-permute-done((f32[2,8,256]{2,1,0:T(8,128)S(1)}, f32[2,8,256]{2,1,0:T(8,128)S(1)}, u32[]{:S(2)}, u32[]{:S(2)}) %collective-permute-start.10) | collective-permute-done | bytes 16416 | tf_op jit(solution)/shard_map/ppermute | solution.py:344
  72.4 3.0 %collective-permute-start.12 = (f32[2,8,256]{2,1,0:T(8,128)S(1)}, f32[2,8,256]{2,1,0:T(8,128)S(1)}, u32[]{:S(2)}, u32[]{:S(2)}) collective-permute-start(f32[2,8,256]{2,1,0:T(8,128)S(1)} %add_add_fusion.2), channel_id=1, source_target_pairs={{0,6},{1,7},{2,4},{3,5},{4,2},{5,3},{6,0},{7,1},{8,14},{9,15},{10,... | collective-permute-start | bytes 49160 | tf_op jit(solution)/shard_map/ppermute | solution.py:326
  75.5 1.1 %collective-permute-start.13 = (f32[2,8,256]{2,1,0:T(8,128)S(1)}, f32[2,8,256]{2,1,0:T(8,128)S(1)}, u32[]{:S(2)}, u32[]{:S(2)}) collective-permute-start(f32[2,8,256]{2,1,0:T(8,128)S(1)} %add_add_fusion.2), channel_id=1, source_target_pairs={{0,4},{1,5},{2,6},{3,7},{4,0},{5,1},{6,2},{7,3},{8,12},{9,13},{10,... | collective-permute-start | bytes 49160 | tf_op jit(solution)/shard_map/ppermute | solution.py:326
  76.5 0.3 collective-permute-done.12
  76.9 2.7 %collective-permute-done.13 = f32[2,8,256]{2,1,0:T(8,128)S(1)} collective-permute-done((f32[2,8,256]{2,1,0:T(8,128)S(1)}, f32[2,8,256]{2,1,0:T(8,128)S(1)}, u32[]{:S(2)}, u32[]{:S(2)}) %collective-permute-start.13) | collective-permute-done | bytes 16416 | tf_op jit(solution)/shard_map/ppermute | solution.py:326
  79.6 4.1 %collective-permute-start.16 = (f32[2,8,256]{2,1,0:T(8,128)S(1)}, f32[2,8,256]{2,1,0:T(8,128)S(1)}, u32[]{:S(2)}, u32[]{:S(2)}) collective-permute-start(f32[2,8,256]{2,1,0:T(8,128)S(1)} %add_add_fusion.1), channel_id=1, source_target_pairs={{0,1},{1,0},{2,3},{3,2},{4,5},{5,4},{6,7},{7,6},{8,9},{9,8},{10,11... | collective-permute-start | bytes 49160 | tf_op jit(solution)/shard_map/ppermute | solution.py:326
  83.7 1.2 %collective-permute-start.17 = (f32[2,8,256]{2,1,0:T(8,128)S(1)}, f32[2,8,256]{2,1,0:T(8,128)S(1)}, u32[]{:S(2)}, u32[]{:S(2)}) collective-permute-start(f32[2,8,256]{2,1,0:T(8,128)S(1)} %add_add_fusion.1), channel_id=1, source_target_pairs={{0,8},{1,9},{2,10},{3,11},{4,12},{5,13},{6,14},{7,15},{8,0},{9,1},... | collective-permute-start | bytes 49160 | tf_op jit(solution)/shard_map/ppermute | solution.py:326
  84.9 2.0 %collective-permute-start.18 = (f32[2,8,256]{2,1,0:T(8,128)S(1)}, f32[2,8,256]{2,1,0:T(8,128)S(1)}, u32[]{:S(2)}, u32[]{:S(2)}) collective-permute-start(f32[2,8,256]{2,1,0:T(8,128)S(1)} %add_add_fusion.1), channel_id=1, source_target_pairs={{0,9},{1,8},{2,11},{3,10},{4,13},{5,12},{6,15},{7,14},{8,1},{9,0},... | collective-permute-start | bytes 49160 | tf_op jit(solution)/shard_map/ppermute | solution.py:326
  86.9 1.3 %halo3.1 = (f32[2,512,128]{2,1,0:T(8,128)}, f32[2,512,128]{2,1,0:T(8,128)}) custom-call(s32[8,128]{1,0:T(8,128)S(1)} %get-tuple-element.41.odd_ref, f32[2,512,128]{2,1,0:T(8,128)S(1)} %collective-permute-done.14.even_pair, f32[2,512,128]{2,1,0:T(8,128)S(1)} %collective-permute-done.15.odd_pair, f32[2,512,128]{2,1,0:T(8,128)S(1)} %get-tuple-element.74.pre_p, ...), custom_call_target="tpu_custom_call" | custom-call | flops 20000000000 | bytes 4198400 | tf_op jit(solution)/shard_map/halo3/pallas_call | solution.py:32
  88.2 1.9 %collective-permute-done.18 = f32[2,8,256]{2,1,0:T(8,128)S(1)} collective-permute-done((f32[2,8,256]{2,1,0:T(8,128)S(1)}, f32[2,8,256]{2,1,0:T(8,128)S(1)}, u32[]{:S(2)}, u32[]{:S(2)}) %collective-permute-start.18) | collective-permute-done | bytes 16416 | tf_op jit(solution)/shard_map/ppermute | solution.py:326
  90.1 0.6 pad_maximum_fusion
  (33 shorter events, 1.1 us)
Async XLA Ops:
  0.6 7.6 %copy-start.3 = (s32[2,1]{0,1:T(1,128)S(1)}, s32[2,1]{0,1:T(1,128)}, u32[]{:S(2)}) copy-start(s32[2,1]{0,1:T(1,128)} %param.18) | copy-start | bytes 28
  2.0 10.2 %collective-permute-start.2 = (f32[3,256,128]{2,1,0:T(8,128)S(1)}, f32[3,256,128]{2,1,0:T(8,128)S(1)}, u32[]{:S(2)}, u32[]{:S(2)}) collective-permute-start(f32[3,256,128]{2,1,0:T(8,128)S(1)} %get-tuple-element.44.own), channel_id=1, source_target_pairs={{0,128},{128,0},{1,129},{129,1},{2,130},{130,2},{3,131},{131,3},{4... | collective-permute-start | bytes 1179656 | tf_op jit(solution)/shard_map/ppermute | solution.py:371
  4.1 8.4 %collective-permute-start = (f32[2,512,128]{2,1,0:T(8,128)S(1)}, f32[2,512,128]{2,1,0:T(8,128)S(1)}, u32[]{:S(2)}, u32[]{:S(2)}) collective-permute-start(f32[2,512,128]{2,1,0:T(8,128)S(1)} %get-tuple-element.42.p0.po), channel_id=1, source_target_pairs={{0,1},{1,0},{2,3},{3,2},{4,5},{5,4},{6,7},{7,6},{8,9},{9,8},{10,11... | collective-permute-start | bytes 1572872 | tf_op jit(solution)/shard_map/ppermute | solution.py:369
  5.4 10.5 %collective-permute-start.1 = (f32[2,512,128]{2,1,0:T(8,128)S(1)}, f32[2,512,128]{2,1,0:T(8,128)S(1)}, u32[]{:S(2)}, u32[]{:S(2)}) collective-permute-start(f32[2,512,128]{2,1,0:T(8,128)S(1)} %get-tuple-element.42.p0.po), channel_id=1, source_target_pairs={{1,2},{3,4},{5,6},{7,8},{9,10},{11,12},{13,14},{15,16},{17,18},{19... | collective-permute-start | bytes 1572872 | tf_op jit(solution)/shard_map/ppermute | solution.py:369
  8.2 0.7 copy-start
  8.2 0.7 copy-start.1
  16.2 5.2 %collective-permute-start.3 = (f32[2,512,128]{2,1,0:T(8,128)S(1)}, f32[2,512,128]{2,1,0:T(8,128)S(1)}, u32[]{:S(2)}, u32[]{:S(2)}) collective-permute-start(f32[2,512,128]{2,1,0:T(8,128)S(1)} %get-tuple-element.53.p.po), channel_id=1, source_target_pairs={{0,1},{1,0},{2,3},{3,2},{4,5},{5,4},{6,7},{7,6},{8,9},{9,8},{10,11... | collective-permute-start | bytes 1572872 | tf_op jit(solution)/shard_map/ppermute | solution.py:369
  16.3 10.5 %collective-permute-start.4 = (f32[2,512,128]{2,1,0:T(8,128)S(1)}, f32[2,512,128]{2,1,0:T(8,128)S(1)}, u32[]{:S(2)}, u32[]{:S(2)}) collective-permute-start(f32[2,512,128]{2,1,0:T(8,128)S(1)} %get-tuple-element.53.p.po), channel_id=1, source_target_pairs={{1,2},{3,4},{5,6},{7,8},{9,10},{11,12},{13,14},{15,16},{17,18},{19... | collective-permute-start | bytes 1572872 | tf_op jit(solution)/shard_map/ppermute | solution.py:369
  27.1 3.4 %copy-start.2 = (s32[2,256]{1,0:T(2,128)S(1)}, s32[2,256]{1,0:T(2,128)}, u32[]{:S(2)}) copy-start(s32[2,256]{1,0:T(2,128)} %cells_ref.3) | copy-start | bytes 6148
  27.1 7.0 %collective-permute-start.5 = (f32[2,512,128]{2,1,0:T(8,128)S(1)}, f32[2,512,128]{2,1,0:T(8,128)S(1)}, u32[]{:S(2)}, u32[]{:S(2)}) collective-permute-start(f32[2,512,128]{2,1,0:T(8,128)S(1)} %get-tuple-element.59.p.po), channel_id=1, source_target_pairs={{0,1},{1,0},{2,3},{3,2},{4,5},{5,4},{6,7},{7,6},{8,9},{9,8},{10,11... | collective-permute-start | bytes 1572872 | tf_op jit(solution)/shard_map/ppermute | solution.py:369
  27.2 10.5 %collective-permute-start.6 = (f32[2,512,128]{2,1,0:T(8,128)S(1)}, f32[2,512,128]{2,1,0:T(8,128)S(1)}, u32[]{:S(2)}, u32[]{:S(2)}) collective-permute-start(f32[2,512,128]{2,1,0:T(8,128)S(1)} %get-tuple-element.59.p.po), channel_id=1, source_target_pairs={{1,2},{3,4},{5,6},{7,8},{9,10},{11,12},{13,14},{15,16},{17,18},{19... | collective-permute-start | bytes 1572872 | tf_op jit(solution)/shard_map/ppermute | solution.py:369
  40.1 22.2 %collective-permute-start.7 = (f32[2,8,256]{2,1,0:T(8,128)S(1)}, f32[2,8,256]{2,1,0:T(8,128)S(1)}, u32[]{:S(2)}, u32[]{:S(2)}) collective-permute-start(f32[2,8,256]{2,1,0:T(8,128)S(1)} %late.1), channel_id=1, source_target_pairs={{0,16},{1,17},{2,18},{3,19},{4,20},{5,21},{6,22},{7,23},{8,24},{9,... | collective-permute-start | bytes 49160 | tf_op jit(solution)/shard_map/ppermute | solution.py:339
  50.9 11.4 %collective-permute-start.8 = (f32[2,8,256]{2,1,0:T(8,128)S(1)}, f32[2,8,256]{2,1,0:T(8,128)S(1)}, u32[]{:S(2)}, u32[]{:S(2)}) collective-permute-start(f32[2,8,256]{2,1,0:T(8,128)S(1)} %late.1), channel_id=1, source_target_pairs={{0,112},{1,113},{2,114},{3,115},{4,116},{5,117},{6,118},{7,119},{8... | collective-permute-start | bytes 49160 | tf_op jit(solution)/shard_map/ppermute | solution.py:339
  55.6 23.9 %collective-permute-start.14 = (f32[2,512,128]{2,1,0:T(8,128)S(1)}, f32[2,512,128]{2,1,0:T(8,128)S(1)}, u32[]{:S(2)}, u32[]{:S(2)}) collective-permute-start(f32[2,512,128]{2,1,0:T(8,128)S(1)} %get-tuple-element.71.p), channel_id=1, source_target_pairs={{0,1},{1,0},{2,3},{3,2},{4,5},{5,4},{6,7},{7,6},{8,9},{9,8},{10,11... | collective-permute-start | bytes 1572872 | tf_op jit(solution)/shard_map/ppermute | solution.py:369
  60.4 19.1 %collective-permute-start.15 = (f32[2,512,128]{2,1,0:T(8,128)S(1)}, f32[2,512,128]{2,1,0:T(8,128)S(1)}, u32[]{:S(2)}, u32[]{:S(2)}) collective-permute-start(f32[2,512,128]{2,1,0:T(8,128)S(1)} %get-tuple-element.71.p), channel_id=1, source_target_pairs={{1,2},{3,4},{5,6},{7,8},{9,10},{11,12},{13,14},{15,16},{17,18},{19... | collective-permute-start | bytes 1572872 | tf_op jit(solution)/shard_map/ppermute | solution.py:369
  62.4 6.2 %collective-permute-start.9 = (f32[2,8,256]{2,1,0:T(8,128)S(1)}, f32[2,8,256]{2,1,0:T(8,128)S(1)}, u32[]{:S(2)}, u32[]{:S(2)}) collective-permute-start(f32[2,8,256]{2,1,0:T(8,128)S(1)} %fusion.2), channel_id=1, source_target_pairs={{0,48},{1,49},{2,50},{3,51},{4,52},{5,53},{6,54},{7,55},{8,56},{9,... | collective-permute-start | bytes 49160 | tf_op jit(solution)/shard_map/ppermute | solution.py:343
  66.8 5.6 %collective-permute-start.10 = (f32[2,8,256]{2,1,0:T(8,128)S(1)}, f32[2,8,256]{2,1,0:T(8,128)S(1)}, u32[]{:S(2)}, u32[]{:S(2)}) collective-permute-start(f32[2,8,256]{2,1,0:T(8,128)S(1)} %get-tuple-element.82), channel_id=1, source_target_pairs={{0,80},{1,81},{2,82},{3,83},{4,84},{5,85},{6,86},{7,87},{8,88},{9,... | collective-permute-start | bytes 49160 | tf_op jit(solution)/shard_map/ppermute | solution.py:344
  72.4 4.1 %collective-permute-start.11 = (f32[2,8,256]{2,1,0:T(8,128)S(1)}, f32[2,8,256]{2,1,0:T(8,128)S(1)}, u32[]{:S(2)}, u32[]{:S(2)}) collective-permute-start(f32[2,8,256]{2,1,0:T(8,128)S(1)} %add_add_fusion.2), channel_id=1, source_target_pairs={{0,2},{1,3},{2,0},{3,1},{4,6},{5,7},{6,4},{7,5},{8,10},{9,11},{10,... | collective-permute-start | bytes 49160 | tf_op jit(solution)/shard_map/ppermute | solution.py:326
  72.4 4.5 %collective-permute-start.12 = (f32[2,8,256]{2,1,0:T(8,128)S(1)}, f32[2,8,256]{2,1,0:T(8,128)S(1)}, u32[]{:S(2)}, u32[]{:S(2)}) collective-permute-start(f32[2,8,256]{2,1,0:T(8,128)S(1)} %add_add_fusion.2), channel_id=1, source_target_pairs={{0,6},{1,7},{2,4},{3,5},{4,2},{5,3},{6,0},{7,1},{8,14},{9,15},{10,... | collective-permute-start | bytes 49160 | tf_op jit(solution)/shard_map/ppermute | solution.py:326
  75.5 4.1 %collective-permute-start.13 = (f32[2,8,256]{2,1,0:T(8,128)S(1)}, f32[2,8,256]{2,1,0:T(8,128)S(1)}, u32[]{:S(2)}, u32[]{:S(2)}) collective-permute-start(f32[2,8,256]{2,1,0:T(8,128)S(1)} %add_add_fusion.2), channel_id=1, source_target_pairs={{0,4},{1,5},{2,6},{3,7},{4,0},{5,1},{6,2},{7,3},{8,12},{9,13},{10,... | collective-permute-start | bytes 49160 | tf_op jit(solution)/shard_map/ppermute | solution.py:326
  79.6 8.6 %collective-permute-start.16 = (f32[2,8,256]{2,1,0:T(8,128)S(1)}, f32[2,8,256]{2,1,0:T(8,128)S(1)}, u32[]{:S(2)}, u32[]{:S(2)}) collective-permute-start(f32[2,8,256]{2,1,0:T(8,128)S(1)} %add_add_fusion.1), channel_id=1, source_target_pairs={{0,1},{1,0},{2,3},{3,2},{4,5},{5,4},{6,7},{7,6},{8,9},{9,8},{10,11... | collective-permute-start | bytes 49160 | tf_op jit(solution)/shard_map/ppermute | solution.py:326
  83.7 4.5 %collective-permute-start.17 = (f32[2,8,256]{2,1,0:T(8,128)S(1)}, f32[2,8,256]{2,1,0:T(8,128)S(1)}, u32[]{:S(2)}, u32[]{:S(2)}) collective-permute-start(f32[2,8,256]{2,1,0:T(8,128)S(1)} %add_add_fusion.1), channel_id=1, source_target_pairs={{0,8},{1,9},{2,10},{3,11},{4,12},{5,13},{6,14},{7,15},{8,0},{9,1},... | collective-permute-start | bytes 49160 | tf_op jit(solution)/shard_map/ppermute | solution.py:326
  84.9 5.1 %collective-permute-start.18 = (f32[2,8,256]{2,1,0:T(8,128)S(1)}, f32[2,8,256]{2,1,0:T(8,128)S(1)}, u32[]{:S(2)}, u32[]{:S(2)}) collective-permute-start(f32[2,8,256]{2,1,0:T(8,128)S(1)} %add_add_fusion.1), channel_id=1, source_target_pairs={{0,9},{1,8},{2,11},{3,10},{4,13},{5,12},{6,15},{7,14},{8,1},{9,0},... | collective-permute-start | bytes 49160 | tf_op jit(solution)/shard_map/ppermute | solution.py:326

commit v7 on v6

--- a/solution.py
+++ b/solution.py
@@ -122,27 +122,27 @@
         add_source(s, 0, at_ref, source_ref, wavelet_ref, base_p, base_q)
 
 
-def halo_diff(x, lower, upper):
-    hor = taps[4] * (lower[x] + upper[x])
+def side_diff(x, rows, upper):
+    above = below = taps[4] * rows[x]
     for k in range(1, 4):
         if x + k < CX:
-            hor = hor + taps[4 - k] * lower[x + k]
+            below = below + taps[4 - k] * rows[x + k]
         if x - k >= 0:
-            hor = hor + taps[4 - k] * upper[x - k]
-    return hor
+            above = above + taps[4 - k] * rows[x - k]
+    return jnp.where(upper, above, below)
 
 
 def tile_at(x, tile):
     return pl.ds(x * CY + tile * 8, 8)
 
 
-def halo_rows(s, tile, odd, even_pair, odd_pair):
-    a = [even_pair[s, tile_at(x, tile), :] for x in range(CX)]
-    b = [odd_pair[s, tile_at(x, tile), :] for x in range(CX)]
-    return [jnp.where(odd, a[x], b[x]) for x in range(CX)], [jnp.where(odd, b[x], a[x]) for x in range(CX)]
-
-
-def first_kernel(side_ref, live_ref, own, other, base_p, base_q, hor_ref, ver_ref, pre_p, pre_q, c_ref, cs_ref, ck_ref):
+def flat_at(s, x, tile):
+    return pl.ds(s * ROWS + x * CY + tile * 8, 8)
+
+
+def first_kernel(side_ref, live_ref, own, other, base_p, base_q, hor_ref, ver_ref, pre_p, pre_q, c_ref, cs_ref, ck_ref, extra_ref):
+    extra_ref[pl.ds(ROWS, 16), :] = live_ref[...]
+
     def work(first, second):
         for tile in range(CY // 8):
             model = []
@@ -150,6 +150,7 @@
                 half = (first, second)[x // 2]
                 at = tile_at(x % 2, tile)
                 model.append((half[0, at, :], half[1, at, :], half[2, at, :]))
+                extra_ref[tile_at(x, tile), :] = model[x][1]
             for s in range(2):
                 live = live_ref[pl.ds(8 * s, 8), :]
                 for x in range(CX):
@@ -180,16 +181,53 @@
         add_source(s, step, at_ref, source_ref, wavelet_ref, pre_p, pre_q)
 
 
-def halo_kernel(odd_ref, even_pair, odd_pair, pre_p, pre_q, cs_ref, ck_ref, p, q):
-    odd = odd_ref[...] == 1
+def chip_kernel(odd_ref, even_pair, pre_p, pre_q, cs_ref, ck_ref, *rest):
+    extra, (out_p, out_q) = rest[:-2], rest[-2:]
+    upper = odd_ref[...] == 0
+    for ref in extra:
+        out_p[pl.ds(2 * ROWS, ROWS + 16), :] = ref[...]
     for s in range(2):
         for tile in range(CY // 8):
-            lower, upper = halo_rows(s, tile, odd, even_pair, odd_pair)
+            rows = [even_pair[s, tile_at(x, tile), :] for x in range(CX)]
             for x in range(CX):
                 at = tile_at(x, tile)
-                hor = halo_diff(x, lower, upper)
-                p[s, at, :] = pre_p[s, at, :] + cs_ref[s, at, :] * hor
-                q[s, at, :] = pre_q[s, at, :] + ck_ref[s, at, :] * hor
+                hor = side_diff(x, rows, upper)
+                out_p[flat_at(s, x, tile), :] = pre_p[s, at, :] + cs_ref[s, at, :] * hor
+                out_q[s, at, :] = pre_q[s, at, :] + ck_ref[s, at, :] * hor
+
+
+def join(odd_ref, other_rows, part_p, part_q, cs_ref, ck_ref, p, q):
+    upper = odd_ref[...] == 1
+    for s in range(2):
+        for tile in range(CY // 8):
+            rows = other_rows(s, tile)
+            for x in range(CX):
+                at = tile_at(x, tile)
+                hor = side_diff(x, rows, upper)
+                p[s, at, :] = part_p[flat_at(s, x, tile), :] + cs_ref[s, at, :] * hor
+                q[s, at, :] = part_q[s, at, :] + ck_ref[s, at, :] * hor
+
+
+def first_join_kernel(odd_ref, got, part_p, part_q, cs_ref, ck_ref, p, q):
+    def other_rows(s, tile):
+        return [got[s, tile_at(x, tile), :] for x in range(CX)]
+
+    join(odd_ref, other_rows, part_p, part_q, cs_ref, ck_ref, p, q)
+
+
+def join_kernel(odd_ref, got, extra, before, part_p, part_q, cs_ref, ck_ref, p, q):
+    upper = odd_ref[...] == 0
+
+    def other_rows(s, tile):
+        mine = [before[s, tile_at(x, tile), :] for x in range(CX)]
+        live = extra[pl.ds(3 * ROWS + 8 * s, 8), :]
+        out = []
+        for x in range(CX):
+            stretch = extra[pl.ds(2 * ROWS + x * CY + tile * 8, 8), :] * live
+            out.append(got[flat_at(s, x, tile), :] + stretch * side_diff(x, mine, upper))
+        return out
+
+    join(odd_ref, other_rows, part_p, part_q, cs_ref, ck_ref, p, q)
 
 
 def samples(field, s, pick_z, pick_y):
@@ -365,52 +403,60 @@
          shape(2, 8, receiver_cells.shape[1], dtype=jnp.int32)),
         10**6, "begin", far=range(8), scratch=ints + [pltpu.SemaphoreType.DMA((7,))])
 
-    def exchange(values):
-        return (lax.ppermute(values, "space", even_pairs(blocks)), lax.ppermute(values, "space", odd_pairs(blocks)))
+    def on_chip(values):
+        return lax.ppermute(values, "space", even_pairs(blocks))
+
+    def off_chip(values):
+        return lax.ppermute(values, "space", odd_pairs(blocks))
 
     other = lax.ppermute(own, "shot", [(0, 1), (1, 0)])
-    halos = exchange(p)
+    got, pair = off_chip(p), on_chip(p)
     base_p, base_q, q, hor, ver = call(
         ready_kernel, (at, active, source_cells, wavelet, p, p_old, q_now, q_old), (field,) * 5, 10**8, "ready",
         far=(5, 6, 7), scratch=[pltpu.SemaphoreType.DMA((3,))])
+    pre_p, pre_q, c, cs, ck, extra = call(
+        first_kernel, (side, live, own, other, base_p, base_q, hor, ver), (*(field,) * 5, shape(ROWS + 16, CZ)),
+        2 * 10**10, "first")
+    part_p, part_q = call(
+        chip_kernel, (odd, pair, pre_p, pre_q, cs, ck, extra), (shape(3 * ROWS + 16, CZ), field), 10**6, "chip0")
+    coming = off_chip(part_p)
     po, qo = p, q
-    pre_p, pre_q, c, cs, ck = call(
-        first_kernel, (side, live, own, other, base_p, base_q, hor, ver), (field,) * 5, 2 * 10**10, "first")
-    p, q = call(halo_kernel, (odd, *halos, pre_p, pre_q, cs, ck), (field, field), 10**6, "halo")
-    halos = exchange(p)
+    p, q = call(first_join_kernel, (odd, got, part_p, part_q, cs, ck), (field, field), 10**6, "join0")
+    extra = coming
     traced = shape(2, 8, receiver_cells.shape[1])
     for step in range(1, STEPS):
+        got = coming
+        pair = on_chip(p)
         now = (at, source_cells, wavelet, p, po, q, qo, c, cs, ck)
-        if step == 1:
-            pre_p, pre_q = call(functools.partial(local_kernel, step), now, (field, field), 10**8, "local")
         if step == 2:
             pre_p, pre_q, early = call(
-                functools.partial(early_kernel, step), (*now, receiver_cells), (field, field, traced), 10**8, "local_early")
+                functools.partial(early_kernel, step), (*now, receiver_cells), (field, field, traced), 10**6, "local_early")
+        else:
+            pre_p, pre_q = call(functools.partial(local_kernel, step), now, (field, field), 10**6, f"local{step}")
+        if step == 3:
+            total, = call(late_kernel, (at, source_cells, wavelet, receiver_cells, early, p, q), (traced,), 10**8, "late")
+        part_p, part_q = call(
+            chip_kernel, (odd, pair, pre_p, pre_q, cs, ck), (shape(2 * ROWS, CZ), field), 10**6, f"chip{step}")
         if step == 3:
             break
-        po, qo = p, q
+        coming = off_chip(part_p)
+        if step == 1:
+            got, coming = lax.optimization_barrier((got, coming))
+            extra = got
+        before, po, qo = po, p, q
         p, q = call(
-            halo_kernel, (odd, *halos, pre_p, pre_q, cs, ck), (field, field), 10**6, f"halo{step}")
-        if step < 2:
-            halos = exchange(p)
-    total, = call(late_kernel, (at, source_cells, wavelet, receiver_cells, early, p, q), (traced,), 10**8, "late")
-    sent, total = lax.optimization_barrier((p, total))
-    halos = exchange(sent)
-
-    local = call(functools.partial(local_kernel, 3), now, (field, field), 10**8, "local3")
+            join_kernel, (odd, got, extra, before, part_p, part_q, cs, ck), (field, field), 10**6, f"join{step}")
+
+    local = (got, part_p, part_q)
 
     def gate(total):
         nonlocal local
         total, local = lax.optimization_barrier((total, local))
         return total
 
-    def last_gate(total):
-        nonlocal halos
-        total, halos = lax.optimization_barrier((total, halos))
-        return total
-
-    total = reduced(total, blocks, z_odd, gate, last_gate)
-    p, q = call(halo_kernel, (odd, *halos, *local, cs, ck), (field, field), 2 * 10**10, "halo3")
+    total = reduced(total, blocks, z_odd, lambda total: total, gate)
+    got, part_p, part_q = local
+    p, q = call(join_kernel, (odd, got, extra, po, part_p, part_q, cs, ck), (field, field), 2 * 10**10, "join3")
     last = total[:, 4] + total[:, 0] * total[:, 5]
     traces = jnp.stack([total[:, 1], total[:, 2], total[:, 3], last], axis=1)
     return (p.reshape(pressure_now.shape), q.reshape(pressure_now.shape), traces)

time: 90.9 us -> 88.7 us (0.976)
  starting transfers between devices: 51 us -> 44.8 us
  waiting for transfers between devices: 21 us -> 23.1 us
  Pallas kernels: 16.5 us -> 17.8 us
    ppermute x8, starting transfers between devices: 17.5 us -> 12.8 us  [the longest x4 10.2 us: off_chip(): return lax.ppermute(values, 'space', odd_pairs(blocks))]
    ppermute x1, starting transfers between devices: 4.39 us -> 1.71 us  [reduced(): plus = lax.ppermute(even_part, 'space', todo[3][0])]
    ppermute x1, waiting for transfers between devices: 0.01 us -> 2.65 us  [reduced(): plus = lax.ppermute(even_part, 'space', todo[3][0])]
    ppermute x8, waiting for transfers between devices: 12.3 us -> 14.5 us  [the longest x4 14.5 us: off_chip(): return lax.ppermute(values, 'space', odd_pairs(blocks))]
    ppermute x6, waiting for transfers between devices: 4.89 us -> 2.91 us  [summed(): lax.ppermute(total, 'space', pairs)]
    pallas_call x11 -> x15, Pallas kernels: 16.5 us -> 17.8 us  [call(): pl.pallas_call(kernel, out_shape=tuple(outs), in_specs=specs, out_specs=t...]
    ppermute x2, starting transfers between devices: 15.5 us -> 16.8 us  [reduced(): first, second = (lax.ppermute(total, 'space', pairs) for pairs in todo[2])]
  transfers between devices with their start and end apart: 19 -> 19, of which waited for: 7 -> 7; matrix products, arithmetic and copies ran while one was open for 0% -> 0% of each run, Pallas kernels for 13% -> 15%
where the time goes in v7:
time: 88.7 us; the launch traced here: 88.5 us
  starting transfers between devices  44.8 us (51%)
  waiting for transfers between devices  23.1 us (26%)
  Pallas kernels  17.8 us (20%)
  local copies, waits for them, and re-layouts  1.25 us (1%)
  between operations  0.91 us (1%)
    pallas_call x15, Pallas kernels, call(): pl.pallas_call(kernel, out_shape=tuple(outs), in_specs=specs, out_specs=t...  17.8 us
    ppermute x2, starting transfers between devices, reduced(): first, second = (lax.ppermute(total, 'space', pairs) for pairs in todo[2])  16.8 us
    ppermute x4, waiting for transfers between devices, off_chip(): return lax.ppermute(values, 'space', odd_pairs(blocks))  14.5 us
    ppermute x6, starting transfers between devices, summed(): lax.ppermute(total, 'space', pairs)  11.2 us
    ppermute x4, starting transfers between devices, off_chip(): return lax.ppermute(values, 'space', odd_pairs(blocks))  10.2 us
    ppermute x1, waiting for transfers between devices, reduced(): minus = lax.ppermute(odd_part, 'space', todo[3][1])  3.01 us
    ppermute x6, waiting for transfers between devices, summed(): lax.ppermute(total, 'space', pairs)  2.91 us
    ppermute x1, waiting for transfers between devices, reduced(): plus = lax.ppermute(even_part, 'space', todo[3][0])  2.65 us
  transfers between devices with their start and end apart: 19, of which 7 were waited for; matrix products, arithmetic and copies ran while one was open for 0% of the time, Pallas kernels for 15%

profile of v7, /device:TPU:1, one launch (start us, length us, event | category | flops | bytes accessed | tf_op | source)
XLA Modules:
  0.0 88.5 jit_solution(18009053885013049460)
XLA Ops:
  0.6 1.4 %begin.1 = (f32[3,256,128]{2,1,0:T(8,128)S(1)}, f32[2,512,128]{2,1,0:T(8,128)S(1)}, s32[8,128]{1,0:T(8,128)S(1)}, f32[16,128]{1,0:T(8,128)S(1)}, s32[2,8,256]{2,1,0:T(8,128)S(1)}) custom-call(s32[1]{0:T(128)} %bitcast.at_far.at_ref, s32[1]{0:T(128)} %bitcast.1.side_far.side_ref, s32[2]{0:T(128)} %bitcast.16, s32[2]{0:T(128)} %source_ref.9, ...), custom_call_target="tpu_custom_call" | custom-call | flops 1000000 | bytes 1863704 | tf_op jit(solution)/shard_map/begin/pallas_call | solution.py:32
  2.0 2.1 %collective-permute-start.1 = (f32[3,256,128]{2,1,0:T(8,128)S(1)}, f32[3,256,128]{2,1,0:T(8,128)S(1)}, u32[]{:S(2)}, u32[]{:S(2)}) collective-permute-start(f32[3,256,128]{2,1,0:T(8,128)S(1)} %get-tuple-element.51.own), channel_id=1, source_target_pairs={{0,128},{128,0},{1,129},{129,1},{2,130},{130,2},{3,131},{131,3},{4... | collective-permute-start | bytes 1179656 | tf_op jit(solution)/shard_map/ppermute | solution.py:412
  4.1 1.3 %collective-permute-start = (f32[2,512,128]{2,1,0:T(8,128)S(1)}, f32[2,512,128]{2,1,0:T(8,128)S(1)}, u32[]{:S(2)}, u32[]{:S(2)}) collective-permute-start(f32[2,512,128]{2,1,0:T(8,128)S(1)} %get-tuple-element.49.p0.po.before), channel_id=1, source_target_pairs={{0,1},{1,0},{2,3},{3,2},{4,5},{5,4},{6,7},{7,6},{8,9},{9,8},{10,11... | collective-permute-start | bytes 1572872 | tf_op jit(solution)/shard_map/ppermute | solution.py:407
  5.4 2.7 %collective-permute-start.3 = (f32[2,512,128]{2,1,0:T(8,128)S(1)}, f32[2,512,128]{2,1,0:T(8,128)S(1)}, u32[]{:S(2)}, u32[]{:S(2)}) collective-permute-start(f32[2,512,128]{2,1,0:T(8,128)S(1)} %get-tuple-element.49.p0.po.before), channel_id=1, source_target_pairs={{1,2},{3,4},{5,6},{7,8},{9,10},{11,12},{13,14},{15,16},{17,18},{19... | collective-permute-start | bytes 1572872 | tf_op jit(solution)/shard_map/ppermute | solution.py:410
  8.2 0.6 copy-done
  8.9 3.3 %ready.1 = (f32[2,512,128]{2,1,0:T(8,128)S(1)}, f32[2,512,128]{2,1,0:T(8,128)S(1)}, f32[2,512,128]{2,1,0:T(8,128)S(1)}, f32[2,512,128]{2,1,0:T(8,128)S(1)}, f32[2,512,128]{2,1,0:T(8,128)S(1)}) custom-call(s32[1]{0:T(128)} %bitcast.at_far.at_ref, s32[2]{0:T(128)S(1)} %bitcast.17, s32[2]{0:T(128)S(1)} %copy-done.1, f32[2,4]{1,0:T(2,128)S(1)} %copy-done, ...), custom_call_target="tpu_custom_call" | custom-call | flops 100000000 | bytes 4718644 | tf_op jit(solution)/shard_map/ready/pallas_call | solution.py:32
  12.8 3.2 %collective-permute-done.3.got = f32[2,512,128]{2,1,0:T(8,128)S(1)} collective-permute-done((f32[2,512,128]{2,1,0:T(8,128)S(1)}, f32[2,512,128]{2,1,0:T(8,128)S(1)}, u32[]{:S(2)}, u32[]{:S(2)}) %collective-permute-start.3) | collective-permute-done | bytes 524320 | tf_op jit(solution)/shard_map/ppermute | solution.py:410
  16.3 3.2 %collective-permute-start.2 = (f32[1552,128]{1,0:T(8,128)S(1)}, f32[1552,128]{1,0:T(8,128)S(1)}, u32[]{:S(2)}, u32[]{:S(2)}) collective-permute-start(f32[1552,128]{1,0:T(8,128)S(1)} %get-tuple-element.61.part_p), channel_id=1, source_target_pairs={{1,2},{3,4},{5,6},{7,8},{9,10},{11,12},{13,14},{15,16},{17,18},{19... | collective-permute-start | bytes 2383880 | tf_op jit(solution)/shard_map/ppermute | solution.py:410
  19.5 1.9 %local1.1 = (f32[2,512,128]{2,1,0:T(8,128)S(1)}, f32[2,512,128]{2,1,0:T(8,128)S(1)}) custom-call(s32[1]{0:T(128)} %bitcast.at_far.at_ref, s32[2]{0:T(128)S(1)} %copy-done.1, f32[2,4]{1,0:T(2,128)S(1)} %copy-done, f32[2,512,128]{2,1,0:T(8,128)S(1)} %get-tuple-element.63.p.po.before, f32[2,512,128]{2,1,0:T(8,128)S(1)} %get-tuple-element.49.p0.po.before, ...), custom_call_target="tpu_custom_call" | custom-call | flops 1000000 | bytes 4718636 | tf_op jit(solution)/shard_map/local1/pallas_call | solution.py:32
  21.6 2.3 %collective-permute-start.5 = (f32[1024,128]{1,0:T(8,128)S(1)}, f32[1024,128]{1,0:T(8,128)S(1)}, u32[]{:S(2)}, u32[]{:S(2)}) collective-permute-start(f32[1024,128]{1,0:T(8,128)S(1)} %get-tuple-element.69.part_p), channel_id=1, source_target_pairs={{1,2},{3,4},{5,6},{7,8},{9,10},{11,12},{13,14},{15,16},{17,18},{19... | collective-permute-start | bytes 1572872 | tf_op jit(solution)/shard_map/ppermute | solution.py:410
  23.9 5.7 %collective-permute-done.2.got.extra = f32[1552,128]{1,0:T(8,128)S(1)} collective-permute-done((f32[1552,128]{1,0:T(8,128)S(1)}, f32[1552,128]{1,0:T(8,128)S(1)}, u32[]{:S(2)}, u32[]{:S(2)}) %collective-permute-start.2) | collective-permute-done | bytes 794656 | tf_op jit(solution)/shard_map/ppermute | solution.py:410
  29.6 5.6 %collective-permute-done.5.got = f32[1024,128]{1,0:T(8,128)S(1)} collective-permute-done((f32[1024,128]{1,0:T(8,128)S(1)}, f32[1024,128]{1,0:T(8,128)S(1)}, u32[]{:S(2)}, u32[]{:S(2)}) %collective-permute-start.5) | collective-permute-done | bytes 524320 | tf_op jit(solution)/shard_map/ppermute | solution.py:410
  35.8 0.6 copy-done.2
  36.4 3.6 %local_early.1 = (f32[2,512,128]{2,1,0:T(8,128)S(1)}, f32[2,512,128]{2,1,0:T(8,128)S(1)}, f32[2,8,256]{2,1,0:T(8,128)S(1)}) custom-call(s32[1]{0:T(128)} %bitcast.at_far.at_ref, s32[2]{0:T(128)S(1)} %copy-done.1, f32[2,4]{1,0:T(2,128)S(1)} %copy-done, f32[2,512,128]{2,1,0:T(8,128)S(1)} %get-tuple-element.72.p.po.before, ...), custom_call_target="tpu_custom_call" | custom-call | flops 1000000 | bytes 4737068 | tf_op jit(solution)/shard_map/local_early/pallas_call | solution.py:32
  40.7 2.1 %late.1 = f32[2,8,256]{2,1,0:T(8,128)S(1)} custom-call(s32[1]{0:T(128)} %bitcast.at_far.at_ref, s32[2]{0:T(128)S(1)} %copy-done.1, f32[2,4]{1,0:T(2,128)S(1)} %copy-done, s32[2,256]{1,0:T(2,128)S(1)} %copy-done.2, f32[2,8,256]{2,1,0:T(8,128)S(1)} %get-tuple-element.74.early_ref, f32[2,512,128]{2,1,0:T(8,128)S(1)} %get-tuple-element.80.p, ...), custom_call_target="tpu_custom_call" | custom-call | flops 100000000 | bytes 1083436 | tf_op jit(solution)/shard_map/late/pallas_call | solution.py:32
  42.8 10.4 %collective-permute-start.7 = (f32[2,8,256]{2,1,0:T(8,128)S(1)}, f32[2,8,256]{2,1,0:T(8,128)S(1)}, u32[]{:S(2)}, u32[]{:S(2)}) collective-permute-start(f32[2,8,256]{2,1,0:T(8,128)S(1)} %late.1), channel_id=1, source_target_pairs={{0,16},{1,17},{2,18},{3,19},{4,20},{5,21},{6,22},{7,23},{8,24},{9,... | collective-permute-start | bytes 49160 | tf_op jit(solution)/shard_map/ppermute | solution.py:377
  53.2 6.4 %collective-permute-start.8 = (f32[2,8,256]{2,1,0:T(8,128)S(1)}, f32[2,8,256]{2,1,0:T(8,128)S(1)}, u32[]{:S(2)}, u32[]{:S(2)}) collective-permute-start(f32[2,8,256]{2,1,0:T(8,128)S(1)} %late.1), channel_id=1, source_target_pairs={{0,112},{1,113},{2,114},{3,115},{4,116},{5,117},{6,118},{7,119},{8... | collective-permute-start | bytes 49160 | tf_op jit(solution)/shard_map/ppermute | solution.py:377
  59.6 1.1 %collective-permute-start.15 = (f32[2,512,128]{2,1,0:T(8,128)S(1)}, f32[2,512,128]{2,1,0:T(8,128)S(1)}, u32[]{:S(2)}, u32[]{:S(2)}) collective-permute-start(f32[2,512,128]{2,1,0:T(8,128)S(1)} %get-tuple-element.80.p), channel_id=1, source_target_pairs={{0,1},{1,0},{2,3},{3,2},{4,5},{5,4},{6,7},{7,6},{8,9},{9,8},{10,11... | collective-permute-start | bytes 1572872 | tf_op jit(solution)/shard_map/ppermute | solution.py:407
  60.7 1.9 %collective-permute-start.14 = (f32[1024,128]{1,0:T(8,128)S(1)}, f32[1024,128]{1,0:T(8,128)S(1)}, u32[]{:S(2)}, u32[]{:S(2)}) collective-permute-start(f32[1024,128]{1,0:T(8,128)S(1)} %get-tuple-element.78.part_p), channel_id=1, source_target_pairs={{1,2},{3,4},{5,6},{7,8},{9,10},{11,12},{13,14},{15,16},{17,18},{19... | collective-permute-start | bytes 1572872 | tf_op jit(solution)/shard_map/ppermute | solution.py:410
  62.7 1.7 %collective-permute-start.9 = (f32[2,8,256]{2,1,0:T(8,128)S(1)}, f32[2,8,256]{2,1,0:T(8,128)S(1)}, u32[]{:S(2)}, u32[]{:S(2)}) collective-permute-start(f32[2,8,256]{2,1,0:T(8,128)S(1)} %fusion.2), channel_id=1, source_target_pairs={{0,48},{1,49},{2,50},{3,51},{4,52},{5,53},{6,54},{7,55},{8,56},{9,... | collective-permute-start | bytes 49160 | tf_op jit(solution)/shard_map/ppermute | solution.py:381
  64.5 2.6 %collective-permute-done.9 = f32[2,8,256]{2,1,0:T(8,128)S(1)} collective-permute-done((f32[2,8,256]{2,1,0:T(8,128)S(1)}, f32[2,8,256]{2,1,0:T(8,128)S(1)}, u32[]{:S(2)}, u32[]{:S(2)}) %collective-permute-start.9) | collective-permute-done | bytes 16416 | tf_op jit(solution)/shard_map/ppermute | solution.py:381
  67.2 3.0 %collective-permute-done.10 = f32[2,8,256]{2,1,0:T(8,128)S(1)} collective-permute-done((f32[2,8,256]{2,1,0:T(8,128)S(1)}, f32[2,8,256]{2,1,0:T(8,128)S(1)}, u32[]{:S(2)}, u32[]{:S(2)}) %collective-permute-start.10) | collective-permute-done | bytes 16416 | tf_op jit(solution)/shard_map/ppermute | solution.py:382
  70.2 4.5 %collective-permute-start.12 = (f32[2,8,256]{2,1,0:T(8,128)S(1)}, f32[2,8,256]{2,1,0:T(8,128)S(1)}, u32[]{:S(2)}, u32[]{:S(2)}) collective-permute-start(f32[2,8,256]{2,1,0:T(8,128)S(1)} %add_add_fusion.2), channel_id=1, source_target_pairs={{0,6},{1,7},{2,4},{3,5},{4,2},{5,3},{6,0},{7,1},{8,14},{9,15},{10,... | collective-permute-start | bytes 49160 | tf_op jit(solution)/shard_map/ppermute | solution.py:364
  74.7 1.1 %collective-permute-start.13 = (f32[2,8,256]{2,1,0:T(8,128)S(1)}, f32[2,8,256]{2,1,0:T(8,128)S(1)}, u32[]{:S(2)}, u32[]{:S(2)}) collective-permute-start(f32[2,8,256]{2,1,0:T(8,128)S(1)} %add_add_fusion.2), channel_id=1, source_target_pairs={{0,4},{1,5},{2,6},{3,7},{4,0},{5,1},{6,2},{7,3},{8,12},{9,13},{10,... | collective-permute-start | bytes 49160 | tf_op jit(solution)/shard_map/ppermute | solution.py:364
  75.8 1.9 %local3.1 = (f32[2,512,128]{2,1,0:T(8,128)S(1)}, f32[2,512,128]{2,1,0:T(8,128)S(1)}) custom-call(s32[1]{0:T(128)} %bitcast.at_far.at_ref, s32[2]{0:T(128)S(1)} %copy-done.1, f32[2,4]{1,0:T(2,128)S(1)} %copy-done, f32[2,512,128]{2,1,0:T(8,128)S(1)} %get-tuple-element.80.p, f32[2,512,128]{2,1,0:T(8,128)S(1)} %get-tuple-element.72.p.po.before, ...), custom_call_target="tpu_custom_call" | custom-call | flops 1000000 | bytes 4718636 | tf_op jit(solution)/shard_map/local3/pallas_call | solution.py:32
  77.7 1.1 %collective-permute-done.13 = f32[2,8,256]{2,1,0:T(8,128)S(1)} collective-permute-done((f32[2,8,256]{2,1,0:T(8,128)S(1)}, f32[2,8,256]{2,1,0:T(8,128)S(1)}, u32[]{:S(2)}, u32[]{:S(2)}) %collective-permute-start.13) | collective-permute-done | bytes 16416 | tf_op jit(solution)/shard_map/ppermute | solution.py:364
  79.1 2.4 %collective-permute-start.16 = (f32[2,8,256]{2,1,0:T(8,128)S(1)}, f32[2,8,256]{2,1,0:T(8,128)S(1)}, u32[]{:S(2)}, u32[]{:S(2)}) collective-permute-start(f32[2,8,256]{2,1,0:T(8,128)S(1)} %add_add_fusion.1), channel_id=1, source_target_pairs={{0,1},{1,0},{2,3},{3,2},{4,5},{5,4},{6,7},{7,6},{8,9},{9,8},{10,11... | collective-permute-start | bytes 49160 | tf_op jit(solution)/shard_map/ppermute | solution.py:364
  81.4 1.3 %collective-permute-start.17 = (f32[2,8,256]{2,1,0:T(8,128)S(1)}, f32[2,8,256]{2,1,0:T(8,128)S(1)}, u32[]{:S(2)}, u32[]{:S(2)}) collective-permute-start(f32[2,8,256]{2,1,0:T(8,128)S(1)} %add_add_fusion.1), channel_id=1, source_target_pairs={{0,8},{1,9},{2,10},{3,11},{4,12},{5,13},{6,14},{7,15},{8,0},{9,1},... | collective-permute-start | bytes 49160 | tf_op jit(solution)/shard_map/ppermute | solution.py:364
  82.7 2.0 %collective-permute-start.18 = (f32[2,8,256]{2,1,0:T(8,128)S(1)}, f32[2,8,256]{2,1,0:T(8,128)S(1)}, u32[]{:S(2)}, u32[]{:S(2)}) collective-permute-start(f32[2,8,256]{2,1,0:T(8,128)S(1)} %add_add_fusion.1), channel_id=1, source_target_pairs={{0,9},{1,8},{2,11},{3,10},{4,13},{5,12},{6,15},{7,14},{8,1},{9,0},... | collective-permute-start | bytes 49160 | tf_op jit(solution)/shard_map/ppermute | solution.py:364
  84.7 1.4 %join3.1 = (f32[2,512,128]{2,1,0:T(8,128)}, f32[2,512,128]{2,1,0:T(8,128)}) custom-call(s32[8,128]{1,0:T(8,128)S(1)} %get-tuple-element.48.odd_ref, f32[1024,128]{1,0:T(8,128)S(1)} %collective-permute-done.14.got, f32[1552,128]{1,0:T(8,128)S(1)} %collective-permute-done.2.got.extra, f32[2,512,128]{2,1,0:T(8,128)S(1)} %get-tuple-element.72.p.po.before, ...), custom_call_target="tpu_custom_call" | custom-call | flops 20000000000 | bytes 4993024 | tf_op jit(solution)/shard_map/join3/pallas_call | solution.py:32
  86.1 1.8 %collective-permute-done.18 = f32[2,8,256]{2,1,0:T(8,128)S(1)} collective-permute-done((f32[2,8,256]{2,1,0:T(8,128)S(1)}, f32[2,8,256]{2,1,0:T(8,128)S(1)}, u32[]{:S(2)}, u32[]{:S(2)}) %collective-permute-start.18) | collective-permute-done | bytes 16416 | tf_op jit(solution)/shard_map/ppermute | solution.py:364
  87.9 0.6 pad_maximum_fusion
  (37 shorter events, 2.7 us)
Async XLA Ops:
  0.6 7.6 %copy-start.3 = (s32[2,1]{0,1:T(1,128)S(1)}, s32[2,1]{0,1:T(1,128)}, u32[]{:S(2)}) copy-start(s32[2,1]{0,1:T(1,128)} %param.18) | copy-start | bytes 28
  2.0 10.2 %collective-permute-start.1 = (f32[3,256,128]{2,1,0:T(8,128)S(1)}, f32[3,256,128]{2,1,0:T(8,128)S(1)}, u32[]{:S(2)}, u32[]{:S(2)}) collective-permute-start(f32[3,256,128]{2,1,0:T(8,128)S(1)} %get-tuple-element.51.own), channel_id=1, source_target_pairs={{0,128},{128,0},{1,129},{129,1},{2,130},{130,2},{3,131},{131,3},{4... | collective-permute-start | bytes 1179656 | tf_op jit(solution)/shard_map/ppermute | solution.py:412
  4.1 8.4 %collective-permute-start = (f32[2,512,128]{2,1,0:T(8,128)S(1)}, f32[2,512,128]{2,1,0:T(8,128)S(1)}, u32[]{:S(2)}, u32[]{:S(2)}) collective-permute-start(f32[2,512,128]{2,1,0:T(8,128)S(1)} %get-tuple-element.49.p0.po.before), channel_id=1, source_target_pairs={{0,1},{1,0},{2,3},{3,2},{4,5},{5,4},{6,7},{7,6},{8,9},{9,8},{10,11... | collective-permute-start | bytes 1572872 | tf_op jit(solution)/shard_map/ppermute | solution.py:407
  5.4 10.5 %collective-permute-start.3 = (f32[2,512,128]{2,1,0:T(8,128)S(1)}, f32[2,512,128]{2,1,0:T(8,128)S(1)}, u32[]{:S(2)}, u32[]{:S(2)}) collective-permute-start(f32[2,512,128]{2,1,0:T(8,128)S(1)} %get-tuple-element.49.p0.po.before), channel_id=1, source_target_pairs={{1,2},{3,4},{5,6},{7,8},{9,10},{11,12},{13,14},{15,16},{17,18},{19... | collective-permute-start | bytes 1572872 | tf_op jit(solution)/shard_map/ppermute | solution.py:410
  8.2 0.7 copy-start
  8.2 0.7 copy-start.1
  16.2 5.2 %collective-permute-start.4 = (f32[2,512,128]{2,1,0:T(8,128)S(1)}, f32[2,512,128]{2,1,0:T(8,128)S(1)}, u32[]{:S(2)}, u32[]{:S(2)}) collective-permute-start(f32[2,512,128]{2,1,0:T(8,128)S(1)} %get-tuple-element.63.p.po.before), channel_id=1, source_target_pairs={{0,1},{1,0},{2,3},{3,2},{4,5},{5,4},{6,7},{7,6},{8,9},{9,8},{10,11... | collective-permute-start | bytes 1572872 | tf_op jit(solution)/shard_map/ppermute | solution.py:407
  16.3 13.4 %collective-permute-start.2 = (f32[1552,128]{1,0:T(8,128)S(1)}, f32[1552,128]{1,0:T(8,128)S(1)}, u32[]{:S(2)}, u32[]{:S(2)}) collective-permute-start(f32[1552,128]{1,0:T(8,128)S(1)} %get-tuple-element.61.part_p), channel_id=1, source_target_pairs={{1,2},{3,4},{5,6},{7,8},{9,10},{11,12},{13,14},{15,16},{17,18},{19... | collective-permute-start | bytes 2383880 | tf_op jit(solution)/shard_map/ppermute | solution.py:410
  21.6 13.7 %collective-permute-start.5 = (f32[1024,128]{1,0:T(8,128)S(1)}, f32[1024,128]{1,0:T(8,128)S(1)}, u32[]{:S(2)}, u32[]{:S(2)}) collective-permute-start(f32[1024,128]{1,0:T(8,128)S(1)} %get-tuple-element.69.part_p), channel_id=1, source_target_pairs={{1,2},{3,4},{5,6},{7,8},{9,10},{11,12},{13,14},{15,16},{17,18},{19... | collective-permute-start | bytes 1572872 | tf_op jit(solution)/shard_map/ppermute | solution.py:410
  35.7 0.7 copy-start.2
  35.7 4.3 %collective-permute-start.6 = (f32[2,512,128]{2,1,0:T(8,128)S(1)}, f32[2,512,128]{2,1,0:T(8,128)S(1)}, u32[]{:S(2)}, u32[]{:S(2)}) collective-permute-start(f32[2,512,128]{2,1,0:T(8,128)S(1)} %get-tuple-element.72.p.po.before), channel_id=1, source_target_pairs={{0,1},{1,0},{2,3},{3,2},{4,5},{5,4},{6,7},{7,6},{8,9},{9,8},{10,11... | collective-permute-start | bytes 1572872 | tf_op jit(solution)/shard_map/ppermute | solution.py:407
  42.8 19.8 %collective-permute-start.7 = (f32[2,8,256]{2,1,0:T(8,128)S(1)}, f32[2,8,256]{2,1,0:T(8,128)S(1)}, u32[]{:S(2)}, u32[]{:S(2)}) collective-permute-start(f32[2,8,256]{2,1,0:T(8,128)S(1)} %late.1), channel_id=1, source_target_pairs={{0,16},{1,17},{2,18},{3,19},{4,20},{5,21},{6,22},{7,23},{8,24},{9,... | collective-permute-start | bytes 49160 | tf_op jit(solution)/shard_map/ppermute | solution.py:377
  53.2 9.5 %collective-permute-start.8 = (f32[2,8,256]{2,1,0:T(8,128)S(1)}, f32[2,8,256]{2,1,0:T(8,128)S(1)}, u32[]{:S(2)}, u32[]{:S(2)}) collective-permute-start(f32[2,8,256]{2,1,0:T(8,128)S(1)} %late.1), channel_id=1, source_target_pairs={{0,112},{1,113},{2,114},{3,115},{4,116},{5,117},{6,118},{7,119},{8... | collective-permute-start | bytes 49160 | tf_op jit(solution)/shard_map/ppermute | solution.py:377
  59.6 19.2 %collective-permute-start.15 = (f32[2,512,128]{2,1,0:T(8,128)S(1)}, f32[2,512,128]{2,1,0:T(8,128)S(1)}, u32[]{:S(2)}, u32[]{:S(2)}) collective-permute-start(f32[2,512,128]{2,1,0:T(8,128)S(1)} %get-tuple-element.80.p), channel_id=1, source_target_pairs={{0,1},{1,0},{2,3},{3,2},{4,5},{5,4},{6,7},{7,6},{8,9},{9,8},{10,11... | collective-permute-start | bytes 1572872 | tf_op jit(solution)/shard_map/ppermute | solution.py:407
  60.7 18.3 %collective-permute-start.14 = (f32[1024,128]{1,0:T(8,128)S(1)}, f32[1024,128]{1,0:T(8,128)S(1)}, u32[]{:S(2)}, u32[]{:S(2)}) collective-permute-start(f32[1024,128]{1,0:T(8,128)S(1)} %get-tuple-element.78.part_p), channel_id=1, source_target_pairs={{1,2},{3,4},{5,6},{7,8},{9,10},{11,12},{13,14},{15,16},{17,18},{19... | collective-permute-start | bytes 1572872 | tf_op jit(solution)/shard_map/ppermute | solution.py:410
  62.7 4.5 %collective-permute-start.9 = (f32[2,8,256]{2,1,0:T(8,128)S(1)}, f32[2,8,256]{2,1,0:T(8,128)S(1)}, u32[]{:S(2)}, u32[]{:S(2)}) collective-permute-start(f32[2,8,256]{2,1,0:T(8,128)S(1)} %fusion.2), channel_id=1, source_target_pairs={{0,48},{1,49},{2,50},{3,51},{4,52},{5,53},{6,54},{7,55},{8,56},{9,... | collective-permute-start | bytes 49160 | tf_op jit(solution)/shard_map/ppermute | solution.py:381
  64.4 5.8 %collective-permute-start.10 = (f32[2,8,256]{2,1,0:T(8,128)S(1)}, f32[2,8,256]{2,1,0:T(8,128)S(1)}, u32[]{:S(2)}, u32[]{:S(2)}) collective-permute-start(f32[2,8,256]{2,1,0:T(8,128)S(1)} %get-tuple-element.96), channel_id=1, source_target_pairs={{0,80},{1,81},{2,82},{3,83},{4,84},{5,85},{6,86},{7,87},{8,88},{9,... | collective-permute-start | bytes 49160 | tf_op jit(solution)/shard_map/ppermute | solution.py:382
  70.2 7.5 %collective-permute-start.11 = (f32[2,8,256]{2,1,0:T(8,128)S(1)}, f32[2,8,256]{2,1,0:T(8,128)S(1)}, u32[]{:S(2)}, u32[]{:S(2)}) collective-permute-start(f32[2,8,256]{2,1,0:T(8,128)S(1)} %add_add_fusion.2), channel_id=1, source_target_pairs={{0,2},{1,3},{2,0},{3,1},{4,6},{5,7},{6,4},{7,5},{8,10},{9,11},{10,... | collective-permute-start | bytes 49160 | tf_op jit(solution)/shard_map/ppermute | solution.py:364
  70.2 7.5 %collective-permute-start.12 = (f32[2,8,256]{2,1,0:T(8,128)S(1)}, f32[2,8,256]{2,1,0:T(8,128)S(1)}, u32[]{:S(2)}, u32[]{:S(2)}) collective-permute-start(f32[2,8,256]{2,1,0:T(8,128)S(1)} %add_add_fusion.2), channel_id=1, source_target_pairs={{0,6},{1,7},{2,4},{3,5},{4,2},{5,3},{6,0},{7,1},{8,14},{9,15},{10,... | collective-permute-start | bytes 49160 | tf_op jit(solution)/shard_map/ppermute | solution.py:364
  74.7 4.1 %collective-permute-start.13 = (f32[2,8,256]{2,1,0:T(8,128)S(1)}, f32[2,8,256]{2,1,0:T(8,128)S(1)}, u32[]{:S(2)}, u32[]{:S(2)}) collective-permute-start(f32[2,8,256]{2,1,0:T(8,128)S(1)} %add_add_fusion.2), channel_id=1, source_target_pairs={{0,4},{1,5},{2,6},{3,7},{4,0},{5,1},{6,2},{7,3},{8,12},{9,13},{10,... | collective-permute-start | bytes 49160 | tf_op jit(solution)/shard_map/ppermute | solution.py:364
  79.1 7.0 %collective-permute-start.16 = (f32[2,8,256]{2,1,0:T(8,128)S(1)}, f32[2,8,256]{2,1,0:T(8,128)S(1)}, u32[]{:S(2)}, u32[]{:S(2)}) collective-permute-start(f32[2,8,256]{2,1,0:T(8,128)S(1)} %add_add_fusion.1), channel_id=1, source_target_pairs={{0,1},{1,0},{2,3},{3,2},{4,5},{5,4},{6,7},{7,6},{8,9},{9,8},{10,11... | collective-permute-start | bytes 49160 | tf_op jit(solution)/shard_map/ppermute | solution.py:364
  81.4 4.6 %collective-permute-start.17 = (f32[2,8,256]{2,1,0:T(8,128)S(1)}, f32[2,8,256]{2,1,0:T(8,128)S(1)}, u32[]{:S(2)}, u32[]{:S(2)}) collective-permute-start(f32[2,8,256]{2,1,0:T(8,128)S(1)} %add_add_fusion.1), channel_id=1, source_target_pairs={{0,8},{1,9},{2,10},{3,11},{4,12},{5,13},{6,14},{7,15},{8,0},{9,1},... | collective-permute-start | bytes 49160 | tf_op jit(solution)/shard_map/ppermute | solution.py:364
  82.7 5.1 %collective-permute-start.18 = (f32[2,8,256]{2,1,0:T(8,128)S(1)}, f32[2,8,256]{2,1,0:T(8,128)S(1)}, u32[]{:S(2)}, u32[]{:S(2)}) collective-permute-start(f32[2,8,256]{2,1,0:T(8,128)S(1)} %add_add_fusion.1), channel_id=1, source_target_pairs={{0,9},{1,8},{2,11},{3,10},{4,13},{5,12},{6,15},{7,14},{8,1},{9,0},... | collective-permute-start | bytes 49160 | tf_op jit(solution)/shard_map/ppermute | solution.py:364

commit v8 on v7

--- a/solution.py
+++ b/solution.py
@@ -263,13 +263,22 @@
     local_part(step, at_ref, source_ref, wavelet_ref, p, po, q, qo, c_ref, cs_ref, ck_ref, pre_p, pre_q)
 
 
-def early_kernel(step, at_ref, source_ref, wavelet_ref, p, po, q, qo, c_ref, cs_ref, ck_ref, cells_ref, pre_p, pre_q, out_ref):
-    local_part(step, at_ref, source_ref, wavelet_ref, p, po, q, qo, c_ref, cs_ref, ck_ref, pre_p, pre_q)
+def early_kernel(at_ref, source_ref, wavelet_ref, p, po, q, qo, c_ref, cs_ref, ck_ref, cells_ref, pre_p, pre_q, out_ref):
+    local_part(1, at_ref, source_ref, wavelet_ref, p, po, q, qo, c_ref, cs_ref, ck_ref, pre_p, pre_q)
     out_ref[...] = jnp.zeros(out_ref.shape, jnp.float32)
     for s in range(2):
         block, x_at, pick_z, pick_y = picks(cells_ref, s)
-        for n, field in ((0, cs_ref), (1, po), (2, p), (7, ck_ref)):
+        for n, field in ((0, cs_ref), (1, p), (7, ck_ref)):
             out_ref[s, pl.ds(n, 1), :] = own_sample(samples(field, s, pick_z, pick_y), block, x_at, at_ref[0])
+
+
+def middle_kernel(at_ref, source_ref, wavelet_ref, p, po, q, qo, c_ref, cs_ref, ck_ref, cells_ref, early_ref,
+                  pre_p, pre_q, out_ref):
+    local_part(2, at_ref, source_ref, wavelet_ref, p, po, q, qo, c_ref, cs_ref, ck_ref, pre_p, pre_q)
+    out_ref[...] = early_ref[...]
+    for s in range(2):
+        block, x_at, pick_z, pick_y = picks(cells_ref, s)
+        out_ref[s, pl.ds(2, 1), :] = own_sample(samples(p, s, pick_z, pick_y), block, x_at, at_ref[0])
 
 
 def weights(apart):
@@ -428,11 +437,14 @@
         got = coming
         pair = on_chip(p)
         now = (at, source_cells, wavelet, p, po, q, qo, c, cs, ck)
-        if step == 2:
+        if step == 1:
             pre_p, pre_q, early = call(
-                functools.partial(early_kernel, step), (*now, receiver_cells), (field, field, traced), 10**6, "local_early")
+                early_kernel, (*now, receiver_cells), (field, field, traced), 2*10**10, "local1")
+        elif step == 2:
+            pre_p, pre_q, early = call(
+                middle_kernel, (*now, receiver_cells, early), (field, field, traced), 10**6, "local2")
         else:
-            pre_p, pre_q = call(functools.partial(local_kernel, step), now, (field, field), 10**6, f"local{step}")
+            pre_p, pre_q = call(functools.partial(local_kernel, step), now, (field, field), 10**6, "local3")
         if step == 3:
             total, = call(late_kernel, (at, source_cells, wavelet, receiver_cells, early, p, q), (traced,), 10**8, "late")
         part_p, part_q = call(

time: 88.7 us -> 86.9 us (0.980)
  waiting for transfers between devices: 23.1 us -> 15.9 us
  starting transfers between devices: 44.8 us -> 49.8 us
    ppermute x4, waiting for transfers between devices: 14.5 us -> 7.31 us  [off_chip(): return lax.ppermute(values, 'space', odd_pairs(blocks))]
    ppermute x4, starting transfers between devices: 10.2 us -> 13.6 us  [off_chip(): return lax.ppermute(values, 'space', odd_pairs(blocks))]
    ppermute x2, starting transfers between devices: 16.8 us -> 19.6 us  [reduced(): first, second = (lax.ppermute(total, 'space', pairs) for pairs in todo[2])]
  transfers between devices with their start and end apart: 19 -> 19, of which waited for: 7 -> 5; matrix products, arithmetic and copies ran while one was open for 0% -> 0% of each run, Pallas kernels for 15% -> 15%
where the time goes in v8:
time: 86.9 us; the launch traced here: 86.6 us
  starting transfers between devices  49.8 us (57%)
  Pallas kernels  18 us (21%)
  waiting for transfers between devices  15.9 us (18%)
  local copies, waits for them, and re-layouts  1.35 us (2%)
  between operations  0.95 us (1%)
    ppermute x2, starting transfers between devices, reduced(): first, second = (lax.ppermute(total, 'space', pairs) for pairs in todo[2])  19.6 us
    pallas_call x15, Pallas kernels, call(): pl.pallas_call(kernel, out_shape=tuple(outs), in_specs=specs, out_specs=t...  18 us
    ppermute x4, starting transfers between devices, off_chip(): return lax.ppermute(values, 'space', odd_pairs(blocks))  13.6 us
    ppermute x6, starting transfers between devices, summed(): lax.ppermute(total, 'space', pairs)  10.6 us
    ppermute x4, waiting for transfers between devices, off_chip(): return lax.ppermute(values, 'space', odd_pairs(blocks))  7.31 us
    ppermute x6, waiting for transfers between devices, summed(): lax.ppermute(total, 'space', pairs)  3.02 us
    ppermute x1, waiting for transfers between devices, reduced(): plus = lax.ppermute(even_part, 'space', todo[3][0])  2.86 us
    ppermute x1, waiting for transfers between devices, reduced(): minus = lax.ppermute(odd_part, 'space', todo[3][1])  2.66 us
  transfers between devices with their start and end apart: 19, of which 5 were waited for; matrix products, arithmetic and copies ran while one was open for 0% of the time, Pallas kernels for 15%

profile of v8, /device:TPU:1, one launch (start us, length us, event | category | flops | bytes accessed | tf_op | source)
XLA Modules:
  0.0 86.6 jit_solution(9271208020443305205)
XLA Ops:
  0.6 1.4 %begin.1 = (f32[3,256,128]{2,1,0:T(8,128)S(1)}, f32[2,512,128]{2,1,0:T(8,128)S(1)}, s32[8,128]{1,0:T(8,128)S(1)}, f32[16,128]{1,0:T(8,128)S(1)}, s32[2,8,256]{2,1,0:T(8,128)S(1)}) custom-call(s32[1]{0:T(128)} %bitcast.at_far.at_ref, s32[1]{0:T(128)} %bitcast.1.side_far.side_ref, s32[2]{0:T(128)} %bitcast.16, s32[2]{0:T(128)} %source_ref.9, ...), custom_call_target="tpu_custom_call" | custom-call | flops 1000000 | bytes 1863704 | tf_op jit(solution)/shard_map/begin/pallas_call | solution.py:32
  2.0 2.1 %collective-permute-start.1 = (f32[3,256,128]{2,1,0:T(8,128)S(1)}, f32[3,256,128]{2,1,0:T(8,128)S(1)}, u32[]{:S(2)}, u32[]{:S(2)}) collective-permute-start(f32[3,256,128]{2,1,0:T(8,128)S(1)} %get-tuple-element.52.own), channel_id=1, source_target_pairs={{0,128},{128,0},{1,129},{129,1},{2,130},{130,2},{3,131},{131,3},{4... | collective-permute-start | bytes 1179656 | tf_op jit(solution)/shard_map/ppermute | solution.py:421
  4.1 1.3 %collective-permute-start = (f32[2,512,128]{2,1,0:T(8,128)S(1)}, f32[2,512,128]{2,1,0:T(8,128)S(1)}, u32[]{:S(2)}, u32[]{:S(2)}) collective-permute-start(f32[2,512,128]{2,1,0:T(8,128)S(1)} %get-tuple-element.50.p0.po.before), channel_id=1, source_target_pairs={{0,1},{1,0},{2,3},{3,2},{4,5},{5,4},{6,7},{7,6},{8,9},{9,8},{10,11... | collective-permute-start | bytes 1572872 | tf_op jit(solution)/shard_map/ppermute | solution.py:416
  5.4 2.7 %collective-permute-start.3 = (f32[2,512,128]{2,1,0:T(8,128)S(1)}, f32[2,512,128]{2,1,0:T(8,128)S(1)}, u32[]{:S(2)}, u32[]{:S(2)}) collective-permute-start(f32[2,512,128]{2,1,0:T(8,128)S(1)} %get-tuple-element.50.p0.po.before), channel_id=1, source_target_pairs={{1,2},{3,4},{5,6},{7,8},{9,10},{11,12},{13,14},{15,16},{17,18},{19... | collective-permute-start | bytes 1572872 | tf_op jit(solution)/shard_map/ppermute | solution.py:419
  8.2 0.6 copy-done
  8.9 3.3 %ready.1 = (f32[2,512,128]{2,1,0:T(8,128)S(1)}, f32[2,512,128]{2,1,0:T(8,128)S(1)}, f32[2,512,128]{2,1,0:T(8,128)S(1)}, f32[2,512,128]{2,1,0:T(8,128)S(1)}, f32[2,512,128]{2,1,0:T(8,128)S(1)}) custom-call(s32[1]{0:T(128)} %bitcast.at_far.at_ref, s32[2]{0:T(128)S(1)} %bitcast.17, s32[2]{0:T(128)S(1)} %copy-done.1, f32[2,4]{1,0:T(2,128)S(1)} %copy-done, ...), custom_call_target="tpu_custom_call" | custom-call | flops 100000000 | bytes 4718644 | tf_op jit(solution)/shard_map/ready/pallas_call | solution.py:32
  12.2 0.3 first.1
  12.8 5.4 %collective-permute-start.2 = (f32[1552,128]{1,0:T(8,128)S(1)}, f32[1552,128]{1,0:T(8,128)S(1)}, u32[]{:S(2)}, u32[]{:S(2)}) collective-permute-start(f32[1552,128]{1,0:T(8,128)S(1)} %get-tuple-element.62.part_p), channel_id=1, source_target_pairs={{1,2},{3,4},{5,6},{7,8},{9,10},{11,12},{13,14},{15,16},{17,18},{19... | collective-permute-start | bytes 2383880 | tf_op jit(solution)/shard_map/ppermute | solution.py:419
  18.5 0.7 copy-done.2
  19.1 3.2 %local1.1 = (f32[2,512,128]{2,1,0:T(8,128)S(1)}, f32[2,512,128]{2,1,0:T(8,128)S(1)}, f32[2,8,256]{2,1,0:T(8,128)S(1)}) custom-call(s32[1]{0:T(128)} %bitcast.at_far.at_ref, s32[2]{0:T(128)S(1)} %copy-done.1, f32[2,4]{1,0:T(2,128)S(1)} %copy-done, f32[2,512,128]{2,1,0:T(8,128)S(1)} %get-tuple-element.64.p.po.before, ...), custom_call_target="tpu_custom_call" | custom-call | flops 20000000000 | bytes 4737068 | tf_op jit(solution)/shard_map/local1/pallas_call | solution.py:32
  22.6 3.6 %collective-permute-start.5 = (f32[1024,128]{1,0:T(8,128)S(1)}, f32[1024,128]{1,0:T(8,128)S(1)}, u32[]{:S(2)}, u32[]{:S(2)}) collective-permute-start(f32[1024,128]{1,0:T(8,128)S(1)} %get-tuple-element.70.part_p), channel_id=1, source_target_pairs={{1,2},{3,4},{5,6},{7,8},{9,10},{11,12},{13,14},{15,16},{17,18},{19... | collective-permute-start | bytes 1572872 | tf_op jit(solution)/shard_map/ppermute | solution.py:419
  26.2 1.7 %collective-permute-done.2.got.extra = f32[1552,128]{1,0:T(8,128)S(1)} collective-permute-done((f32[1552,128]{1,0:T(8,128)S(1)}, f32[1552,128]{1,0:T(8,128)S(1)}, u32[]{:S(2)}, u32[]{:S(2)}) %collective-permute-start.2) | collective-permute-done | bytes 794656 | tf_op jit(solution)/shard_map/ppermute | solution.py:419
  27.9 5.6 %collective-permute-done.5.got = f32[1024,128]{1,0:T(8,128)S(1)} collective-permute-done((f32[1024,128]{1,0:T(8,128)S(1)}, f32[1024,128]{1,0:T(8,128)S(1)}, u32[]{:S(2)}, u32[]{:S(2)}) %collective-permute-start.5) | collective-permute-done | bytes 524320 | tf_op jit(solution)/shard_map/ppermute | solution.py:419
  33.5 0.4 join1.1
  34.0 2.4 %local2.1 = (f32[2,512,128]{2,1,0:T(8,128)S(1)}, f32[2,512,128]{2,1,0:T(8,128)S(1)}, f32[2,8,256]{2,1,0:T(8,128)S(1)}) custom-call(s32[1]{0:T(128)} %bitcast.at_far.at_ref, s32[2]{0:T(128)S(1)} %copy-done.1, f32[2,4]{1,0:T(2,128)S(1)} %copy-done, f32[2,512,128]{2,1,0:T(8,128)S(1)} %get-tuple-element.73.p.po.before, ...), custom_call_target="tpu_custom_call" | custom-call | flops 1000000 | bytes 4753452 | tf_op jit(solution)/shard_map/local2/pallas_call | solution.py:32
  36.6 0.4 join2.1
  37.1 2.1 %late.1 = f32[2,8,256]{2,1,0:T(8,128)S(1)} custom-call(s32[1]{0:T(128)} %bitcast.at_far.at_ref, s32[2]{0:T(128)S(1)} %copy-done.1, f32[2,4]{1,0:T(2,128)S(1)} %copy-done, s32[2,256]{1,0:T(2,128)S(1)} %copy-done.2, f32[2,8,256]{2,1,0:T(8,128)S(1)} %get-tuple-element.76.early_ref, f32[2,512,128]{2,1,0:T(8,128)S(1)} %get-tuple-element.82.p, ...), custom_call_target="tpu_custom_call" | custom-call | flops 100000000 | bytes 1083436 | tf_op jit(solution)/shard_map/late/pallas_call | solution.py:32
  39.2 8.4 %collective-permute-start.7 = (f32[2,8,256]{2,1,0:T(8,128)S(1)}, f32[2,8,256]{2,1,0:T(8,128)S(1)}, u32[]{:S(2)}, u32[]{:S(2)}) collective-permute-start(f32[2,8,256]{2,1,0:T(8,128)S(1)} %late.1), channel_id=1, source_target_pairs={{0,16},{1,17},{2,18},{3,19},{4,20},{5,21},{6,22},{7,23},{8,24},{9,... | collective-permute-start | bytes 49160 | tf_op jit(solution)/shard_map/ppermute | solution.py:386
  47.6 11.2 %collective-permute-start.8 = (f32[2,8,256]{2,1,0:T(8,128)S(1)}, f32[2,8,256]{2,1,0:T(8,128)S(1)}, u32[]{:S(2)}, u32[]{:S(2)}) collective-permute-start(f32[2,8,256]{2,1,0:T(8,128)S(1)} %late.1), channel_id=1, source_target_pairs={{0,112},{1,113},{2,114},{3,115},{4,116},{5,117},{6,118},{7,119},{8... | collective-permute-start | bytes 49160 | tf_op jit(solution)/shard_map/ppermute | solution.py:386
  58.8 0.6 collective-permute-start.15
  59.4 1.9 %collective-permute-start.14 = (f32[1024,128]{1,0:T(8,128)S(1)}, f32[1024,128]{1,0:T(8,128)S(1)}, u32[]{:S(2)}, u32[]{:S(2)}) collective-permute-start(f32[1024,128]{1,0:T(8,128)S(1)} %get-tuple-element.80.part_p), channel_id=1, source_target_pairs={{1,2},{3,4},{5,6},{7,8},{9,10},{11,12},{13,14},{15,16},{17,18},{19... | collective-permute-start | bytes 1572872 | tf_op jit(solution)/shard_map/ppermute | solution.py:419
  61.4 1.7 %collective-permute-start.9 = (f32[2,8,256]{2,1,0:T(8,128)S(1)}, f32[2,8,256]{2,1,0:T(8,128)S(1)}, u32[]{:S(2)}, u32[]{:S(2)}) collective-permute-start(f32[2,8,256]{2,1,0:T(8,128)S(1)} %fusion.2), channel_id=1, source_target_pairs={{0,48},{1,49},{2,50},{3,51},{4,52},{5,53},{6,54},{7,55},{8,56},{9,... | collective-permute-start | bytes 49160 | tf_op jit(solution)/shard_map/ppermute | solution.py:390
  63.2 2.9 %collective-permute-done.9 = f32[2,8,256]{2,1,0:T(8,128)S(1)} collective-permute-done((f32[2,8,256]{2,1,0:T(8,128)S(1)}, f32[2,8,256]{2,1,0:T(8,128)S(1)}, u32[]{:S(2)}, u32[]{:S(2)}) %collective-permute-start.9) | collective-permute-done | bytes 16416 | tf_op jit(solution)/shard_map/ppermute | solution.py:390
  66.1 2.7 %collective-permute-done.10 = f32[2,8,256]{2,1,0:T(8,128)S(1)} collective-permute-done((f32[2,8,256]{2,1,0:T(8,128)S(1)}, f32[2,8,256]{2,1,0:T(8,128)S(1)}, u32[]{:S(2)}, u32[]{:S(2)}) %collective-permute-start.10) | collective-permute-done | bytes 16416 | tf_op jit(solution)/shard_map/ppermute | solution.py:391
  68.8 3.1 %collective-permute-start.13 = (f32[2,8,256]{2,1,0:T(8,128)S(1)}, f32[2,8,256]{2,1,0:T(8,128)S(1)}, u32[]{:S(2)}, u32[]{:S(2)}) collective-permute-start(f32[2,8,256]{2,1,0:T(8,128)S(1)} %add_add_fusion.2), channel_id=1, source_target_pairs={{0,4},{1,5},{2,6},{3,7},{4,0},{5,1},{6,2},{7,3},{8,12},{9,13},{10,... | collective-permute-start | bytes 49160 | tf_op jit(solution)/shard_map/ppermute | solution.py:373
  72.0 1.9 %local3.1 = (f32[2,512,128]{2,1,0:T(8,128)S(1)}, f32[2,512,128]{2,1,0:T(8,128)S(1)}) custom-call(s32[1]{0:T(128)} %bitcast.at_far.at_ref, s32[2]{0:T(128)S(1)} %copy-done.1, f32[2,4]{1,0:T(2,128)S(1)} %copy-done, f32[2,512,128]{2,1,0:T(8,128)S(1)} %get-tuple-element.82.p, f32[2,512,128]{2,1,0:T(8,128)S(1)} %get-tuple-element.73.p.po.before, ...), custom_call_target="tpu_custom_call" | custom-call | flops 1000000 | bytes 4718636 | tf_op jit(solution)/shard_map/local3/pallas_call | solution.py:32
  74.2 4.2 %collective-permute-start.16 = (f32[2,8,256]{2,1,0:T(8,128)S(1)}, f32[2,8,256]{2,1,0:T(8,128)S(1)}, u32[]{:S(2)}, u32[]{:S(2)}) collective-permute-start(f32[2,8,256]{2,1,0:T(8,128)S(1)} %add_add_fusion.1), channel_id=1, source_target_pairs={{0,1},{1,0},{2,3},{3,2},{4,5},{5,4},{6,7},{7,6},{8,9},{9,8},{10,11... | collective-permute-start | bytes 49160 | tf_op jit(solution)/shard_map/ppermute | solution.py:373
  78.3 2.5 %collective-permute-start.17 = (f32[2,8,256]{2,1,0:T(8,128)S(1)}, f32[2,8,256]{2,1,0:T(8,128)S(1)}, u32[]{:S(2)}, u32[]{:S(2)}) collective-permute-start(f32[2,8,256]{2,1,0:T(8,128)S(1)} %add_add_fusion.1), channel_id=1, source_target_pairs={{0,8},{1,9},{2,10},{3,11},{4,12},{5,13},{6,14},{7,15},{8,0},{9,1},... | collective-permute-start | bytes 49160 | tf_op jit(solution)/shard_map/ppermute | solution.py:373
  80.8 0.7 collective-permute-start.18
  81.6 1.4 %join3.1 = (f32[2,512,128]{2,1,0:T(8,128)}, f32[2,512,128]{2,1,0:T(8,128)}) custom-call(s32[8,128]{1,0:T(8,128)S(1)} %get-tuple-element.49.odd_ref, f32[1024,128]{1,0:T(8,128)S(1)} %collective-permute-done.14.got, f32[1552,128]{1,0:T(8,128)S(1)} %collective-permute-done.2.got.extra, f32[2,512,128]{2,1,0:T(8,128)S(1)} %get-tuple-element.73.p.po.before, ...), custom_call_target="tpu_custom_call" | custom-call | flops 20000000000 | bytes 4993024 | tf_op jit(solution)/shard_map/join3/pallas_call | solution.py:32
  83.0 3.0 %collective-permute-done.18 = f32[2,8,256]{2,1,0:T(8,128)S(1)} collective-permute-done((f32[2,8,256]{2,1,0:T(8,128)S(1)}, f32[2,8,256]{2,1,0:T(8,128)S(1)}, u32[]{:S(2)}, u32[]{:S(2)}) %collective-permute-start.18) | collective-permute-done | bytes 16416 | tf_op jit(solution)/shard_map/ppermute | solution.py:373
  86.0 0.6 pad_maximum_fusion
  (37 shorter events, 1.6 us)
Async XLA Ops:
  0.6 7.6 %copy-start.3 = (s32[2,1]{0,1:T(1,128)S(1)}, s32[2,1]{0,1:T(1,128)}, u32[]{:S(2)}) copy-start(s32[2,1]{0,1:T(1,128)} %param.18) | copy-start | bytes 28
  2.0 10.2 %collective-permute-start.1 = (f32[3,256,128]{2,1,0:T(8,128)S(1)}, f32[3,256,128]{2,1,0:T(8,128)S(1)}, u32[]{:S(2)}, u32[]{:S(2)}) collective-permute-start(f32[3,256,128]{2,1,0:T(8,128)S(1)} %get-tuple-element.52.own), channel_id=1, source_target_pairs={{0,128},{128,0},{1,129},{129,1},{2,130},{130,2},{3,131},{131,3},{4... | collective-permute-start | bytes 1179656 | tf_op jit(solution)/shard_map/ppermute | solution.py:421
  4.1 8.4 %collective-permute-start = (f32[2,512,128]{2,1,0:T(8,128)S(1)}, f32[2,512,128]{2,1,0:T(8,128)S(1)}, u32[]{:S(2)}, u32[]{:S(2)}) collective-permute-start(f32[2,512,128]{2,1,0:T(8,128)S(1)} %get-tuple-element.50.p0.po.before), channel_id=1, source_target_pairs={{0,1},{1,0},{2,3},{3,2},{4,5},{5,4},{6,7},{7,6},{8,9},{9,8},{10,11... | collective-permute-start | bytes 1572872 | tf_op jit(solution)/shard_map/ppermute | solution.py:416
  5.4 12.7 %collective-permute-start.3 = (f32[2,512,128]{2,1,0:T(8,128)S(1)}, f32[2,512,128]{2,1,0:T(8,128)S(1)}, u32[]{:S(2)}, u32[]{:S(2)}) collective-permute-start(f32[2,512,128]{2,1,0:T(8,128)S(1)} %get-tuple-element.50.p0.po.before), channel_id=1, source_target_pairs={{1,2},{3,4},{5,6},{7,8},{9,10},{11,12},{13,14},{15,16},{17,18},{19... | collective-permute-start | bytes 1572872 | tf_op jit(solution)/shard_map/ppermute | solution.py:419
  8.2 0.7 copy-start
  8.2 0.7 copy-start.1
  12.8 15.1 %collective-permute-start.2 = (f32[1552,128]{1,0:T(8,128)S(1)}, f32[1552,128]{1,0:T(8,128)S(1)}, u32[]{:S(2)}, u32[]{:S(2)}) collective-permute-start(f32[1552,128]{1,0:T(8,128)S(1)} %get-tuple-element.62.part_p), channel_id=1, source_target_pairs={{1,2},{3,4},{5,6},{7,8},{9,10},{11,12},{13,14},{15,16},{17,18},{19... | collective-permute-start | bytes 2383880 | tf_op jit(solution)/shard_map/ppermute | solution.py:419
  18.3 4.0 %collective-permute-start.4 = (f32[2,512,128]{2,1,0:T(8,128)S(1)}, f32[2,512,128]{2,1,0:T(8,128)S(1)}, u32[]{:S(2)}, u32[]{:S(2)}) collective-permute-start(f32[2,512,128]{2,1,0:T(8,128)S(1)} %get-tuple-element.64.p.po.before), channel_id=1, source_target_pairs={{0,1},{1,0},{2,3},{3,2},{4,5},{5,4},{6,7},{7,6},{8,9},{9,8},{10,11... | collective-permute-start | bytes 1572872 | tf_op jit(solution)/shard_map/ppermute | solution.py:416
  18.4 0.7 copy-start.2
  22.6 10.9 %collective-permute-start.5 = (f32[1024,128]{1,0:T(8,128)S(1)}, f32[1024,128]{1,0:T(8,128)S(1)}, u32[]{:S(2)}, u32[]{:S(2)}) collective-permute-start(f32[1024,128]{1,0:T(8,128)S(1)} %get-tuple-element.70.part_p), channel_id=1, source_target_pairs={{1,2},{3,4},{5,6},{7,8},{9,10},{11,12},{13,14},{15,16},{17,18},{19... | collective-permute-start | bytes 1572872 | tf_op jit(solution)/shard_map/ppermute | solution.py:419
  33.9 2.5 %collective-permute-start.6 = (f32[2,512,128]{2,1,0:T(8,128)S(1)}, f32[2,512,128]{2,1,0:T(8,128)S(1)}, u32[]{:S(2)}, u32[]{:S(2)}) collective-permute-start(f32[2,512,128]{2,1,0:T(8,128)S(1)} %get-tuple-element.73.p.po.before), channel_id=1, source_target_pairs={{0,1},{1,0},{2,3},{3,2},{4,5},{5,4},{6,7},{7,6},{8,9},{9,8},{10,11... | collective-permute-start | bytes 1572872 | tf_op jit(solution)/shard_map/ppermute | solution.py:416
  39.2 22.1 %collective-permute-start.7 = (f32[2,8,256]{2,1,0:T(8,128)S(1)}, f32[2,8,256]{2,1,0:T(8,128)S(1)}, u32[]{:S(2)}, u32[]{:S(2)}) collective-permute-start(f32[2,8,256]{2,1,0:T(8,128)S(1)} %late.1), channel_id=1, source_target_pairs={{0,16},{1,17},{2,18},{3,19},{4,20},{5,21},{6,22},{7,23},{8,24},{9,... | collective-permute-start | bytes 49160 | tf_op jit(solution)/shard_map/ppermute | solution.py:386
  47.6 13.7 %collective-permute-start.8 = (f32[2,8,256]{2,1,0:T(8,128)S(1)}, f32[2,8,256]{2,1,0:T(8,128)S(1)}, u32[]{:S(2)}, u32[]{:S(2)}) collective-permute-start(f32[2,8,256]{2,1,0:T(8,128)S(1)} %late.1), channel_id=1, source_target_pairs={{0,112},{1,113},{2,114},{3,115},{4,116},{5,117},{6,118},{7,119},{8... | collective-permute-start | bytes 49160 | tf_op jit(solution)/shard_map/ppermute | solution.py:386
  58.8 15.1 %collective-permute-start.15 = (f32[2,512,128]{2,1,0:T(8,128)S(1)}, f32[2,512,128]{2,1,0:T(8,128)S(1)}, u32[]{:S(2)}, u32[]{:S(2)}) collective-permute-start(f32[2,512,128]{2,1,0:T(8,128)S(1)} %get-tuple-element.82.p), channel_id=1, source_target_pairs={{0,1},{1,0},{2,3},{3,2},{4,5},{5,4},{6,7},{7,6},{8,9},{9,8},{10,11... | collective-permute-start | bytes 1572872 | tf_op jit(solution)/shard_map/ppermute | solution.py:416
  59.4 14.8 %collective-permute-start.14 = (f32[1024,128]{1,0:T(8,128)S(1)}, f32[1024,128]{1,0:T(8,128)S(1)}, u32[]{:S(2)}, u32[]{:S(2)}) collective-permute-start(f32[1024,128]{1,0:T(8,128)S(1)} %get-tuple-element.80.part_p), channel_id=1, source_target_pairs={{1,2},{3,4},{5,6},{7,8},{9,10},{11,12},{13,14},{15,16},{17,18},{19... | collective-permute-start | bytes 1572872 | tf_op jit(solution)/shard_map/ppermute | solution.py:419
  61.4 4.7 %collective-permute-start.9 = (f32[2,8,256]{2,1,0:T(8,128)S(1)}, f32[2,8,256]{2,1,0:T(8,128)S(1)}, u32[]{:S(2)}, u32[]{:S(2)}) collective-permute-start(f32[2,8,256]{2,1,0:T(8,128)S(1)} %fusion.2), channel_id=1, source_target_pairs={{0,48},{1,49},{2,50},{3,51},{4,52},{5,53},{6,54},{7,55},{8,56},{9,... | collective-permute-start | bytes 49160 | tf_op jit(solution)/shard_map/ppermute | solution.py:390
  63.1 5.6 %collective-permute-start.10 = (f32[2,8,256]{2,1,0:T(8,128)S(1)}, f32[2,8,256]{2,1,0:T(8,128)S(1)}, u32[]{:S(2)}, u32[]{:S(2)}) collective-permute-start(f32[2,8,256]{2,1,0:T(8,128)S(1)} %get-tuple-element.98), channel_id=1, source_target_pairs={{0,80},{1,81},{2,82},{3,83},{4,84},{5,85},{6,86},{7,87},{8,88},{9,... | collective-permute-start | bytes 49160 | tf_op jit(solution)/shard_map/ppermute | solution.py:391
  68.7 5.1 %collective-permute-start.11 = (f32[2,8,256]{2,1,0:T(8,128)S(1)}, f32[2,8,256]{2,1,0:T(8,128)S(1)}, u32[]{:S(2)}, u32[]{:S(2)}) collective-permute-start(f32[2,8,256]{2,1,0:T(8,128)S(1)} %add_add_fusion.2), channel_id=1, source_target_pairs={{0,2},{1,3},{2,0},{3,1},{4,6},{5,7},{6,4},{7,5},{8,10},{9,11},{10,... | collective-permute-start | bytes 49160 | tf_op jit(solution)/shard_map/ppermute | solution.py:373
  68.7 5.1 %collective-permute-start.12 = (f32[2,8,256]{2,1,0:T(8,128)S(1)}, f32[2,8,256]{2,1,0:T(8,128)S(1)}, u32[]{:S(2)}, u32[]{:S(2)}) collective-permute-start(f32[2,8,256]{2,1,0:T(8,128)S(1)} %add_add_fusion.2), channel_id=1, source_target_pairs={{0,6},{1,7},{2,4},{3,5},{4,2},{5,3},{6,0},{7,1},{8,14},{9,15},{10,... | collective-permute-start | bytes 49160 | tf_op jit(solution)/shard_map/ppermute | solution.py:373
  68.8 5.1 %collective-permute-start.13 = (f32[2,8,256]{2,1,0:T(8,128)S(1)}, f32[2,8,256]{2,1,0:T(8,128)S(1)}, u32[]{:S(2)}, u32[]{:S(2)}) collective-permute-start(f32[2,8,256]{2,1,0:T(8,128)S(1)} %add_add_fusion.2), channel_id=1, source_target_pairs={{0,4},{1,5},{2,6},{3,7},{4,0},{5,1},{6,2},{7,3},{8,12},{9,13},{10,... | collective-permute-start | bytes 49160 | tf_op jit(solution)/shard_map/ppermute | solution.py:373
  74.2 8.8 %collective-permute-start.16 = (f32[2,8,256]{2,1,0:T(8,128)S(1)}, f32[2,8,256]{2,1,0:T(8,128)S(1)}, u32[]{:S(2)}, u32[]{:S(2)}) collective-permute-start(f32[2,8,256]{2,1,0:T(8,128)S(1)} %add_add_fusion.1), channel_id=1, source_target_pairs={{0,1},{1,0},{2,3},{3,2},{4,5},{5,4},{6,7},{7,6},{8,9},{9,8},{10,11... | collective-permute-start | bytes 49160 | tf_op jit(solution)/shard_map/ppermute | solution.py:373
  78.3 4.6 %collective-permute-start.17 = (f32[2,8,256]{2,1,0:T(8,128)S(1)}, f32[2,8,256]{2,1,0:T(8,128)S(1)}, u32[]{:S(2)}, u32[]{:S(2)}) collective-permute-start(f32[2,8,256]{2,1,0:T(8,128)S(1)} %add_add_fusion.1), channel_id=1, source_target_pairs={{0,8},{1,9},{2,10},{3,11},{4,12},{5,13},{6,14},{7,15},{8,0},{9,1},... | collective-permute-start | bytes 49160 | tf_op jit(solution)/shard_map/ppermute | solution.py:373
  80.8 5.1 %collective-permute-start.18 = (f32[2,8,256]{2,1,0:T(8,128)S(1)}, f32[2,8,256]{2,1,0:T(8,128)S(1)}, u32[]{:S(2)}, u32[]{:S(2)}) collective-permute-start(f32[2,8,256]{2,1,0:T(8,128)S(1)} %add_add_fusion.1), channel_id=1, source_target_pairs={{0,9},{1,8},{2,11},{3,10},{4,13},{5,12},{6,15},{7,14},{8,1},{9,0},... | collective-permute-start | bytes 49160 | tf_op jit(solution)/shard_map/ppermute | solution.py:373

commit v9 on v8

--- a/solution.py
+++ b/solution.py
@@ -263,8 +263,7 @@
     local_part(step, at_ref, source_ref, wavelet_ref, p, po, q, qo, c_ref, cs_ref, ck_ref, pre_p, pre_q)
 
 
-def early_kernel(at_ref, source_ref, wavelet_ref, p, po, q, qo, c_ref, cs_ref, ck_ref, cells_ref, pre_p, pre_q, out_ref):
-    local_part(1, at_ref, source_ref, wavelet_ref, p, po, q, qo, c_ref, cs_ref, ck_ref, pre_p, pre_q)
+def early_kernel(at_ref, cells_ref, p, cs_ref, ck_ref, out_ref):
     out_ref[...] = jnp.zeros(out_ref.shape, jnp.float32)
     for s in range(2):
         block, x_at, pick_z, pick_y = picks(cells_ref, s)
@@ -438,8 +437,8 @@
         pair = on_chip(p)
         now = (at, source_cells, wavelet, p, po, q, qo, c, cs, ck)
         if step == 1:
-            pre_p, pre_q, early = call(
-                early_kernel, (*now, receiver_cells), (field, field, traced), 2*10**10, "local1")
+            pre_p, pre_q = call(functools.partial(local_kernel, step), now, (field, field), 2 * 10**10, "local1")
+            early, = call(early_kernel, (at, receiver_cells, p, cs, ck), (traced,), 10**6, "early")
         elif step == 2:
             pre_p, pre_q, early = call(
                 middle_kernel, (*now, receiver_cells, early), (field, field, traced), 10**6, "local2")
@@ -453,7 +452,7 @@
             break
         coming = off_chip(part_p)
         if step == 1:
-            got, coming = lax.optimization_barrier((got, coming))
+            got, coming, early = lax.optimization_barrier((got, coming, early))
             extra = got
         before, po, qo = po, p, q
         p, q = call(

time: 86.9 us -> 85.3 us (0.982)
  waiting for transfers between devices: 15.9 us -> 14.8 us
    ppermute x2, starting transfers between devices: 19.6 us -> 17.6 us  [reduced(): first, second = (lax.ppermute(total, 'space', pairs) for pairs in todo[2])]
    ppermute x6, starting transfers between devices: 10.6 us -> 12.3 us  [summed(): lax.ppermute(total, 'space', pairs)]
    ppermute x6, waiting for transfers between devices: 3.02 us -> 1.39 us  [summed(): lax.ppermute(total, 'space', pairs)]
    pallas_call x15 -> x16, Pallas kernels: 18 us -> 18.1 us  [call(): pl.pallas_call(kernel, out_shape=tuple(outs), in_specs=specs, out_specs=t...]
  transfers between devices with their start and end apart: 19 -> 19, of which waited for: 5 -> 5; matrix products, arithmetic and copies ran while one was open for 0% -> 0% of each run, Pallas kernels for 15% -> 16%
where the time goes in v9:
time: 85.3 us; the launch traced here: 84.7 us
  starting transfers between devices  49.5 us (58%)
  Pallas kernels  18.1 us (21%)
  waiting for transfers between devices  14.8 us (17%)
  between operations  0.94 us (1%)
    pallas_call x16, Pallas kernels, call(): pl.pallas_call(kernel, out_shape=tuple(outs), in_specs=specs, out_specs=t...  18.1 us
    ppermute x2, starting transfers between devices, reduced(): first, second = (lax.ppermute(total, 'space', pairs) for pairs in todo[2])  17.6 us
    ppermute x4, starting transfers between devices, off_chip(): return lax.ppermute(values, 'space', odd_pairs(blocks))  13.6 us
    ppermute x6, starting transfers between devices, summed(): lax.ppermute(total, 'space', pairs)  12.3 us
    ppermute x4, waiting for transfers between devices, off_chip(): return lax.ppermute(values, 'space', odd_pairs(blocks))  7.84 us
    ppermute x1, waiting for transfers between devices, reduced(): minus = lax.ppermute(odd_part, 'space', todo[3][1])  2.86 us
    ppermute x1, waiting for transfers between devices, reduced(): plus = lax.ppermute(even_part, 'space', todo[3][0])  2.65 us
    ppermute x1, starting transfers between devices, per_device(): other = lax.ppermute(own, 'shot', [(0, 1), (1, 0)])  2.13 us
  transfers between devices with their start and end apart: 19, of which 5 were waited for; matrix products, arithmetic and copies ran while one was open for 0% of the time, Pallas kernels for 16%

profile of v9, /device:TPU:1, one launch (start us, length us, event | category | flops | bytes accessed | tf_op | source)
XLA Modules:
  0.0 84.7 jit_solution(1021279814694368992)
XLA Ops:
  0.6 1.4 %begin.1 = (f32[3,256,128]{2,1,0:T(8,128)S(1)}, f32[2,512,128]{2,1,0:T(8,128)S(1)}, s32[8,128]{1,0:T(8,128)S(1)}, f32[16,128]{1,0:T(8,128)S(1)}, s32[2,8,256]{2,1,0:T(8,128)S(1)}) custom-call(s32[1]{0:T(128)} %bitcast.at_far.at_ref, s32[1]{0:T(128)} %bitcast.1.side_far.side_ref, s32[2]{0:T(128)} %bitcast.16, s32[2]{0:T(128)} %source_ref.9, ...), custom_call_target="tpu_custom_call" | custom-call | flops 1000000 | bytes 1863704 | tf_op jit(solution)/shard_map/begin/pallas_call | solution.py:32
  2.0 2.1 %collective-permute-start.1 = (f32[3,256,128]{2,1,0:T(8,128)S(1)}, f32[3,256,128]{2,1,0:T(8,128)S(1)}, u32[]{:S(2)}, u32[]{:S(2)}) collective-permute-start(f32[3,256,128]{2,1,0:T(8,128)S(1)} %get-tuple-element.52.own), channel_id=1, source_target_pairs={{0,128},{128,0},{1,129},{129,1},{2,130},{130,2},{3,131},{131,3},{4... | collective-permute-start | bytes 1179656 | tf_op jit(solution)/shard_map/ppermute | solution.py:420
  4.1 1.3 %collective-permute-start = (f32[2,512,128]{2,1,0:T(8,128)S(1)}, f32[2,512,128]{2,1,0:T(8,128)S(1)}, u32[]{:S(2)}, u32[]{:S(2)}) collective-permute-start(f32[2,512,128]{2,1,0:T(8,128)S(1)} %get-tuple-element.50.p0.po.before), channel_id=1, source_target_pairs={{0,1},{1,0},{2,3},{3,2},{4,5},{5,4},{6,7},{7,6},{8,9},{9,8},{10,11... | collective-permute-start | bytes 1572872 | tf_op jit(solution)/shard_map/ppermute | solution.py:415
  5.4 2.7 %collective-permute-start.3 = (f32[2,512,128]{2,1,0:T(8,128)S(1)}, f32[2,512,128]{2,1,0:T(8,128)S(1)}, u32[]{:S(2)}, u32[]{:S(2)}) collective-permute-start(f32[2,512,128]{2,1,0:T(8,128)S(1)} %get-tuple-element.50.p0.po.before), channel_id=1, source_target_pairs={{1,2},{3,4},{5,6},{7,8},{9,10},{11,12},{13,14},{15,16},{17,18},{19... | collective-permute-start | bytes 1572872 | tf_op jit(solution)/shard_map/ppermute | solution.py:418
  8.2 0.6 copy-done.1
  8.9 3.3 %ready.1 = (f32[2,512,128]{2,1,0:T(8,128)S(1)}, f32[2,512,128]{2,1,0:T(8,128)S(1)}, f32[2,512,128]{2,1,0:T(8,128)S(1)}, f32[2,512,128]{2,1,0:T(8,128)S(1)}, f32[2,512,128]{2,1,0:T(8,128)S(1)}) custom-call(s32[1]{0:T(128)} %bitcast.at_far.at_ref, s32[2]{0:T(128)S(1)} %bitcast.17, s32[2]{0:T(128)S(1)} %copy-done.2, f32[2,4]{1,0:T(2,128)S(1)} %copy-done.1, ...), custom_call_target="tpu_custom_call" | custom-call | flops 100000000 | bytes 4718644 | tf_op jit(solution)/shard_map/ready/pallas_call | solution.py:32
  12.2 0.3 first.1
  12.8 5.4 %collective-permute-start.2 = (f32[1552,128]{1,0:T(8,128)S(1)}, f32[1552,128]{1,0:T(8,128)S(1)}, u32[]{:S(2)}, u32[]{:S(2)}) collective-permute-start(f32[1552,128]{1,0:T(8,128)S(1)} %get-tuple-element.62.part_p), channel_id=1, source_target_pairs={{1,2},{3,4},{5,6},{7,8},{9,10},{11,12},{13,14},{15,16},{17,18},{19... | collective-permute-start | bytes 2383880 | tf_op jit(solution)/shard_map/ppermute | solution.py:418
  18.5 1.9 %local1.1 = (f32[2,512,128]{2,1,0:T(8,128)S(1)}, f32[2,512,128]{2,1,0:T(8,128)S(1)}) custom-call(s32[1]{0:T(128)} %bitcast.at_far.at_ref, s32[2]{0:T(128)S(1)} %copy-done.2, f32[2,4]{1,0:T(2,128)S(1)} %copy-done.1, f32[2,512,128]{2,1,0:T(8,128)S(1)} %get-tuple-element.64.p.po.before, f32[2,512,128]{2,1,0:T(8,128)S(1)} %get-tuple-element.50.p0.po.before, ...), custom_call_target="tpu_custom_call" | custom-call | flops 20000000000 | bytes 4718636 | tf_op jit(solution)/shard_map/local1/pallas_call | solution.py:32
  20.6 3.6 %collective-permute-start.5 = (f32[1024,128]{1,0:T(8,128)S(1)}, f32[1024,128]{1,0:T(8,128)S(1)}, u32[]{:S(2)}, u32[]{:S(2)}) collective-permute-start(f32[1024,128]{1,0:T(8,128)S(1)} %get-tuple-element.70.part_p), channel_id=1, source_target_pairs={{1,2},{3,4},{5,6},{7,8},{9,10},{11,12},{13,14},{15,16},{17,18},{19... | collective-permute-start | bytes 1572872 | tf_op jit(solution)/shard_map/ppermute | solution.py:418
  24.2 1.4 %early.1.early_ref = f32[2,8,256]{2,1,0:T(8,128)S(1)} custom-call(s32[1]{0:T(128)} %bitcast.at_far.at_ref, s32[2,256]{1,0:T(2,128)S(1)} %copy-done, f32[2,512,128]{2,1,0:T(8,128)S(1)} %get-tuple-element.64.p.po.before, f32[2,512,128]{2,1,0:T(8,128)S(1)} %get-tuple-element.59.cs_ref, f32[2,512,128]{2,1,0:T(8,128)S(1)} %get-tuple-element.60.ck_ref), custom_call_target="tpu_custom_call" | custom-call | flops 1000000 | bytes 1591300 | tf_op jit(solution)/shard_map/early/pallas_call | solution.py:32
  25.6 2.2 %collective-permute-done.2.got.extra = f32[1552,128]{1,0:T(8,128)S(1)} collective-permute-done((f32[1552,128]{1,0:T(8,128)S(1)}, f32[1552,128]{1,0:T(8,128)S(1)}, u32[]{:S(2)}, u32[]{:S(2)}) %collective-permute-start.2) | collective-permute-done | bytes 794656 | tf_op jit(solution)/shard_map/ppermute | solution.py:418
  27.9 5.6 %collective-permute-done.5.got = f32[1024,128]{1,0:T(8,128)S(1)} collective-permute-done((f32[1024,128]{1,0:T(8,128)S(1)}, f32[1024,128]{1,0:T(8,128)S(1)}, u32[]{:S(2)}, u32[]{:S(2)}) %collective-permute-start.5) | collective-permute-done | bytes 524320 | tf_op jit(solution)/shard_map/ppermute | solution.py:418
  33.5 0.4 join1.1
  34.0 2.4 %local2.1 = (f32[2,512,128]{2,1,0:T(8,128)S(1)}, f32[2,512,128]{2,1,0:T(8,128)S(1)}, f32[2,8,256]{2,1,0:T(8,128)S(1)}) custom-call(s32[1]{0:T(128)} %bitcast.at_far.at_ref, s32[2]{0:T(128)S(1)} %copy-done.2, f32[2,4]{1,0:T(2,128)S(1)} %copy-done.1, f32[2,512,128]{2,1,0:T(8,128)S(1)} %get-tuple-element.73.p.po.before, ...), custom_call_target="tpu_custom_call" | custom-call | flops 1000000 | bytes 4753452 | tf_op jit(solution)/shard_map/local2/pallas_call | solution.py:32
  36.7 0.4 join2.1
  37.1 2.1 %late.1 = f32[2,8,256]{2,1,0:T(8,128)S(1)} custom-call(s32[1]{0:T(128)} %bitcast.at_far.at_ref, s32[2]{0:T(128)S(1)} %copy-done.2, f32[2,4]{1,0:T(2,128)S(1)} %copy-done.1, s32[2,256]{1,0:T(2,128)S(1)} %copy-done, f32[2,8,256]{2,1,0:T(8,128)S(1)} %get-tuple-element.76.early_ref, f32[2,512,128]{2,1,0:T(8,128)S(1)} %get-tuple-element.82.p, ...), custom_call_target="tpu_custom_call" | custom-call | flops 100000000 | bytes 1083436 | tf_op jit(solution)/shard_map/late/pallas_call | solution.py:32
  39.3 8.3 %collective-permute-start.7 = (f32[2,8,256]{2,1,0:T(8,128)S(1)}, f32[2,8,256]{2,1,0:T(8,128)S(1)}, u32[]{:S(2)}, u32[]{:S(2)}) collective-permute-start(f32[2,8,256]{2,1,0:T(8,128)S(1)} %late.1), channel_id=1, source_target_pairs={{0,16},{1,17},{2,18},{3,19},{4,20},{5,21},{6,22},{7,23},{8,24},{9,... | collective-permute-start | bytes 49160 | tf_op jit(solution)/shard_map/ppermute | solution.py:385
  47.6 9.3 %collective-permute-start.8 = (f32[2,8,256]{2,1,0:T(8,128)S(1)}, f32[2,8,256]{2,1,0:T(8,128)S(1)}, u32[]{:S(2)}, u32[]{:S(2)}) collective-permute-start(f32[2,8,256]{2,1,0:T(8,128)S(1)} %late.1), channel_id=1, source_target_pairs={{0,112},{1,113},{2,114},{3,115},{4,116},{5,117},{6,118},{7,119},{8... | collective-permute-start | bytes 49160 | tf_op jit(solution)/shard_map/ppermute | solution.py:385
  56.9 0.6 collective-permute-start.15
  57.5 1.9 %collective-permute-start.14 = (f32[1024,128]{1,0:T(8,128)S(1)}, f32[1024,128]{1,0:T(8,128)S(1)}, u32[]{:S(2)}, u32[]{:S(2)}) collective-permute-start(f32[1024,128]{1,0:T(8,128)S(1)} %get-tuple-element.80.part_p), channel_id=1, source_target_pairs={{1,2},{3,4},{5,6},{7,8},{9,10},{11,12},{13,14},{15,16},{17,18},{19... | collective-permute-start | bytes 1572872 | tf_op jit(solution)/shard_map/ppermute | solution.py:418
  59.4 1.7 %collective-permute-start.9 = (f32[2,8,256]{2,1,0:T(8,128)S(1)}, f32[2,8,256]{2,1,0:T(8,128)S(1)}, u32[]{:S(2)}, u32[]{:S(2)}) collective-permute-start(f32[2,8,256]{2,1,0:T(8,128)S(1)} %fusion.2), channel_id=1, source_target_pairs={{0,48},{1,49},{2,50},{3,51},{4,52},{5,53},{6,54},{7,55},{8,56},{9,... | collective-permute-start | bytes 49160 | tf_op jit(solution)/shard_map/ppermute | solution.py:389
  61.2 2.7 %collective-permute-done.9 = f32[2,8,256]{2,1,0:T(8,128)S(1)} collective-permute-done((f32[2,8,256]{2,1,0:T(8,128)S(1)}, f32[2,8,256]{2,1,0:T(8,128)S(1)}, u32[]{:S(2)}, u32[]{:S(2)}) %collective-permute-start.9) | collective-permute-done | bytes 16416 | tf_op jit(solution)/shard_map/ppermute | solution.py:389
  63.9 2.9 %collective-permute-done.10 = f32[2,8,256]{2,1,0:T(8,128)S(1)} collective-permute-done((f32[2,8,256]{2,1,0:T(8,128)S(1)}, f32[2,8,256]{2,1,0:T(8,128)S(1)}, u32[]{:S(2)}, u32[]{:S(2)}) %collective-permute-start.10) | collective-permute-done | bytes 16416 | tf_op jit(solution)/shard_map/ppermute | solution.py:390
  66.9 3.1 %collective-permute-start.13 = (f32[2,8,256]{2,1,0:T(8,128)S(1)}, f32[2,8,256]{2,1,0:T(8,128)S(1)}, u32[]{:S(2)}, u32[]{:S(2)}) collective-permute-start(f32[2,8,256]{2,1,0:T(8,128)S(1)} %add_add_fusion.2), channel_id=1, source_target_pairs={{0,4},{1,5},{2,6},{3,7},{4,0},{5,1},{6,2},{7,3},{8,12},{9,13},{10,... | collective-permute-start | bytes 49160 | tf_op jit(solution)/shard_map/ppermute | solution.py:372
  70.0 1.9 %local3.1 = (f32[2,512,128]{2,1,0:T(8,128)S(1)}, f32[2,512,128]{2,1,0:T(8,128)S(1)}) custom-call(s32[1]{0:T(128)} %bitcast.at_far.at_ref, s32[2]{0:T(128)S(1)} %copy-done.2, f32[2,4]{1,0:T(2,128)S(1)} %copy-done.1, f32[2,512,128]{2,1,0:T(8,128)S(1)} %get-tuple-element.82.p, f32[2,512,128]{2,1,0:T(8,128)S(1)} %get-tuple-element.73.p.po.before, ...), custom_call_target="tpu_custom_call" | custom-call | flops 1000000 | bytes 4718636 | tf_op jit(solution)/shard_map/local3/pallas_call | solution.py:32
  72.2 5.8 %collective-permute-start.16 = (f32[2,8,256]{2,1,0:T(8,128)S(1)}, f32[2,8,256]{2,1,0:T(8,128)S(1)}, u32[]{:S(2)}, u32[]{:S(2)}) collective-permute-start(f32[2,8,256]{2,1,0:T(8,128)S(1)} %add_add_fusion.1), channel_id=1, source_target_pairs={{0,1},{1,0},{2,3},{3,2},{4,5},{5,4},{6,7},{7,6},{8,9},{9,8},{10,11... | collective-permute-start | bytes 49160 | tf_op jit(solution)/shard_map/ppermute | solution.py:372
  78.0 0.9 %collective-permute-start.17 = (f32[2,8,256]{2,1,0:T(8,128)S(1)}, f32[2,8,256]{2,1,0:T(8,128)S(1)}, u32[]{:S(2)}, u32[]{:S(2)}) collective-permute-start(f32[2,8,256]{2,1,0:T(8,128)S(1)} %add_add_fusion.1), channel_id=1, source_target_pairs={{0,8},{1,9},{2,10},{3,11},{4,12},{5,13},{6,14},{7,15},{8,0},{9,1},... | collective-permute-start | bytes 49160 | tf_op jit(solution)/shard_map/ppermute | solution.py:372
  78.9 2.4 %collective-permute-start.18 = (f32[2,8,256]{2,1,0:T(8,128)S(1)}, f32[2,8,256]{2,1,0:T(8,128)S(1)}, u32[]{:S(2)}, u32[]{:S(2)}) collective-permute-start(f32[2,8,256]{2,1,0:T(8,128)S(1)} %add_add_fusion.1), channel_id=1, source_target_pairs={{0,9},{1,8},{2,11},{3,10},{4,13},{5,12},{6,15},{7,14},{8,1},{9,0},... | collective-permute-start | bytes 49160 | tf_op jit(solution)/shard_map/ppermute | solution.py:372
  81.2 1.4 %join3.1 = (f32[2,512,128]{2,1,0:T(8,128)}, f32[2,512,128]{2,1,0:T(8,128)}) custom-call(s32[8,128]{1,0:T(8,128)S(1)} %get-tuple-element.49.odd_ref, f32[1024,128]{1,0:T(8,128)S(1)} %collective-permute-done.14.got, f32[1552,128]{1,0:T(8,128)S(1)} %collective-permute-done.2.got.extra, f32[2,512,128]{2,1,0:T(8,128)S(1)} %get-tuple-element.73.p.po.before, ...), custom_call_target="tpu_custom_call" | custom-call | flops 20000000000 | bytes 4993024 | tf_op jit(solution)/shard_map/join3/pallas_call | solution.py:32
  82.6 1.4 %collective-permute-done.18 = f32[2,8,256]{2,1,0:T(8,128)S(1)} collective-permute-done((f32[2,8,256]{2,1,0:T(8,128)S(1)}, f32[2,8,256]{2,1,0:T(8,128)S(1)}, u32[]{:S(2)}, u32[]{:S(2)}) %collective-permute-start.18) | collective-permute-done | bytes 16416 | tf_op jit(solution)/shard_map/ppermute | solution.py:372
  84.0 0.6 pad_maximum_fusion
  (38 shorter events, 1.7 us)
Async XLA Ops:
  0.6 7.6 %copy-start.3 = (s32[2,1]{0,1:T(1,128)S(1)}, s32[2,1]{0,1:T(1,128)}, u32[]{:S(2)}) copy-start(s32[2,1]{0,1:T(1,128)} %param.18) | copy-start | bytes 28
  2.0 10.2 %collective-permute-start.1 = (f32[3,256,128]{2,1,0:T(8,128)S(1)}, f32[3,256,128]{2,1,0:T(8,128)S(1)}, u32[]{:S(2)}, u32[]{:S(2)}) collective-permute-start(f32[3,256,128]{2,1,0:T(8,128)S(1)} %get-tuple-element.52.own), channel_id=1, source_target_pairs={{0,128},{128,0},{1,129},{129,1},{2,130},{130,2},{3,131},{131,3},{4... | collective-permute-start | bytes 1179656 | tf_op jit(solution)/shard_map/ppermute | solution.py:420
  4.1 8.4 %collective-permute-start = (f32[2,512,128]{2,1,0:T(8,128)S(1)}, f32[2,512,128]{2,1,0:T(8,128)S(1)}, u32[]{:S(2)}, u32[]{:S(2)}) collective-permute-start(f32[2,512,128]{2,1,0:T(8,128)S(1)} %get-tuple-element.50.p0.po.before), channel_id=1, source_target_pairs={{0,1},{1,0},{2,3},{3,2},{4,5},{5,4},{6,7},{7,6},{8,9},{9,8},{10,11... | collective-permute-start | bytes 1572872 | tf_op jit(solution)/shard_map/ppermute | solution.py:415
  5.4 12.7 %collective-permute-start.3 = (f32[2,512,128]{2,1,0:T(8,128)S(1)}, f32[2,512,128]{2,1,0:T(8,128)S(1)}, u32[]{:S(2)}, u32[]{:S(2)}) collective-permute-start(f32[2,512,128]{2,1,0:T(8,128)S(1)} %get-tuple-element.50.p0.po.before), channel_id=1, source_target_pairs={{1,2},{3,4},{5,6},{7,8},{9,10},{11,12},{13,14},{15,16},{17,18},{19... | collective-permute-start | bytes 1572872 | tf_op jit(solution)/shard_map/ppermute | solution.py:418
  8.2 0.7 copy-start.1
  8.2 0.7 copy-start.2
  12.8 15.1 %collective-permute-start.2 = (f32[1552,128]{1,0:T(8,128)S(1)}, f32[1552,128]{1,0:T(8,128)S(1)}, u32[]{:S(2)}, u32[]{:S(2)}) collective-permute-start(f32[1552,128]{1,0:T(8,128)S(1)} %get-tuple-element.62.part_p), channel_id=1, source_target_pairs={{1,2},{3,4},{5,6},{7,8},{9,10},{11,12},{13,14},{15,16},{17,18},{19... | collective-permute-start | bytes 2383880 | tf_op jit(solution)/shard_map/ppermute | solution.py:418
  18.4 2.0 %collective-permute-start.4 = (f32[2,512,128]{2,1,0:T(8,128)S(1)}, f32[2,512,128]{2,1,0:T(8,128)S(1)}, u32[]{:S(2)}, u32[]{:S(2)}) collective-permute-start(f32[2,512,128]{2,1,0:T(8,128)S(1)} %get-tuple-element.64.p.po.before), channel_id=1, source_target_pairs={{0,1},{1,0},{2,3},{3,2},{4,5},{5,4},{6,7},{7,6},{8,9},{9,8},{10,11... | collective-permute-start | bytes 1572872 | tf_op jit(solution)/shard_map/ppermute | solution.py:415
  20.4 3.8 %copy-start = (s32[2,256]{1,0:T(2,128)S(1)}, s32[2,256]{1,0:T(2,128)}, u32[]{:S(2)}) copy-start(s32[2,256]{1,0:T(2,128)} %cells_ref.5) | copy-start | bytes 6148
  20.6 12.9 %collective-permute-start.5 = (f32[1024,128]{1,0:T(8,128)S(1)}, f32[1024,128]{1,0:T(8,128)S(1)}, u32[]{:S(2)}, u32[]{:S(2)}) collective-permute-start(f32[1024,128]{1,0:T(8,128)S(1)} %get-tuple-element.70.part_p), channel_id=1, source_target_pairs={{1,2},{3,4},{5,6},{7,8},{9,10},{11,12},{13,14},{15,16},{17,18},{19... | collective-permute-start | bytes 1572872 | tf_op jit(solution)/shard_map/ppermute | solution.py:418
  33.9 2.5 %collective-permute-start.6 = (f32[2,512,128]{2,1,0:T(8,128)S(1)}, f32[2,512,128]{2,1,0:T(8,128)S(1)}, u32[]{:S(2)}, u32[]{:S(2)}) collective-permute-start(f32[2,512,128]{2,1,0:T(8,128)S(1)} %get-tuple-element.73.p.po.before), channel_id=1, source_target_pairs={{0,1},{1,0},{2,3},{3,2},{4,5},{5,4},{6,7},{7,6},{8,9},{9,8},{10,11... | collective-permute-start | bytes 1572872 | tf_op jit(solution)/shard_map/ppermute | solution.py:415
  39.3 20.1 %collective-permute-start.7 = (f32[2,8,256]{2,1,0:T(8,128)S(1)}, f32[2,8,256]{2,1,0:T(8,128)S(1)}, u32[]{:S(2)}, u32[]{:S(2)}) collective-permute-start(f32[2,8,256]{2,1,0:T(8,128)S(1)} %late.1), channel_id=1, source_target_pairs={{0,16},{1,17},{2,18},{3,19},{4,20},{5,21},{6,22},{7,23},{8,24},{9,... | collective-permute-start | bytes 49160 | tf_op jit(solution)/shard_map/ppermute | solution.py:385
  47.6 11.8 %collective-permute-start.8 = (f32[2,8,256]{2,1,0:T(8,128)S(1)}, f32[2,8,256]{2,1,0:T(8,128)S(1)}, u32[]{:S(2)}, u32[]{:S(2)}) collective-permute-start(f32[2,8,256]{2,1,0:T(8,128)S(1)} %late.1), channel_id=1, source_target_pairs={{0,112},{1,113},{2,114},{3,115},{4,116},{5,117},{6,118},{7,119},{8... | collective-permute-start | bytes 49160 | tf_op jit(solution)/shard_map/ppermute | solution.py:385
  56.9 15.1 %collective-permute-start.15 = (f32[2,512,128]{2,1,0:T(8,128)S(1)}, f32[2,512,128]{2,1,0:T(8,128)S(1)}, u32[]{:S(2)}, u32[]{:S(2)}) collective-permute-start(f32[2,512,128]{2,1,0:T(8,128)S(1)} %get-tuple-element.82.p), channel_id=1, source_target_pairs={{0,1},{1,0},{2,3},{3,2},{4,5},{5,4},{6,7},{7,6},{8,9},{9,8},{10,11... | collective-permute-start | bytes 1572872 | tf_op jit(solution)/shard_map/ppermute | solution.py:415
  57.5 14.7 %collective-permute-start.14 = (f32[1024,128]{1,0:T(8,128)S(1)}, f32[1024,128]{1,0:T(8,128)S(1)}, u32[]{:S(2)}, u32[]{:S(2)}) collective-permute-start(f32[1024,128]{1,0:T(8,128)S(1)} %get-tuple-element.80.part_p), channel_id=1, source_target_pairs={{1,2},{3,4},{5,6},{7,8},{9,10},{11,12},{13,14},{15,16},{17,18},{19... | collective-permute-start | bytes 1572872 | tf_op jit(solution)/shard_map/ppermute | solution.py:418
  59.4 4.5 %collective-permute-start.9 = (f32[2,8,256]{2,1,0:T(8,128)S(1)}, f32[2,8,256]{2,1,0:T(8,128)S(1)}, u32[]{:S(2)}, u32[]{:S(2)}) collective-permute-start(f32[2,8,256]{2,1,0:T(8,128)S(1)} %fusion.2), channel_id=1, source_target_pairs={{0,48},{1,49},{2,50},{3,51},{4,52},{5,53},{6,54},{7,55},{8,56},{9,... | collective-permute-start | bytes 49160 | tf_op jit(solution)/shard_map/ppermute | solution.py:389
  61.1 5.6 %collective-permute-start.10 = (f32[2,8,256]{2,1,0:T(8,128)S(1)}, f32[2,8,256]{2,1,0:T(8,128)S(1)}, u32[]{:S(2)}, u32[]{:S(2)}) collective-permute-start(f32[2,8,256]{2,1,0:T(8,128)S(1)} %get-tuple-element.98), channel_id=1, source_target_pairs={{0,80},{1,81},{2,82},{3,83},{4,84},{5,85},{6,86},{7,87},{8,88},{9,... | collective-permute-start | bytes 49160 | tf_op jit(solution)/shard_map/ppermute | solution.py:390
  66.8 5.1 %collective-permute-start.11 = (f32[2,8,256]{2,1,0:T(8,128)S(1)}, f32[2,8,256]{2,1,0:T(8,128)S(1)}, u32[]{:S(2)}, u32[]{:S(2)}) collective-permute-start(f32[2,8,256]{2,1,0:T(8,128)S(1)} %add_add_fusion.2), channel_id=1, source_target_pairs={{0,2},{1,3},{2,0},{3,1},{4,6},{5,7},{6,4},{7,5},{8,10},{9,11},{10,... | collective-permute-start | bytes 49160 | tf_op jit(solution)/shard_map/ppermute | solution.py:372
  66.8 5.1 %collective-permute-start.12 = (f32[2,8,256]{2,1,0:T(8,128)S(1)}, f32[2,8,256]{2,1,0:T(8,128)S(1)}, u32[]{:S(2)}, u32[]{:S(2)}) collective-permute-start(f32[2,8,256]{2,1,0:T(8,128)S(1)} %add_add_fusion.2), channel_id=1, source_target_pairs={{0,6},{1,7},{2,4},{3,5},{4,2},{5,3},{6,0},{7,1},{8,14},{9,15},{10,... | collective-permute-start | bytes 49160 | tf_op jit(solution)/shard_map/ppermute | solution.py:372
  66.9 5.0 %collective-permute-start.13 = (f32[2,8,256]{2,1,0:T(8,128)S(1)}, f32[2,8,256]{2,1,0:T(8,128)S(1)}, u32[]{:S(2)}, u32[]{:S(2)}) collective-permute-start(f32[2,8,256]{2,1,0:T(8,128)S(1)} %add_add_fusion.2), channel_id=1, source_target_pairs={{0,4},{1,5},{2,6},{3,7},{4,0},{5,1},{6,2},{7,3},{8,12},{9,13},{10,... | collective-permute-start | bytes 49160 | tf_op jit(solution)/shard_map/ppermute | solution.py:372
  72.2 10.4 %collective-permute-start.16 = (f32[2,8,256]{2,1,0:T(8,128)S(1)}, f32[2,8,256]{2,1,0:T(8,128)S(1)}, u32[]{:S(2)}, u32[]{:S(2)}) collective-permute-start(f32[2,8,256]{2,1,0:T(8,128)S(1)} %add_add_fusion.1), channel_id=1, source_target_pairs={{0,1},{1,0},{2,3},{3,2},{4,5},{5,4},{6,7},{7,6},{8,9},{9,8},{10,11... | collective-permute-start | bytes 49160 | tf_op jit(solution)/shard_map/ppermute | solution.py:372
  78.0 4.6 %collective-permute-start.17 = (f32[2,8,256]{2,1,0:T(8,128)S(1)}, f32[2,8,256]{2,1,0:T(8,128)S(1)}, u32[]{:S(2)}, u32[]{:S(2)}) collective-permute-start(f32[2,8,256]{2,1,0:T(8,128)S(1)} %add_add_fusion.1), channel_id=1, source_target_pairs={{0,8},{1,9},{2,10},{3,11},{4,12},{5,13},{6,14},{7,15},{8,0},{9,1},... | collective-permute-start | bytes 49160 | tf_op jit(solution)/shard_map/ppermute | solution.py:372
  78.9 5.1 %collective-permute-start.18 = (f32[2,8,256]{2,1,0:T(8,128)S(1)}, f32[2,8,256]{2,1,0:T(8,128)S(1)}, u32[]{:S(2)}, u32[]{:S(2)}) collective-permute-start(f32[2,8,256]{2,1,0:T(8,128)S(1)} %add_add_fusion.1), channel_id=1, source_target_pairs={{0,9},{1,8},{2,11},{3,10},{4,13},{5,12},{6,15},{7,14},{8,1},{9,0},... | collective-permute-start | bytes 49160 | tf_op jit(solution)/shard_map/ppermute | solution.py:372

commit v10 on v9

--- a/solution.py
+++ b/solution.py
@@ -83,12 +83,15 @@
     return out
 
 
-def second_diffs(s, x, p, q, mat):
+def vertical(s, q, mat):
+    return jnp.dot(q[s], mat, precision=EXACT, preferred_element_type=jnp.float32)
+
+
+def horizontal(s, x, p, mat):
     hor = jnp.dot(mat, p[s, row(x), :], precision=EXACT, preferred_element_type=jnp.float32)
     for other in range(CX):
         hor = hor + taps[abs(other - x)] * p[s, row(other), :]
-    ver = jnp.dot(q[s, row(x), :], mat, precision=EXACT, preferred_element_type=jnp.float32)
-    return hor, ver
+    return hor
 
 
 def add_source(s, step, at_ref, source_ref, wavelet_ref, *refs):
@@ -117,8 +120,9 @@
         q[s] = q[s] * live
         base_p[s] = 2.0 * p0[s] - base_p[s] * live
         base_q[s] = 2.0 * q[s] - base_q[s] * live
+        ver_ref[s] = vertical(s, q, mat)
         for x in range(CX):
-            hor_ref[s, row(x), :], ver_ref[s, row(x), :] = second_diffs(s, x, p0, q, mat)
+            hor_ref[s, row(x), :] = horizontal(s, x, p0, mat)
         add_source(s, 0, at_ref, source_ref, wavelet_ref, base_p, base_q)
 
 
@@ -173,9 +177,10 @@
 def local_part(step, at_ref, source_ref, wavelet_ref, p, po, q, qo, c_ref, cs_ref, ck_ref, pre_p, pre_q):
     mat = band()
     for s in range(2):
+        all_ver = vertical(s, q, mat)
         for x in range(CX):
             here = row(x)
-            hor, ver = second_diffs(s, x, p, q, mat)
+            hor, ver = horizontal(s, x, p, mat), all_ver[x * CY:(x + 1) * CY]
             pre_p[s, here, :] = 2.0 * p[s, here, :] - po[s, here, :] + (cs_ref[s, here, :] * hor + ck_ref[s, here, :] * ver)
             pre_q[s, here, :] = 2.0 * q[s, here, :] - qo[s, here, :] + (ck_ref[s, here, :] * hor + c_ref[s, here, :] * ver)
         add_source(s, step, at_ref, source_ref, wavelet_ref, pre_p, pre_q)
@@ -230,15 +235,19 @@
     join(odd_ref, other_rows, part_p, part_q, cs_ref, ck_ref, p, q)
 
 
+def spread_rows(field, s, pick_z):
+    rest, spread = field[s], None
+    for _ in range(3):
+        part = rest.astype(jnp.bfloat16)
+        rest = rest - part.astype(jnp.float32)
+        picked = jnp.dot(part, pick_z, preferred_element_type=jnp.float32)
+        spread = picked if spread is None else spread + picked
+    return [spread[x * CY:(x + 1) * CY] for x in range(CX)]
+
+
 def samples(field, s, pick_z, pick_y):
     out = []
-    for x in range(CX):
-        rest, spread = field[s, row(x), :], None
-        for _ in range(3):
-            part = rest.astype(jnp.bfloat16)
-            rest = rest - part.astype(jnp.float32)
-            picked = jnp.dot(part, pick_z, preferred_element_type=jnp.float32)
-            spread = picked if spread is None else spread + picked
+    for spread in spread_rows(field, s, pick_z):
         out.append(jnp.sum(jnp.where(pick_y, spread, 0.0), axis=0, keepdims=True))
     return out
 
@@ -298,17 +307,11 @@
         band_y = weights(jnp.abs(lax.broadcasted_iota(jnp.int32, (CY, n), 0) - (cells // CZ) % CY))
         here = jnp.zeros(block.shape, jnp.float32)
         hor, ver, across = here, here, here
-        for x in range(CX):
-            rest, spread = p[s, row(x), :], None
-            for _ in range(3):
-                part = rest.astype(jnp.bfloat16)
-                rest = rest - part.astype(jnp.float32)
-                picked = jnp.dot(part, pick_z, preferred_element_type=jnp.float32)
-                spread = picked if spread is None else spread + picked
+        all_z = jnp.dot(q[s], band_z, precision=EXACT, preferred_element_type=jnp.float32)
+        for x, spread in enumerate(spread_rows(p, s, pick_z)):
             value = jnp.sum(jnp.where(pick_y, spread, 0.0), axis=0, keepdims=True)
             along_y = jnp.sum(band_y * spread, axis=0, keepdims=True)
-            along_z = jnp.dot(q[s, row(x), :], band_z, precision=EXACT, preferred_element_type=jnp.float32)
-            along_z = jnp.sum(jnp.where(pick_y, along_z, 0.0), axis=0, keepdims=True)
+            along_z = jnp.sum(jnp.where(pick_y, all_z[x * CY:(x + 1) * CY], 0.0), axis=0, keepdims=True)
             here = jnp.where(x_at == x, value, here)
             hor = hor + weights(jnp.abs(x_at - x)) * value + jnp.where(x_at == x, along_y, 0.0)
             ver = jnp.where(x_at == x, along_z, ver)

time: 85.3 us -> 85.5 us (level)
  no operation moved by 1% of the time
where the time goes in v10:
time: 85.5 us; the launch traced here: 84.8 us
  starting transfers between devices  49.5 us (58%)
  Pallas kernels  18.4 us (22%)
  waiting for transfers between devices  14.6 us (17%)
  between operations  0.96 us (1%)
    pallas_call x16, Pallas kernels, call(): pl.pallas_call(kernel, out_shape=tuple(outs), in_specs=specs, out_specs=t...  18.4 us
    ppermute x2, starting transfers between devices, reduced(): first, second = (lax.ppermute(total, 'space', pairs) for pairs in todo[2])  17.5 us
    ppermute x4, starting transfers between devices, off_chip(): return lax.ppermute(values, 'space', odd_pairs(blocks))  13.6 us
    ppermute x6, starting transfers between devices, summed(): lax.ppermute(total, 'space', pairs)  12.2 us
    ppermute x4, waiting for transfers between devices, off_chip(): return lax.ppermute(values, 'space', odd_pairs(blocks))  7.74 us
    ppermute x1, waiting for transfers between devices, reduced(): minus = lax.ppermute(odd_part, 'space', todo[3][1])  2.85 us
    ppermute x1, waiting for transfers between devices, reduced(): plus = lax.ppermute(even_part, 'space', todo[3][0])  2.66 us
    ppermute x4, starting transfers between devices, on_chip(): return lax.ppermute(values, 'space', even_pairs(blocks))  2.25 us
  transfers between devices with their start and end apart: 19, of which 5 were waited for; matrix products, arithmetic and copies ran while one was open for 0% of the time, Pallas kernels for 16%

profile of v10, /device:TPU:1, one launch (start us, length us, event | category | flops | bytes accessed | tf_op | source)
XLA Modules:
  0.0 84.8 jit_solution(15900883725822197217)
XLA Ops:
  0.6 1.4 %begin.1 = (f32[3,256,128]{2,1,0:T(8,128)S(1)}, f32[2,512,128]{2,1,0:T(8,128)S(1)}, s32[8,128]{1,0:T(8,128)S(1)}, f32[16,128]{1,0:T(8,128)S(1)}, s32[2,8,256]{2,1,0:T(8,128)S(1)}) custom-call(s32[1]{0:T(128)} %bitcast.at_far.at_ref, s32[1]{0:T(128)} %bitcast.1.side_far.side_ref, s32[2]{0:T(128)} %bitcast.16, s32[2]{0:T(128)} %source_ref.9, ...), custom_call_target="tpu_custom_call" | custom-call | flops 1000000 | bytes 1863704 | tf_op jit(solution)/shard_map/begin/pallas_call | solution.py:32
  2.0 2.1 %collective-permute-start.1 = (f32[3,256,128]{2,1,0:T(8,128)S(1)}, f32[3,256,128]{2,1,0:T(8,128)S(1)}, u32[]{:S(2)}, u32[]{:S(2)}) collective-permute-start(f32[3,256,128]{2,1,0:T(8,128)S(1)} %get-tuple-element.52.own), channel_id=1, source_target_pairs={{0,128},{128,0},{1,129},{129,1},{2,130},{130,2},{3,131},{131,3},{4... | collective-permute-start | bytes 1179656 | tf_op jit(solution)/shard_map/ppermute | solution.py:423
  4.1 1.3 %collective-permute-start = (f32[2,512,128]{2,1,0:T(8,128)S(1)}, f32[2,512,128]{2,1,0:T(8,128)S(1)}, u32[]{:S(2)}, u32[]{:S(2)}) collective-permute-start(f32[2,512,128]{2,1,0:T(8,128)S(1)} %get-tuple-element.50.p0.po.before), channel_id=1, source_target_pairs={{0,1},{1,0},{2,3},{3,2},{4,5},{5,4},{6,7},{7,6},{8,9},{9,8},{10,11... | collective-permute-start | bytes 1572872 | tf_op jit(solution)/shard_map/ppermute | solution.py:418
  5.4 2.7 %collective-permute-start.3 = (f32[2,512,128]{2,1,0:T(8,128)S(1)}, f32[2,512,128]{2,1,0:T(8,128)S(1)}, u32[]{:S(2)}, u32[]{:S(2)}) collective-permute-start(f32[2,512,128]{2,1,0:T(8,128)S(1)} %get-tuple-element.50.p0.po.before), channel_id=1, source_target_pairs={{1,2},{3,4},{5,6},{7,8},{9,10},{11,12},{13,14},{15,16},{17,18},{19... | collective-permute-start | bytes 1572872 | tf_op jit(solution)/shard_map/ppermute | solution.py:421
  8.2 0.6 copy-done.1
  8.9 3.3 %ready.1 = (f32[2,512,128]{2,1,0:T(8,128)S(1)}, f32[2,512,128]{2,1,0:T(8,128)S(1)}, f32[2,512,128]{2,1,0:T(8,128)S(1)}, f32[2,512,128]{2,1,0:T(8,128)S(1)}, f32[2,512,128]{2,1,0:T(8,128)S(1)}) custom-call(s32[1]{0:T(128)} %bitcast.at_far.at_ref, s32[2]{0:T(128)S(1)} %bitcast.17, s32[2]{0:T(128)S(1)} %copy-done.2, f32[2,4]{1,0:T(2,128)S(1)} %copy-done.1, ...), custom_call_target="tpu_custom_call" | custom-call | flops 100000000 | bytes 4718644 | tf_op jit(solution)/shard_map/ready/pallas_call | solution.py:32
  12.1 0.3 first.1
  12.7 5.4 %collective-permute-start.2 = (f32[1552,128]{1,0:T(8,128)S(1)}, f32[1552,128]{1,0:T(8,128)S(1)}, u32[]{:S(2)}, u32[]{:S(2)}) collective-permute-start(f32[1552,128]{1,0:T(8,128)S(1)} %get-tuple-element.62.part_p), channel_id=1, source_target_pairs={{1,2},{3,4},{5,6},{7,8},{9,10},{11,12},{13,14},{15,16},{17,18},{19... | collective-permute-start | bytes 2383880 | tf_op jit(solution)/shard_map/ppermute | solution.py:421
  18.5 1.9 %local1.1 = (f32[2,512,128]{2,1,0:T(8,128)S(1)}, f32[2,512,128]{2,1,0:T(8,128)S(1)}) custom-call(s32[1]{0:T(128)} %bitcast.at_far.at_ref, s32[2]{0:T(128)S(1)} %copy-done.2, f32[2,4]{1,0:T(2,128)S(1)} %copy-done.1, f32[2,512,128]{2,1,0:T(8,128)S(1)} %get-tuple-element.64.p.po.before, f32[2,512,128]{2,1,0:T(8,128)S(1)} %get-tuple-element.50.p0.po.before, ...), custom_call_target="tpu_custom_call" | custom-call | flops 20000000000 | bytes 4718636 | tf_op jit(solution)/shard_map/local1/pallas_call | solution.py:32
  20.7 3.6 %collective-permute-start.5 = (f32[1024,128]{1,0:T(8,128)S(1)}, f32[1024,128]{1,0:T(8,128)S(1)}, u32[]{:S(2)}, u32[]{:S(2)}) collective-permute-start(f32[1024,128]{1,0:T(8,128)S(1)} %get-tuple-element.70.part_p), channel_id=1, source_target_pairs={{1,2},{3,4},{5,6},{7,8},{9,10},{11,12},{13,14},{15,16},{17,18},{19... | collective-permute-start | bytes 1572872 | tf_op jit(solution)/shard_map/ppermute | solution.py:421
  24.3 1.5 %early.1.early_ref = f32[2,8,256]{2,1,0:T(8,128)S(1)} custom-call(s32[1]{0:T(128)} %bitcast.at_far.at_ref, s32[2,256]{1,0:T(2,128)S(1)} %copy-done, f32[2,512,128]{2,1,0:T(8,128)S(1)} %get-tuple-element.64.p.po.before, f32[2,512,128]{2,1,0:T(8,128)S(1)} %get-tuple-element.59.cs_ref, f32[2,512,128]{2,1,0:T(8,128)S(1)} %get-tuple-element.60.ck_ref), custom_call_target="tpu_custom_call" | custom-call | flops 1000000 | bytes 1591300 | tf_op jit(solution)/shard_map/early/pallas_call | solution.py:32
  25.8 2.1 %collective-permute-done.2.got.extra = f32[1552,128]{1,0:T(8,128)S(1)} collective-permute-done((f32[1552,128]{1,0:T(8,128)S(1)}, f32[1552,128]{1,0:T(8,128)S(1)}, u32[]{:S(2)}, u32[]{:S(2)}) %collective-permute-start.2) | collective-permute-done | bytes 794656 | tf_op jit(solution)/shard_map/ppermute | solution.py:421
  27.9 5.6 %collective-permute-done.5.got = f32[1024,128]{1,0:T(8,128)S(1)} collective-permute-done((f32[1024,128]{1,0:T(8,128)S(1)}, f32[1024,128]{1,0:T(8,128)S(1)}, u32[]{:S(2)}, u32[]{:S(2)}) %collective-permute-start.5) | collective-permute-done | bytes 524320 | tf_op jit(solution)/shard_map/ppermute | solution.py:421
  33.5 0.4 join1.1
  34.2 2.5 %local2.1 = (f32[2,512,128]{2,1,0:T(8,128)S(1)}, f32[2,512,128]{2,1,0:T(8,128)S(1)}, f32[2,8,256]{2,1,0:T(8,128)S(1)}) custom-call(s32[1]{0:T(128)} %bitcast.at_far.at_ref, s32[2]{0:T(128)S(1)} %copy-done.2, f32[2,4]{1,0:T(2,128)S(1)} %copy-done.1, f32[2,512,128]{2,1,0:T(8,128)S(1)} %get-tuple-element.73.p.po.before, ...), custom_call_target="tpu_custom_call" | custom-call | flops 1000000 | bytes 4753452 | tf_op jit(solution)/shard_map/local2/pallas_call | solution.py:32
  37.0 0.4 join2.1
  37.4 2.2 %late.1 = f32[2,8,256]{2,1,0:T(8,128)S(1)} custom-call(s32[1]{0:T(128)} %bitcast.at_far.at_ref, s32[2]{0:T(128)S(1)} %copy-done.2, f32[2,4]{1,0:T(2,128)S(1)} %copy-done.1, s32[2,256]{1,0:T(2,128)S(1)} %copy-done, f32[2,8,256]{2,1,0:T(8,128)S(1)} %get-tuple-element.76.early_ref, f32[2,512,128]{2,1,0:T(8,128)S(1)} %get-tuple-element.82.p, ...), custom_call_target="tpu_custom_call" | custom-call | flops 100000000 | bytes 1083436 | tf_op jit(solution)/shard_map/late/pallas_call | solution.py:32
  39.6 8.1 %collective-permute-start.7 = (f32[2,8,256]{2,1,0:T(8,128)S(1)}, f32[2,8,256]{2,1,0:T(8,128)S(1)}, u32[]{:S(2)}, u32[]{:S(2)}) collective-permute-start(f32[2,8,256]{2,1,0:T(8,128)S(1)} %late.1), channel_id=1, source_target_pairs={{0,16},{1,17},{2,18},{3,19},{4,20},{5,21},{6,22},{7,23},{8,24},{9,... | collective-permute-start | bytes 49160 | tf_op jit(solution)/shard_map/ppermute | solution.py:388
  47.7 9.4 %collective-permute-start.8 = (f32[2,8,256]{2,1,0:T(8,128)S(1)}, f32[2,8,256]{2,1,0:T(8,128)S(1)}, u32[]{:S(2)}, u32[]{:S(2)}) collective-permute-start(f32[2,8,256]{2,1,0:T(8,128)S(1)} %late.1), channel_id=1, source_target_pairs={{0,112},{1,113},{2,114},{3,115},{4,116},{5,117},{6,118},{7,119},{8... | collective-permute-start | bytes 49160 | tf_op jit(solution)/shard_map/ppermute | solution.py:388
  57.1 0.6 collective-permute-start.15
  57.6 1.9 %collective-permute-start.14 = (f32[1024,128]{1,0:T(8,128)S(1)}, f32[1024,128]{1,0:T(8,128)S(1)}, u32[]{:S(2)}, u32[]{:S(2)}) collective-permute-start(f32[1024,128]{1,0:T(8,128)S(1)} %get-tuple-element.80.part_p), channel_id=1, source_target_pairs={{1,2},{3,4},{5,6},{7,8},{9,10},{11,12},{13,14},{15,16},{17,18},{19... | collective-permute-start | bytes 1572872 | tf_op jit(solution)/shard_map/ppermute | solution.py:421
  59.6 1.7 %collective-permute-start.9 = (f32[2,8,256]{2,1,0:T(8,128)S(1)}, f32[2,8,256]{2,1,0:T(8,128)S(1)}, u32[]{:S(2)}, u32[]{:S(2)}) collective-permute-start(f32[2,8,256]{2,1,0:T(8,128)S(1)} %fusion.2), channel_id=1, source_target_pairs={{0,48},{1,49},{2,50},{3,51},{4,52},{5,53},{6,54},{7,55},{8,56},{9,... | collective-permute-start | bytes 49160 | tf_op jit(solution)/shard_map/ppermute | solution.py:392
  61.4 2.7 %collective-permute-done.9 = f32[2,8,256]{2,1,0:T(8,128)S(1)} collective-permute-done((f32[2,8,256]{2,1,0:T(8,128)S(1)}, f32[2,8,256]{2,1,0:T(8,128)S(1)}, u32[]{:S(2)}, u32[]{:S(2)}) %collective-permute-start.9) | collective-permute-done | bytes 16416 | tf_op jit(solution)/shard_map/ppermute | solution.py:392
  64.1 2.9 %collective-permute-done.10 = f32[2,8,256]{2,1,0:T(8,128)S(1)} collective-permute-done((f32[2,8,256]{2,1,0:T(8,128)S(1)}, f32[2,8,256]{2,1,0:T(8,128)S(1)}, u32[]{:S(2)}, u32[]{:S(2)}) %collective-permute-start.10) | collective-permute-done | bytes 16416 | tf_op jit(solution)/shard_map/ppermute | solution.py:393
  67.1 3.1 %collective-permute-start.13 = (f32[2,8,256]{2,1,0:T(8,128)S(1)}, f32[2,8,256]{2,1,0:T(8,128)S(1)}, u32[]{:S(2)}, u32[]{:S(2)}) collective-permute-start(f32[2,8,256]{2,1,0:T(8,128)S(1)} %add_add_fusion.2), channel_id=1, source_target_pairs={{0,4},{1,5},{2,6},{3,7},{4,0},{5,1},{6,2},{7,3},{8,12},{9,13},{10,... | collective-permute-start | bytes 49160 | tf_op jit(solution)/shard_map/ppermute | solution.py:375
  70.2 1.9 %local3.1 = (f32[2,512,128]{2,1,0:T(8,128)S(1)}, f32[2,512,128]{2,1,0:T(8,128)S(1)}) custom-call(s32[1]{0:T(128)} %bitcast.at_far.at_ref, s32[2]{0:T(128)S(1)} %copy-done.2, f32[2,4]{1,0:T(2,128)S(1)} %copy-done.1, f32[2,512,128]{2,1,0:T(8,128)S(1)} %get-tuple-element.82.p, f32[2,512,128]{2,1,0:T(8,128)S(1)} %get-tuple-element.73.p.po.before, ...), custom_call_target="tpu_custom_call" | custom-call | flops 1000000 | bytes 4718636 | tf_op jit(solution)/shard_map/local3/pallas_call | solution.py:32
  72.4 5.7 %collective-permute-start.16 = (f32[2,8,256]{2,1,0:T(8,128)S(1)}, f32[2,8,256]{2,1,0:T(8,128)S(1)}, u32[]{:S(2)}, u32[]{:S(2)}) collective-permute-start(f32[2,8,256]{2,1,0:T(8,128)S(1)} %add_add_fusion.1), channel_id=1, source_target_pairs={{0,1},{1,0},{2,3},{3,2},{4,5},{5,4},{6,7},{7,6},{8,9},{9,8},{10,11... | collective-permute-start | bytes 49160 | tf_op jit(solution)/shard_map/ppermute | solution.py:375
  78.2 0.9 %collective-permute-start.17 = (f32[2,8,256]{2,1,0:T(8,128)S(1)}, f32[2,8,256]{2,1,0:T(8,128)S(1)}, u32[]{:S(2)}, u32[]{:S(2)}) collective-permute-start(f32[2,8,256]{2,1,0:T(8,128)S(1)} %add_add_fusion.1), channel_id=1, source_target_pairs={{0,8},{1,9},{2,10},{3,11},{4,12},{5,13},{6,14},{7,15},{8,0},{9,1},... | collective-permute-start | bytes 49160 | tf_op jit(solution)/shard_map/ppermute | solution.py:375
  79.1 2.4 %collective-permute-start.18 = (f32[2,8,256]{2,1,0:T(8,128)S(1)}, f32[2,8,256]{2,1,0:T(8,128)S(1)}, u32[]{:S(2)}, u32[]{:S(2)}) collective-permute-start(f32[2,8,256]{2,1,0:T(8,128)S(1)} %add_add_fusion.1), channel_id=1, source_target_pairs={{0,9},{1,8},{2,11},{3,10},{4,13},{5,12},{6,15},{7,14},{8,1},{9,0},... | collective-permute-start | bytes 49160 | tf_op jit(solution)/shard_map/ppermute | solution.py:375
  81.4 1.4 %join3.1 = (f32[2,512,128]{2,1,0:T(8,128)}, f32[2,512,128]{2,1,0:T(8,128)}) custom-call(s32[8,128]{1,0:T(8,128)S(1)} %get-tuple-element.49.odd_ref, f32[1024,128]{1,0:T(8,128)S(1)} %collective-permute-done.14.got, f32[1552,128]{1,0:T(8,128)S(1)} %collective-permute-done.2.got.extra, f32[2,512,128]{2,1,0:T(8,128)S(1)} %get-tuple-element.73.p.po.before, ...), custom_call_target="tpu_custom_call" | custom-call | flops 20000000000 | bytes 4993024 | tf_op jit(solution)/shard_map/join3/pallas_call | solution.py:32
  82.8 1.4 %collective-permute-done.18 = f32[2,8,256]{2,1,0:T(8,128)S(1)} collective-permute-done((f32[2,8,256]{2,1,0:T(8,128)S(1)}, f32[2,8,256]{2,1,0:T(8,128)S(1)}, u32[]{:S(2)}, u32[]{:S(2)}) %collective-permute-start.18) | collective-permute-done | bytes 16416 | tf_op jit(solution)/shard_map/ppermute | solution.py:375
  84.2 0.6 pad_maximum_fusion
  (38 shorter events, 1.8 us)
Async XLA Ops:
  0.6 7.6 %copy-start.3 = (s32[2,1]{0,1:T(1,128)S(1)}, s32[2,1]{0,1:T(1,128)}, u32[]{:S(2)}) copy-start(s32[2,1]{0,1:T(1,128)} %param.18) | copy-start | bytes 28
  2.0 10.1 %collective-permute-start.1 = (f32[3,256,128]{2,1,0:T(8,128)S(1)}, f32[3,256,128]{2,1,0:T(8,128)S(1)}, u32[]{:S(2)}, u32[]{:S(2)}) collective-permute-start(f32[3,256,128]{2,1,0:T(8,128)S(1)} %get-tuple-element.52.own), channel_id=1, source_target_pairs={{0,128},{128,0},{1,129},{129,1},{2,130},{130,2},{3,131},{131,3},{4... | collective-permute-start | bytes 1179656 | tf_op jit(solution)/shard_map/ppermute | solution.py:423
  4.1 8.3 %collective-permute-start = (f32[2,512,128]{2,1,0:T(8,128)S(1)}, f32[2,512,128]{2,1,0:T(8,128)S(1)}, u32[]{:S(2)}, u32[]{:S(2)}) collective-permute-start(f32[2,512,128]{2,1,0:T(8,128)S(1)} %get-tuple-element.50.p0.po.before), channel_id=1, source_target_pairs={{0,1},{1,0},{2,3},{3,2},{4,5},{5,4},{6,7},{7,6},{8,9},{9,8},{10,11... | collective-permute-start | bytes 1572872 | tf_op jit(solution)/shard_map/ppermute | solution.py:418
  5.4 12.7 %collective-permute-start.3 = (f32[2,512,128]{2,1,0:T(8,128)S(1)}, f32[2,512,128]{2,1,0:T(8,128)S(1)}, u32[]{:S(2)}, u32[]{:S(2)}) collective-permute-start(f32[2,512,128]{2,1,0:T(8,128)S(1)} %get-tuple-element.50.p0.po.before), channel_id=1, source_target_pairs={{1,2},{3,4},{5,6},{7,8},{9,10},{11,12},{13,14},{15,16},{17,18},{19... | collective-permute-start | bytes 1572872 | tf_op jit(solution)/shard_map/ppermute | solution.py:421
  8.2 0.7 copy-start.1
  8.2 0.7 copy-start.2
  12.7 15.1 %collective-permute-start.2 = (f32[1552,128]{1,0:T(8,128)S(1)}, f32[1552,128]{1,0:T(8,128)S(1)}, u32[]{:S(2)}, u32[]{:S(2)}) collective-permute-start(f32[1552,128]{1,0:T(8,128)S(1)} %get-tuple-element.62.part_p), channel_id=1, source_target_pairs={{1,2},{3,4},{5,6},{7,8},{9,10},{11,12},{13,14},{15,16},{17,18},{19... | collective-permute-start | bytes 2383880 | tf_op jit(solution)/shard_map/ppermute | solution.py:421
  18.4 2.1 %collective-permute-start.4 = (f32[2,512,128]{2,1,0:T(8,128)S(1)}, f32[2,512,128]{2,1,0:T(8,128)S(1)}, u32[]{:S(2)}, u32[]{:S(2)}) collective-permute-start(f32[2,512,128]{2,1,0:T(8,128)S(1)} %get-tuple-element.64.p.po.before), channel_id=1, source_target_pairs={{0,1},{1,0},{2,3},{3,2},{4,5},{5,4},{6,7},{7,6},{8,9},{9,8},{10,11... | collective-permute-start | bytes 1572872 | tf_op jit(solution)/shard_map/ppermute | solution.py:418
  20.4 3.8 %copy-start = (s32[2,256]{1,0:T(2,128)S(1)}, s32[2,256]{1,0:T(2,128)}, u32[]{:S(2)}) copy-start(s32[2,256]{1,0:T(2,128)} %cells_ref.5) | copy-start | bytes 6148
  20.7 12.8 %collective-permute-start.5 = (f32[1024,128]{1,0:T(8,128)S(1)}, f32[1024,128]{1,0:T(8,128)S(1)}, u32[]{:S(2)}, u32[]{:S(2)}) collective-permute-start(f32[1024,128]{1,0:T(8,128)S(1)} %get-tuple-element.70.part_p), channel_id=1, source_target_pairs={{1,2},{3,4},{5,6},{7,8},{9,10},{11,12},{13,14},{15,16},{17,18},{19... | collective-permute-start | bytes 1572872 | tf_op jit(solution)/shard_map/ppermute | solution.py:421
  33.9 2.8 %collective-permute-start.6 = (f32[2,512,128]{2,1,0:T(8,128)S(1)}, f32[2,512,128]{2,1,0:T(8,128)S(1)}, u32[]{:S(2)}, u32[]{:S(2)}) collective-permute-start(f32[2,512,128]{2,1,0:T(8,128)S(1)} %get-tuple-element.73.p.po.before), channel_id=1, source_target_pairs={{0,1},{1,0},{2,3},{3,2},{4,5},{5,4},{6,7},{7,6},{8,9},{9,8},{10,11... | collective-permute-start | bytes 1572872 | tf_op jit(solution)/shard_map/ppermute | solution.py:418
  39.6 20.0 %collective-permute-start.7 = (f32[2,8,256]{2,1,0:T(8,128)S(1)}, f32[2,8,256]{2,1,0:T(8,128)S(1)}, u32[]{:S(2)}, u32[]{:S(2)}) collective-permute-start(f32[2,8,256]{2,1,0:T(8,128)S(1)} %late.1), channel_id=1, source_target_pairs={{0,16},{1,17},{2,18},{3,19},{4,20},{5,21},{6,22},{7,23},{8,24},{9,... | collective-permute-start | bytes 49160 | tf_op jit(solution)/shard_map/ppermute | solution.py:388
  47.7 11.9 %collective-permute-start.8 = (f32[2,8,256]{2,1,0:T(8,128)S(1)}, f32[2,8,256]{2,1,0:T(8,128)S(1)}, u32[]{:S(2)}, u32[]{:S(2)}) collective-permute-start(f32[2,8,256]{2,1,0:T(8,128)S(1)} %late.1), channel_id=1, source_target_pairs={{0,112},{1,113},{2,114},{3,115},{4,116},{5,117},{6,118},{7,119},{8... | collective-permute-start | bytes 49160 | tf_op jit(solution)/shard_map/ppermute | solution.py:388
  57.1 15.1 %collective-permute-start.15 = (f32[2,512,128]{2,1,0:T(8,128)S(1)}, f32[2,512,128]{2,1,0:T(8,128)S(1)}, u32[]{:S(2)}, u32[]{:S(2)}) collective-permute-start(f32[2,512,128]{2,1,0:T(8,128)S(1)} %get-tuple-element.82.p), channel_id=1, source_target_pairs={{0,1},{1,0},{2,3},{3,2},{4,5},{5,4},{6,7},{7,6},{8,9},{9,8},{10,11... | collective-permute-start | bytes 1572872 | tf_op jit(solution)/shard_map/ppermute | solution.py:418
  57.6 14.8 %collective-permute-start.14 = (f32[1024,128]{1,0:T(8,128)S(1)}, f32[1024,128]{1,0:T(8,128)S(1)}, u32[]{:S(2)}, u32[]{:S(2)}) collective-permute-start(f32[1024,128]{1,0:T(8,128)S(1)} %get-tuple-element.80.part_p), channel_id=1, source_target_pairs={{1,2},{3,4},{5,6},{7,8},{9,10},{11,12},{13,14},{15,16},{17,18},{19... | collective-permute-start | bytes 1572872 | tf_op jit(solution)/shard_map/ppermute | solution.py:421
  59.6 4.5 %collective-permute-start.9 = (f32[2,8,256]{2,1,0:T(8,128)S(1)}, f32[2,8,256]{2,1,0:T(8,128)S(1)}, u32[]{:S(2)}, u32[]{:S(2)}) collective-permute-start(f32[2,8,256]{2,1,0:T(8,128)S(1)} %fusion.2), channel_id=1, source_target_pairs={{0,48},{1,49},{2,50},{3,51},{4,52},{5,53},{6,54},{7,55},{8,56},{9,... | collective-permute-start | bytes 49160 | tf_op jit(solution)/shard_map/ppermute | solution.py:392
  61.3 5.6 %collective-permute-start.10 = (f32[2,8,256]{2,1,0:T(8,128)S(1)}, f32[2,8,256]{2,1,0:T(8,128)S(1)}, u32[]{:S(2)}, u32[]{:S(2)}) collective-permute-start(f32[2,8,256]{2,1,0:T(8,128)S(1)} %get-tuple-element.98), channel_id=1, source_target_pairs={{0,80},{1,81},{2,82},{3,83},{4,84},{5,85},{6,86},{7,87},{8,88},{9,... | collective-permute-start | bytes 49160 | tf_op jit(solution)/shard_map/ppermute | solution.py:393
  66.9 5.2 %collective-permute-start.11 = (f32[2,8,256]{2,1,0:T(8,128)S(1)}, f32[2,8,256]{2,1,0:T(8,128)S(1)}, u32[]{:S(2)}, u32[]{:S(2)}) collective-permute-start(f32[2,8,256]{2,1,0:T(8,128)S(1)} %add_add_fusion.2), channel_id=1, source_target_pairs={{0,2},{1,3},{2,0},{3,1},{4,6},{5,7},{6,4},{7,5},{8,10},{9,11},{10,... | collective-permute-start | bytes 49160 | tf_op jit(solution)/shard_map/ppermute | solution.py:375
  67.0 5.2 %collective-permute-start.12 = (f32[2,8,256]{2,1,0:T(8,128)S(1)}, f32[2,8,256]{2,1,0:T(8,128)S(1)}, u32[]{:S(2)}, u32[]{:S(2)}) collective-permute-start(f32[2,8,256]{2,1,0:T(8,128)S(1)} %add_add_fusion.2), channel_id=1, source_target_pairs={{0,6},{1,7},{2,4},{3,5},{4,2},{5,3},{6,0},{7,1},{8,14},{9,15},{10,... | collective-permute-start | bytes 49160 | tf_op jit(solution)/shard_map/ppermute | solution.py:375
  67.1 5.1 %collective-permute-start.13 = (f32[2,8,256]{2,1,0:T(8,128)S(1)}, f32[2,8,256]{2,1,0:T(8,128)S(1)}, u32[]{:S(2)}, u32[]{:S(2)}) collective-permute-start(f32[2,8,256]{2,1,0:T(8,128)S(1)} %add_add_fusion.2), channel_id=1, source_target_pairs={{0,4},{1,5},{2,6},{3,7},{4,0},{5,1},{6,2},{7,3},{8,12},{9,13},{10,... | collective-permute-start | bytes 49160 | tf_op jit(solution)/shard_map/ppermute | solution.py:375
  72.4 10.4 %collective-permute-start.16 = (f32[2,8,256]{2,1,0:T(8,128)S(1)}, f32[2,8,256]{2,1,0:T(8,128)S(1)}, u32[]{:S(2)}, u32[]{:S(2)}) collective-permute-start(f32[2,8,256]{2,1,0:T(8,128)S(1)} %add_add_fusion.1), channel_id=1, source_target_pairs={{0,1},{1,0},{2,3},{3,2},{4,5},{5,4},{6,7},{7,6},{8,9},{9,8},{10,11... | collective-permute-start | bytes 49160 | tf_op jit(solution)/shard_map/ppermute | solution.py:375
  78.2 4.6 %collective-permute-start.17 = (f32[2,8,256]{2,1,0:T(8,128)S(1)}, f32[2,8,256]{2,1,0:T(8,128)S(1)}, u32[]{:S(2)}, u32[]{:S(2)}) collective-permute-start(f32[2,8,256]{2,1,0:T(8,128)S(1)} %add_add_fusion.1), channel_id=1, source_target_pairs={{0,8},{1,9},{2,10},{3,11},{4,12},{5,13},{6,14},{7,15},{8,0},{9,1},... | collective-permute-start | bytes 49160 | tf_op jit(solution)/shard_map/ppermute | solution.py:375
  79.1 5.1 %collective-permute-start.18 = (f32[2,8,256]{2,1,0:T(8,128)S(1)}, f32[2,8,256]{2,1,0:T(8,128)S(1)}, u32[]{:S(2)}, u32[]{:S(2)}) collective-permute-start(f32[2,8,256]{2,1,0:T(8,128)S(1)} %add_add_fusion.1), channel_id=1, source_target_pairs={{0,9},{1,8},{2,11},{3,10},{4,13},{5,12},{6,15},{7,14},{8,1},{9,0},... | collective-permute-start | bytes 49160 | tf_op jit(solution)/shard_map/ppermute | solution.py:375
